TPU v7x, 32 devices: a whole 2x2x4 slice. The times are simulated.
32 devices in a mesh: cls: 4 (over x, core), lvl: 8 (over z, y).
Axes of the slice: x: 2, y: 2, z: 4, core: 2. Of those that a mesh axis runs over, the one named last changes fastest.
Arguments:
- occupancy: float32 [8, 256, 256, 256], P('lvl', 'cls'), may hold values from 0.1 to 10
- rates: float32 [3, 256, 256], replicated, may hold values from 0.01 to 1
- increments: int32 [3, 256], replicated, may hold values from 0 to 1
- draw: int32 [256], replicated, may hold values from 1 to 2
- crusher_rate: float32 [256], replicated, may hold values from 2 to 60
- bounds: int32 [2], replicated, may hold values from -2 to 8, as said below
Outputs:
- new_occupancy: float32 [8, 256, 256, 256], P('lvl', 'cls')
Inputs may be any that keep to these rules, and one draw needn't show every extreme that they name: bounds[0] is at most 0 and bounds[1] is at least 7.
All inputs are finite; a program needn't handle non-finite values.
Results may differ from a plain program's by a relative error of at most 0.0003.
Values sent between devices are 32-bit elements; how exact they have to be, the bound alone decides.
No kernel may reach another device: no remote copies, remote signals or barrier semaphores. Data moves between devices by JAX's collectives and lax.ppermute only.
A program may use at most 320 MiB of HBM per device.

v0:
```python
import jax
import jax.numpy as jnp
from jax import lax
from jax.sharding import PartitionSpec as P


def passed_along(shard, axis, by):
    length = lax.axis_size(axis)
    pairs = [(i, i + by) for i in range(length) if 0 <= i + by < length]
    return lax.ppermute(shard, axis, pairs)


def paired(rates_k, inc_k):
    stay_rows = rates_k * jnp.where(inc_k == 0, 1.0, 0.0).astype(jnp.float32)[:, None]
    rise_rows = rates_k * jnp.where(inc_k == 1, 1.0, 0.0).astype(jnp.float32)[:, None]
    return jnp.concatenate([stay_rows, rise_rows], axis=1)


def flag(cond):
    return jnp.where(cond, 1.0, 0.0).astype(jnp.float32)


def lift_level(values):
    return passed_along(values, "lvl", 1)


def local(occupancy, rates, increments, draw, crusher_rate, bounds):
    local_a = occupancy.shape[1]
    phases = occupancy.shape[3]
    level = lax.axis_index("lvl")
    start = lax.axis_index("cls") * local_a
    bottom = bounds[0]
    top = bounds[1]
    highest = lax.Precision.HIGHEST
    row_total = jnp.sum(rates, axis=2)
    uniform_rate = jnp.sum(jnp.max(row_total, axis=1)) + jnp.max(crusher_rate)
    out_rows = row_total * flag((increments == 0) | (level + increments <= top))
    drop_ok = flag(level - draw >= bottom)
    out_first = lax.dynamic_slice_in_dim(out_rows[0], start, local_a)
    outflow = (
        out_first[None, :, None, None]
        + out_rows[1][None, None, :, None]
        + (out_rows[2] + crusher_rate * drop_ok)[None, None, None, :]
    )
    rise_ok = flag(level + 1 <= top)
    fall_once = (crusher_rate * flag(draw == 1) * drop_ok)[None, None, None, :]
    fall_twice = (crusher_rate * flag(draw == 2) * drop_ok)[None, None, None, :]
    cat_a = paired(rates[0], increments[0])
    cat_b = paired(rates[1], increments[1])
    cat_c = paired(rates[2], increments[2])
    state = occupancy
    both = jnp.einsum(
        "labc,ax->lxbc",
        lax.all_to_all(state, "cls", split_axis=2, concat_axis=1, tiled=True),
        cat_a,
        precision=highest,
    )
    stay_a = both[:, :phases]
    rise_a = both[:, phases:]
    both_b = jnp.einsum("labc,bx->laxc", state, cat_b, precision=highest)
    both_c = jnp.dot(state.reshape(-1, phases), cat_c, precision=highest).reshape(
        state.shape[0], local_a, phases, 2 * phases
    )
    stay_local = both_b[:, :, :phases] + both_c[:, :, :, :phases]
    rise_local = both_b[:, :, phases:] + both_c[:, :, :, phases:]
    once = state * fall_once
    twice = state * fall_twice
    fallen = passed_along(once, "lvl", -1) + passed_along(twice, "lvl", -2)
    home_stay = lax.all_to_all(stay_a, "cls", split_axis=1, concat_axis=2, tiled=True)
    home_rise = lax.all_to_all(rise_a, "cls", split_axis=1, concat_axis=2, tiled=True)
    inflow = home_stay + stay_local + lift_level((home_rise + rise_local) * rise_ok)
    state = state + (inflow + fallen - outflow * state) / uniform_rate
    return state


def solution(mesh):
    in_specs = (P("lvl", "cls", None, None), P(), P(), P(), P(), P())
    out_specs = P("lvl", "cls", None, None)
    return jax.shard_map(local, mesh=mesh, in_specs=in_specs, out_specs=out_specs, check_vma=False)
```

profile of v0, /device:TPU:21, one launch (start us, length us, event | category | flops | bytes accessed | tf_op | source)
XLA Modules:
  0.0 1078.9 jit_solution(256191854163879559)
XLA Ops:
  0.0 17.8 %copy.14 = f32[1,64,256,256]{3,1,0,2:T(8,128)} copy(f32[1,64,256,256]{3,2,1,0:T(8,128)} %param.6) | data formatting | bytes 33554432 | tf_op args[0]
  17.8 0.0 copy-start
  17.8 0.0 copy-start.1
  17.8 7.9 all-to-all-start
  25.7 0.0 copy-done
  25.8 0.1 copy.22
  25.9 0.0 copy-done.1
  26.0 181.9 %all-to-all-done = f32[1,64,256,256]{3,1,0,2:T(8,128)} async-done(((f32[1,64,256,256]{3,1,0,2:T(8,128)}), f32[1,64,256,256]{3,1,0,2:T(8,128)}, u32[]{:S(2)}, u32[]{:S(2)}) %all-to-all-start) | async-done | bytes 16777248 | tf_op jit(solution)/shard_map/all_to_all | solution.py:54
  207.9 6.6 copy.15
  214.5 30.9 %convolution_bitcast_fusion.1 = f32[1,512,64,256]{3,1,2,0:T(8,128)} fusion(f32[256,64,256]{2,0,1:T(8,128)S(1)} %bitcast.61, f32[256,256]{0,1:T(8,128)S(1)} %get-tuple-element.14, f32[256,256]{0,1:T(8,128)S(1)} %get-tuple-element.13), kind=kOutput, calls=%fused_computation.14 | convolution fusion | flops 25769934848 | bytes 50855936 | tf_op jit(solution)/shard_map/labc,ax->lxbc/dot_general | solution.py:52
  245.4 17.9 %fusion.28 = (f32[1,256,64,256]{3,1,2,0:T(8,128)}, f32[1,256,64,256]{3,1,2,0:T(8,128)S(1)}) fusion(f32[1,512,64,256]{3,1,2,0:T(8,128)} %convolution_bitcast_fusion.1), kind=kLoop, calls=%fused_computation.54 | loop fusion | bytes 67108864 | tf_op jit(solution)/shard_map/slice | solution.py:58
  263.4 20.2 %copy.20 = f32[1,256,64,256]{3,2,0,1:T(8,128)} copy(f32[1,256,64,256]{3,1,2,0:T(8,128)S(1)} %get-tuple-element.6) | data formatting | bytes 33554432 | tf_op jit(solution)/shard_map/slice | solution.py:59
  283.6 0.0 copy-start.2
  283.6 0.0 copy-start.3
  283.6 0.0 copy-start.4
  283.6 8.0 all-to-all-start.2
  291.5 0.2 reduce_sum.18
  291.7 0.0 copy-done.2
  291.7 0.6 fusion.31
  292.3 0.7 select_multiply_fusion
  293.1 0.0 copy-done.3
  293.1 0.0 copy-done.4
  293.1 1.2 multiply_add_fusion
  294.3 16.9 %broadcast_multiply_fusion = (f32[1,64,256,256]{3,2,1,0:T(8,128)}, f32[1,64,256,256]{3,2,1,0:T(8,128)}) fusion(f32[1,64,256,256]{3,2,1,0:T(8,128)} %param.6, f32[256]{0:T(256)S(1)} %get-tuple-element.29, f32[256]{0:T(256)S(1)} %get-tuple-element.30), kind=kLoop, calls=%fused_computation.15 | loop fusion | flops 8388608 | bytes 50333696 | tf_op jit(solution)/shard_map/mul | solution.py:67
  311.2 2.1 collective-permute-start.1
  313.3 2.1 collective-permute-start.2
  315.4 0.1 copy.23
  315.5 0.1 bitcast_multiply_fusion.1
  315.7 59.2 %convolution_bitcast_fusion = f32[16384,512]{0,1:T(8,128)} fusion(f32[16384,256]{1,0:T(8,128)} %bitcast.58, f32[256,256]{1,0:T(8,128)S(1)} %get-tuple-element.12, f32[256,256]{1,0:T(8,128)S(1)} %get-tuple-element.11), kind=kOutput, calls=%fused_computation | convolution fusion | flops 25769934848 | bytes 50855936 | tf_op jit(solution)/shard_map/dot_general | solution.py:61
  374.9 33.4 %copy.19 = f32[16384,512]{1,0:T(8,128)} copy(f32[16384,512]{0,1:T(8,128)} %convolution_bitcast_fusion) | data formatting | bytes 67108864 | tf_op jit(solution)/shard_map/dot_general | solution.py:61
  409.0 33.1 %fusion.10 = f32[1,64,512,256]{3,2,1,0:T(8,128)} fusion(f32[1,64,256,256]{3,2,1,0:T(8,128)} %param.6, f32[256,256]{0,1:T(8,128)S(1)} %get-tuple-element.16, f32[256,256]{0,1:T(8,128)S(1)} %get-tuple-element.15), kind=kOutput, calls=%fused_computation.13 | convolution fusion | flops 25769934848 | bytes 50855936 | tf_op jit(solution)/shard_map/labc,bx->laxc/dot_general | solution.py:60
  442.1 31.7 %all-to-all-done.2 = f32[1,256,64,256]{3,2,0,1:T(8,128)} async-done(((f32[1,256,64,256]{3,2,0,1:T(8,128)}), f32[1,256,64,256]{3,2,0,1:T(8,128)}, u32[]{:S(2)}, u32[]{:S(2)}) %all-to-all-start.2) | async-done | bytes 16777248 | tf_op jit(solution)/shard_map/all_to_all | solution.py:70
  473.7 6.5 copy.21
  480.3 17.6 %fusion.1 = f32[1,64,256,256]{3,2,1,0:T(8,128)} fusion(f32[1,64,256,512]{3,2,1,0:T(8,128)} %bitcast.59, f32[1,64,512,256]{3,2,1,0:T(8,128)} %fusion.10, f32[1,4,64,64,256]{4,3,1,2,0:T(8,128)S(1)} %copy.21, f32[]{:T(128)S(6)} %select_n.93), kind=kLoop, calls=%fused_computation.3 | loop fusion | flops 12582912 | bytes 67108864 | tf_op jit(solution)/shard_map/mul | solution.py:71
  497.9 3.1 collective-permute-start
  501.0 17.9 %copy.16 = f32[1,256,64,256]{3,2,0,1:T(8,128)} copy(f32[1,256,64,256]{3,1,2,0:T(8,128)} %get-tuple-element.5) | data formatting | bytes 33554432 | tf_op jit(solution)/shard_map/slice | solution.py:58
  519.0 8.2 all-to-all-start.1
  527.2 0.6 reduce_sum.19
  529.0 0.1 dynamic-slice_bitcast_fusion
  529.1 0.1 broadcast_add_fusion
  529.2 180.2 %all-to-all-done.1 = f32[1,256,64,256]{3,2,0,1:T(8,128)} async-done(((f32[1,256,64,256]{3,2,0,1:T(8,128)}), f32[1,256,64,256]{3,2,0,1:T(8,128)}, u32[]{:S(2)}, u32[]{:S(2)}) %all-to-all-start.1) | async-done | bytes 16777248 | tf_op jit(solution)/shard_map/all_to_all | solution.py:69
  709.4 11.6 %copy.17 = f32[1,4,64,64,256]{4,3,1,2,0:T(8,128)} copy(f32[1,4,64,64,256]{4,3,2,1,0:T(8,128)} %bitcast.8) | data formatting | bytes 33554432 | tf_op jit(solution)/shard_map/all_to_all | solution.py:69
  721.0 311.7 %collective-permute-done.1 = f32[1,64,256,256]{3,2,1,0:T(8,128)} collective-permute-done((f32[1,64,256,256]{3,2,1,0:T(8,128)}, f32[1,64,256,256]{3,2,1,0:T(8,128)}, u32[]{:S(2)}, u32[]{:S(2)}) %collective-permute-start.1) | collective-permute-done | bytes 16777248 | tf_op jit(solution)/shard_map/ppermute | solution.py:10
  1032.7 0.0 collective-permute-done.2
  1032.7 3.2 collective-permute-done
  1035.9 42.7 %fusion.7 = f32[1,64,256,256]{3,2,1,0:T(8,128)} fusion(f32[1,64,256,256]{3,2,1,0:T(8,128)} %param.6, f32[1,64,256,256]{3,2,1,0:T(8,128)} %collective-permute-done, f32[1,64,256,512]{3,2,1,0:T(8,128)} %bitcast.60, f32[1,64,512,256]{3,2,1,0:T(8,128)} %fusion.10, f32[1,4,64,64,256]{4,3,1,2,0:T(8,128)} %copy.17, f32[1,64,256,256]{3,2,1,0:T(8,128)} %collective-permute-done.1, ...), kind=kLoop, calls=%fused_computation.10 | loop fusion | flops 41943040 | bytes 134284288 | tf_op jit(solution)/shard_map/add | solution.py:72
  (5 shorter events, 0.1 us)
Async XLA Ops:
  17.8 7.9 copy-start
  17.8 8.1 copy-start.1
  17.8 190.1 %all-to-all-start = ((f32[1,64,256,256]{3,1,0,2:T(8,128)}), f32[1,64,256,256]{3,1,0,2:T(8,128)}, u32[]{:S(2)}, u32[]{:S(2)}) async-start(f32[1,64,256,256]{3,1,0,2:T(8,128)} %copy.14), calls=%async_computation | async-start | bytes 33554432 | tf_op jit(solution)/shard_map/all_to_all | solution.py:54
  283.6 8.1 copy-start.2
  283.6 9.5 copy-start.3
  283.6 9.5 copy-start.4
  283.6 190.2 %all-to-all-start.2 = ((f32[1,256,64,256]{3,2,0,1:T(8,128)}), f32[1,256,64,256]{3,2,0,1:T(8,128)}, u32[]{:S(2)}, u32[]{:S(2)}) async-start(f32[1,256,64,256]{3,2,0,1:T(8,128)} %copy.20), calls=%async_computation.2 | async-start | bytes 33554432 | tf_op jit(solution)/shard_map/all_to_all | solution.py:70
  311.2 721.5 %collective-permute-start.1 = (f32[1,64,256,256]{3,2,1,0:T(8,128)}, f32[1,64,256,256]{3,2,1,0:T(8,128)}, u32[]{:S(2)}, u32[]{:S(2)}) collective-permute-start(f32[1,64,256,256]{3,2,1,0:T(8,128)} %get-tuple-element.8), channel_id=1, source_target_pairs={{1,0},{2,1},{3,2},{4,3},{5,4},{6,5},{7,6},{9,8},{10,9},{11,10},{12... | collective-permute-start | bytes 50331656 | tf_op jit(solution)/shard_map/ppermute | solution.py:10
  313.3 719.4 %collective-permute-start.2 = (f32[1,64,256,256]{3,2,1,0:T(8,128)}, f32[1,64,256,256]{3,2,1,0:T(8,128)}, u32[]{:S(2)}, u32[]{:S(2)}) collective-permute-start(f32[1,64,256,256]{3,2,1,0:T(8,128)} %get-tuple-element.7), channel_id=1, source_target_pairs={{2,0},{3,1},{4,2},{5,3},{6,4},{7,5},{10,8},{11,9},{12,10},{13,11},... | collective-permute-start | bytes 50331656 | tf_op jit(solution)/shard_map/ppermute | solution.py:10
  497.9 538.0 %collective-permute-start = (f32[1,64,256,256]{3,2,1,0:T(8,128)}, f32[1,64,256,256]{3,2,1,0:T(8,128)}, u32[]{:S(2)}, u32[]{:S(2)}) collective-permute-start(f32[1,64,256,256]{3,2,1,0:T(8,128)} %fusion.1), channel_id=1, source_target_pairs={{0,1},{1,2},{2,3},{3,4},{4,5},{5,6},{6,7},{8,9},{9,10},{10,11},{11... | collective-permute-start | bytes 50331656 | tf_op jit(solution)/shard_map/ppermute | solution.py:10
  519.0 190.4 %all-to-all-start.1 = ((f32[1,256,64,256]{3,2,0,1:T(8,128)}), f32[1,256,64,256]{3,2,0,1:T(8,128)}, u32[]{:S(2)}, u32[]{:S(2)}) async-start(f32[1,256,64,256]{3,2,0,1:T(8,128)} %copy.16), calls=%async_computation.1 | async-start | bytes 33554432 | tf_op jit(solution)/shard_map/all_to_all | solution.py:69
where the time goes:
time: 1090 us; the launch traced here: 1080 us
  waiting for transfers between devices  709 us (65%)
  local copies, waits for them, and re-layouts  133 us (12%)
  matrix products  123 us (11%)
  other arithmetic  80.2 us (7%)
  starting transfers between devices  31.4 us (3%)
    ppermute x3, waiting for transfers between devices, passed_along(): return lax.ppermute(shard, axis, pairs)  315 us
    all_to_all x1, waiting for transfers between devices, local(): lax.all_to_all(state, 'cls', split_axis=2, concat_axis=1, tiled=True)  182 us
    all_to_all x1, waiting for transfers between devices, local(): lax.all_to_all(stay_a, 'cls', split_axis=1, concat_axis=2, tiled=True)  180 us
    dot_general x1, matrix products, local(): jnp.dot(state.reshape(-1, phases), cat_c, precision=highest)  59.2 us
    add x1, other arithmetic, local(): state = state + (inflow + fallen - outflow * state) / uniform_rate  42.7 us
    slice x2, local copies, waits for them, and re-layouts, local(): stay_a = both[:, :phases]  35.9 us
    dot_general x1, local copies, waits for them, and re-layouts, local(): jnp.dot(state.reshape(-1, phases), cat_c, precision=highest)  33.4 us
    dot_general x1, matrix products, local(): both_b = jnp.einsum('labc,bx->laxc', state, cat_b, precision=highest)  33.1 us
  transfers between devices with their start and end apart: 6, of which 5 were waited for; matrix products, arithmetic and copies ran while one was open for 19% of the time, Pallas kernels for 0%

commit v1 on v0

v1 whole, which is shorter than its diff:
```python
import functools

import jax
import jax.numpy as jnp
from jax import lax
from jax.experimental import pallas as pl
from jax.experimental.pallas import tpu as pltpu
from jax.sharding import PartitionSpec as P

F32 = jnp.float32
BF16 = jnp.bfloat16
VMEM_LIMIT = 56 * 2**20


def flag(cond):
    return jnp.where(cond, 1.0, 0.0).astype(F32)


def halves(x):
    high = x.astype(BF16)
    low = (x - high.astype(F32)).astype(BF16)
    return high, low


def halves_outside(x):
    high = lax.reduce_precision(x, 8, 7)
    return high.astype(BF16), (x - high).astype(BF16)


def dot(a, b):
    return jnp.dot(a, b, preferred_element_type=F32)


def chunk_bounds(length):
    unit = length // 32
    sizes = [1, 2, 3, 4, 4, 4, 4, 4, 3, 2, 1]
    starts, at = [], 0
    for size in sizes:
        starts.append((at * unit, size * unit))
        at += size
    assert at == 32
    return starts


def local_kernel(own_rows, occ, c_hi, c_lo, b_hi, b_lo, row_b, row_c, base, rise):
    block, phases = occ.shape[0], occ.shape[2]
    first = pl.program_id(0) * block
    for i in range(block):
        x = occ[i]
        x_hi, x_lo = halves(x)
        by_c = dot(x_hi, c_hi[...]) + dot(x_lo, c_hi[...]) + dot(x_hi, c_lo[...])
        by_b = dot(b_hi[...], x_hi) + dot(b_hi[...], x_lo) + dot(b_lo[...], x_hi)
        left = row_c[...] - own_rows[first + i] - row_b[...]
        base[i] = by_c[:, :phases] + by_b[: x.shape[0]] + x * left
        rise[i] = by_c[:, phases:] + by_b[x.shape[0] :]


def local_terms(occ, own_rows, cat_c, cat_b_t, row_b, row_c):
    rows, mid, phases = occ.shape
    block = 4
    c_hi, c_lo = halves_outside(cat_c)
    b_hi, b_lo = halves_outside(cat_b_t)
    whole = pl.BlockSpec(memory_space=pltpu.VMEM)
    slab = pl.BlockSpec((block, mid, phases), lambda i: (i, 0, 0))
    return pl.pallas_call(
        local_kernel,
        grid=(rows // block,),
        in_specs=[pl.BlockSpec(memory_space=pltpu.SMEM), slab] + [whole] * 6,
        out_specs=[slab, slab],
        out_shape=[jax.ShapeDtypeStruct(occ.shape, F32)] * 2,
        compiler_params=pltpu.CompilerParams(vmem_limit_bytes=VMEM_LIMIT),
        cost_estimate=pl.CostEstimate(
            flops=rows * mid * phases * phases * 24, transcendentals=0, bytes_accessed=occ.size * 12
        ),
        name="local_terms",
    )(own_rows, occ, c_hi, c_lo, b_hi, b_lo, row_b, row_c)


def first_kernel(n_slabs, *refs):
    w_both, w_hi = refs[0], refs[1]
    slabs = refs[2 : 2 + n_slabs]
    base, rise_in, stay_out, rise_out = refs[2 + n_slabs :]
    rows, span, lanes = base.shape
    flat = [ref.reshape(rows * span, lanes) for ref in slabs]
    stay_flat = stay_out.reshape(rows * span, lanes)
    rise_flat = rise_out.reshape(rows * span, lanes)
    for b in range(0, span, 2):
        ats = [pl.ds(b, rows, stride=span), pl.ds(b + 1, rows, stride=span)]
        parts = [halves(jnp.concatenate([ref[at, :] for at in ats], axis=1)) for ref in flat]
        g_hi = jnp.concatenate([p[0] for p in parts], axis=0)
        g_lo = jnp.concatenate([p[1] for p in parts], axis=0)
        both = dot(w_both[...], g_hi)
        out = both[: 2 * rows] + both[2 * rows :] + dot(w_hi[...], g_lo)
        for n, at in enumerate(ats):
            stay_flat[at, :] = out[:rows, n * lanes : (n + 1) * lanes]
            rise_flat[at, :] = out[rows:, n * lanes : (n + 1) * lanes]
    stay_out[...] += base[...]
    rise_out[...] += rise_in[...]


def first_terms(w_both, w_hi, slabs, base, rise, start, size):
    rows, _, phases = base.shape
    span, lanes = 8, 128

    def at(offset):
        return pl.BlockSpec((rows, span, lanes), lambda j, h: (0, offset // span + j, h))

    whole = pl.BlockSpec(memory_space=pltpu.VMEM)
    n = len(slabs)
    return pl.pallas_call(
        functools.partial(first_kernel, n),
        grid=(size // span, phases // lanes),
        in_specs=[whole, whole] + [at(off) for _, off in slabs] + [at(start), at(start)],
        out_specs=[at(0), at(0)],
        out_shape=[jax.ShapeDtypeStruct((rows, size, phases), F32)] * 2,
        compiler_params=pltpu.CompilerParams(vmem_limit_bytes=VMEM_LIMIT),
        cost_estimate=pl.CostEstimate(
            flops=6 * 2 * rows * rows * n * size * phases,
            transcendentals=0,
            bytes_accessed=rows * size * phases * 4 * (n + 4),
        ),
        name="first_terms",
    )(w_both, w_hi, *[a for a, _ in slabs], base, rise)


def finish_kernel(scale, stay, fall, risen, deep, *refs):
    out = refs[-1]
    out[...] = (stay[...] + risen[...] + fall[...] * deep[...]) * scale[0]


def finish(out, shape, scale, stay, fall, risen, deep, start, size):
    rows, _, phases = shape
    span = 8
    chunk = pl.BlockSpec((rows, span, phases), lambda j: (0, j, 0))
    args = [scale, stay, fall, risen, deep]
    specs = [pl.BlockSpec(memory_space=pltpu.SMEM), chunk, pl.BlockSpec(memory_space=pltpu.VMEM), chunk, chunk]
    alias = {}
    if out is not None:
        args.append(out)
        specs.append(pl.BlockSpec(memory_space=pl.ANY))
        alias = {5: 0}
    return pl.pallas_call(
        finish_kernel,
        grid=(size // span,),
        in_specs=specs,
        out_specs=pl.BlockSpec((rows, span, phases), lambda j: (0, start // span + j, 0)),
        out_shape=jax.ShapeDtypeStruct(shape, F32),
        input_output_aliases=alias,
        compiler_params=pltpu.CompilerParams(vmem_limit_bytes=VMEM_LIMIT),
        cost_estimate=pl.CostEstimate(
            flops=3 * rows * size * phases, transcendentals=0, bytes_accessed=rows * size * phases * 16
        ),
        name="finish",
    )(*args)


def local(occupancy, rates, increments, draw, crusher_rate, bounds):
    n_cls, n_lvl = lax.axis_size("cls"), lax.axis_size("lvl")
    occ = occupancy[0]
    rows, mid, phases = occ.shape
    level = lax.axis_index("lvl")
    place = lax.axis_index("cls")
    even = level % 2 == 0
    bottom, top = bounds[0], bounds[1]

    row_total = jnp.sum(rates, axis=2)
    uniform_rate = jnp.sum(jnp.max(row_total, axis=1)) + jnp.max(crusher_rate)
    out_rows = row_total * flag((increments == 0) | (level + increments <= top))
    rise_ok = flag(level + 1 <= top)
    drop_here = crusher_rate * flag(level - draw >= bottom)
    drop_deep = crusher_rate * flag(level + 2 - draw >= bottom)
    once_here = (drop_here * flag(draw == 1) * flag(~even))[None, None, :]
    once_deep = (drop_deep * flag(draw == 1) * flag(even))[None, None, :]
    twice_deep = (drop_deep * flag(draw == 2))[None, :]

    stay_rows = rates * flag(increments == 0)[:, :, None]
    rise_rows = rates * (flag(increments == 1) * rise_ok)[:, :, None]

    def along_cls(v, by):
        return lax.ppermute(v, "cls", [(i, (i + by) % n_cls) for i in range(n_cls)])

    def other_core(v):
        return lax.ppermute(v, "cls", [(i, i ^ 1) for i in range(n_cls)])

    def two_down(v):
        return lax.ppermute(v, "lvl", [(i, i - 2) for i in range(2, n_lvl)])

    def two_up(v):
        return lax.ppermute(v, "lvl", [(i, i + 2) for i in range(1, n_lvl - 2, 2)])

    def pair_swap(v):
        return lax.ppermute(v, "lvl", [(i, i ^ 1) for i in range(n_lvl)])

    chunks = chunk_bounds(mid)
    shifts = [2 * s for s in range(1, n_cls // 2)]
    sent = [lax.slice_in_dim(occ, at, at + size, axis=1) for at, size in chunks]
    far = [[along_cls(v, by) for by in shifts] for v in sent]
    deep = [two_down(v) for v in sent]
    core_own = other_core(occ)

    origin = [place, place ^ 1]
    for by in shifts:
        origin += [(place - by) % n_cls, ((place ^ 1) - by) % n_cls]
    mine = jnp.concatenate(
        [lax.dynamic_slice_in_dim(r, place * rows, rows, axis=1) for r in (stay_rows[0], rise_rows[0])], axis=1
    ).T
    mine = jnp.concatenate([lax.dynamic_slice_in_dim(mine, o * rows, rows, axis=1) for o in origin], axis=1)
    a_hi, a_lo = halves_outside(mine)
    a_both = jnp.concatenate([a_hi, a_lo], axis=0)

    base, rise = local_terms(
        occ,
        lax.dynamic_slice_in_dim(out_rows[0], place * rows, rows),
        jnp.concatenate([stay_rows[2], rise_rows[2]], axis=1),
        jnp.concatenate([stay_rows[1], rise_rows[1]], axis=1).T,
        out_rows[1][:, None],
        (uniform_rate - out_rows[2] - drop_here)[None, :],
    )

    scale = (1.0 / uniform_rate)[None]
    out = None
    for k, (at, size) in enumerate(chunks):
        slabs = [(occ, at), (core_own, at)]
        for v in far[k]:
            slabs += [(v, 0), (other_core(v), 0)]
        stay_k, rise_k = first_terms(a_both, a_hi, slabs, base, rise, at, size)
        lifted = two_up(rise_k)
        send = jnp.where(even, rise_k, lifted) + once_deep * deep[k] + once_here * sent[k]
        risen = pair_swap(send)
        out = finish(out, occ.shape, scale, stay_k, twice_deep, risen, deep[k], at, size)
    return out[None]


def solution(mesh):
    in_specs = (P("lvl", "cls", None, None), P(), P(), P(), P(), P())
    out_specs = P("lvl", "cls", None, None)
    return jax.shard_map(local, mesh=mesh, in_specs=in_specs, out_specs=out_specs, check_vma=False)
```

time: 1090 us -> 1190 us (1.092)
  Pallas kernels: 0 us -> 162 us
  waiting for transfers between devices: 709 us -> 855 us
  matrix products: 123 us -> 0 us
  local copies, waits for them, and re-layouts: 133 us -> 23.8 us
  starting transfers between devices: 31.4 us -> 96.2 us
  other arithmetic: 80.2 us -> 40.1 us
    ppermute x3 -> x56, waiting for transfers between devices: 315 us -> 855 us  [the longest x11 277 us: pair_swap(): return lax.ppermute(v, 'lvl', [(i, i ^ 1) for i in range(n_lvl)])]
    all_to_all x3 -> x0, waiting for transfers between devices: 394 us -> none  [the longest x1 182 us: local(): lax.all_to_all(state, 'cls', split_axis=2, concat_axis=1, tiled=True)]
    pallas_call x0 -> x23, Pallas kernels: none -> 162 us  [the longest x11 87.4 us: first_terms(): pl.pallas_call(functools.partial(first_kernel, n), grid=(size // span, ph...]
    dot_general x3 -> x0, matrix products: 123 us -> none  [the longest x1 59.2 us: local(): jnp.dot(state.reshape(-1, phases), cat_c, precision=highest)]
    ppermute x3 -> x56, starting transfers between devices: 7.34 us -> 96.2 us  [the longest x11 29.1 us: two_up(): return lax.ppermute(v, 'lvl', [(i, i + 2) for i in range(1, n_lvl - 2, 2)])]
    slice x6 -> x5, local copies, waits for them, and re-layouts: 56.7 us -> 12.9 us  [the longest x4 12.2 us: local(): sent = [lax.slice_in_dim(occ, at, at + size, axis=1) for at, size in chunks]]
    dot_general x1 -> x0, local copies, waits for them, and re-layouts: 33.4 us -> none  [local(): jnp.dot(state.reshape(-1, phases), cat_c, precision=highest)]
    mul x5 -> x2, other arithmetic: 34.7 us -> 1.36 us  [the longest x1 1.22 us: local(): once_deep = (drop_deep * flag(draw == 1) * flag(even))[None, None, :]]
  transfers between devices with their start and end apart: 6 -> 56, of which waited for: 5 -> 25; matrix products, arithmetic and copies ran while one was open for 19% -> 5% of each run, Pallas kernels for 0% -> 14%
where the time goes in v1:
time: 1190 us; the launch traced here: 1180 us
  waiting for transfers between devices  855 us (72%)
  Pallas kernels  162 us (14%)
  starting transfers between devices  96.2 us (8%)
  other arithmetic  40.1 us (3%)
  local copies, waits for them, and re-layouts  23.8 us (2%)
    ppermute x11, waiting for transfers between devices, pair_swap(): return lax.ppermute(v, 'lvl', [(i, i ^ 1) for i in range(n_lvl)])  277 us
    ppermute x11, waiting for transfers between devices, along_cls(): return lax.ppermute(v, 'cls', [(i, (i + by) % n_cls) for i in range(n_cls)])  268 us
    ppermute x11, waiting for transfers between devices, two_up(): return lax.ppermute(v, 'lvl', [(i, i + 2) for i in range(1, n_lvl - 2, 2)])  156 us
    ppermute x11, waiting for transfers between devices, two_down(): return lax.ppermute(v, 'lvl', [(i, i - 2) for i in range(2, n_lvl)])  148 us
    pallas_call x11, Pallas kernels, first_terms(): pl.pallas_call(functools.partial(first_kernel, n), grid=(size // span, ph...  87.4 us
    pallas_call x11, Pallas kernels, finish(): pl.pallas_call(finish_kernel, grid=(size // span,), in_specs=specs, out_s...  41.8 us
    pallas_call x1, Pallas kernels, local_terms(): pl.pallas_call(local_kernel, grid=(rows // block,), in_specs=[pl.BlockSpe...  32.7 us
    ppermute x11, starting transfers between devices, two_up(): return lax.ppermute(v, 'lvl', [(i, i + 2) for i in range(1, n_lvl - 2, 2)])  29.1 us
  transfers between devices with their start and end apart: 56, of which 25 were waited for; matrix products, arithmetic and copies ran while one was open for 5% of the time, Pallas kernels for 14%

profile of v1, /device:TPU:21, one launch (start us, length us, event | category | flops | bytes accessed | tf_op | source)
XLA Modules:
  0.0 1179.8 jit_solution(10411525676031708671)
XLA Ops:
  0.7 3.0 fusion.18
  7.1 3.2 slice.100
  25.5 61.3 %collective-permute-done.51.refs_4_ = f32[64,8,256]{2,1,0:T(8,128)} collective-permute-done((f32[64,8,256]{2,1,0:T(8,128)}, f32[64,8,256]{2,1,0:T(8,128)}, u32[]{:S(2)}, u32[]{:S(2)}) %collective-permute-start.51) | collective-permute-done | bytes 524320 | tf_op jit(solution)/shard_map/ppermute | solution.py:180
  89.4 32.7 %local_terms.1 = (f32[64,256,256]{2,1,0:T(8,128)}, f32[64,256,256]{2,1,0:T(8,128)}) custom-call(f32[64]{0:T(128)} %fusion.15.own_rows, f32[64,256,256]{2,1,0:T(8,128)} %bitcast.42, bf16[256,512]{1,0:T(8,128)(2,1)} %copy.23.c_hi, bf16[256,512]{1,0:T(8,128)(2,1)} %copy.24.c_lo, bf16[512,256]{1,0:T(8,128)(2,1)} %get-tuple-element.83.b_hi, ...), custom_call_target="tpu_custom_call" | custom-call | flops 25769803776 | bytes 50331648 | tf_op jit(solution)/shard_map/local_terms/pallas_call | solution.py:65
  126.8 10.4 first_terms.14
  140.0 3.5 collective-permute-start.18
  143.4 3.8 fusion.19
  151.8 90.7 %collective-permute-done.9.deep = f32[64,16,256]{2,1,0:T(8,128)S(1)} collective-permute-done((f32[64,16,256]{2,1,0:T(8,128)S(1)}, f32[64,16,256]{2,1,0:T(8,128)S(1)}, u32[]{:S(2)}, u32[]{:S(2)}) %collective-permute-start.9) | collective-permute-done | bytes 1048608 | tf_op jit(solution)/shard_map/ppermute | solution.py:186
  250.1 9.7 fusion.20
  259.9 17.2 %collective-permute-done.41.refs_4_ = f32[64,24,256]{2,1,0:T(8,128)} collective-permute-done((f32[64,24,256]{2,1,0:T(8,128)}, f32[64,24,256]{2,1,0:T(8,128)}, u32[]{:S(2)}, u32[]{:S(2)}) %collective-permute-start.41) | collective-permute-done | bytes 1572896 | tf_op jit(solution)/shard_map/ppermute | solution.py:180
  280.1 30.6 %collective-permute-done.11.refs_4_ = f32[64,24,256]{2,1,0:T(8,128)} collective-permute-done((f32[64,24,256]{2,1,0:T(8,128)}, f32[64,24,256]{2,1,0:T(8,128)}, u32[]{:S(2)}, u32[]{:S(2)}) %collective-permute-start.11) | collective-permute-done | bytes 1572896 | tf_op jit(solution)/shard_map/ppermute | solution.py:180
  312.2 5.4 collective-permute-start.42
  317.6 38.0 %collective-permute-done.36.refs_4_ = f32[64,32,256]{2,1,0:T(8,128)S(1)} collective-permute-done((f32[64,32,256]{2,1,0:T(8,128)}, f32[64,32,256]{2,1,0:T(8,128)S(1)}, u32[]{:S(2)}, u32[]{:S(2)}) %collective-permute-start.36) | collective-permute-done | bytes 2097184 | tf_op jit(solution)/shard_map/ppermute | solution.py:180
  355.6 4.8 collective-permute-start.37
  360.4 40.1 %collective-permute-done.31.refs_4_ = f32[64,32,256]{2,1,0:T(8,128)S(1)} collective-permute-done((f32[64,32,256]{2,1,0:T(8,128)}, f32[64,32,256]{2,1,0:T(8,128)S(1)}, u32[]{:S(2)}, u32[]{:S(2)}) %collective-permute-start.31) | collective-permute-done | bytes 2097184 | tf_op jit(solution)/shard_map/ppermute | solution.py:180
  400.5 4.8 collective-permute-start.32
  405.3 40.2 %collective-permute-done.26.refs_4_ = f32[64,32,256]{2,1,0:T(8,128)} collective-permute-done((f32[64,32,256]{2,1,0:T(8,128)}, f32[64,32,256]{2,1,0:T(8,128)}, u32[]{:S(2)}, u32[]{:S(2)}) %collective-permute-start.26) | collective-permute-done | bytes 2097184 | tf_op jit(solution)/shard_map/ppermute | solution.py:180
  445.6 4.8 collective-permute-start.27
  450.4 40.1 %collective-permute-done.21.refs_4_ = f32[64,32,256]{2,1,0:T(8,128)} collective-permute-done((f32[64,32,256]{2,1,0:T(8,128)}, f32[64,32,256]{2,1,0:T(8,128)}, u32[]{:S(2)}, u32[]{:S(2)}) %collective-permute-start.21) | collective-permute-done | bytes 2097184 | tf_op jit(solution)/shard_map/ppermute | solution.py:180
  490.5 2.6 collective-permute-start.22
  493.2 6.2 collective-permute-done.12.refs_5_
  507.1 8.2 first_terms.19
  515.3 8.2 first_terms.13
  523.5 3.5 collective-permute-start.13
  529.2 10.4 first_terms.18
  539.5 10.3 first_terms.17
  549.9 10.4 first_terms.16
  560.2 10.3 first_terms.15
  570.6 3.3 collective-permute-start.24
  574.0 20.4 %collective-permute-done.43 = f32[64,24,256]{2,1,0:T(8,128)} collective-permute-done((f32[64,24,256]{2,1,0:T(8,128)S(1)}, f32[64,24,256]{2,1,0:T(8,128)}, u32[]{:S(2)}, u32[]{:S(2)}) %collective-permute-start.43) | collective-permute-done | bytes 1572896 | tf_op jit(solution)/shard_map/ppermute | solution.py:189
  594.4 3.2 collective-permute-start.38
  601.5 36.8 %collective-permute-done.29.deep = f32[64,32,256]{2,1,0:T(8,128)S(1)} collective-permute-done((f32[64,32,256]{2,1,0:T(8,128)}, f32[64,32,256]{2,1,0:T(8,128)S(1)}, u32[]{:S(2)}, u32[]{:S(2)}) %collective-permute-start.29) | collective-permute-done | bytes 2097184 | tf_op jit(solution)/shard_map/ppermute | solution.py:186
  640.2 3.6 first_terms.21
  643.8 3.5 first_terms.11
  647.4 6.0 first_terms.20
  653.4 6.0 first_terms.12
  659.5 6.0 multiply_add_fusion.5
  665.5 17.7 %collective-permute-done.24.deep = f32[64,32,256]{2,1,0:T(8,128)} collective-permute-done((f32[64,32,256]{2,1,0:T(8,128)}, f32[64,32,256]{2,1,0:T(8,128)}, u32[]{:S(2)}, u32[]{:S(2)}) %collective-permute-start.24) | collective-permute-done | bytes 2097184 | tf_op jit(solution)/shard_map/ppermute | solution.py:186
  685.3 3.2 collective-permute-start.3
  690.5 41.3 %collective-permute-done.28 = f32[64,32,256]{2,1,0:T(8,128)} collective-permute-done((f32[64,32,256]{2,1,0:T(8,128)}, f32[64,32,256]{2,1,0:T(8,128)}, u32[]{:S(2)}, u32[]{:S(2)}) %collective-permute-start.28) | collective-permute-done | bytes 2097184 | tf_op jit(solution)/shard_map/ppermute | solution.py:189
  731.7 2.9 collective-permute-start.8
  734.7 42.0 %collective-permute-done.23 = f32[64,32,256]{2,1,0:T(8,128)} collective-permute-done((f32[64,32,256]{2,1,0:T(8,128)}, f32[64,32,256]{2,1,0:T(8,128)}, u32[]{:S(2)}, u32[]{:S(2)}) %collective-permute-start.23) | collective-permute-done | bytes 2097184 | tf_op jit(solution)/shard_map/ppermute | solution.py:189
  776.7 3.0 collective-permute-start.48
  779.8 11.6 multiply_add_fusion
  791.3 30.3 %collective-permute-done.8 = f32[64,16,256]{2,1,0:T(8,128)} collective-permute-done((f32[64,16,256]{2,1,0:T(8,128)}, f32[64,16,256]{2,1,0:T(8,128)}, u32[]{:S(2)}, u32[]{:S(2)}) %collective-permute-start.8) | collective-permute-done | bytes 1048608 | tf_op jit(solution)/shard_map/ppermute | solution.py:189
  821.6 22.5 %collective-permute-done.48 = f32[64,16,256]{2,1,0:T(8,128)} collective-permute-done((f32[64,16,256]{2,1,0:T(8,128)S(1)}, f32[64,16,256]{2,1,0:T(8,128)}, u32[]{:S(2)}, u32[]{:S(2)}) %collective-permute-start.48) | collective-permute-done | bytes 1048608 | tf_op jit(solution)/shard_map/ppermute | solution.py:189
  844.1 4.4 multiply_add_fusion.7
  849.7 3.0 multiply_add_fusion.9
  854.2 122.0 %collective-permute-done.55.risen = f32[64,8,256]{2,1,0:T(8,128)S(1)} collective-permute-done((f32[64,8,256]{2,1,0:T(8,128)S(1)}, f32[64,8,256]{2,1,0:T(8,128)S(1)}, u32[]{:S(2)}, u32[]{:S(2)}) %collective-permute-start.55) | collective-permute-done | bytes 524320 | tf_op jit(solution)/shard_map/ppermute | solution.py:192
  980.3 40.0 %collective-permute-done.35.risen = f32[64,32,256]{2,1,0:T(8,128)S(1)} collective-permute-done((f32[64,32,256]{2,1,0:T(8,128)S(1)}, f32[64,32,256]{2,1,0:T(8,128)S(1)}, u32[]{:S(2)}, u32[]{:S(2)}) %collective-permute-start.35) | collective-permute-done | bytes 2097184 | tf_op jit(solution)/shard_map/ppermute | solution.py:192
  1024.1 2.7 finish.12.refs_0_
  1026.8 4.2 finish.13.refs_0_
  1031.0 4.7 finish.14.refs_0_
  1035.7 4.7 finish.15.refs_0_
  1040.4 4.7 finish.16.refs_0_
  1045.1 20.2 %collective-permute-done.25.risen = f32[64,32,256]{2,1,0:T(8,128)} collective-permute-done((f32[64,32,256]{2,1,0:T(8,128)}, f32[64,32,256]{2,1,0:T(8,128)}, u32[]{:S(2)}, u32[]{:S(2)}) %collective-permute-start.25) | collective-permute-done | bytes 2097184 | tf_op jit(solution)/shard_map/ppermute | solution.py:192
  1065.3 4.7 finish.17.refs_0_
  1070.0 40.3 %collective-permute-done.20.risen = f32[64,32,256]{2,1,0:T(8,128)} collective-permute-done((f32[64,32,256]{2,1,0:T(8,128)S(1)}, f32[64,32,256]{2,1,0:T(8,128)}, u32[]{:S(2)}, u32[]{:S(2)}) %collective-permute-start.20) | collective-permute-done | bytes 2097184 | tf_op jit(solution)/shard_map/ppermute | solution.py:192
  1110.2 4.8 finish.18.refs_0_
  1115.1 28.9 %collective-permute-done.15.risen = f32[64,24,256]{2,1,0:T(8,128)} collective-permute-done((f32[64,24,256]{2,1,0:T(8,128)}, f32[64,24,256]{2,1,0:T(8,128)}, u32[]{:S(2)}, u32[]{:S(2)}) %collective-permute-start.15) | collective-permute-done | bytes 1572896 | tf_op jit(solution)/shard_map/ppermute | solution.py:192
  1143.9 4.2 finish.19.refs_0_
  1148.1 18.2 %collective-permute-done.10.risen = f32[64,16,256]{2,1,0:T(8,128)S(1)} collective-permute-done((f32[64,16,256]{2,1,0:T(8,128)}, f32[64,16,256]{2,1,0:T(8,128)S(1)}, u32[]{:S(2)}, u32[]{:S(2)}) %collective-permute-start.10) | collective-permute-done | bytes 1048608 | tf_op jit(solution)/shard_map/ppermute | solution.py:192
  1167.3 2.7 finish.20.refs_0_
  1170.0 7.5 collective-permute-done.5.risen
  (191 shorter events, 77.3 us)
Async XLA Ops:
  0.0 125.9 %collective-permute-start = (f32[64,256,256]{2,1,0:T(8,128)}, f32[64,256,256]{2,1,0:T(8,128)}, u32[]{:S(2)}, u32[]{:S(2)}) collective-permute-start(f32[64,256,256]{2,1,0:T(8,128)} %bitcast.38), channel_id=1, source_target_pairs={{0,8},{8,0},{16,24},{24,16},{1,9},{9,1},{17,25},{25,17},{2,10},{10... | collective-permute-start | bytes 50331656 | tf_op jit(solution)/shard_map/ppermute | solution.py:183
  3.7 145.4 %collective-permute-start.49 = (f32[64,16,256]{2,1,0:T(8,128)}, f32[64,16,256]{2,1,0:T(8,128)S(1)}, u32[]{:S(2)}, u32[]{:S(2)}) collective-permute-start(f32[64,16,256]{2,1,0:T(8,128)} %get-tuple-element.65), channel_id=1, source_target_pairs={{2,0},{3,1},{4,2},{5,3},{6,4},{7,5},{10,8},{11,9},{12,10},{13,11},... | collective-permute-start | bytes 3145736 | tf_op jit(solution)/shard_map/ppermute | solution.py:186
  5.8 145.7 %collective-permute-start.46 = (f32[64,16,256]{2,1,0:T(8,128)}, f32[64,16,256]{2,1,0:T(8,128)}, u32[]{:S(2)}, u32[]{:S(2)}) collective-permute-start(f32[64,16,256]{2,1,0:T(8,128)} %get-tuple-element.65), channel_id=1, source_target_pairs={{0,16},{8,24},{16,0},{24,8},{1,17},{9,25},{17,1},{25,9},{2,18},{10... | collective-permute-start | bytes 3145736 | tf_op jit(solution)/shard_map/ppermute | solution.py:180
  10.2 77.8 %collective-permute-start.16 = (f32[64,32,256]{2,1,0:T(8,128)}, f32[64,32,256]{2,1,0:T(8,128)}, u32[]{:S(2)}, u32[]{:S(2)}) collective-permute-start(f32[64,32,256]{2,1,0:T(8,128)} %slice.100), channel_id=1, source_target_pairs={{0,16},{8,24},{16,0},{24,8},{1,17},{9,25},{17,1},{25,9},{2,18},{10... | collective-permute-start | bytes 6291464 | tf_op jit(solution)/shard_map/ppermute | solution.py:180
  12.8 74.0 %collective-permute-start.51 = (f32[64,8,256]{2,1,0:T(8,128)}, f32[64,8,256]{2,1,0:T(8,128)}, u32[]{:S(2)}, u32[]{:S(2)}) collective-permute-start(f32[64,8,256]{2,1,0:T(8,128)} %get-tuple-element.63), channel_id=1, source_target_pairs={{0,16},{8,24},{16,0},{24,8},{1,17},{9,25},{17,1},{25,9},{2,18},{10... | collective-permute-start | bytes 1572872 | tf_op jit(solution)/shard_map/ppermute | solution.py:180
  25.5 224.7 %copy-start.37 = (f32[256]{0:T(256)}, f32[256]{0:T(256)S(1)}, u32[]{:S(2)}) copy-start(f32[256]{0:T(256)S(1)} %get-tuple-element.99) | copy-start | bytes 3076
  25.5 224.7 %copy-start.39 = (f32[256]{0:T(256)}, f32[256]{0:T(256)S(1)}, u32[]{:S(2)}) copy-start(f32[256]{0:T(256)S(1)} %get-tuple-element.100) | copy-start | bytes 3076
  86.8 35.3 %collective-permute-start.1 = (f32[64,8,256]{2,1,0:T(8,128)}, f32[64,8,256]{2,1,0:T(8,128)S(1)}, u32[]{:S(2)}, u32[]{:S(2)}) collective-permute-start(f32[64,8,256]{2,1,0:T(8,128)} %get-tuple-element.64), channel_id=1, source_target_pairs={{0,16},{8,24},{16,0},{24,8},{1,17},{9,25},{17,1},{25,9},{2,18},{10... | collective-permute-start | bytes 1572872 | tf_op jit(solution)/shard_map/ppermute | solution.py:180
  88.0 36.2 %collective-permute-start.17 = (f32[64,32,256]{2,1,0:T(8,128)}, f32[64,32,256]{2,1,0:T(8,128)S(1)}, u32[]{:S(2)}, u32[]{:S(2)}) collective-permute-start(f32[64,32,256]{2,1,0:T(8,128)} %collective-permute-done.16.refs_4_), channel_id=1, source_target_pairs={{0,8},{8,0},{16,24},{24,16},{1,9},{9,1},{17,25},{25,17},{2,10},{10... | collective-permute-start | bytes 6291464 | tf_op jit(solution)/shard_map/ppermute | solution.py:183
  122.1 15.8 %collective-permute-start.54 = (f32[64,8,256]{2,1,0:T(8,128)}, f32[64,8,256]{2,1,0:T(8,128)}, u32[]{:S(2)}, u32[]{:S(2)}) collective-permute-start(f32[64,8,256]{2,1,0:T(8,128)} %get-tuple-element.63), channel_id=1, source_target_pairs={{2,0},{3,1},{4,2},{5,3},{6,4},{7,5},{10,8},{11,9},{12,10},{13,11},... | collective-permute-start | bytes 1572872 | tf_op jit(solution)/shard_map/ppermute | solution.py:186
  124.2 15.7 %collective-permute-start.52 = (f32[64,8,256]{2,1,0:T(8,128)}, f32[64,8,256]{2,1,0:T(8,128)}, u32[]{:S(2)}, u32[]{:S(2)}) collective-permute-start(f32[64,8,256]{2,1,0:T(8,128)} %collective-permute-done.51.refs_4_), channel_id=1, source_target_pairs={{0,8},{8,0},{16,24},{24,16},{1,9},{9,1},{17,25},{25,17},{2,10},{10... | collective-permute-start | bytes 1572872 | tf_op jit(solution)/shard_map/ppermute | solution.py:183
  125.9 21.3 %collective-permute-start.2 = (f32[64,8,256]{2,1,0:T(8,128)}, f32[64,8,256]{2,1,0:T(8,128)S(1)}, u32[]{:S(2)}, u32[]{:S(2)}) collective-permute-start(f32[64,8,256]{2,1,0:T(8,128)} %copy-done.34), channel_id=1, source_target_pairs={{0,8},{8,0},{16,24},{24,16},{1,9},{9,1},{17,25},{25,17},{2,10},{10... | collective-permute-start | bytes 1572872 | tf_op jit(solution)/shard_map/ppermute | solution.py:183
  137.9 108.3 %collective-permute-start.19 = (f32[64,32,256]{2,1,0:T(8,128)}, f32[64,32,256]{2,1,0:T(8,128)S(1)}, u32[]{:S(2)}, u32[]{:S(2)}) collective-permute-start(f32[64,32,256]{2,1,0:T(8,128)} %slice.100), channel_id=1, source_target_pairs={{2,0},{3,1},{4,2},{5,3},{6,4},{7,5},{10,8},{11,9},{12,10},{13,11},... | collective-permute-start | bytes 6291464 | tf_op jit(solution)/shard_map/ppermute | solution.py:186
  140.0 108.8 %collective-permute-start.18 = (f32[64,32,256]{2,1,0:T(8,128)}, f32[64,32,256]{2,1,0:T(8,128)S(1)}, u32[]{:S(2)}, u32[]{:S(2)}) collective-permute-start(f32[64,32,256]{2,1,0:T(8,128)} %get-tuple-element.38), channel_id=1, source_target_pairs={{1,3},{3,5},{5,7},{9,11},{11,13},{13,15},{17,19},{19,21},{21,23},{... | collective-permute-start | bytes 6291464 | tf_op jit(solution)/shard_map/ppermute | solution.py:189
  147.2 97.6 %collective-permute-start.44 = (f32[64,24,256]{2,1,0:T(8,128)}, f32[64,24,256]{2,1,0:T(8,128)S(1)}, u32[]{:S(2)}, u32[]{:S(2)}) collective-permute-start(f32[64,24,256]{2,1,0:T(8,128)} %get-tuple-element.67), channel_id=1, source_target_pairs={{2,0},{3,1},{4,2},{5,3},{6,4},{7,5},{10,8},{11,9},{12,10},{13,11},... | collective-permute-start | bytes 4718600 | tf_op jit(solution)/shard_map/ppermute | solution.py:186
  149.2 93.3 %collective-permute-start.9 = (f32[64,16,256]{2,1,0:T(8,128)S(1)}, f32[64,16,256]{2,1,0:T(8,128)S(1)}, u32[]{:S(2)}, u32[]{:S(2)}) collective-permute-start(f32[64,16,256]{2,1,0:T(8,128)S(1)} %copy-done.33), channel_id=1, source_target_pairs={{2,0},{3,1},{4,2},{5,3},{6,4},{7,5},{10,8},{11,9},{12,10},{13,11},... | collective-permute-start | bytes 3145736 | tf_op jit(solution)/shard_map/ppermute | solution.py:186
  151.5 91.3 %collective-permute-start.6 = (f32[64,16,256]{2,1,0:T(8,128)S(1)}, f32[64,16,256]{2,1,0:T(8,128)}, u32[]{:S(2)}, u32[]{:S(2)}) collective-permute-start(f32[64,16,256]{2,1,0:T(8,128)S(1)} %copy-done.33), channel_id=1, source_target_pairs={{0,16},{8,24},{16,0},{24,8},{1,17},{9,25},{17,1},{25,9},{2,18},{10... | collective-permute-start | bytes 3145736 | tf_op jit(solution)/shard_map/ppermute | solution.py:180
  242.5 34.5 %collective-permute-start.41 = (f32[64,24,256]{2,1,0:T(8,128)}, f32[64,24,256]{2,1,0:T(8,128)}, u32[]{:S(2)}, u32[]{:S(2)}) collective-permute-start(f32[64,24,256]{2,1,0:T(8,128)} %get-tuple-element.67), channel_id=1, source_target_pairs={{0,16},{8,24},{16,0},{24,8},{1,17},{9,25},{17,1},{25,9},{2,18},{10... | collective-permute-start | bytes 4718600 | tf_op jit(solution)/shard_map/ppermute | solution.py:180
  242.8 36.1 %collective-permute-start.14 = (f32[64,24,256]{2,1,0:T(8,128)}, f32[64,24,256]{2,1,0:T(8,128)}, u32[]{:S(2)}, u32[]{:S(2)}) collective-permute-start(f32[64,24,256]{2,1,0:T(8,128)} %get-tuple-element.68), channel_id=1, source_target_pairs={{2,0},{3,1},{4,2},{5,3},{6,4},{7,5},{10,8},{11,9},{12,10},{13,11},... | collective-permute-start | bytes 4718600 | tf_op jit(solution)/shard_map/ppermute | solution.py:186
  244.9 65.9 %collective-permute-start.11 = (f32[64,24,256]{2,1,0:T(8,128)}, f32[64,24,256]{2,1,0:T(8,128)}, u32[]{:S(2)}, u32[]{:S(2)}) collective-permute-start(f32[64,24,256]{2,1,0:T(8,128)} %get-tuple-element.68), channel_id=1, source_target_pairs={{0,16},{8,24},{16,0},{24,8},{1,17},{9,25},{17,1},{25,9},{2,18},{10... | collective-permute-start | bytes 4718600 | tf_op jit(solution)/shard_map/ppermute | solution.py:180
  246.2 64.8 %collective-permute-start.47 = (f32[64,16,256]{2,1,0:T(8,128)}, f32[64,16,256]{2,1,0:T(8,128)}, u32[]{:S(2)}, u32[]{:S(2)}) collective-permute-start(f32[64,16,256]{2,1,0:T(8,128)} %collective-permute-done.46.refs_4_), channel_id=1, source_target_pairs={{0,8},{8,0},{16,24},{24,16},{1,9},{9,1},{17,25},{25,17},{2,10},{10... | collective-permute-start | bytes 3145736 | tf_op jit(solution)/shard_map/ppermute | solution.py:183
  250.0 62.2 %collective-permute-start.7 = (f32[64,16,256]{2,1,0:T(8,128)}, f32[64,16,256]{2,1,0:T(8,128)}, u32[]{:S(2)}, u32[]{:S(2)}) collective-permute-start(f32[64,16,256]{2,1,0:T(8,128)} %collective-permute-done.6.refs_4_), channel_id=1, source_target_pairs={{0,8},{8,0},{16,24},{24,16},{1,9},{9,1},{17,25},{25,17},{2,10},{10... | collective-permute-start | bytes 3145736 | tf_op jit(solution)/shard_map/ppermute | solution.py:183
  277.0 78.5 %collective-permute-start.36 = (f32[64,32,256]{2,1,0:T(8,128)}, f32[64,32,256]{2,1,0:T(8,128)S(1)}, u32[]{:S(2)}, u32[]{:S(2)}) collective-permute-start(f32[64,32,256]{2,1,0:T(8,128)} %get-tuple-element.69), channel_id=1, source_target_pairs={{0,16},{8,24},{16,0},{24,8},{1,17},{9,25},{17,1},{25,9},{2,18},{10... | collective-permute-start | bytes 6291464 | tf_op jit(solution)/shard_map/ppermute | solution.py:180
  278.9 121.6 %collective-permute-start.31 = (f32[64,32,256]{2,1,0:T(8,128)}, f32[64,32,256]{2,1,0:T(8,128)S(1)}, u32[]{:S(2)}, u32[]{:S(2)}) collective-permute-start(f32[64,32,256]{2,1,0:T(8,128)} %get-tuple-element.71), channel_id=1, source_target_pairs={{0,16},{8,24},{16,0},{24,8},{1,17},{9,25},{17,1},{25,9},{2,18},{10... | collective-permute-start | bytes 6291464 | tf_op jit(solution)/shard_map/ppermute | solution.py:180
  310.7 134.8 %collective-permute-start.26 = (f32[64,32,256]{2,1,0:T(8,128)}, f32[64,32,256]{2,1,0:T(8,128)}, u32[]{:S(2)}, u32[]{:S(2)}) collective-permute-start(f32[64,32,256]{2,1,0:T(8,128)} %get-tuple-element.72), channel_id=1, source_target_pairs={{0,16},{8,24},{16,0},{24,8},{1,17},{9,25},{17,1},{25,9},{2,18},{10... | collective-permute-start | bytes 6291464 | tf_op jit(solution)/shard_map/ppermute | solution.py:180
  311.0 179.5 %collective-permute-start.21 = (f32[64,32,256]{2,1,0:T(8,128)}, f32[64,32,256]{2,1,0:T(8,128)}, u32[]{:S(2)}, u32[]{:S(2)}) collective-permute-start(f32[64,32,256]{2,1,0:T(8,128)} %get-tuple-element.73), channel_id=1, source_target_pairs={{0,16},{8,24},{16,0},{24,8},{1,17},{9,25},{17,1},{25,9},{2,18},{10... | collective-permute-start | bytes 6291464 | tf_op jit(solution)/shard_map/ppermute | solution.py:180
  312.2 180.9 %collective-permute-start.42 = (f32[64,24,256]{2,1,0:T(8,128)}, f32[64,24,256]{2,1,0:T(8,128)S(1)}, u32[]{:S(2)}, u32[]{:S(2)}) collective-permute-start(f32[64,24,256]{2,1,0:T(8,128)} %collective-permute-done.41.refs_4_), channel_id=1, source_target_pairs={{0,8},{8,0},{16,24},{24,16},{1,9},{9,1},{17,25},{25,17},{2,10},{10... | collective-permute-start | bytes 4718600 | tf_op jit(solution)/shard_map/ppermute | solution.py:183
  355.6 148.2 %copy-start.17 = (f32[64,32,256]{2,1,0:T(8,128)}, f32[64,32,256]{2,1,0:T(8,128)S(1)}, u32[]{:S(2)}) copy-start(f32[64,32,256]{2,1,0:T(8,128)S(1)} %collective-permute-done.36.refs_4_) | copy-start | bytes 6291460
  355.6 145.9 %collective-permute-start.37 = (f32[64,32,256]{2,1,0:T(8,128)S(1)}, f32[64,32,256]{2,1,0:T(8,128)S(1)}, u32[]{:S(2)}, u32[]{:S(2)}) collective-permute-start(f32[64,32,256]{2,1,0:T(8,128)S(1)} %collective-permute-done.36.refs_4_), channel_id=1, source_target_pairs={{0,8},{8,0},{16,24},{24,16},{1,9},{9,1},{17,25},{25,17},{2,10},{10... | collective-permute-start | bytes 6291464 | tf_op jit(solution)/shard_map/ppermute | solution.py:183
  400.5 103.3 %collective-permute-start.32 = (f32[64,32,256]{2,1,0:T(8,128)S(1)}, f32[64,32,256]{2,1,0:T(8,128)S(1)}, u32[]{:S(2)}, u32[]{:S(2)}) collective-permute-start(f32[64,32,256]{2,1,0:T(8,128)S(1)} %collective-permute-done.31.refs_4_), channel_id=1, source_target_pairs={{0,8},{8,0},{16,24},{24,16},{1,9},{9,1},{17,25},{25,17},{2,10},{10... | collective-permute-start | bytes 6291464 | tf_op jit(solution)/shard_map/ppermute | solution.py:183
  445.6 78.0 %collective-permute-start.27 = (f32[64,32,256]{2,1,0:T(8,128)}, f32[64,32,256]{2,1,0:T(8,128)}, u32[]{:S(2)}, u32[]{:S(2)}) collective-permute-start(f32[64,32,256]{2,1,0:T(8,128)} %collective-permute-done.26.refs_4_), channel_id=1, source_target_pairs={{0,8},{8,0},{16,24},{24,16},{1,9},{9,1},{17,25},{25,17},{2,10},{10... | collective-permute-start | bytes 6291464 | tf_op jit(solution)/shard_map/ppermute | solution.py:183
  490.5 36.5 %collective-permute-start.22 = (f32[64,32,256]{2,1,0:T(8,128)}, f32[64,32,256]{2,1,0:T(8,128)}, u32[]{:S(2)}, u32[]{:S(2)}) collective-permute-start(f32[64,32,256]{2,1,0:T(8,128)} %collective-permute-done.21.refs_4_), channel_id=1, source_target_pairs={{0,8},{8,0},{16,24},{24,16},{1,9},{9,1},{17,25},{25,17},{2,10},{10... | collective-permute-start | bytes 6291464 | tf_op jit(solution)/shard_map/ppermute | solution.py:183
  493.1 6.2 collective-permute-start.12
  499.4 98.2 %collective-permute-start.39 = (f32[64,32,256]{2,1,0:T(8,128)}, f32[64,32,256]{2,1,0:T(8,128)S(1)}, u32[]{:S(2)}, u32[]{:S(2)}) collective-permute-start(f32[64,32,256]{2,1,0:T(8,128)} %get-tuple-element.69), channel_id=1, source_target_pairs={{2,0},{3,1},{4,2},{5,3},{6,4},{7,5},{10,8},{11,9},{12,10},{13,11},... | collective-permute-start | bytes 6291464 | tf_op jit(solution)/shard_map/ppermute | solution.py:186
  501.5 98.1 %collective-permute-start.34 = (f32[64,32,256]{2,1,0:T(8,128)}, f32[64,32,256]{2,1,0:T(8,128)S(1)}, u32[]{:S(2)}, u32[]{:S(2)}) collective-permute-start(f32[64,32,256]{2,1,0:T(8,128)} %get-tuple-element.71), channel_id=1, source_target_pairs={{2,0},{3,1},{4,2},{5,3},{6,4},{7,5},{10,8},{11,9},{12,10},{13,11},... | collective-permute-start | bytes 6291464 | tf_op jit(solution)/shard_map/ppermute | solution.py:186
  505.2 133.1 %collective-permute-start.29 = (f32[64,32,256]{2,1,0:T(8,128)}, f32[64,32,256]{2,1,0:T(8,128)S(1)}, u32[]{:S(2)}, u32[]{:S(2)}) collective-permute-start(f32[64,32,256]{2,1,0:T(8,128)} %get-tuple-element.72), channel_id=1, source_target_pairs={{2,0},{3,1},{4,2},{5,3},{6,4},{7,5},{10,8},{11,9},{12,10},{13,11},... | collective-permute-start | bytes 6291464 | tf_op jit(solution)/shard_map/ppermute | solution.py:186
  523.5 47.1 %collective-permute-start.13 = (f32[64,24,256]{2,1,0:T(8,128)}, f32[64,24,256]{2,1,0:T(8,128)}, u32[]{:S(2)}, u32[]{:S(2)}) collective-permute-start(f32[64,24,256]{2,1,0:T(8,128)} %get-tuple-element.36), channel_id=1, source_target_pairs={{1,3},{3,5},{5,7},{9,11},{11,13},{13,15},{17,19},{19,21},{21,23},{... | collective-permute-start | bytes 4718600 | tf_op jit(solution)/shard_map/ppermute | solution.py:189
  527.0 67.4 %collective-permute-start.43 = (f32[64,24,256]{2,1,0:T(8,128)S(1)}, f32[64,24,256]{2,1,0:T(8,128)}, u32[]{:S(2)}, u32[]{:S(2)}) collective-permute-start(f32[64,24,256]{2,1,0:T(8,128)S(1)} %copy-done.27), channel_id=1, source_target_pairs={{1,3},{3,5},{5,7},{9,11},{11,13},{13,15},{17,19},{19,21},{21,23},{... | collective-permute-start | bytes 4718600 | tf_op jit(solution)/shard_map/ppermute | solution.py:189
  570.6 112.6 %collective-permute-start.24 = (f32[64,32,256]{2,1,0:T(8,128)}, f32[64,32,256]{2,1,0:T(8,128)}, u32[]{:S(2)}, u32[]{:S(2)}) collective-permute-start(f32[64,32,256]{2,1,0:T(8,128)} %get-tuple-element.73), channel_id=1, source_target_pairs={{2,0},{3,1},{4,2},{5,3},{6,4},{7,5},{10,8},{11,9},{12,10},{13,11},... | collective-permute-start | bytes 6291464 | tf_op jit(solution)/shard_map/ppermute | solution.py:186
  594.4 90.9 %collective-permute-start.38 = (f32[64,32,256]{2,1,0:T(8,128)}, f32[64,32,256]{2,1,0:T(8,128)}, u32[]{:S(2)}, u32[]{:S(2)}) collective-permute-start(f32[64,32,256]{2,1,0:T(8,128)} %get-tuple-element.46), channel_id=1, source_target_pairs={{1,3},{3,5},{5,7},{9,11},{11,13},{13,15},{17,19},{19,21},{21,23},{... | collective-permute-start | bytes 6291464 | tf_op jit(solution)/shard_map/ppermute | solution.py:189
  597.6 182.1 %copy-start.2 = (f32[64,32,256]{2,1,0:T(8,128)}, f32[64,32,256]{2,1,0:T(8,128)S(1)}, u32[]{:S(2)}) copy-start(f32[64,32,256]{2,1,0:T(8,128)S(1)} %collective-permute-done.39.deep) | copy-start | bytes 6291460
  597.6 90.9 %collective-permute-start.33 = (f32[64,32,256]{2,1,0:T(8,128)}, f32[64,32,256]{2,1,0:T(8,128)}, u32[]{:S(2)}, u32[]{:S(2)}) collective-permute-start(f32[64,32,256]{2,1,0:T(8,128)} %get-tuple-element.44), channel_id=1, source_target_pairs={{1,3},{3,5},{5,7},{9,11},{11,13},{13,15},{17,19},{19,21},{21,23},{... | collective-permute-start | bytes 6291464 | tf_op jit(solution)/shard_map/ppermute | solution.py:189
  599.6 180.2 %copy-start.3 = (f32[64,32,256]{2,1,0:T(8,128)}, f32[64,32,256]{2,1,0:T(8,128)S(1)}, u32[]{:S(2)}) copy-start(f32[64,32,256]{2,1,0:T(8,128)S(1)} %collective-permute-done.34.deep) | copy-start | bytes 6291460
  599.6 132.2 %collective-permute-start.28 = (f32[64,32,256]{2,1,0:T(8,128)}, f32[64,32,256]{2,1,0:T(8,128)}, u32[]{:S(2)}, u32[]{:S(2)}) collective-permute-start(f32[64,32,256]{2,1,0:T(8,128)} %get-tuple-element.42), channel_id=1, source_target_pairs={{1,3},{3,5},{5,7},{9,11},{11,13},{13,15},{17,19},{19,21},{21,23},{... | collective-permute-start | bytes 6291464 | tf_op jit(solution)/shard_map/ppermute | solution.py:189
  638.3 141.5 %copy-start.4 = (f32[64,32,256]{2,1,0:T(8,128)}, f32[64,32,256]{2,1,0:T(8,128)S(1)}, u32[]{:S(2)}) copy-start(f32[64,32,256]{2,1,0:T(8,128)S(1)} %collective-permute-done.29.deep) | copy-start | bytes 6291460
  638.3 138.4 %collective-permute-start.23 = (f32[64,32,256]{2,1,0:T(8,128)}, f32[64,32,256]{2,1,0:T(8,128)}, u32[]{:S(2)}, u32[]{:S(2)}) collective-permute-start(f32[64,32,256]{2,1,0:T(8,128)} %get-tuple-element.40), channel_id=1, source_target_pairs={{1,3},{3,5},{5,7},{9,11},{11,13},{13,15},{17,19},{19,21},{21,23},{... | collective-permute-start | bytes 6291464 | tf_op jit(solution)/shard_map/ppermute | solution.py:189
  683.2 165.3 %collective-permute-start.4 = (f32[64,8,256]{2,1,0:T(8,128)}, f32[64,8,256]{2,1,0:T(8,128)S(1)}, u32[]{:S(2)}, u32[]{:S(2)}) collective-permute-start(f32[64,8,256]{2,1,0:T(8,128)} %get-tuple-element.64), channel_id=1, source_target_pairs={{2,0},{3,1},{4,2},{5,3},{6,4},{7,5},{10,8},{11,9},{12,10},{13,11},... | collective-permute-start | bytes 1572872 | tf_op jit(solution)/shard_map/ppermute | solution.py:186
  685.3 164.4 %collective-permute-start.3 = (f32[64,8,256]{2,1,0:T(8,128)}, f32[64,8,256]{2,1,0:T(8,128)}, u32[]{:S(2)}, u32[]{:S(2)}) collective-permute-start(f32[64,8,256]{2,1,0:T(8,128)} %get-tuple-element.32), channel_id=1, source_target_pairs={{1,3},{3,5},{5,7},{9,11},{11,13},{13,15},{17,19},{19,21},{21,23},{... | collective-permute-start | bytes 1572872 | tf_op jit(solution)/shard_map/ppermute | solution.py:189
  688.6 161.1 %collective-permute-start.53 = (f32[64,8,256]{2,1,0:T(8,128)}, f32[64,8,256]{2,1,0:T(8,128)}, u32[]{:S(2)}, u32[]{:S(2)}) collective-permute-start(f32[64,8,256]{2,1,0:T(8,128)} %get-tuple-element.52), channel_id=1, source_target_pairs={{1,3},{3,5},{5,7},{9,11},{11,13},{13,15},{17,19},{19,21},{21,23},{... | collective-permute-start | bytes 1572872 | tf_op jit(solution)/shard_map/ppermute | solution.py:189
  731.7 89.9 %collective-permute-start.8 = (f32[64,16,256]{2,1,0:T(8,128)}, f32[64,16,256]{2,1,0:T(8,128)}, u32[]{:S(2)}, u32[]{:S(2)}) collective-permute-start(f32[64,16,256]{2,1,0:T(8,128)} %get-tuple-element.34), channel_id=1, source_target_pairs={{1,3},{3,5},{5,7},{9,11},{11,13},{13,15},{17,19},{19,21},{21,23},{... | collective-permute-start | bytes 3145736 | tf_op jit(solution)/shard_map/ppermute | solution.py:189
  776.7 67.4 %collective-permute-start.48 = (f32[64,16,256]{2,1,0:T(8,128)S(1)}, f32[64,16,256]{2,1,0:T(8,128)}, u32[]{:S(2)}, u32[]{:S(2)}) collective-permute-start(f32[64,16,256]{2,1,0:T(8,128)S(1)} %copy-done.31), channel_id=1, source_target_pairs={{1,3},{3,5},{5,7},{9,11},{11,13},{13,15},{17,19},{19,21},{21,23},{... | collective-permute-start | bytes 3145736 | tf_op jit(solution)/shard_map/ppermute | solution.py:189
  821.6 156.8 %collective-permute-start.45 = (f32[64,24,256]{2,1,0:T(8,128)}, f32[64,24,256]{2,1,0:T(8,128)S(1)}, u32[]{:S(2)}, u32[]{:S(2)}) collective-permute-start(f32[64,24,256]{2,1,0:T(8,128)} %get-tuple-element.57), channel_id=1, source_target_pairs={{0,1},{1,0},{2,3},{3,2},{4,5},{5,4},{6,7},{7,6},{8,9},{9,8},{10,11... | collective-permute-start | bytes 4718600 | tf_op jit(solution)/shard_map/ppermute | solution.py:192
  844.1 134.7 %collective-permute-start.40 = (f32[64,32,256]{2,1,0:T(8,128)}, f32[64,32,256]{2,1,0:T(8,128)}, u32[]{:S(2)}, u32[]{:S(2)}) collective-permute-start(f32[64,32,256]{2,1,0:T(8,128)} %get-tuple-element.59), channel_id=1, source_target_pairs={{0,1},{1,0},{2,3},{3,2},{4,5},{5,4},{6,7},{7,6},{8,9},{9,8},{10,11... | collective-permute-start | bytes 6291464 | tf_op jit(solution)/shard_map/ppermute | solution.py:192
  848.5 128.5 %copy-start.19 = (f32[64,32,256]{2,1,0:T(8,128)S(1)}, f32[64,32,256]{2,1,0:T(8,128)}, u32[]{:S(2)}) copy-start(f32[64,32,256]{2,1,0:T(8,128)} %get-tuple-element.62) | copy-start | bytes 6291460
  848.5 130.0 %copy-start.13 = (f32[64,32,256]{2,1,0:T(8,128)S(1)}, f32[64,32,256]{2,1,0:T(8,128)}, u32[]{:S(2)}) copy-start(f32[64,32,256]{2,1,0:T(8,128)} %get-tuple-element.70) | copy-start | bytes 6291460
  848.5 128.7 %collective-permute-start.50 = (f32[64,16,256]{2,1,0:T(8,128)S(1)}, f32[64,16,256]{2,1,0:T(8,128)S(1)}, u32[]{:S(2)}, u32[]{:S(2)}) collective-permute-start(f32[64,16,256]{2,1,0:T(8,128)S(1)} %get-tuple-element.55), channel_id=1, source_target_pairs={{0,1},{1,0},{2,3},{3,2},{4,5},{5,4},{6,7},{7,6},{8,9},{9,8},{10,11... | collective-permute-start | bytes 3145736 | tf_op jit(solution)/shard_map/ppermute | solution.py:192
  852.7 127.3 %collective-permute-start.30 = (f32[64,32,256]{2,1,0:T(8,128)S(1)}, f32[64,32,256]{2,1,0:T(8,128)S(1)}, u32[]{:S(2)}, u32[]{:S(2)}) collective-permute-start(f32[64,32,256]{2,1,0:T(8,128)S(1)} %copy-done.20), channel_id=1, source_target_pairs={{0,1},{1,0},{2,3},{3,2},{4,5},{5,4},{6,7},{7,6},{8,9},{9,8},{10,11... | collective-permute-start | bytes 6291464 | tf_op jit(solution)/shard_map/ppermute | solution.py:192
  853.2 123.0 %collective-permute-start.55 = (f32[64,8,256]{2,1,0:T(8,128)S(1)}, f32[64,8,256]{2,1,0:T(8,128)S(1)}, u32[]{:S(2)}, u32[]{:S(2)}) collective-permute-start(f32[64,8,256]{2,1,0:T(8,128)S(1)} %get-tuple-element.53), channel_id=1, source_target_pairs={{0,1},{1,0},{2,3},{3,2},{4,5},{5,4},{6,7},{7,6},{8,9},{9,8},{10,11... | collective-permute-start | bytes 1572872 | tf_op jit(solution)/shard_map/ppermute | solution.py:192
  977.0 43.3 %collective-permute-start.35 = (f32[64,32,256]{2,1,0:T(8,128)S(1)}, f32[64,32,256]{2,1,0:T(8,128)S(1)}, u32[]{:S(2)}, u32[]{:S(2)}) collective-permute-start(f32[64,32,256]{2,1,0:T(8,128)S(1)} %copy-done.19), channel_id=1, source_target_pairs={{0,1},{1,0},{2,3},{3,2},{4,5},{5,4},{6,7},{7,6},{8,9},{9,8},{10,11... | collective-permute-start | bytes 6291464 | tf_op jit(solution)/shard_map/ppermute | solution.py:192
  977.2 88.1 %collective-permute-start.25 = (f32[64,32,256]{2,1,0:T(8,128)}, f32[64,32,256]{2,1,0:T(8,128)}, u32[]{:S(2)}, u32[]{:S(2)}) collective-permute-start(f32[64,32,256]{2,1,0:T(8,128)} %get-tuple-element.60), channel_id=1, source_target_pairs={{0,1},{1,0},{2,3},{3,2},{4,5},{5,4},{6,7},{7,6},{8,9},{9,8},{10,11... | collective-permute-start | bytes 6291464 | tf_op jit(solution)/shard_map/ppermute | solution.py:192
  978.4 131.8 %collective-permute-start.20 = (f32[64,32,256]{2,1,0:T(8,128)S(1)}, f32[64,32,256]{2,1,0:T(8,128)}, u32[]{:S(2)}, u32[]{:S(2)}) collective-permute-start(f32[64,32,256]{2,1,0:T(8,128)S(1)} %copy-done.13), channel_id=1, source_target_pairs={{0,1},{1,0},{2,3},{3,2},{4,5},{5,4},{6,7},{7,6},{8,9},{9,8},{10,11... | collective-permute-start | bytes 6291464 | tf_op jit(solution)/shard_map/ppermute | solution.py:192
  978.8 165.2 %collective-permute-start.15 = (f32[64,24,256]{2,1,0:T(8,128)}, f32[64,24,256]{2,1,0:T(8,128)}, u32[]{:S(2)}, u32[]{:S(2)}) collective-permute-start(f32[64,24,256]{2,1,0:T(8,128)} %get-tuple-element.58), channel_id=1, source_target_pairs={{0,1},{1,0},{2,3},{3,2},{4,5},{5,4},{6,7},{7,6},{8,9},{9,8},{10,11... | collective-permute-start | bytes 4718600 | tf_op jit(solution)/shard_map/ppermute | solution.py:192
  980.0 186.3 %collective-permute-start.10 = (f32[64,16,256]{2,1,0:T(8,128)}, f32[64,16,256]{2,1,0:T(8,128)S(1)}, u32[]{:S(2)}, u32[]{:S(2)}) collective-permute-start(f32[64,16,256]{2,1,0:T(8,128)} %get-tuple-element.56), channel_id=1, source_target_pairs={{0,1},{1,0},{2,3},{3,2},{4,5},{5,4},{6,7},{7,6},{8,9},{9,8},{10,11... | collective-permute-start | bytes 3145736 | tf_op jit(solution)/shard_map/ppermute | solution.py:192
  1021.6 156.0 %collective-permute-start.5 = (f32[64,8,256]{2,1,0:T(8,128)}, f32[64,8,256]{2,1,0:T(8,128)}, u32[]{:S(2)}, u32[]{:S(2)}) collective-permute-start(f32[64,8,256]{2,1,0:T(8,128)} %get-tuple-element.54), channel_id=1, source_target_pairs={{0,1},{1,0},{2,3},{3,2},{4,5},{5,4},{6,7},{7,6},{8,9},{9,8},{10,11... | collective-permute-start | bytes 1572872 | tf_op jit(solution)/shard_map/ppermute | solution.py:192
  (37 other events, 1065.8 us)

commit v2 on v1

v2 whole, which is shorter than its diff:
```python
import functools

import jax
import jax.numpy as jnp
from jax import lax
from jax.experimental import pallas as pl
from jax.experimental.pallas import tpu as pltpu
from jax.sharding import PartitionSpec as P

F32 = jnp.float32
BF16 = jnp.bfloat16
VMEM_LIMIT = 56 * 2**20
SPAN, LANES = 8, 128
LIGHT = pl.CostEstimate(flops=1000, transcendentals=0, bytes_accessed=1000)
PARAMS = pltpu.CompilerParams(vmem_limit_bytes=VMEM_LIMIT)
WHOLE = pl.BlockSpec(memory_space=pltpu.VMEM)


def gate(*values):
    return lax.optimization_barrier(values)


def flag(cond):
    return jnp.where(cond, 1.0, 0.0).astype(F32)


def halves(x):
    high = x.astype(BF16)
    low = (x - high.astype(F32)).astype(BF16)
    return high, low


def halves_outside(x):
    high = lax.reduce_precision(x, 8, 7)
    return high.astype(BF16), (x - high).astype(BF16)


def dot(a, b):
    return jnp.dot(a, b, preferred_element_type=F32)


def chunk_bounds(length):
    sizes = [1, 1, 2, 2, 2, 2, 2, 2, 1, 1]
    unit = length // sum(sizes)
    bounds, at = [], 0
    for size in sizes:
        bounds.append((at, size * unit))
        at += size * unit
    return bounds


def local_kernel(at, half, core, own_rows, occ, c_hi, c_lo, b_hi, b_lo, row_b, row_c, mine, peer):
    block, phases = occ.shape[0], occ.shape[2]
    size = mine.shape[2]
    first = pl.program_id(0) * block
    rows = [pl.ds(pl.multiple_of(core[n] * half + at, SPAN), size) for n in range(2)]
    for i in range(block):
        x = occ[i]
        x_hi, x_lo = halves(x)
        by_b = dot(b_hi[...], x_hi) + dot(b_hi[...], x_lo) + dot(b_lo[...], x_hi)
        y = jnp.concatenate([occ[i, rows[0]], occ[i, rows[1]]], axis=0)
        y_hi, y_lo = halves(y)
        by_c = dot(y_hi, c_hi[...]) + dot(y_lo, c_hi[...]) + dot(y_hi, c_lo[...])
        left = row_c[...] - own_rows[first + i] - row_b[...]
        base = by_c[:, :phases] + by_b[: 2 * size] + y * left
        rise = by_c[:, phases:] + by_b[2 * size :]
        mine[0, i] = base[:size]
        peer[0, i] = base[size:]
        mine[1, i] = rise[:size]
        peer[1, i] = rise[size:]


def local_terms(core, occ, own_rows, c_split, b_split, row_b, row_c, at, size):
    rows, mid, phases = occ.shape
    block = 4
    out = pl.BlockSpec((2, block, size, phases), lambda i, c: (0, i, 0, 0))
    return pl.pallas_call(
        functools.partial(local_kernel, at, mid // 2),
        grid_spec=pltpu.PrefetchScalarGridSpec(
            num_scalar_prefetch=1,
            grid=(rows // block,),
            in_specs=[
                pl.BlockSpec(memory_space=pltpu.SMEM),
                pl.BlockSpec((block, mid, phases), lambda i, c: (i, 0, 0)),
            ]
            + [WHOLE] * 6,
            out_specs=[out, out],
        ),
        out_shape=[jax.ShapeDtypeStruct((2, rows, size, phases), F32)] * 2,
        compiler_params=PARAMS,
        cost_estimate=LIGHT,
        name="local_terms",
    )(core, own_rows, occ, *c_split, *b_split, row_b, row_c)


def first_kernel(n_slabs, *refs):
    w_both, w_hi = refs[0], refs[1]
    slabs = refs[2 : 2 + n_slabs]
    mine, peer, stay_out, rise_out = refs[2 + n_slabs :]
    rows, span, lanes = stay_out.shape
    flat = [ref.reshape(rows * span, lanes) for ref in slabs]
    stay_flat = stay_out.reshape(rows * span, lanes)
    rise_flat = rise_out.reshape(rows * span, lanes)
    for b in range(0, span, 2):
        ats = [pl.ds(b, rows, stride=span), pl.ds(b + 1, rows, stride=span)]
        parts = [halves(jnp.concatenate([ref[at, :] for at in ats], axis=1)) for ref in flat]
        g_hi = jnp.concatenate([p[0] for p in parts], axis=0)
        g_lo = jnp.concatenate([p[1] for p in parts], axis=0)
        both = dot(w_both[...], g_hi)
        out = both[: 2 * rows] + both[2 * rows :] + dot(w_hi[...], g_lo)
        for n, at in enumerate(ats):
            stay_flat[at, :] = out[:rows, n * lanes : (n + 1) * lanes]
            rise_flat[at, :] = out[rows:, n * lanes : (n + 1) * lanes]
    half = rows // 2
    stay_out[:half] += mine[0]
    stay_out[half:] += peer[0]
    rise_out[:half] += mine[1]
    rise_out[half:] += peer[1]


def first_terms(w_both, w_hi, slabs, mine, peer, start):
    rows, size, phases = slabs[0].shape
    chunk = pl.BlockSpec((rows, SPAN, LANES), lambda j, h: (0, j, h))
    local_part = pl.BlockSpec((2, rows // 2, SPAN, LANES), lambda j, h: (0, 0, start // SPAN + j, h))
    return pl.pallas_call(
        functools.partial(first_kernel, len(slabs)),
        grid=(size // SPAN, phases // LANES),
        in_specs=[WHOLE, WHOLE] + [chunk] * len(slabs) + [local_part] * 2,
        out_specs=[chunk, chunk],
        out_shape=[jax.ShapeDtypeStruct((rows, size, phases), F32)] * 2,
        compiler_params=PARAMS,
        cost_estimate=LIGHT,
        name="first_terms",
    )(w_both, w_hi, *slabs, mine, peer)


def turn_kernel(parity, rise, lifted, deep, here, fall, out):
    @pl.when(parity[0] == 0)
    def _():
        out[...] = rise[...] + fall[1:2] * deep[...]

    @pl.when(parity[0] != 0)
    def _():
        out[...] = lifted[...] + fall[0:1] * here[...]


def turn(parity, rise, lifted, deep, here, fall):
    rows, size, phases = rise.shape
    chunk = pl.BlockSpec((rows, SPAN, phases), lambda j: (0, j, 0))
    return pl.pallas_call(
        turn_kernel,
        grid=(size // SPAN,),
        in_specs=[pl.BlockSpec(memory_space=pltpu.SMEM)] + [chunk] * 4 + [WHOLE],
        out_specs=chunk,
        out_shape=jax.ShapeDtypeStruct(rise.shape, F32),
        compiler_params=PARAMS,
        cost_estimate=LIGHT,
        name="turn",
    )(parity, rise, lifted, deep, here, fall)


def finish_kernel(has_out, core, scale, stay, fall, risen, deep, *refs):
    out, back = refs[has_out:]
    value = (stay[...] + risen[...] + fall[2:3] * deep[...]) * scale[0]
    half = value.shape[0] // 2
    out[...] = value[:half]
    back[...] = value[half:]


def finish(core, out, shape, scale, stay, fall, risen, deep, start):
    rows, size, phases = stay.shape
    chunk = pl.BlockSpec((rows, SPAN, phases), lambda j, c: (0, j, 0))
    steps = shape[1] // 2 // SPAN
    args = [core, scale, stay, fall, risen, deep]
    specs = [pl.BlockSpec(memory_space=pltpu.SMEM), chunk, WHOLE, chunk, chunk]
    alias = {}
    if out is not None:
        alias = {len(args): 0}
        args.append(out)
        specs.append(pl.BlockSpec(memory_space=pl.ANY))
    return pl.pallas_call(
        functools.partial(finish_kernel, len(alias)),
        grid_spec=pltpu.PrefetchScalarGridSpec(
            num_scalar_prefetch=1,
            grid=(size // SPAN,),
            in_specs=specs,
            out_specs=[
                pl.BlockSpec((rows // 2, SPAN, phases), lambda j, c: (0, c[0] * steps + start // SPAN + j, 0)),
                pl.BlockSpec((rows // 2, SPAN, phases), lambda j, c: (0, j, 0)),
            ],
        ),
        out_shape=[jax.ShapeDtypeStruct(shape, F32), jax.ShapeDtypeStruct((rows // 2, size, phases), F32)],
        input_output_aliases=alias,
        compiler_params=PARAMS,
        cost_estimate=LIGHT,
        name="finish",
    )(*args)


def place_kernel(core, piece, _, out):
    out[...] = piece[...]


def put(core, out, piece, start):
    rows, size, phases = piece.shape
    steps = out.shape[1] // 2 // SPAN
    return pl.pallas_call(
        place_kernel,
        grid_spec=pltpu.PrefetchScalarGridSpec(
            num_scalar_prefetch=1,
            grid=(size // SPAN,),
            in_specs=[
                pl.BlockSpec((rows, SPAN, phases), lambda j, c: (0, j, 0)),
                pl.BlockSpec(memory_space=pl.ANY),
            ],
            out_specs=pl.BlockSpec((rows, SPAN, phases), lambda j, c: (0, c[1] * steps + start // SPAN + j, 0)),
        ),
        out_shape=jax.ShapeDtypeStruct(out.shape, F32),
        input_output_aliases={2: 0},
        compiler_params=PARAMS,
        cost_estimate=LIGHT,
        name="put",
    )(core, piece, out)


def local(occupancy, rates, increments, draw, crusher_rate, bounds):
    n_cls, n_lvl = lax.axis_size("cls"), lax.axis_size("lvl")
    occ = occupancy[0]
    rows, mid, phases = occ.shape
    half = mid // 2
    level = lax.axis_index("lvl")
    place = lax.axis_index("cls")
    k = place % 2
    core = jnp.stack([k, 1 - k])
    even = level % 2 == 0
    bottom, top = bounds[0], bounds[1]

    def along_cls(v, by):
        return lax.ppermute(v, "cls", [(i, (i + by) % n_cls) for i in range(n_cls)])

    def other_core(v):
        return lax.ppermute(v, "cls", [(i, i ^ 1) for i in range(n_cls)])

    def two_down(v):
        return lax.ppermute(v, "lvl", [(i, i - 2) for i in range(2, n_lvl)])

    def two_up(v):
        return lax.ppermute(v, "lvl", [(i, i + 2) for i in range(1, n_lvl - 2, 2)])

    def pair_swap(v):
        return lax.ppermute(v, "lvl", [(i, i ^ 1) for i in range(n_lvl)])

    def cut(array, which, at, size):
        return lax.dynamic_slice_in_dim(array, core[which] * half + at, size, axis=1)

    chunks = chunk_bounds(half)
    n = len(chunks)
    shifts = [2 * s for s in range(1, n_cls // 2)]
    pieces = [(0, 1), (1, 3), (3, n)]
    sent = [None] * n
    token, tokens = None, []
    for lo, hi in pieces:
        at = chunks[lo][0]
        size = chunks[hi - 1][0] + chunks[hi - 1][1] - at
        give = cut(occ, 1, at, size)
        if token is not None:
            give, _ = gate(give, token)
        token = got = other_core(give)
        tokens.append(got)
        for s in range(lo, hi):
            start, length = chunks[s]
            own = cut(occ, 0, start, length)
            sent[s] = jnp.concatenate([own, lax.slice_in_dim(got, start - at, start - at + length, axis=1)], axis=0)

    far, deep = [None] * n, [None] * n

    def start_far(s, *after):
        operand = gate(sent[s], *after)[0] if after else sent[s]
        far[s] = [along_cls(operand, by) for by in shifts]

    def start_deep(s, *after):
        operand = gate(sent[s], *after)[0] if after else sent[s]
        deep[s] = two_down(operand)

    start_far(0)
    start_far(1)
    start_deep(0)

    row_total = jnp.sum(rates, axis=2)
    uniform_rate = jnp.sum(jnp.max(row_total, axis=1)) + jnp.max(crusher_rate)
    out_rows = row_total * flag((increments == 0) | (level + increments <= top))
    rise_ok = flag(level + 1 <= top)
    drop_here = crusher_rate * flag(level - draw >= bottom)
    drop_deep = crusher_rate * flag(level + 2 - draw >= bottom)
    once_here = (drop_here * flag(draw == 1) * flag(~even))[None, :]
    once_deep = (drop_deep * flag(draw == 1) * flag(even))[None, :]
    twice_deep = (drop_deep * flag(draw == 2))[None, :]
    fall_vec = jnp.concatenate([once_here, once_deep, twice_deep], axis=0)
    parity = (level % 2)[None]
    scale = (1.0 / uniform_rate)[None]

    stay_rows = rates * flag(increments == 0)[:, :, None]
    rise_rows = rates * (flag(increments == 1) * rise_ok)[:, :, None]

    c_split = halves_outside(jnp.concatenate([stay_rows[2], rise_rows[2]], axis=1))
    own_rows = lax.dynamic_slice_in_dim(out_rows[0], place * rows, rows)
    row_c = (uniform_rate - out_rows[2] - drop_here)[None, :]
    cuts = [(0, 2), (2, n)]
    parts = []
    for lo, hi in cuts:
        at = chunks[lo][0]
        size = chunks[hi - 1][0] + chunks[hi - 1][1] - at
        cat_b = jnp.concatenate([cut(r, w, at, size) for r in (stay_rows[1], rise_rows[1]) for w in range(2)], axis=1)
        row_b = jnp.concatenate([lax.dynamic_slice_in_dim(out_rows[1], core[w] * half + at, size) for w in range(2)])
        here = gate(occ, tokens[len(parts)], *(p[3] for p in parts))[0]
        mine, give = local_terms(
            core, here, own_rows, c_split, halves_outside(cat_b.T), row_b[:, None], row_c, at, size
        )
        parts += [(lo, hi, at, mine, other_core(give))]

    origin = [place, place ^ 1]
    for by in shifts:
        origin += [(place - by) % n_cls, ((place - by) % n_cls) ^ 1]
    mine = jnp.concatenate(
        [
            lax.dynamic_slice_in_dim(r, p * rows, rows, axis=1)
            for r in (stay_rows[0], rise_rows[0])
            for p in (place, place ^ 1)
        ],
        axis=1,
    ).T
    mine = jnp.concatenate([lax.dynamic_slice_in_dim(mine, o * rows, rows, axis=1) for o in origin], axis=1)
    a_hi, a_lo = halves_outside(mine)
    a_both = jnp.concatenate([a_hi, a_lo], axis=0)

    out = None
    stay, rise, lifted, risen, back = ([None] * n for _ in range(5))

    def close(s):
        return finish(core, out, occ.shape, scale, stay[s], fall_vec, risen[s], deep[s], chunks[s][0])

    for s in range(n + 3):
        if s < n:
            if s >= 3:
                far[s][0], risen[s - 3] = gate(far[s][0], risen[s - 3])
            if s >= 4:
                far[s][0], out = gate(far[s][0], out)
            if s + 2 < n:
                start_far(s + 2, far[s][0])
            if s + 1 < n:
                start_deep(s + 1, far[s][0], deep[s])
            lo, hi, at, mine, peer = next(p for p in parts if p[0] <= s < p[1])
            stay[s], rise[s] = first_terms(a_both, a_hi, [sent[s]] + far[s], mine, peer, chunks[s][0] - at)
            lift_me = rise[s]
            if s >= 1:
                lift_me, lifted[s - 1] = gate(lift_me, lifted[s - 1])
            lifted[s] = two_up(lift_me)
        if 1 <= s <= n:
            p = s - 1
            swap_me = turn(parity, rise[p], lifted[p], deep[p], sent[p], fall_vec)
            if p >= 1:
                swap_me, risen[p - 1] = gate(swap_me, risen[p - 1])
            risen[p] = pair_swap(swap_me)
        if 0 <= s - 2 < n:
            out, give = close(s - 2)
            back[s - 2] = other_core(give)
        if 0 <= s - 3 < n:
            out = put(core, out, back[s - 3], chunks[s - 3][0])
    return out[None]


def solution(mesh):
    in_specs = (P("lvl", "cls", None, None), P(), P(), P(), P(), P())
    out_specs = P("lvl", "cls", None, None)
    return jax.shard_map(local, mesh=mesh, in_specs=in_specs, out_specs=out_specs, check_vma=False)
```

time: 1190 us -> 580 us (0.49)
  waiting for transfers between devices: 855 us -> 158 us
  Pallas kernels: 162 us -> 225 us
  starting transfers between devices: 96.2 us -> 124 us
  local copies, waits for them, and re-layouts: 23.8 us -> 48.3 us
  other arithmetic: 40.1 us -> 17.2 us
    ppermute x11 -> x10, waiting for transfers between devices: 277 us -> 26.5 us  [pair_swap(): return lax.ppermute(v, 'lvl', [(i, i ^ 1) for i in range(n_lvl)])]
    ppermute x11 -> x10, waiting for transfers between devices: 268 us -> 51.5 us  [along_cls(): return lax.ppermute(v, 'cls', [(i, (i + by) % n_cls) for i in range(n_cls)])]
    ppermute x11 -> x10, waiting for transfers between devices: 156 us -> 22.8 us  [two_up(): return lax.ppermute(v, 'lvl', [(i, i + 2) for i in range(1, n_lvl - 2, 2)])]
    ppermute x11 -> x10, waiting for transfers between devices: 148 us -> 56.7 us  [two_down(): return lax.ppermute(v, 'lvl', [(i, i - 2) for i in range(2, n_lvl)])]
    pallas_call x23 -> x42, Pallas kernels: 162 us -> 225 us  [the longest x10 63.1 us: first_terms(): pl.pallas_call(functools.partial(first_kernel, len(slabs)), grid=(size //...]
    ppermute x12 -> x15, starting transfers between devices: 27.9 us -> 55.5 us  [other_core(): return lax.ppermute(v, 'cls', [(i, i ^ 1) for i in range(n_cls)])]
    add x4 -> x0, other arithmetic: 24.9 us -> none  [local(): jnp.where(even, rise_k, lifted) + once_deep * deep[k] + once_here * sent[k]]
    dynamic_slice x2 -> x26, local copies, waits for them, and re-layouts: 1.55 us -> 25.9 us  [the longest x16 19.1 us: cut(): lax.dynamic_slice_in_dim(array, core[which] * half + at, size, axis=1)]
  transfers between devices with their start and end apart: 56 -> 55, of which waited for: 25 -> 17; matrix products, arithmetic and copies ran while one was open for 5% -> 8% of each run, Pallas kernels for 14% -> 33%
where the time goes in v2:
time: 580 us; the launch traced here: 575 us
  Pallas kernels  225 us (39%)
  waiting for transfers between devices  158 us (27%)
  starting transfers between devices  124 us (21%)
  local copies, waits for them, and re-layouts  48.3 us (8%)
  other arithmetic  17.2 us (3%)
    pallas_call x10, Pallas kernels, first_terms(): pl.pallas_call(functools.partial(first_kernel, len(slabs)), grid=(size //...  63.1 us
    ppermute x10, waiting for transfers between devices, two_down(): return lax.ppermute(v, 'lvl', [(i, i - 2) for i in range(2, n_lvl)])  56.7 us
    ppermute x15, starting transfers between devices, other_core(): return lax.ppermute(v, 'cls', [(i, i ^ 1) for i in range(n_cls)])  55.5 us
    pallas_call x2, Pallas kernels, local_terms(): pl.pallas_call(functools.partial(local_kernel, at, mid // 2), grid_spec=p...  52.6 us
    ppermute x10, waiting for transfers between devices, along_cls(): return lax.ppermute(v, 'cls', [(i, (i + by) % n_cls) for i in range(n_cls)])  51.5 us
    pallas_call x10, Pallas kernels, finish(): pl.pallas_call(functools.partial(finish_kernel, len(alias)), grid_spec=pl...  42.3 us
    pallas_call x10, Pallas kernels, turn(): pl.pallas_call(turn_kernel, grid=(size // SPAN,), in_specs=[pl.BlockSpec(...  40.6 us
    ppermute x10, starting transfers between devices, two_up(): return lax.ppermute(v, 'lvl', [(i, i + 2) for i in range(1, n_lvl - 2, 2)])  34.3 us
  transfers between devices with their start and end apart: 55, of which 17 were waited for; matrix products, arithmetic and copies ran while one was open for 8% of the time, Pallas kernels for 33%

profile of v2, /device:TPU:21, one launch (start us, length us, event | category | flops | bytes accessed | tf_op | source)
XLA Modules:
  0.0 575.3 jit_solution(14978668250986289274)
XLA Ops:
  21.0 20.9 %local_terms.2 = (f32[2,64,16,256]{3,2,1,0:T(8,128)}, f32[2,64,16,256]{3,2,1,0:T(8,128)}) custom-call(s32[2]{0:T(128)} %pad_add_fusion.core, f32[64]{0:T(128)} %fusion.8.own_rows, f32[64,256,256]{2,1,0:T(8,128)} %bitcast.88, bf16[256,512]{1,0:T(8,128)(2,1)} %get-tuple-element.273.c_hi, bf16[256,512]{1,0:T(8,128)(2,1)} %get-tuple-element.272.c_lo, ...), custom_call_target="tpu_custom_call" | custom-call | flops 1000 | bytes 1000 | tf_op jit(solution)/shard_map/local_terms/pallas_call | solution.py:77
  41.9 31.7 %local_terms.3 = (f32[2,64,112,256]{3,2,1,0:T(8,128)}, f32[2,64,112,256]{3,2,1,0:T(8,128)}) custom-call(s32[2]{0:T(128)} %pad_add_fusion.core, f32[64]{0:T(128)} %fusion.8.own_rows, f32[64,256,256]{2,1,0:T(8,128)} %bitcast.89, bf16[256,512]{1,0:T(8,128)(2,1)} %get-tuple-element.273.c_hi, bf16[256,512]{1,0:T(8,128)(2,1)} %get-tuple-element.272.c_lo, ...), custom_call_target="tpu_custom_call" | custom-call | flops 1000 | bytes 1000 | tf_op jit(solution)/shard_map/local_terms/pallas_call | solution.py:77
  74.2 6.2 %dynamic-slice_bitcast_fusion = f32[64,96,256]{2,1,0:T(8,128)} fusion(f32[1,64,256,256]{3,2,1,0:T(8,128)} %param.6, s32[]{:T(128)S(6)} %select_n.133), kind=kLoop, calls=%fused_computation | loop fusion | bytes 12582916 | tf_op jit(solution)/shard_map/dynamic_slice | solution.py:254
  92.9 14.1 %collective-permute-done.6.refs_3_ = f32[128,8,256]{2,1,0:T(8,128)} collective-permute-done((f32[128,8,256]{2,1,0:T(8,128)S(1)}, f32[128,8,256]{2,1,0:T(8,128)}, u32[]{:S(2)}, u32[]{:S(2)}) %collective-permute-start.6) | collective-permute-done | bytes 1048608 | tf_op jit(solution)/shard_map/ppermute | solution.py:239
  108.9 5.2 dynamic-slice_bitcast_fusion.2
  116.9 4.5 first_terms.12
  121.4 3.2 collective-permute-start.9
  125.0 6.0 %collective-permute-done.3.refs_3_ = f32[128,8,256]{2,1,0:T(8,128)} collective-permute-done((f32[128,8,256]{2,1,0:T(8,128)S(1)}, f32[128,8,256]{2,1,0:T(8,128)}, u32[]{:S(2)}, u32[]{:S(2)}) %collective-permute-start.3) | collective-permute-done | bytes 1048608 | tf_op jit(solution)/shard_map/ppermute | solution.py:239
  133.0 4.5 first_terms.10
  137.5 9.7 %collective-permute-done.9.lifted = f32[128,8,256]{2,1,0:T(8,128)S(1)} collective-permute-done((f32[128,8,256]{2,1,0:T(8,128)}, f32[128,8,256]{2,1,0:T(8,128)S(1)}, u32[]{:S(2)}, u32[]{:S(2)}) %collective-permute-start.9) | collective-permute-done | bytes 1048608 | tf_op jit(solution)/shard_map/ppermute | solution.py:248
  147.2 3.3 collective-permute-start.10
  150.5 4.0 collective-permute-done.12.deep
  156.6 4.4 fusion.15
  163.8 12.0 %collective-permute-done.7.refs_3_ = f32[128,16,256]{2,1,0:T(8,128)} collective-permute-done((f32[128,16,256]{2,1,0:T(8,128)S(1)}, f32[128,16,256]{2,1,0:T(8,128)}, u32[]{:S(2)}, u32[]{:S(2)}) %collective-permute-start.7) | collective-permute-done | bytes 2097184 | tf_op jit(solution)/shard_map/ppermute | solution.py:239
  175.9 7.5 %first_terms.11 = (f32[128,16,256]{2,1,0:T(8,128)}, f32[128,16,256]{2,1,0:T(8,128)}) custom-call(bf16[512,256]{1,0:T(8,128)(2,1)} %pad_maximum_fusion.13.refs_0_, bf16[256,256]{1,0:T(8,128)(2,1)} %copy-done, f32[128,16,256]{2,1,0:T(8,128)} %copy-done.5, f32[128,16,256]{2,1,0:T(8,128)} %collective-permute-done.7.refs_3_, ...), custom_call_target="tpu_custom_call" | custom-call | flops 1000 | bytes 1000 | tf_op jit(solution)/shard_map/first_terms/pallas_call | solution.py:125
  183.3 3.2 collective-permute-start.16
  187.2 3.3 turn.11
  190.4 3.3 turn.10
  193.7 18.4 %collective-permute-done.13.risen = f32[128,8,256]{2,1,0:T(8,128)S(1)} collective-permute-done((f32[128,8,256]{2,1,0:T(8,128)}, f32[128,8,256]{2,1,0:T(8,128)S(1)}, u32[]{:S(2)}, u32[]{:S(2)}) %collective-permute-start.13) | collective-permute-done | bytes 1048608 | tf_op jit(solution)/shard_map/ppermute | solution.py:251
  220.8 7.5 %first_terms.13 = (f32[128,16,256]{2,1,0:T(8,128)}, f32[128,16,256]{2,1,0:T(8,128)}) custom-call(bf16[512,256]{1,0:T(8,128)(2,1)} %pad_maximum_fusion.13.refs_0_, bf16[256,256]{1,0:T(8,128)(2,1)} %copy-done, f32[128,16,256]{2,1,0:T(8,128)} %pad_maximum_fusion.2.refs_2_.here, f32[128,16,256]{2,1,0:T(8,128)} %collective-permute-done.4.refs_3_, ...), custom_call_target="tpu_custom_call" | custom-call | flops 1000 | bytes 1000 | tf_op jit(solution)/shard_map/first_terms/pallas_call | solution.py:125
  229.6 3.2 collective-permute-start.20
  232.8 4.6 turn.12
  237.5 3.7 finish.10
  241.3 4.2 collective-permute-start.19
  245.7 11.4 %collective-permute-done.21.deep = f32[128,16,256]{2,1,0:T(8,128)} collective-permute-done((f32[128,16,256]{2,1,0:T(8,128)}, f32[128,16,256]{2,1,0:T(8,128)}, u32[]{:S(2)}, u32[]{:S(2)}) %collective-permute-start.21) | collective-permute-done | bytes 2097184 | tf_op jit(solution)/shard_map/ppermute | solution.py:245
  259.1 3.6 finish.11
  266.5 7.6 %first_terms.14 = (f32[128,16,256]{2,1,0:T(8,128)}, f32[128,16,256]{2,1,0:T(8,128)}) custom-call(bf16[512,256]{1,0:T(8,128)(2,1)} %pad_maximum_fusion.13.refs_0_, bf16[256,256]{1,0:T(8,128)(2,1)} %copy-done, f32[128,16,256]{2,1,0:T(8,128)} %copy-done.4, f32[128,16,256]{2,1,0:T(8,128)} %collective-permute-done.15.refs_3_, ...), custom_call_target="tpu_custom_call" | custom-call | flops 1000 | bytes 1000 | tf_op jit(solution)/shard_map/first_terms/pallas_call | solution.py:125
  275.0 3.6 collective-permute-start.26
  278.6 4.6 turn.13
  283.2 6.8 %collective-permute-start.23 = (f32[64,8,256]{2,1,0:T(8,128)}, f32[64,8,256]{2,1,0:T(8,128)S(1)}, u32[]{:S(2)}, u32[]{:S(2)}) collective-permute-start(f32[64,8,256]{2,1,0:T(8,128)} %get-tuple-element.166), channel_id=1, source_target_pairs={{0,8},{8,0},{16,24},{24,16},{1,9},{9,1},{17,25},{25,17},{2,10},{10... | collective-permute-start | bytes 1572872 | tf_op jit(solution)/shard_map/ppermute | solution.py:242
  291.8 9.4 %collective-permute-done.27.deep = f32[128,16,256]{2,1,0:T(8,128)} collective-permute-done((f32[128,16,256]{2,1,0:T(8,128)S(1)}, f32[128,16,256]{2,1,0:T(8,128)}, u32[]{:S(2)}, u32[]{:S(2)}) %collective-permute-start.27) | collective-permute-done | bytes 2097184 | tf_op jit(solution)/shard_map/ppermute | solution.py:245
  303.2 4.6 finish.12
  311.7 7.6 %first_terms.15 = (f32[128,16,256]{2,1,0:T(8,128)}, f32[128,16,256]{2,1,0:T(8,128)}) custom-call(bf16[512,256]{1,0:T(8,128)(2,1)} %pad_maximum_fusion.13.refs_0_, bf16[256,256]{1,0:T(8,128)(2,1)} %copy-done, f32[128,16,256]{2,1,0:T(8,128)} %copy-done.1, f32[128,16,256]{2,1,0:T(8,128)} %collective-permute-done.14.refs_3_, ...), custom_call_target="tpu_custom_call" | custom-call | flops 1000 | bytes 1000 | tf_op jit(solution)/shard_map/first_terms/pallas_call | solution.py:125
  319.3 4.6 collective-permute-start.30
  323.9 4.5 turn.14
  328.4 8.6 %collective-permute-start.29 = (f32[64,16,256]{2,1,0:T(8,128)}, f32[64,16,256]{2,1,0:T(8,128)}, u32[]{:S(2)}, u32[]{:S(2)}) collective-permute-start(f32[64,16,256]{2,1,0:T(8,128)} %get-tuple-element.180), channel_id=1, source_target_pairs={{0,8},{8,0},{16,24},{24,16},{1,9},{9,1},{17,25},{25,17},{2,10},{10... | collective-permute-start | bytes 3145736 | tf_op jit(solution)/shard_map/ppermute | solution.py:242
  338.4 6.8 %collective-permute-done.31.deep = f32[128,16,256]{2,1,0:T(8,128)} collective-permute-done((f32[128,16,256]{2,1,0:T(8,128)S(1)}, f32[128,16,256]{2,1,0:T(8,128)}, u32[]{:S(2)}, u32[]{:S(2)}) %collective-permute-start.31) | collective-permute-done | bytes 2097184 | tf_op jit(solution)/shard_map/ppermute | solution.py:245
  347.3 4.7 finish.13
  355.9 7.6 %first_terms.16 = (f32[128,16,256]{2,1,0:T(8,128)}, f32[128,16,256]{2,1,0:T(8,128)}) custom-call(bf16[512,256]{1,0:T(8,128)(2,1)} %pad_maximum_fusion.13.refs_0_, bf16[256,256]{1,0:T(8,128)(2,1)} %copy-done, f32[128,16,256]{2,1,0:T(8,128)} %copy-done.2, f32[128,16,256]{2,1,0:T(8,128)} %collective-permute-done.25.refs_3_, ...), custom_call_target="tpu_custom_call" | custom-call | flops 1000 | bytes 1000 | tf_op jit(solution)/shard_map/first_terms/pallas_call | solution.py:125
  363.5 3.3 collective-permute-start.36
  366.8 4.6 turn.15
  371.5 10.6 %collective-permute-start.33 = (f32[64,16,256]{2,1,0:T(8,128)}, f32[64,16,256]{2,1,0:T(8,128)S(1)}, u32[]{:S(2)}, u32[]{:S(2)}) collective-permute-start(f32[64,16,256]{2,1,0:T(8,128)} %get-tuple-element.192), channel_id=1, source_target_pairs={{0,8},{8,0},{16,24},{24,16},{1,9},{9,1},{17,25},{25,17},{2,10},{10... | collective-permute-start | bytes 3145736 | tf_op jit(solution)/shard_map/ppermute | solution.py:242
  382.0 7.3 %collective-permute-done.37.deep = f32[128,16,256]{2,1,0:T(8,128)S(1)} collective-permute-done((f32[128,16,256]{2,1,0:T(8,128)S(1)}, f32[128,16,256]{2,1,0:T(8,128)S(1)}, u32[]{:S(2)}, u32[]{:S(2)}) %collective-permute-start.37) | collective-permute-done | bytes 2097184 | tf_op jit(solution)/shard_map/ppermute | solution.py:245
  391.4 4.7 finish.14
  399.8 7.5 %first_terms.17 = (f32[128,16,256]{2,1,0:T(8,128)}, f32[128,16,256]{2,1,0:T(8,128)}) custom-call(bf16[512,256]{1,0:T(8,128)(2,1)} %pad_maximum_fusion.13.refs_0_, bf16[256,256]{1,0:T(8,128)(2,1)} %copy-done, f32[128,16,256]{2,1,0:T(8,128)} %copy-done.3, f32[128,16,256]{2,1,0:T(8,128)} %collective-permute-done.24.refs_3_, ...), custom_call_target="tpu_custom_call" | custom-call | flops 1000 | bytes 1000 | tf_op jit(solution)/shard_map/first_terms/pallas_call | solution.py:125
  407.3 3.3 collective-permute-start.40
  410.7 4.6 turn.16
  416.8 11.9 %collective-permute-start.39 = (f32[64,16,256]{2,1,0:T(8,128)}, f32[64,16,256]{2,1,0:T(8,128)}, u32[]{:S(2)}, u32[]{:S(2)}) collective-permute-start(f32[64,16,256]{2,1,0:T(8,128)} %get-tuple-element.206), channel_id=1, source_target_pairs={{0,8},{8,0},{16,24},{24,16},{1,9},{9,1},{17,25},{25,17},{2,10},{10... | collective-permute-start | bytes 3145736 | tf_op jit(solution)/shard_map/ppermute | solution.py:242
  429.9 4.6 finish.15
  437.2 16.3 %collective-permute-done.35.refs_3_ = f32[128,8,256]{2,1,0:T(8,128)S(1)} collective-permute-done((f32[128,8,256]{2,1,0:T(8,128)S(1)}, f32[128,8,256]{2,1,0:T(8,128)S(1)}, u32[]{:S(2)}, u32[]{:S(2)}) %collective-permute-start.35) | collective-permute-done | bytes 1048608 | tf_op jit(solution)/shard_map/ppermute | solution.py:239
  454.5 4.4 first_terms.18
  460.4 4.6 turn.17
  471.0 3.4 collective-permute-start.44
  474.4 17.8 %collective-permute-done.46.deep = f32[128,8,256]{2,1,0:T(8,128)S(1)} collective-permute-done((f32[128,8,256]{2,1,0:T(8,128)S(1)}, f32[128,8,256]{2,1,0:T(8,128)S(1)}, u32[]{:S(2)}, u32[]{:S(2)}) %collective-permute-start.46) | collective-permute-done | bytes 1048608 | tf_op jit(solution)/shard_map/ppermute | solution.py:245
  494.6 4.6 finish.16
  503.9 4.5 first_terms.19
  511.6 3.2 turn.19
  517.3 4.6 finish.17
  523.2 10.8 %collective-permute-done.45.lifted = f32[128,8,256]{2,1,0:T(8,128)S(1)} collective-permute-done((f32[128,8,256]{2,1,0:T(8,128)}, f32[128,8,256]{2,1,0:T(8,128)S(1)}, u32[]{:S(2)}, u32[]{:S(2)}) %collective-permute-start.45) | collective-permute-done | bytes 1048608 | tf_op jit(solution)/shard_map/ppermute | solution.py:248
  535.0 3.3 turn.18
  542.0 3.6 finish.18
  552.2 8.1 %collective-permute-done.50.risen = f32[128,8,256]{2,1,0:T(8,128)S(1)} collective-permute-done((f32[128,8,256]{2,1,0:T(8,128)}, f32[128,8,256]{2,1,0:T(8,128)S(1)}, u32[]{:S(2)}, u32[]{:S(2)}) %collective-permute-start.50) | collective-permute-done | bytes 1048608 | tf_op jit(solution)/shard_map/ppermute | solution.py:251
  561.2 3.6 finish.19
  564.8 3.8 collective-permute-start.53
  (251 shorter events, 128.9 us)
Async XLA Ops:
  3.2 10.2 %collective-permute-start = (f32[64,8,256]{2,1,0:T(8,128)S(1)}, f32[64,8,256]{2,1,0:T(8,128)}, u32[]{:S(2)}, u32[]{:S(2)}) collective-permute-start(f32[64,8,256]{2,1,0:T(8,128)S(1)} %get-tuple-element.248), channel_id=1, source_target_pairs={{0,8},{8,0},{16,24},{24,16},{1,9},{9,1},{17,25},{25,17},{2,10},{10... | collective-permute-start | bytes 1572872 | tf_op jit(solution)/shard_map/ppermute | solution.py:242
  13.4 28.5 %collective-permute-start.1 = (f32[64,24,256]{2,1,0:T(8,128)}, f32[64,24,256]{2,1,0:T(8,128)S(1)}, u32[]{:S(2)}, u32[]{:S(2)}) collective-permute-start(f32[64,24,256]{2,1,0:T(8,128)} %dynamic-slice_bitcast_fusion.1), channel_id=1, source_target_pairs={{0,8},{8,0},{16,24},{24,16},{1,9},{9,1},{17,25},{25,17},{2,10},{10... | collective-permute-start | bytes 4718600 | tf_op jit(solution)/shard_map/ppermute | solution.py:242
  41.9 31.7 %copy-start.20 = (f32[64,24,256]{2,1,0:T(8,128)}, f32[64,24,256]{2,1,0:T(8,128)S(1)}, u32[]{:S(2)}) copy-start(f32[64,24,256]{2,1,0:T(8,128)S(1)} %collective-permute-done.1) | copy-start | bytes 4718596
  73.6 102.3 %collective-permute-start.8 = (f32[2,64,112,256]{3,2,1,0:T(8,128)}, f32[2,64,112,256]{3,2,1,0:T(8,128)}, u32[]{:S(2)}, u32[]{:S(2)}) collective-permute-start(f32[2,64,112,256]{3,2,1,0:T(8,128)} %get-tuple-element.135), channel_id=1, source_target_pairs={{0,8},{8,0},{16,24},{24,16},{1,9},{9,1},{17,25},{25,17},{2,10},{10... | collective-permute-start | bytes 44040200 | tf_op jit(solution)/shard_map/ppermute | solution.py:242
  80.4 76.2 %collective-permute-start.2 = (f32[64,96,256]{2,1,0:T(8,128)}, f32[64,96,256]{2,1,0:T(8,128)}, u32[]{:S(2)}, u32[]{:S(2)}) collective-permute-start(f32[64,96,256]{2,1,0:T(8,128)} %dynamic-slice_bitcast_fusion), channel_id=1, source_target_pairs={{0,8},{8,0},{16,24},{24,16},{1,9},{9,1},{17,25},{25,17},{2,10},{10... | collective-permute-start | bytes 18874376 | tf_op jit(solution)/shard_map/ppermute | solution.py:242
  80.4 35.1 %collective-permute-start.5 = (f32[2,64,16,256]{3,2,1,0:T(8,128)}, f32[2,64,16,256]{3,2,1,0:T(8,128)S(1)}, u32[]{:S(2)}, u32[]{:S(2)}) collective-permute-start(f32[2,64,16,256]{3,2,1,0:T(8,128)} %get-tuple-element.130), channel_id=1, source_target_pairs={{0,8},{8,0},{16,24},{24,16},{1,9},{9,1},{17,25},{25,17},{2,10},{10... | collective-permute-start | bytes 6291464 | tf_op jit(solution)/shard_map/ppermute | solution.py:242
  82.0 24.9 %collective-permute-start.6 = (f32[128,8,256]{2,1,0:T(8,128)S(1)}, f32[128,8,256]{2,1,0:T(8,128)}, u32[]{:S(2)}, u32[]{:S(2)}) collective-permute-start(f32[128,8,256]{2,1,0:T(8,128)S(1)} %pad_maximum_fusion.8.refs_2_.here), channel_id=1, source_target_pairs={{0,16},{8,24},{16,0},{24,8},{1,17},{9,25},{17,1},{25,9},{2,18},{10... | collective-permute-start | bytes 3145736 | tf_op jit(solution)/shard_map/ppermute | solution.py:239
  89.2 35.4 %collective-permute-start.11 = (f32[128,8,256]{2,1,0:T(8,128)S(1)}, f32[128,8,256]{2,1,0:T(8,128)S(1)}, u32[]{:S(2)}, u32[]{:S(2)}) collective-permute-start(f32[128,8,256]{2,1,0:T(8,128)S(1)} %pad_maximum_fusion.8.refs_2_.here), channel_id=1, source_target_pairs={{2,0},{3,1},{4,2},{5,3},{6,4},{7,5},{10,8},{11,9},{12,10},{13,11},... | collective-permute-start | bytes 3145736 | tf_op jit(solution)/shard_map/ppermute | solution.py:245
  92.8 21.4 %copy-start = (bf16[256,256]{1,0:T(8,128)(2,1)}, bf16[256,256]{1,0:T(8,128)(2,1)S(1)}, u32[]{:S(2)}) copy-start(bf16[256,256]{1,0:T(8,128)(2,1)S(1)} %get-tuple-element.274.refs_1_) | copy-start | bytes 393220
  92.9 38.1 %copy-start.7 = (f32[128,8,256]{2,1,0:T(8,128)}, f32[128,8,256]{2,1,0:T(8,128)S(1)}, u32[]{:S(2)}) copy-start(f32[128,8,256]{2,1,0:T(8,128)S(1)} %pad_maximum_fusion.7.refs_2_.here) | copy-start | bytes 3145732
  107.0 24.0 %collective-permute-start.3 = (f32[128,8,256]{2,1,0:T(8,128)S(1)}, f32[128,8,256]{2,1,0:T(8,128)}, u32[]{:S(2)}, u32[]{:S(2)}) collective-permute-start(f32[128,8,256]{2,1,0:T(8,128)S(1)} %pad_maximum_fusion.7.refs_2_.here), channel_id=1, source_target_pairs={{0,16},{8,24},{16,0},{24,8},{1,17},{9,25},{17,1},{25,9},{2,18},{10... | collective-permute-start | bytes 3145736 | tf_op jit(solution)/shard_map/ppermute | solution.py:239
  115.5 39.0 %copy-start.5 = (f32[128,16,256]{2,1,0:T(8,128)}, f32[128,16,256]{2,1,0:T(8,128)S(1)}, u32[]{:S(2)}) copy-start(f32[128,16,256]{2,1,0:T(8,128)S(1)} %pad_maximum_fusion.3.refs_2_.here) | copy-start | bytes 6291460
  121.4 25.7 %collective-permute-start.9 = (f32[128,8,256]{2,1,0:T(8,128)}, f32[128,8,256]{2,1,0:T(8,128)S(1)}, u32[]{:S(2)}, u32[]{:S(2)}) collective-permute-start(f32[128,8,256]{2,1,0:T(8,128)} %get-tuple-element.137.rise), channel_id=1, source_target_pairs={{1,3},{3,5},{5,7},{9,11},{11,13},{13,15},{17,19},{19,21},{21,23},{... | collective-permute-start | bytes 3145736 | tf_op jit(solution)/shard_map/ppermute | solution.py:248
  124.6 51.2 %collective-permute-start.7 = (f32[128,16,256]{2,1,0:T(8,128)S(1)}, f32[128,16,256]{2,1,0:T(8,128)}, u32[]{:S(2)}, u32[]{:S(2)}) collective-permute-start(f32[128,16,256]{2,1,0:T(8,128)S(1)} %pad_maximum_fusion.3.refs_2_.here), channel_id=1, source_target_pairs={{0,16},{8,24},{16,0},{24,8},{1,17},{9,25},{17,1},{25,9},{2,18},{10... | collective-permute-start | bytes 6291464 | tf_op jit(solution)/shard_map/ppermute | solution.py:239
  130.9 23.6 %collective-permute-start.12 = (f32[128,8,256]{2,1,0:T(8,128)S(1)}, f32[128,8,256]{2,1,0:T(8,128)S(1)}, u32[]{:S(2)}, u32[]{:S(2)}) collective-permute-start(f32[128,8,256]{2,1,0:T(8,128)S(1)} %pad_maximum_fusion.7.refs_2_.here), channel_id=1, source_target_pairs={{2,0},{3,1},{4,2},{5,3},{6,4},{7,5},{10,8},{11,9},{12,10},{13,11},... | collective-permute-start | bytes 3145736 | tf_op jit(solution)/shard_map/ppermute | solution.py:245
  147.2 36.2 %collective-permute-start.10 = (f32[128,8,256]{2,1,0:T(8,128)}, f32[128,8,256]{2,1,0:T(8,128)}, u32[]{:S(2)}, u32[]{:S(2)}) collective-permute-start(f32[128,8,256]{2,1,0:T(8,128)} %get-tuple-element.138.rise), channel_id=1, source_target_pairs={{1,3},{3,5},{5,7},{9,11},{11,13},{13,15},{17,19},{19,21},{21,23},{... | collective-permute-start | bytes 3145736 | tf_op jit(solution)/shard_map/ppermute | solution.py:248
  154.5 57.8 %collective-permute-start.17 = (f32[128,16,256]{2,1,0:T(8,128)S(1)}, f32[128,16,256]{2,1,0:T(8,128)S(1)}, u32[]{:S(2)}, u32[]{:S(2)}) collective-permute-start(f32[128,16,256]{2,1,0:T(8,128)S(1)} %pad_maximum_fusion.3.refs_2_.here), channel_id=1, source_target_pairs={{2,0},{3,1},{4,2},{5,3},{6,4},{7,5},{10,8},{11,9},{12,10},{13,11},... | collective-permute-start | bytes 6291464 | tf_op jit(solution)/shard_map/ppermute | solution.py:245
  162.6 58.2 %collective-permute-start.4 = (f32[128,16,256]{2,1,0:T(8,128)}, f32[128,16,256]{2,1,0:T(8,128)}, u32[]{:S(2)}, u32[]{:S(2)}) collective-permute-start(f32[128,16,256]{2,1,0:T(8,128)} %pad_maximum_fusion.2.refs_2_.here), channel_id=1, source_target_pairs={{0,16},{8,24},{16,0},{24,8},{1,17},{9,25},{17,1},{25,9},{2,18},{10... | collective-permute-start | bytes 6291464 | tf_op jit(solution)/shard_map/ppermute | solution.py:239
  183.3 46.3 %collective-permute-start.16 = (f32[128,16,256]{2,1,0:T(8,128)}, f32[128,16,256]{2,1,0:T(8,128)}, u32[]{:S(2)}, u32[]{:S(2)}) collective-permute-start(f32[128,16,256]{2,1,0:T(8,128)} %get-tuple-element.147.rise), channel_id=1, source_target_pairs={{1,3},{3,5},{5,7},{9,11},{11,13},{13,15},{17,19},{19,21},{21,23},{... | collective-permute-start | bytes 6291464 | tf_op jit(solution)/shard_map/ppermute | solution.py:248
  190.4 21.6 %collective-permute-start.13 = (f32[128,8,256]{2,1,0:T(8,128)}, f32[128,8,256]{2,1,0:T(8,128)S(1)}, u32[]{:S(2)}, u32[]{:S(2)}) collective-permute-start(f32[128,8,256]{2,1,0:T(8,128)} %turn.11), channel_id=1, source_target_pairs={{0,1},{1,0},{2,3},{3,2},{4,5},{5,4},{6,7},{7,6},{8,9},{9,8},{10,11... | collective-permute-start | bytes 3145736 | tf_op jit(solution)/shard_map/ppermute | solution.py:251
  212.1 25.4 %collective-permute-start.18 = (f32[128,8,256]{2,1,0:T(8,128)}, f32[128,8,256]{2,1,0:T(8,128)}, u32[]{:S(2)}, u32[]{:S(2)}) collective-permute-start(f32[128,8,256]{2,1,0:T(8,128)} %turn.10), channel_id=1, source_target_pairs={{0,1},{1,0},{2,3},{3,2},{4,5},{5,4},{6,7},{7,6},{8,9},{9,8},{10,11... | collective-permute-start | bytes 3145736 | tf_op jit(solution)/shard_map/ppermute | solution.py:251
  212.4 44.7 %collective-permute-start.21 = (f32[128,16,256]{2,1,0:T(8,128)}, f32[128,16,256]{2,1,0:T(8,128)}, u32[]{:S(2)}, u32[]{:S(2)}) collective-permute-start(f32[128,16,256]{2,1,0:T(8,128)} %pad_maximum_fusion.2.refs_2_.here), channel_id=1, source_target_pairs={{2,0},{3,1},{4,2},{5,3},{6,4},{7,5},{10,8},{11,9},{12,10},{13,11},... | collective-permute-start | bytes 6291464 | tf_op jit(solution)/shard_map/ppermute | solution.py:245
  216.4 40.7 %copy-start.4 = (f32[128,16,256]{2,1,0:T(8,128)}, f32[128,16,256]{2,1,0:T(8,128)S(1)}, u32[]{:S(2)}) copy-start(f32[128,16,256]{2,1,0:T(8,128)S(1)} %pad_maximum_fusion.4.refs_2_.here) | copy-start | bytes 6291460
  216.4 50.1 %collective-permute-start.15 = (f32[128,16,256]{2,1,0:T(8,128)S(1)}, f32[128,16,256]{2,1,0:T(8,128)}, u32[]{:S(2)}, u32[]{:S(2)}) collective-permute-start(f32[128,16,256]{2,1,0:T(8,128)S(1)} %pad_maximum_fusion.4.refs_2_.here), channel_id=1, source_target_pairs={{0,16},{8,24},{16,0},{24,8},{1,17},{9,25},{17,1},{25,9},{2,18},{10... | collective-permute-start | bytes 6291464 | tf_op jit(solution)/shard_map/ppermute | solution.py:239
  229.6 45.4 %collective-permute-start.20 = (f32[128,16,256]{2,1,0:T(8,128)}, f32[128,16,256]{2,1,0:T(8,128)}, u32[]{:S(2)}, u32[]{:S(2)}) collective-permute-start(f32[128,16,256]{2,1,0:T(8,128)} %get-tuple-element.160.rise), channel_id=1, source_target_pairs={{1,3},{3,5},{5,7},{9,11},{11,13},{13,15},{17,19},{19,21},{21,23},{... | collective-permute-start | bytes 6291464 | tf_op jit(solution)/shard_map/ppermute | solution.py:248
  237.5 45.7 %collective-permute-start.22 = (f32[128,16,256]{2,1,0:T(8,128)}, f32[128,16,256]{2,1,0:T(8,128)}, u32[]{:S(2)}, u32[]{:S(2)}) collective-permute-start(f32[128,16,256]{2,1,0:T(8,128)} %turn.12), channel_id=1, source_target_pairs={{0,1},{1,0},{2,3},{3,2},{4,5},{5,4},{6,7},{7,6},{8,9},{9,8},{10,11... | collective-permute-start | bytes 6291464 | tf_op jit(solution)/shard_map/ppermute | solution.py:251
  241.3 21.5 %collective-permute-start.19 = (f32[64,8,256]{2,1,0:T(8,128)}, f32[64,8,256]{2,1,0:T(8,128)S(1)}, u32[]{:S(2)}, u32[]{:S(2)}) collective-permute-start(f32[64,8,256]{2,1,0:T(8,128)} %get-tuple-element.154), channel_id=1, source_target_pairs={{0,8},{8,0},{16,24},{24,16},{1,9},{9,1},{17,25},{25,17},{2,10},{10... | collective-permute-start | bytes 1572872 | tf_op jit(solution)/shard_map/ppermute | solution.py:242
  245.7 55.5 %copy-start.1 = (f32[128,16,256]{2,1,0:T(8,128)}, f32[128,16,256]{2,1,0:T(8,128)S(1)}, u32[]{:S(2)}) copy-start(f32[128,16,256]{2,1,0:T(8,128)S(1)} %pad_maximum_fusion.1.refs_2_.here) | copy-start | bytes 6291460
  257.1 44.1 %collective-permute-start.27 = (f32[128,16,256]{2,1,0:T(8,128)S(1)}, f32[128,16,256]{2,1,0:T(8,128)}, u32[]{:S(2)}, u32[]{:S(2)}) collective-permute-start(f32[128,16,256]{2,1,0:T(8,128)S(1)} %pad_maximum_fusion.4.refs_2_.here), channel_id=1, source_target_pairs={{2,0},{3,1},{4,2},{5,3},{6,4},{7,5},{10,8},{11,9},{12,10},{13,11},... | collective-permute-start | bytes 6291464 | tf_op jit(solution)/shard_map/ppermute | solution.py:245
  262.7 48.9 %collective-permute-start.14 = (f32[128,16,256]{2,1,0:T(8,128)S(1)}, f32[128,16,256]{2,1,0:T(8,128)}, u32[]{:S(2)}, u32[]{:S(2)}) collective-permute-start(f32[128,16,256]{2,1,0:T(8,128)S(1)} %pad_maximum_fusion.1.refs_2_.here), channel_id=1, source_target_pairs={{0,16},{8,24},{16,0},{24,8},{1,17},{9,25},{17,1},{25,9},{2,18},{10... | collective-permute-start | bytes 6291464 | tf_op jit(solution)/shard_map/ppermute | solution.py:239
  275.0 44.3 %collective-permute-start.26 = (f32[128,16,256]{2,1,0:T(8,128)}, f32[128,16,256]{2,1,0:T(8,128)}, u32[]{:S(2)}, u32[]{:S(2)}) collective-permute-start(f32[128,16,256]{2,1,0:T(8,128)} %get-tuple-element.174.rise), channel_id=1, source_target_pairs={{1,3},{3,5},{5,7},{9,11},{11,13},{13,15},{17,19},{19,21},{21,23},{... | collective-permute-start | bytes 6291464 | tf_op jit(solution)/shard_map/ppermute | solution.py:248
  283.2 45.2 %collective-permute-start.28 = (f32[128,16,256]{2,1,0:T(8,128)}, f32[128,16,256]{2,1,0:T(8,128)}, u32[]{:S(2)}, u32[]{:S(2)}) collective-permute-start(f32[128,16,256]{2,1,0:T(8,128)} %turn.13), channel_id=1, source_target_pairs={{0,1},{1,0},{2,3},{3,2},{4,5},{5,4},{6,7},{7,6},{8,9},{9,8},{10,11... | collective-permute-start | bytes 6291464 | tf_op jit(solution)/shard_map/ppermute | solution.py:251
  283.2 24.7 %collective-permute-start.23 = (f32[64,8,256]{2,1,0:T(8,128)}, f32[64,8,256]{2,1,0:T(8,128)S(1)}, u32[]{:S(2)}, u32[]{:S(2)}) collective-permute-start(f32[64,8,256]{2,1,0:T(8,128)} %get-tuple-element.166), channel_id=1, source_target_pairs={{0,8},{8,0},{16,24},{24,16},{1,9},{9,1},{17,25},{25,17},{2,10},{10... | collective-permute-start | bytes 1572872 | tf_op jit(solution)/shard_map/ppermute | solution.py:242
  291.8 53.5 %copy-start.2 = (f32[128,16,256]{2,1,0:T(8,128)}, f32[128,16,256]{2,1,0:T(8,128)S(1)}, u32[]{:S(2)}) copy-start(f32[128,16,256]{2,1,0:T(8,128)S(1)} %pad_maximum_fusion.5.refs_2_.here) | copy-start | bytes 6291460
  301.2 44.1 %collective-permute-start.31 = (f32[128,16,256]{2,1,0:T(8,128)S(1)}, f32[128,16,256]{2,1,0:T(8,128)}, u32[]{:S(2)}, u32[]{:S(2)}) collective-permute-start(f32[128,16,256]{2,1,0:T(8,128)S(1)} %pad_maximum_fusion.1.refs_2_.here), channel_id=1, source_target_pairs={{2,0},{3,1},{4,2},{5,3},{6,4},{7,5},{10,8},{11,9},{12,10},{13,11},... | collective-permute-start | bytes 6291464 | tf_op jit(solution)/shard_map/ppermute | solution.py:245
  307.9 48.0 %collective-permute-start.25 = (f32[128,16,256]{2,1,0:T(8,128)S(1)}, f32[128,16,256]{2,1,0:T(8,128)}, u32[]{:S(2)}, u32[]{:S(2)}) collective-permute-start(f32[128,16,256]{2,1,0:T(8,128)S(1)} %pad_maximum_fusion.5.refs_2_.here), channel_id=1, source_target_pairs={{0,16},{8,24},{16,0},{24,8},{1,17},{9,25},{17,1},{25,9},{2,18},{10... | collective-permute-start | bytes 6291464 | tf_op jit(solution)/shard_map/ppermute | solution.py:239
  319.3 44.2 %collective-permute-start.30 = (f32[128,16,256]{2,1,0:T(8,128)}, f32[128,16,256]{2,1,0:T(8,128)}, u32[]{:S(2)}, u32[]{:S(2)}) collective-permute-start(f32[128,16,256]{2,1,0:T(8,128)} %get-tuple-element.186.rise), channel_id=1, source_target_pairs={{1,3},{3,5},{5,7},{9,11},{11,13},{13,15},{17,19},{19,21},{21,23},{... | collective-permute-start | bytes 6291464 | tf_op jit(solution)/shard_map/ppermute | solution.py:248
  328.4 43.0 %collective-permute-start.32 = (f32[128,16,256]{2,1,0:T(8,128)}, f32[128,16,256]{2,1,0:T(8,128)}, u32[]{:S(2)}, u32[]{:S(2)}) collective-permute-start(f32[128,16,256]{2,1,0:T(8,128)} %turn.14), channel_id=1, source_target_pairs={{0,1},{1,0},{2,3},{3,2},{4,5},{5,4},{6,7},{7,6},{8,9},{9,8},{10,11... | collective-permute-start | bytes 6291464 | tf_op jit(solution)/shard_map/ppermute | solution.py:251
  328.4 23.5 %collective-permute-start.29 = (f32[64,16,256]{2,1,0:T(8,128)}, f32[64,16,256]{2,1,0:T(8,128)}, u32[]{:S(2)}, u32[]{:S(2)}) collective-permute-start(f32[64,16,256]{2,1,0:T(8,128)} %get-tuple-element.180), channel_id=1, source_target_pairs={{0,8},{8,0},{16,24},{24,16},{1,9},{9,1},{17,25},{25,17},{2,10},{10... | collective-permute-start | bytes 3145736 | tf_op jit(solution)/shard_map/ppermute | solution.py:242
  338.4 50.9 %copy-start.3 = (f32[128,16,256]{2,1,0:T(8,128)}, f32[128,16,256]{2,1,0:T(8,128)S(1)}, u32[]{:S(2)}) copy-start(f32[128,16,256]{2,1,0:T(8,128)S(1)} %pad_maximum_fusion.refs_2_.here) | copy-start | bytes 6291460
  345.2 44.1 %collective-permute-start.37 = (f32[128,16,256]{2,1,0:T(8,128)S(1)}, f32[128,16,256]{2,1,0:T(8,128)S(1)}, u32[]{:S(2)}, u32[]{:S(2)}) collective-permute-start(f32[128,16,256]{2,1,0:T(8,128)S(1)} %pad_maximum_fusion.5.refs_2_.here), channel_id=1, source_target_pairs={{2,0},{3,1},{4,2},{5,3},{6,4},{7,5},{10,8},{11,9},{12,10},{13,11},... | collective-permute-start | bytes 6291464 | tf_op jit(solution)/shard_map/ppermute | solution.py:245
  352.0 47.8 %collective-permute-start.24 = (f32[128,16,256]{2,1,0:T(8,128)S(1)}, f32[128,16,256]{2,1,0:T(8,128)}, u32[]{:S(2)}, u32[]{:S(2)}) collective-permute-start(f32[128,16,256]{2,1,0:T(8,128)S(1)} %pad_maximum_fusion.refs_2_.here), channel_id=1, source_target_pairs={{0,16},{8,24},{16,0},{24,8},{1,17},{9,25},{17,1},{25,9},{2,18},{10... | collective-permute-start | bytes 6291464 | tf_op jit(solution)/shard_map/ppermute | solution.py:239
  363.5 43.9 %collective-permute-start.36 = (f32[128,16,256]{2,1,0:T(8,128)}, f32[128,16,256]{2,1,0:T(8,128)}, u32[]{:S(2)}, u32[]{:S(2)}) collective-permute-start(f32[128,16,256]{2,1,0:T(8,128)} %get-tuple-element.200.rise), channel_id=1, source_target_pairs={{1,3},{3,5},{5,7},{9,11},{11,13},{13,15},{17,19},{19,21},{21,23},{... | collective-permute-start | bytes 6291464 | tf_op jit(solution)/shard_map/ppermute | solution.py:248
  371.5 43.8 %collective-permute-start.38 = (f32[128,16,256]{2,1,0:T(8,128)}, f32[128,16,256]{2,1,0:T(8,128)}, u32[]{:S(2)}, u32[]{:S(2)}) collective-permute-start(f32[128,16,256]{2,1,0:T(8,128)} %turn.15), channel_id=1, source_target_pairs={{0,1},{1,0},{2,3},{3,2},{4,5},{5,4},{6,7},{7,6},{8,9},{9,8},{10,11... | collective-permute-start | bytes 6291464 | tf_op jit(solution)/shard_map/ppermute | solution.py:251
  371.5 24.6 %collective-permute-start.33 = (f32[64,16,256]{2,1,0:T(8,128)}, f32[64,16,256]{2,1,0:T(8,128)S(1)}, u32[]{:S(2)}, u32[]{:S(2)}) collective-permute-start(f32[64,16,256]{2,1,0:T(8,128)} %get-tuple-element.192), channel_id=1, source_target_pairs={{0,8},{8,0},{16,24},{24,16},{1,9},{9,1},{17,25},{25,17},{2,10},{10... | collective-permute-start | bytes 3145736 | tf_op jit(solution)/shard_map/ppermute | solution.py:242
  389.3 69.7 %collective-permute-start.41 = (f32[128,16,256]{2,1,0:T(8,128)S(1)}, f32[128,16,256]{2,1,0:T(8,128)S(1)}, u32[]{:S(2)}, u32[]{:S(2)}) collective-permute-start(f32[128,16,256]{2,1,0:T(8,128)S(1)} %pad_maximum_fusion.refs_2_.here), channel_id=1, source_target_pairs={{2,0},{3,1},{4,2},{5,3},{6,4},{7,5},{10,8},{11,9},{12,10},{13,11},... | collective-permute-start | bytes 6291464 | tf_op jit(solution)/shard_map/ppermute | solution.py:245
  407.3 51.7 %collective-permute-start.40 = (f32[128,16,256]{2,1,0:T(8,128)}, f32[128,16,256]{2,1,0:T(8,128)}, u32[]{:S(2)}, u32[]{:S(2)}) collective-permute-start(f32[128,16,256]{2,1,0:T(8,128)} %get-tuple-element.212.rise), channel_id=1, source_target_pairs={{1,3},{3,5},{5,7},{9,11},{11,13},{13,15},{17,19},{19,21},{21,23},{... | collective-permute-start | bytes 6291464 | tf_op jit(solution)/shard_map/ppermute | solution.py:248
  415.3 49.7 %collective-permute-start.42 = (f32[128,16,256]{2,1,0:T(8,128)}, f32[128,16,256]{2,1,0:T(8,128)}, u32[]{:S(2)}, u32[]{:S(2)}) collective-permute-start(f32[128,16,256]{2,1,0:T(8,128)} %turn.16), channel_id=1, source_target_pairs={{0,1},{1,0},{2,3},{3,2},{4,5},{5,4},{6,7},{7,6},{8,9},{9,8},{10,11... | collective-permute-start | bytes 6291464 | tf_op jit(solution)/shard_map/ppermute | solution.py:251
  416.8 17.7 %collective-permute-start.39 = (f32[64,16,256]{2,1,0:T(8,128)}, f32[64,16,256]{2,1,0:T(8,128)}, u32[]{:S(2)}, u32[]{:S(2)}) collective-permute-start(f32[64,16,256]{2,1,0:T(8,128)} %get-tuple-element.206), channel_id=1, source_target_pairs={{0,8},{8,0},{16,24},{24,16},{1,9},{9,1},{17,25},{25,17},{2,10},{10... | collective-permute-start | bytes 3145736 | tf_op jit(solution)/shard_map/ppermute | solution.py:242
  428.6 24.8 %collective-permute-start.35 = (f32[128,8,256]{2,1,0:T(8,128)S(1)}, f32[128,8,256]{2,1,0:T(8,128)S(1)}, u32[]{:S(2)}, u32[]{:S(2)}) collective-permute-start(f32[128,8,256]{2,1,0:T(8,128)S(1)} %pad_maximum_fusion.9.refs_2_.here), channel_id=1, source_target_pairs={{0,16},{8,24},{16,0},{24,8},{1,17},{9,25},{17,1},{25,9},{2,18},{10... | collective-permute-start | bytes 3145736 | tf_op jit(solution)/shard_map/ppermute | solution.py:239
  465.0 49.8 %collective-permute-start.48 = (f32[128,16,256]{2,1,0:T(8,128)}, f32[128,16,256]{2,1,0:T(8,128)S(1)}, u32[]{:S(2)}, u32[]{:S(2)}) collective-permute-start(f32[128,16,256]{2,1,0:T(8,128)} %turn.17), channel_id=1, source_target_pairs={{0,1},{1,0},{2,3},{3,2},{4,5},{5,4},{6,7},{7,6},{8,9},{9,8},{10,11... | collective-permute-start | bytes 6291464 | tf_op jit(solution)/shard_map/ppermute | solution.py:251
  466.6 25.6 %collective-permute-start.46 = (f32[128,8,256]{2,1,0:T(8,128)S(1)}, f32[128,8,256]{2,1,0:T(8,128)S(1)}, u32[]{:S(2)}, u32[]{:S(2)}) collective-permute-start(f32[128,8,256]{2,1,0:T(8,128)S(1)} %copy-done.9), channel_id=1, source_target_pairs={{2,0},{3,1},{4,2},{5,3},{6,4},{7,5},{10,8},{11,9},{12,10},{13,11},... | collective-permute-start | bytes 3145736 | tf_op jit(solution)/shard_map/ppermute | solution.py:245
  468.6 30.7 %copy-start.10 = (f32[128,8,256]{2,1,0:T(8,128)}, f32[128,8,256]{2,1,0:T(8,128)S(1)}, u32[]{:S(2)}) copy-start(f32[128,8,256]{2,1,0:T(8,128)S(1)} %pad_maximum_fusion.6.refs_2_.here) | copy-start | bytes 3145732
  468.6 30.7 %collective-permute-start.43 = (f32[64,16,256]{2,1,0:T(8,128)}, f32[64,16,256]{2,1,0:T(8,128)S(1)}, u32[]{:S(2)}, u32[]{:S(2)}) collective-permute-start(f32[64,16,256]{2,1,0:T(8,128)} %get-tuple-element.218), channel_id=1, source_target_pairs={{0,8},{8,0},{16,24},{24,16},{1,9},{9,1},{17,25},{25,17},{2,10},{10... | collective-permute-start | bytes 3145736 | tf_op jit(solution)/shard_map/ppermute | solution.py:242
  469.8 33.2 %collective-permute-start.34 = (f32[128,8,256]{2,1,0:T(8,128)S(1)}, f32[128,8,256]{2,1,0:T(8,128)S(1)}, u32[]{:S(2)}, u32[]{:S(2)}) collective-permute-start(f32[128,8,256]{2,1,0:T(8,128)S(1)} %pad_maximum_fusion.6.refs_2_.here), channel_id=1, source_target_pairs={{0,16},{8,24},{16,0},{24,8},{1,17},{9,25},{17,1},{25,9},{2,18},{10... | collective-permute-start | bytes 3145736 | tf_op jit(solution)/shard_map/ppermute | solution.py:239
  471.0 37.4 %collective-permute-start.44 = (f32[128,8,256]{2,1,0:T(8,128)}, f32[128,8,256]{2,1,0:T(8,128)}, u32[]{:S(2)}, u32[]{:S(2)}) collective-permute-start(f32[128,8,256]{2,1,0:T(8,128)} %get-tuple-element.225.rise), channel_id=1, source_target_pairs={{1,3},{3,5},{5,7},{9,11},{11,13},{13,15},{17,19},{19,21},{21,23},{... | collective-permute-start | bytes 3145736 | tf_op jit(solution)/shard_map/ppermute | solution.py:248
  492.2 31.0 %collective-permute-start.47 = (f32[128,8,256]{2,1,0:T(8,128)S(1)}, f32[128,8,256]{2,1,0:T(8,128)S(1)}, u32[]{:S(2)}, u32[]{:S(2)}) collective-permute-start(f32[128,8,256]{2,1,0:T(8,128)S(1)} %pad_maximum_fusion.6.refs_2_.here), channel_id=1, source_target_pairs={{2,0},{3,1},{4,2},{5,3},{6,4},{7,5},{10,8},{11,9},{12,10},{13,11},... | collective-permute-start | bytes 3145736 | tf_op jit(solution)/shard_map/ppermute | solution.py:245
  508.4 25.5 %collective-permute-start.45 = (f32[128,8,256]{2,1,0:T(8,128)}, f32[128,8,256]{2,1,0:T(8,128)S(1)}, u32[]{:S(2)}, u32[]{:S(2)}) collective-permute-start(f32[128,8,256]{2,1,0:T(8,128)} %get-tuple-element.226.rise), channel_id=1, source_target_pairs={{1,3},{3,5},{5,7},{9,11},{11,13},{13,15},{17,19},{19,21},{21,23},{... | collective-permute-start | bytes 3145736 | tf_op jit(solution)/shard_map/ppermute | solution.py:248
  514.8 23.4 %collective-permute-start.49 = (f32[128,8,256]{2,1,0:T(8,128)}, f32[128,8,256]{2,1,0:T(8,128)S(1)}, u32[]{:S(2)}, u32[]{:S(2)}) collective-permute-start(f32[128,8,256]{2,1,0:T(8,128)} %turn.19), channel_id=1, source_target_pairs={{0,1},{1,0},{2,3},{3,2},{4,5},{5,4},{6,7},{7,6},{8,9},{9,8},{10,11... | collective-permute-start | bytes 3145736 | tf_op jit(solution)/shard_map/ppermute | solution.py:251
  514.8 23.5 %collective-permute-start.52 = (f32[64,16,256]{2,1,0:T(8,128)}, f32[64,16,256]{2,1,0:T(8,128)S(1)}, u32[]{:S(2)}, u32[]{:S(2)}) collective-permute-start(f32[64,16,256]{2,1,0:T(8,128)} %get-tuple-element.239), channel_id=1, source_target_pairs={{0,8},{8,0},{16,24},{24,16},{1,9},{9,1},{17,25},{25,17},{2,10},{10... | collective-permute-start | bytes 3145736 | tf_op jit(solution)/shard_map/ppermute | solution.py:242
  521.9 26.5 %collective-permute-start.51 = (f32[64,16,256]{2,1,0:T(8,128)}, f32[64,16,256]{2,1,0:T(8,128)S(1)}, u32[]{:S(2)}, u32[]{:S(2)}) collective-permute-start(f32[64,16,256]{2,1,0:T(8,128)} %get-tuple-element.236), channel_id=1, source_target_pairs={{0,8},{8,0},{16,24},{24,16},{1,9},{9,1},{17,25},{25,17},{2,10},{10... | collective-permute-start | bytes 3145736 | tf_op jit(solution)/shard_map/ppermute | solution.py:242
  538.3 22.0 %collective-permute-start.50 = (f32[128,8,256]{2,1,0:T(8,128)}, f32[128,8,256]{2,1,0:T(8,128)S(1)}, u32[]{:S(2)}, u32[]{:S(2)}) collective-permute-start(f32[128,8,256]{2,1,0:T(8,128)} %turn.18), channel_id=1, source_target_pairs={{0,1},{1,0},{2,3},{3,2},{4,5},{5,4},{6,7},{7,6},{8,9},{9,8},{10,11... | collective-permute-start | bytes 3145736 | tf_op jit(solution)/shard_map/ppermute | solution.py:251
  545.6 23.0 %collective-permute-start.54 = (f32[64,8,256]{2,1,0:T(8,128)}, f32[64,8,256]{2,1,0:T(8,128)S(1)}, u32[]{:S(2)}, u32[]{:S(2)}) collective-permute-start(f32[64,8,256]{2,1,0:T(8,128)} %get-tuple-element.243), channel_id=1, source_target_pairs={{0,8},{8,0},{16,24},{24,16},{1,9},{9,1},{17,25},{25,17},{2,10},{10... | collective-permute-start | bytes 1572872 | tf_op jit(solution)/shard_map/ppermute | solution.py:242
  564.8 7.1 %collective-permute-start.53 = (f32[64,8,256]{2,1,0:T(8,128)}, f32[64,8,256]{2,1,0:T(8,128)S(1)}, u32[]{:S(2)}, u32[]{:S(2)}) collective-permute-start(f32[64,8,256]{2,1,0:T(8,128)} %get-tuple-element.242), channel_id=1, source_target_pairs={{0,8},{8,0},{16,24},{24,16},{1,9},{9,1},{17,25},{25,17},{2,10},{10... | collective-permute-start | bytes 1572872 | tf_op jit(solution)/shard_map/ppermute | solution.py:242
  (43 other events, 204.8 us)

commit v3 on v2

v3 whole, which is shorter than its diff:
```python
import functools

import jax
import jax.numpy as jnp
from jax import lax
from jax.experimental import pallas as pl
from jax.experimental.pallas import tpu as pltpu
from jax.sharding import PartitionSpec as P

F32 = jnp.float32
BF16 = jnp.bfloat16
VMEM_LIMIT = 56 * 2**20
SPAN, LANES = 8, 128
LIGHT = pl.CostEstimate(flops=1000, transcendentals=0, bytes_accessed=1000)
PARAMS = pltpu.CompilerParams(vmem_limit_bytes=VMEM_LIMIT)
WHOLE = pl.BlockSpec(memory_space=pltpu.VMEM)


def gate(*values):
    return lax.optimization_barrier(values)


def flag(cond):
    return jnp.where(cond, 1.0, 0.0).astype(F32)


def halves(x):
    high = x.astype(BF16)
    low = (x - high.astype(F32)).astype(BF16)
    return high, low


def halves_outside(x):
    high = lax.reduce_precision(x, 8, 7)
    return high.astype(BF16), (x - high).astype(BF16)


def dot(a, b):
    return jnp.dot(a, b, preferred_element_type=F32)


def plan(rows, length):
    n = max(4, min(length // SPAN, rows // 4))
    size = length // n
    chunks = [(s * size, size) for s in range(n)]
    groups, at = [], 0
    while at < n:
        step = 4 if n - at > 4 else max(1, (n - at) // 2)
        groups.append((at, at + step))
        at += step
    return chunks, groups


def spans(*bounds):
    return list(zip(bounds[:-1], bounds[1:]))


def local_kernel(at, half, core, own_rows, occ, c_hi, c_lo, b_hi, b_lo, row_b, row_c, *outs):
    block, phases = occ.shape[0], occ.shape[2]
    size = outs[0].shape[1]
    first = pl.program_id(0) * block
    rows = [pl.ds(pl.multiple_of(core[n] * half + at, SPAN), size) for n in range(2)]
    y = jnp.concatenate([occ[i, r] for i in range(block) for r in rows], axis=0)
    y_hi, y_lo = halves(y)
    by_c = dot(y_hi, c_hi[...]) + dot(y_lo, c_hi[...]) + dot(y_hi, c_lo[...])
    for i in range(block):
        x_hi, x_lo = halves(occ[i])
        by_b = dot(b_hi[...], x_hi) + dot(b_hi[...], x_lo) + dot(b_lo[...], x_hi)
        here = slice(2 * size * i, 2 * size * (i + 1))
        left = row_c[...] - own_rows[first + i] - row_b[...]
        base = by_c[here, :phases] + by_b[: 2 * size] + y[here] * left
        rise = by_c[here, phases:] + by_b[2 * size :]
        for n, value in enumerate((base, rise)):
            outs[n][i] = value[:size]
            outs[n + 2][i] = value[size:]


def local_terms(core, occ, own_rows, c_split, b_split, row_b, row_c, at, size):
    rows, mid, phases = occ.shape
    block = 4
    out = pl.BlockSpec((block, size, phases), lambda i, c: (i, 0, 0))
    return pl.pallas_call(
        functools.partial(local_kernel, at, mid // 2),
        grid_spec=pltpu.PrefetchScalarGridSpec(
            num_scalar_prefetch=1,
            grid=(rows // block,),
            in_specs=[
                pl.BlockSpec(memory_space=pltpu.SMEM),
                pl.BlockSpec((block, mid, phases), lambda i, c: (i, 0, 0)),
            ]
            + [WHOLE] * 6,
            out_specs=[out] * 4,
        ),
        out_shape=[jax.ShapeDtypeStruct((rows, size, phases), F32)] * 4,
        compiler_params=PARAMS,
        cost_estimate=LIGHT,
        name="local_terms",
    )(core, own_rows, occ, *c_split, *b_split, row_b, row_c)


def first_kernel(n_slabs, *refs):
    w_both, w_hi = refs[0], refs[1]
    slabs = refs[2 : 2 + n_slabs]
    mine_base, mine_rise, peer_base, peer_rise, stay_out, rise_out = refs[2 + n_slabs :]
    rows, span, lanes = stay_out.shape
    flat = [ref.reshape(ref.shape[0] * span, lanes) for ref in slabs]
    stay_flat = stay_out.reshape(rows * span, lanes)
    rise_flat = rise_out.reshape(rows * span, lanes)
    for b in range(0, span, 2):
        ats = [pl.ds(b, rows, stride=span), pl.ds(b + 1, rows, stride=span)]
        parts = []
        for ref in flat:
            picks = [pl.ds(b + n, ref.shape[0] // span, stride=span) for n in range(2)]
            parts.append(halves(jnp.concatenate([ref[pick, :] for pick in picks], axis=1)))
        g_hi = jnp.concatenate([p[0] for p in parts], axis=0)
        g_lo = jnp.concatenate([p[1] for p in parts], axis=0)
        both = dot(w_both[...], g_hi)
        out = both[: 2 * rows] + both[2 * rows :] + dot(w_hi[...], g_lo)
        for n, at in enumerate(ats):
            stay_flat[at, :] = out[:rows, n * lanes : (n + 1) * lanes]
            rise_flat[at, :] = out[rows:, n * lanes : (n + 1) * lanes]
    half = rows // 2
    stay_out[:half] += mine_base[...]
    stay_out[half:] += peer_base[...]
    rise_out[:half] += mine_rise[...]
    rise_out[half:] += peer_rise[...]


def first_terms(w_both, w_hi, slabs, near, start):
    rows, size, phases = slabs[0].shape
    slab_specs = [pl.BlockSpec((v.shape[0], SPAN, LANES), lambda j, h: (0, j, h)) for v in slabs]
    chunk = pl.BlockSpec((rows, SPAN, LANES), lambda j, h: (0, j, h))
    local_part = pl.BlockSpec((rows // 2, SPAN, LANES), lambda j, h: (0, start // SPAN + j, h))
    return pl.pallas_call(
        functools.partial(first_kernel, len(slabs)),
        grid=(size // SPAN, phases // LANES),
        in_specs=[WHOLE, WHOLE] + slab_specs + [local_part] * 4,
        out_specs=[chunk, chunk],
        out_shape=[jax.ShapeDtypeStruct((rows, size, phases), F32)] * 2,
        compiler_params=PARAMS,
        cost_estimate=LIGHT,
        name="first_terms",
    )(w_both, w_hi, *slabs, *near)


def turn_kernel(parity, rise, lifted, deep, here, fall, out):
    @pl.when(parity[0] == 0)
    def _():
        out[...] = rise[...] + fall[1:2] * deep[...]

    @pl.when(parity[0] != 0)
    def _():
        out[...] = lifted[...] + fall[0:1] * here[...]


def turn(parity, rise, lifted, deep, deep_at, here, fall):
    rows, size, phases = rise.shape
    block = min(32, rows)
    chunk = pl.BlockSpec((block, SPAN, phases), lambda i, j: (i, j, 0))
    deep_chunk = pl.BlockSpec((block, SPAN, phases), lambda i, j: (i, deep_at // SPAN + j, 0))
    return pl.pallas_call(
        turn_kernel,
        grid=(rows // block, size // SPAN),
        in_specs=[pl.BlockSpec(memory_space=pltpu.SMEM), chunk, chunk, deep_chunk, chunk, WHOLE],
        out_specs=chunk,
        out_shape=jax.ShapeDtypeStruct(rise.shape, F32),
        compiler_params=PARAMS,
        cost_estimate=LIGHT,
        name="turn",
    )(parity, rise, lifted, deep, here, fall)


def finish_kernel(n_alias, core, scale, fall, *refs):
    out, back = refs[6 + n_alias :]
    for n, target in enumerate((out, back)):
        stay, risen, deep = refs[n], refs[2 + n], refs[4 + n]
        target[...] = (stay[...] + risen[...] + fall[2:3] * deep[...]) * scale[0]


def finish(core, out, back, shape, back_size, scale, stay, fall, risen, deep, deep_at, start, back_at):
    rows, size, phases = stay.shape
    block = min(32, rows // 2)
    blocks = rows // 2 // block
    steps = shape[1] // 2 // SPAN

    def part(offset, which):
        return pl.BlockSpec((block, SPAN, phases), lambda i, j, c: (which * blocks + i, offset // SPAN + j, 0))

    args = [core, scale, fall]
    specs = [pl.BlockSpec(memory_space=pltpu.SMEM), WHOLE]
    for array, offset in ((stay, 0), (risen, 0), (deep, deep_at)):
        args += [array, array]
        specs += [part(offset, 0), part(offset, 1)]
    alias = {}
    for n, old in enumerate((out, back)):
        if old is not None:
            alias[len(args)] = n
            args.append(old)
            specs.append(pl.BlockSpec(memory_space=pl.ANY))
    return pl.pallas_call(
        functools.partial(finish_kernel, len(alias)),
        grid_spec=pltpu.PrefetchScalarGridSpec(
            num_scalar_prefetch=1,
            grid=(blocks, size // SPAN),
            in_specs=specs,
            out_specs=[
                pl.BlockSpec((block, SPAN, phases), lambda i, j, c: (i, c[0] * steps + start // SPAN + j, 0)),
                pl.BlockSpec((block, SPAN, phases), lambda i, j, c: (i, back_at // SPAN + j, 0)),
            ],
        ),
        out_shape=[jax.ShapeDtypeStruct(shape, F32), jax.ShapeDtypeStruct((rows // 2, back_size, phases), F32)],
        input_output_aliases=alias,
        compiler_params=PARAMS,
        cost_estimate=LIGHT,
        name="finish",
    )(*args)


def put_kernel(core, piece, _, out):
    out[...] = piece[...]


def put(core, out, piece, start):
    rows, size, phases = piece.shape
    block = min(16, rows)
    steps = out.shape[1] // 2 // SPAN
    return pl.pallas_call(
        put_kernel,
        grid_spec=pltpu.PrefetchScalarGridSpec(
            num_scalar_prefetch=1,
            grid=(rows // block, size // SPAN),
            in_specs=[
                pl.BlockSpec((block, SPAN, phases), lambda i, j, c: (i, j, 0)),
                pl.BlockSpec(memory_space=pl.ANY),
            ],
            out_specs=pl.BlockSpec((block, SPAN, phases), lambda i, j, c: (i, c[1] * steps + start // SPAN + j, 0)),
        ),
        out_shape=jax.ShapeDtypeStruct(out.shape, F32),
        input_output_aliases={2: 0},
        compiler_params=PARAMS,
        cost_estimate=LIGHT,
        name="put",
    )(core, piece, out)


def local(occupancy, rates, increments, draw, crusher_rate, bounds):
    n_cls, n_lvl = lax.axis_size("cls"), lax.axis_size("lvl")
    occ = occupancy[0]
    rows, mid, phases = occ.shape
    half = mid // 2
    level = lax.axis_index("lvl")
    place = lax.axis_index("cls")
    k = place % 2
    core = jnp.stack([k, 1 - k])
    even = level % 2 == 0
    bottom, top = bounds[0], bounds[1]

    def along_cls(v, by):
        return lax.ppermute(v, "cls", [(i, (i + by) % n_cls) for i in range(n_cls)])

    def other_core(v):
        return lax.ppermute(v, "cls", [(i, i ^ 1) for i in range(n_cls)])

    def two_down(v):
        return lax.ppermute(v, "lvl", [(i, i - 2) for i in range(2, n_lvl)])

    def two_up(v):
        return lax.ppermute(v, "lvl", [(i, i + 2) for i in range(1, n_lvl - 2, 2)])

    def pair_swap(v):
        return lax.ppermute(v, "lvl", [(i, i ^ 1) for i in range(n_lvl)])

    def cut(array, which, at, size):
        return lax.dynamic_slice_in_dim(array, core[which] * half + at, size, axis=1)

    chunks, groups = plan(rows, half)
    n = len(chunks)
    size = chunks[0][1]
    shifts = [2 * s for s in range(1, n_cls // 2)]
    sent = [None] * n
    tokens = []
    for lo, hi in spans(*sorted({0, 1, 4, n})):
        at = chunks[lo][0]
        give = cut(occ, 1, at, (hi - lo) * size)
        if tokens:
            give, _ = gate(give, tokens[-1])
        got = other_core(give)
        tokens.append(got)
        for s in range(lo, hi):
            start = chunks[s][0]
            part = lax.slice_in_dim(got, start - at, start - at + size, axis=1)
            sent[s] = jnp.concatenate([cut(occ, 0, start, size), part], axis=0)

    far, deep = [None] * n, [None] * n

    def start_early(s):
        for by in shifts:
            straight = along_cls(cut(occ, 0, s * size, size), by)
            crossed = [(i, ((i + by) % n_cls) ^ 1) for i in range(n_cls)]
            cross = lax.ppermute(cut(occ, 1, s * size, size), "cls", crossed)
            far[s] = (far[s] or []) + [straight, cross]

    def start_far(s, *after):
        operand = gate(sent[s], *after)[0] if after else sent[s]
        far[s] = [along_cls(operand, by) for by in shifts]

    def start_deep(s, *after):
        operand = jnp.concatenate([sent[s], sent[s + 1]], axis=1)
        if after:
            operand = gate(operand, *after)[0]
        got = two_down(operand)
        deep[s], deep[s + 1] = (got, 0), (got, size)

    start_early(0)
    start_early(1)
    start_deep(0)

    row_total = jnp.sum(rates, axis=2)
    uniform_rate = jnp.sum(jnp.max(row_total, axis=1)) + jnp.max(crusher_rate)
    out_rows = row_total * flag((increments == 0) | (level + increments <= top))
    rise_ok = flag(level + 1 <= top)
    drop_here = crusher_rate * flag(level - draw >= bottom)
    drop_deep = crusher_rate * flag(level + 2 - draw >= bottom)
    once_here = (drop_here * flag(draw == 1) * flag(~even))[None, :]
    once_deep = (drop_deep * flag(draw == 1) * flag(even))[None, :]
    twice_deep = (drop_deep * flag(draw == 2))[None, :]
    fall_vec = jnp.concatenate([once_here, once_deep, twice_deep], axis=0)
    parity = (level % 2)[None]
    scale = (1.0 / uniform_rate)[None]

    stay_rows = rates * flag(increments == 0)[:, :, None]
    rise_rows = rates * (flag(increments == 1) * rise_ok)[:, :, None]

    c_split = halves_outside(jnp.concatenate([stay_rows[2], rise_rows[2]], axis=1))
    own_rows = lax.dynamic_slice_in_dim(out_rows[0], place * rows, rows)
    row_c = (uniform_rate - out_rows[2] - drop_here)[None, :]
    parts = []

    def start_part(lo, hi, *after):
        at, span = chunks[lo][0], (hi - lo) * size
        cat_b = jnp.concatenate([cut(r, w, at, span) for r in (stay_rows[1], rise_rows[1]) for w in range(2)], axis=1)
        row_b = jnp.concatenate([lax.dynamic_slice_in_dim(out_rows[1], core[w] * half + at, span) for w in range(2)])
        base, rise, give_base, give_rise = local_terms(
            core, gate(occ, *after)[0], own_rows, c_split, halves_outside(cat_b.T), row_b[:, None], row_c, at, span
        )
        parts.append((lo, hi, at, (base, rise, other_core(give_base), other_core(give_rise))))
        return base

    local_spans = spans(*sorted({0, 1, n // 4, n // 2, n}))
    token = start_part(*local_spans[0], tokens[0])
    token = start_part(*local_spans[1], token)
    far[0][0], _ = gate(far[0][0], token)

    origin = [place, place ^ 1]
    for by in shifts:
        origin += [(place - by) % n_cls, ((place - by) % n_cls) ^ 1]
    mine = jnp.concatenate(
        [
            lax.dynamic_slice_in_dim(r, p * rows, rows, axis=1)
            for r in (stay_rows[0], rise_rows[0])
            for p in (place, place ^ 1)
        ],
        axis=1,
    ).T
    mine = jnp.concatenate([lax.dynamic_slice_in_dim(mine, o * rows, rows, axis=1) for o in origin], axis=1)
    a_hi, a_lo = halves_outside(mine)
    a_both = jnp.concatenate([a_hi, a_lo], axis=0)

    out = None
    stay, rise, lifted, risen = ([None] * n for _ in range(4))
    back = [None] * len(groups)
    group_of = {s: g for g, (lo, hi) in enumerate(groups) for s in range(lo, hi)}

    for s in range(n + 4):
        if s < n:
            if s >= 3:
                far[s][0], risen[s - 3] = gate(far[s][0], risen[s - 3])
            if s >= 4:
                far[s][0], out = gate(far[s][0], out)
            if s + 2 < n:
                start_far(s + 2, far[s][0])
            if s % 2 and s + 1 < n:
                start_deep(s + 1, far[s][0], deep[s][0])
            lo, hi, at, near = next(p for p in parts if p[0] <= s < p[1])
            stay[s], rise[s] = first_terms(a_both, a_hi, [sent[s]] + far[s], near, chunks[s][0] - at)
            if s + 1 in (lo for lo, _ in local_spans[2:]):
                start_part(*next(v for v in local_spans if v[0] == s + 1), rise[max(0, s - 2)])
            lift_me = rise[s]
            if s >= 1:
                lift_me, lifted[s - 1] = gate(lift_me, lifted[s - 1])
            lifted[s] = two_up(lift_me)
        if 1 <= s <= n:
            p = s - 1
            swap_me = turn(parity, rise[p], lifted[p], *deep[p], sent[p], fall_vec)
            if p >= 1:
                swap_me, risen[p - 1] = gate(swap_me, risen[p - 1])
            risen[p] = pair_swap(swap_me)
        if 0 <= s - 2 < n:
            p = s - 2
            g = group_of[p]
            lo, hi = groups[g]
            out, back[g] = finish(
                core, out, back[g], occ.shape, (hi - lo) * size, scale, stay[p], fall_vec, risen[p], *deep[p],
                chunks[p][0], (p - lo) * size,
            )
            if p == hi - 1:
                back[g] = other_core(back[g])
        if 0 <= s - 3 < n:
            p = s - 3
            lo, hi = groups[group_of[p]]
            if p == hi - 1:
                out = put(core, out, back[group_of[p]], chunks[lo][0])
    return out[None]


def solution(mesh):
    in_specs = (P("lvl", "cls", None, None), P(), P(), P(), P(), P())
    out_specs = P("lvl", "cls", None, None)
    return jax.shard_map(local, mesh=mesh, in_specs=in_specs, out_specs=out_specs, check_vma=False)
```

time: 580 us -> 681 us (1.17)
  Pallas kernels: 225 us -> 313 us
  starting transfers between devices: 124 us -> 102 us
  local copies, waits for them, and re-layouts: 48.3 us -> 65.4 us
  other arithmetic: 17.2 us -> 33.1 us
    ppermute x10 -> x16, waiting for transfers between devices: 22.8 us -> 106 us  [two_up(): return lax.ppermute(v, 'lvl', [(i, i + 2) for i in range(1, n_lvl - 2, 2)])]
    ppermute x10 -> x16, waiting for transfers between devices: 51.5 us -> 1.98 us  [along_cls(): return lax.ppermute(v, 'cls', [(i, (i + by) % n_cls) for i in range(n_cls)])]
    ppermute x10 -> x8, waiting for transfers between devices: 56.7 us -> 12.8 us  [two_down(): return lax.ppermute(v, 'lvl', [(i, i - 2) for i in range(2, n_lvl)])]
    pallas_call x20 -> x22, Pallas kernels: 67.1 us -> 108 us  [the longest x16 63.9 us: turn(): pl.pallas_call(turn_kernel, grid=(rows // block, size // SPAN), in_specs=...]
    ppermute x15 -> x17, starting transfers between devices: 55.5 us -> 21.7 us  [other_core(): return lax.ppermute(v, 'cls', [(i, i ^ 1) for i in range(n_cls)])]
    pallas_call x2 -> x4, Pallas kernels: 52.6 us -> 77.2 us  [local_terms(): pl.pallas_call(functools.partial(local_kernel, at, mid // 2), grid_spec=p...]
    pallas_call x10 -> x16, Pallas kernels: 42.3 us -> 54.9 us  [finish(): pl.pallas_call(functools.partial(finish_kernel, len(alias)), grid_spec=pl...]
    concatenate x11 -> x18, other arithmetic: 8.11 us -> 19.9 us  [the longest x8 13.4 us: start_deep(): operand = jnp.concatenate([sent[s], sent[s + 1]], axis=1)]
  transfers between devices with their start and end apart: 55 -> 75, of which waited for: 17 -> 22; matrix products, arithmetic and copies ran while one was open for 8% -> 11% of each run, Pallas kernels for 33% -> 46%
where the time goes in v3:
time: 681 us; the launch traced here: 674 us
  Pallas kernels  313 us (46%)
  waiting for transfers between devices  156 us (23%)
  starting transfers between devices  102 us (15%)
  local copies, waits for them, and re-layouts  65.4 us (10%)
  other arithmetic  33.1 us (5%)
    ppermute x16, waiting for transfers between devices, two_up(): return lax.ppermute(v, 'lvl', [(i, i + 2) for i in range(1, n_lvl - 2, 2)])  106 us
    pallas_call x4, Pallas kernels, local_terms(): pl.pallas_call(functools.partial(local_kernel, at, mid // 2), grid_spec=p...  77.2 us
    pallas_call x16, Pallas kernels, first_terms(): pl.pallas_call(functools.partial(first_kernel, len(slabs)), grid=(size //...  73.4 us
    pallas_call x16, Pallas kernels, turn(): pl.pallas_call(turn_kernel, grid=(rows // block, size // SPAN), in_specs=...  63.9 us
    pallas_call x16, Pallas kernels, finish(): pl.pallas_call(functools.partial(finish_kernel, len(alias)), grid_spec=pl...  54.9 us
    pallas_call x6, Pallas kernels, put(): pl.pallas_call(put_kernel, grid_spec=pltpu.PrefetchScalarGridSpec(num_sca...  44 us
    ppermute x16, starting transfers between devices, two_up(): return lax.ppermute(v, 'lvl', [(i, i + 2) for i in range(1, n_lvl - 2, 2)])  40.8 us
    ppermute x16, waiting for transfers between devices, pair_swap(): return lax.ppermute(v, 'lvl', [(i, i ^ 1) for i in range(n_lvl)])  29.8 us
  transfers between devices with their start and end apart: 75, of which 22 were waited for; matrix products, arithmetic and copies ran while one was open for 11% of the time, Pallas kernels for 46%

profile of v3, /device:TPU:21, one launch (start us, length us, event | category | flops | bytes accessed | tf_op | source)
XLA Modules:
  0.0 673.5 jit_solution(7085057141153108508)
XLA Ops:
  0.0 7.1 %dynamic-slice_bitcast_fusion.2 = (f32[64,8,256]{2,1,0:T(8,128)}, f32[64,8,256]{2,1,0:T(8,128)}, f32[64,8,256]{2,1,0:T(8,128)}, f32[64,8,256]{2,1,0:T(8,128)}, f...) fusion(f32[1,64,256,256]{3,2,1,0:T(8,128)} %param.6, ...), kind=kLoop, calls=%fused_computation.30 | loop fusion | bytes 18874440 | tf_op jit(solution)/shard_map/dynamic_slice | solution.py:274
  17.4 6.3 dynamic-slice_bitcast_fusion
  35.1 17.0 %local_terms.4 = (f32[64,8,256]{2,1,0:T(8,128)}, f32[64,8,256]{2,1,0:T(8,128)}, f32[64,8,256]{2,1,0:T(8,128)}, f32[64,8,256]{2,1,0:T(8,128)}) custom-call(s32[2]{0:T(128)} %pad_add_fusion.core, f32[64]{0:T(128)} %fusion.10.own_rows, f32[64,256,256]{2,1,0:T(8,128)} %bitcast.135, bf16[256,512]{1,0:T(8,128)(2,1)} %get-tuple-element.458.c_hi, ...), custom_call_target="tpu_custom_call" | custom-call | flops 1000 | bytes 1000 | tf_op jit(solution)/shard_map/local_terms/pallas_call | solution.py:82
  52.2 18.0 %local_terms.5 = (f32[64,24,256]{2,1,0:T(8,128)}, f32[64,24,256]{2,1,0:T(8,128)}, f32[64,24,256]{2,1,0:T(8,128)}, f32[64,24,256]{2,1,0:T(8,128)}) custom-call(s32[2]{0:T(128)} %pad_add_fusion.core, f32[64]{0:T(128)} %fusion.10.own_rows, f32[64,256,256]{2,1,0:T(8,128)} %bitcast.136, bf16[256,512]{1,0:T(8,128)(2,1)} %get-tuple-element.458.c_hi, ...), custom_call_target="tpu_custom_call" | custom-call | flops 1000 | bytes 1000 | tf_op jit(solution)/shard_map/local_terms/pallas_call | solution.py:82
  84.4 4.7 first_terms.18
  89.1 6.0 collective-permute-done.5.refs_4_
  101.1 4.6 first_terms.16
  105.7 16.0 %collective-permute-done.13.lifted = f32[128,8,256]{2,1,0:T(8,128)} collective-permute-done((f32[128,8,256]{2,1,0:T(8,128)}, f32[128,8,256]{2,1,0:T(8,128)}, u32[]{:S(2)}, u32[]{:S(2)}) %collective-permute-start.13) | collective-permute-done | bytes 1048608 | tf_op jit(solution)/shard_map/ppermute | solution.py:268
  128.2 4.0 turn.17
  142.5 4.6 first_terms.17
  147.3 3.5 collective-permute-start.19
  150.8 18.6 %local_terms.6 = (f32[64,32,256]{2,1,0:T(8,128)}, f32[64,32,256]{2,1,0:T(8,128)}, f32[64,32,256]{2,1,0:T(8,128)}, f32[64,32,256]{2,1,0:T(8,128)}) custom-call(s32[2]{0:T(128)} %pad_add_fusion.core, f32[64]{0:T(128)} %fusion.10.own_rows, f32[64,256,256]{2,1,0:T(8,128)} %bitcast.137, bf16[256,512]{1,0:T(8,128)(2,1)} %get-tuple-element.458.c_hi, ...), custom_call_target="tpu_custom_call" | custom-call | flops 1000 | bytes 1000 | tf_op jit(solution)/shard_map/local_terms/pallas_call | solution.py:82
  172.1 3.9 turn.16
  176.1 5.4 fusion.20
  183.4 4.6 first_terms.19
  193.6 4.0 turn.18
  201.0 3.6 finish.17
  209.8 4.7 first_terms.20
  214.5 3.5 collective-permute-start.28
  219.2 4.3 turn.19
  232.1 4.6 first_terms.21
  251.8 23.6 %local_terms.7 = (f32[64,64,256]{2,1,0:T(8,128)}, f32[64,64,256]{2,1,0:T(8,128)}, f32[64,64,256]{2,1,0:T(8,128)}, f32[64,64,256]{2,1,0:T(8,128)}) custom-call(s32[2]{0:T(128)} %pad_add_fusion.core, f32[64]{0:T(128)} %fusion.10.own_rows, f32[64,256,256]{2,1,0:T(8,128)} %bitcast.138, bf16[256,512]{1,0:T(8,128)(2,1)} %get-tuple-element.458.c_hi, ...), custom_call_target="tpu_custom_call" | custom-call | flops 1000 | bytes 1000 | tf_op jit(solution)/shard_map/local_terms/pallas_call | solution.py:82
  278.8 3.9 turn.20
  284.0 3.6 finish.19
  289.3 4.6 first_terms.22
  296.1 12.9 %collective-permute-done.32.refs_2_.refs_3_ = f32[128,8,256]{2,1,0:T(8,128)} collective-permute-done((f32[128,8,256]{2,1,0:T(8,128)}, f32[128,8,256]{2,1,0:T(8,128)}, u32[]{:S(2)}, u32[]{:S(2)}) %collective-permute-start.32) | collective-permute-done | bytes 1048608 | tf_op jit(solution)/shard_map/ppermute | solution.py:271
  313.5 4.3 turn.21
  317.8 17.2 %collective-permute-done.36.lifted = f32[128,8,256]{2,1,0:T(8,128)} collective-permute-done((f32[128,8,256]{2,1,0:T(8,128)}, f32[128,8,256]{2,1,0:T(8,128)}, u32[]{:S(2)}, u32[]{:S(2)}) %collective-permute-start.36) | collective-permute-done | bytes 1048608 | tf_op jit(solution)/shard_map/ppermute | solution.py:268
  342.4 10.2 %put.6.refs_6_ = f32[64,256,256]{2,1,0:T(8,128)} custom-call(s32[2]{0:T(128)} %pad_add_fusion.core, f32[64,32,256]{2,1,0:T(8,128)} %collective-permute-done.33.piece, f32[64,256,256]{2,1,0:T(8,128)} %get-tuple-element.287._), custom_call_target="tpu_custom_call", output_to_operand_aliasing={{}: (2, {})} | custom-call | flops 1000 | bytes 1000 | tf_op jit(solution)/shard_map/put/pallas_call | solution.py:227
  352.6 4.6 first_terms.23
  359.4 4.0 turn.22
  372.1 4.6 first_terms.24
  376.6 5.3 collective-permute-done.41.lifted
  384.7 3.9 turn.23
  392.6 4.6 first_terms.25
  397.2 8.8 %collective-permute-done.45.lifted = f32[128,8,256]{2,1,0:T(8,128)} collective-permute-done((f32[128,8,256]{2,1,0:T(8,128)}, f32[128,8,256]{2,1,0:T(8,128)}, u32[]{:S(2)}, u32[]{:S(2)}) %collective-permute-start.45) | collective-permute-done | bytes 1048608 | tf_op jit(solution)/shard_map/ppermute | solution.py:268
  406.0 5.0 collective-permute-done.46.deep.refs_4_.refs_5_
  412.2 4.0 turn.24
  419.7 3.5 collective-permute-start.50
  430.5 4.5 first_terms.26
  435.1 16.4 %collective-permute-done.48.lifted = f32[128,8,256]{2,1,0:T(8,128)S(1)} collective-permute-done((f32[128,8,256]{2,1,0:T(8,128)S(1)}, f32[128,8,256]{2,1,0:T(8,128)S(1)}, u32[]{:S(2)}, u32[]{:S(2)}) %collective-permute-start.48) | collective-permute-done | bytes 1048608 | tf_op jit(solution)/shard_map/ppermute | solution.py:268
  454.7 3.9 turn.25
  465.2 10.2 %put.7.refs_6_ = f32[64,256,256]{2,1,0:T(8,128)} custom-call(s32[2]{0:T(128)} %pad_add_fusion.core, f32[64,32,256]{2,1,0:T(8,128)} %collective-permute-done.50.piece, f32[64,256,256]{2,1,0:T(8,128)} %get-tuple-element.342._), custom_call_target="tpu_custom_call", output_to_operand_aliasing={{}: (2, {})} | custom-call | flops 1000 | bytes 1000 | tf_op jit(solution)/shard_map/put/pallas_call | solution.py:227
  475.3 4.6 first_terms.27
  481.9 3.9 turn.26
  494.8 4.6 first_terms.28
  499.4 6.4 collective-permute-done.56.lifted
  509.1 4.0 turn.27
  518.9 4.6 first_terms.29
  523.4 8.4 %collective-permute-done.60.lifted = f32[128,8,256]{2,1,0:T(8,128)} collective-permute-done((f32[128,8,256]{2,1,0:T(8,128)}, f32[128,8,256]{2,1,0:T(8,128)}, u32[]{:S(2)}, u32[]{:S(2)}) %collective-permute-start.60) | collective-permute-done | bytes 1048608 | tf_op jit(solution)/shard_map/ppermute | solution.py:268
  534.9 3.9 turn.28
  553.9 4.6 first_terms.30
  558.4 4.9 collective-permute-done.63.lifted
  565.8 3.9 turn.29
  577.5 10.2 %put.8.refs_6_ = f32[64,256,256]{2,1,0:T(8,128)} custom-call(s32[2]{0:T(128)} %pad_add_fusion.core, f32[64,32,256]{2,1,0:T(8,128)} %collective-permute-done.65.piece, f32[64,256,256]{2,1,0:T(8,128)} %get-tuple-element.392._), custom_call_target="tpu_custom_call", output_to_operand_aliasing={{}: (2, {})} | custom-call | flops 1000 | bytes 1000 | tf_op jit(solution)/shard_map/put/pallas_call | solution.py:227
  587.7 4.6 first_terms.31
  592.3 6.1 collective-permute-done.68.deep.refs_4_.refs_5_
  599.7 3.9 turn.31
  610.2 18.9 %collective-permute-done.67.lifted = f32[128,8,256]{2,1,0:T(8,128)S(1)} collective-permute-done((f32[128,8,256]{2,1,0:T(8,128)S(1)}, f32[128,8,256]{2,1,0:T(8,128)S(1)}, u32[]{:S(2)}, u32[]{:S(2)}) %collective-permute-start.67) | collective-permute-done | bytes 1048608 | tf_op jit(solution)/shard_map/ppermute | solution.py:268
  630.1 3.9 turn.30
  641.3 5.9 put.9.refs_6_
  647.2 9.7 %collective-permute-done.71.refs_2_.refs_3_ = f32[128,8,256]{2,1,0:T(8,128)S(1)} collective-permute-done((f32[128,8,256]{2,1,0:T(8,128)}, f32[128,8,256]{2,1,0:T(8,128)S(1)}, u32[]{:S(2)}, u32[]{:S(2)}) %collective-permute-start.71) | collective-permute-done | bytes 1048608 | tf_op jit(solution)/shard_map/ppermute | solution.py:271
  665.1 3.8 put.10._
  669.7 3.8 put.11
  (404 shorter events, 233.3 us)
Async XLA Ops:
  10.8 64.0 %collective-permute-start.10 = (f32[64,8,256]{2,1,0:T(8,128)}, f32[64,8,256]{2,1,0:T(8,128)}, u32[]{:S(2)}, u32[]{:S(2)}) collective-permute-start(f32[64,8,256]{2,1,0:T(8,128)} %get-tuple-element.430), channel_id=1, source_target_pairs={{0,24},{8,16},{16,8},{24,0},{1,25},{9,17},{17,9},{25,1},{2,26},{10... | collective-permute-start | bytes 1572872 | tf_op jit(solution)/shard_map/ppermute | solution.py:300
  12.3 58.0 %collective-permute-start.3 = (f32[64,8,256]{2,1,0:T(8,128)S(1)}, f32[64,8,256]{2,1,0:T(8,128)}, u32[]{:S(2)}, u32[]{:S(2)}) collective-permute-start(f32[64,8,256]{2,1,0:T(8,128)S(1)} %get-tuple-element.423), channel_id=1, source_target_pairs={{0,16},{8,24},{16,0},{24,8},{1,17},{9,25},{17,1},{25,9},{2,18},{10... | collective-permute-start | bytes 1572872 | tf_op jit(solution)/shard_map/ppermute | solution.py:259
  12.5 58.2 %collective-permute-start.8 = (f32[64,8,256]{2,1,0:T(8,128)S(1)}, f32[64,8,256]{2,1,0:T(8,128)}, u32[]{:S(2)}, u32[]{:S(2)}) collective-permute-start(f32[64,8,256]{2,1,0:T(8,128)S(1)} %get-tuple-element.420), channel_id=1, source_target_pairs={{0,16},{8,24},{16,0},{24,8},{1,17},{9,25},{17,1},{25,9},{2,18},{10... | collective-permute-start | bytes 1572872 | tf_op jit(solution)/shard_map/ppermute | solution.py:259
  23.7 152.2 %collective-permute-start.2 = (f32[64,96,256]{2,1,0:T(8,128)}, f32[64,96,256]{2,1,0:T(8,128)}, u32[]{:S(2)}, u32[]{:S(2)}) collective-permute-start(f32[64,96,256]{2,1,0:T(8,128)} %dynamic-slice_bitcast_fusion), channel_id=1, source_target_pairs={{0,8},{8,0},{16,24},{24,16},{1,9},{9,1},{17,25},{25,17},{2,10},{10... | collective-permute-start | bytes 18874376 | tf_op jit(solution)/shard_map/ppermute | solution.py:262
  70.2 28.5 %collective-permute-start.6 = (f32[64,24,256]{2,1,0:T(8,128)}, f32[64,24,256]{2,1,0:T(8,128)}, u32[]{:S(2)}, u32[]{:S(2)}) collective-permute-start(f32[64,24,256]{2,1,0:T(8,128)} %get-tuple-element.218), channel_id=1, source_target_pairs={{0,8},{8,0},{16,24},{24,16},{1,9},{9,1},{17,25},{25,17},{2,10},{10... | collective-permute-start | bytes 4718600 | tf_op jit(solution)/shard_map/ppermute | solution.py:262
  74.8 52.1 %collective-permute-start.15 = (f32[128,16,256]{2,1,0:T(8,128)}, f32[128,16,256]{2,1,0:T(8,128)S(1)}, u32[]{:S(2)}, u32[]{:S(2)}) collective-permute-start(f32[128,16,256]{2,1,0:T(8,128)} %maximum_maximum_fusion), channel_id=1, source_target_pairs={{2,0},{3,1},{4,2},{5,3},{6,4},{7,5},{10,8},{11,9},{12,10},{13,11},... | collective-permute-start | bytes 6291464 | tf_op jit(solution)/shard_map/ppermute | solution.py:265
  95.2 26.5 %collective-permute-start.13 = (f32[128,8,256]{2,1,0:T(8,128)}, f32[128,8,256]{2,1,0:T(8,128)}, u32[]{:S(2)}, u32[]{:S(2)}) collective-permute-start(f32[128,8,256]{2,1,0:T(8,128)} %get-tuple-element.227.rise), channel_id=1, source_target_pairs={{1,3},{3,5},{5,7},{9,11},{11,13},{13,15},{17,19},{19,21},{21,23},{... | collective-permute-start | bytes 3145736 | tf_op jit(solution)/shard_map/ppermute | solution.py:268
  98.7 33.5 %collective-permute-start.9 = (f32[128,8,256]{2,1,0:T(8,128)S(1)}, f32[128,8,256]{2,1,0:T(8,128)}, u32[]{:S(2)}, u32[]{:S(2)}) collective-permute-start(f32[128,8,256]{2,1,0:T(8,128)S(1)} %get-tuple-element.222.refs_2_.here), channel_id=1, source_target_pairs={{0,16},{8,24},{16,0},{24,8},{1,17},{9,25},{17,1},{25,9},{2,18},{10... | collective-permute-start | bytes 3145736 | tf_op jit(solution)/shard_map/ppermute | solution.py:259
  121.7 25.6 %collective-permute-start.14 = (f32[128,8,256]{2,1,0:T(8,128)}, f32[128,8,256]{2,1,0:T(8,128)}, u32[]{:S(2)}, u32[]{:S(2)}) collective-permute-start(f32[128,8,256]{2,1,0:T(8,128)} %get-tuple-element.228.rise), channel_id=1, source_target_pairs={{1,3},{3,5},{5,7},{9,11},{11,13},{13,15},{17,19},{19,21},{21,23},{... | collective-permute-start | bytes 3145736 | tf_op jit(solution)/shard_map/ppermute | solution.py:268
  125.0 44.4 %collective-permute-start.4 = (f32[128,8,256]{2,1,0:T(8,128)S(1)}, f32[128,8,256]{2,1,0:T(8,128)}, u32[]{:S(2)}, u32[]{:S(2)}) collective-permute-start(f32[128,8,256]{2,1,0:T(8,128)S(1)} %get-tuple-element.212.refs_2_.here), channel_id=1, source_target_pairs={{0,16},{8,24},{16,0},{24,8},{1,17},{9,25},{17,1},{25,9},{2,18},{10... | collective-permute-start | bytes 3145736 | tf_op jit(solution)/shard_map/ppermute | solution.py:259
  132.2 39.8 %collective-permute-start.16 = (f32[128,8,256]{2,1,0:T(8,128)}, f32[128,8,256]{2,1,0:T(8,128)}, u32[]{:S(2)}, u32[]{:S(2)}) collective-permute-start(f32[128,8,256]{2,1,0:T(8,128)} %turn.17), channel_id=1, source_target_pairs={{0,1},{1,0},{2,3},{3,2},{4,5},{5,4},{6,7},{7,6},{8,9},{9,8},{10,11... | collective-permute-start | bytes 3145736 | tf_op jit(solution)/shard_map/ppermute | solution.py:271
  132.2 55.8 %collective-permute-start.20 = (f32[128,16,256]{2,1,0:T(8,128)}, f32[128,16,256]{2,1,0:T(8,128)S(1)}, u32[]{:S(2)}, u32[]{:S(2)}) collective-permute-start(f32[128,16,256]{2,1,0:T(8,128)} %maximum_maximum_fusion.1), channel_id=1, source_target_pairs={{2,0},{3,1},{4,2},{5,3},{6,4},{7,5},{10,8},{11,9},{12,10},{13,11},... | collective-permute-start | bytes 6291464 | tf_op jit(solution)/shard_map/ppermute | solution.py:265
  147.3 35.0 %collective-permute-start.19 = (f32[128,8,256]{2,1,0:T(8,128)}, f32[128,8,256]{2,1,0:T(8,128)S(1)}, u32[]{:S(2)}, u32[]{:S(2)}) collective-permute-start(f32[128,8,256]{2,1,0:T(8,128)} %get-tuple-element.236.rise), channel_id=1, source_target_pairs={{1,3},{3,5},{5,7},{9,11},{11,13},{13,15},{17,19},{19,21},{21,23},{... | collective-permute-start | bytes 3145736 | tf_op jit(solution)/shard_map/ppermute | solution.py:268
  169.4 38.4 %collective-permute-start.22 = (f32[64,32,256]{2,1,0:T(8,128)}, f32[64,32,256]{2,1,0:T(8,128)}, u32[]{:S(2)}, u32[]{:S(2)}) collective-permute-start(f32[64,32,256]{2,1,0:T(8,128)} %get-tuple-element.251), channel_id=1, source_target_pairs={{0,8},{8,0},{16,24},{24,16},{1,9},{9,1},{17,25},{25,17},{2,10},{10... | collective-permute-start | bytes 6291464 | tf_op jit(solution)/shard_map/ppermute | solution.py:262
  172.0 37.8 %collective-permute-start.23 = (f32[64,32,256]{2,1,0:T(8,128)}, f32[64,32,256]{2,1,0:T(8,128)}, u32[]{:S(2)}, u32[]{:S(2)}) collective-permute-start(f32[64,32,256]{2,1,0:T(8,128)} %get-tuple-element.252), channel_id=1, source_target_pairs={{0,8},{8,0},{16,24},{24,16},{1,9},{9,1},{17,25},{25,17},{2,10},{10... | collective-permute-start | bytes 6291464 | tf_op jit(solution)/shard_map/ppermute | solution.py:262
  176.0 24.7 %collective-permute-start.21 = (f32[128,8,256]{2,1,0:T(8,128)}, f32[128,8,256]{2,1,0:T(8,128)}, u32[]{:S(2)}, u32[]{:S(2)}) collective-permute-start(f32[128,8,256]{2,1,0:T(8,128)} %turn.16), channel_id=1, source_target_pairs={{0,1},{1,0},{2,3},{3,2},{4,5},{5,4},{6,7},{7,6},{8,9},{9,8},{10,11... | collective-permute-start | bytes 3145736 | tf_op jit(solution)/shard_map/ppermute | solution.py:271
  182.3 24.4 %collective-permute-start.18 = (f32[128,8,256]{2,1,0:T(8,128)S(1)}, f32[128,8,256]{2,1,0:T(8,128)}, u32[]{:S(2)}, u32[]{:S(2)}) collective-permute-start(f32[128,8,256]{2,1,0:T(8,128)S(1)} %pad_maximum_fusion.10.refs_2_.here), channel_id=1, source_target_pairs={{0,16},{8,24},{16,0},{24,8},{1,17},{9,25},{17,1},{25,9},{2,18},{10... | collective-permute-start | bytes 3145736 | tf_op jit(solution)/shard_map/ppermute | solution.py:259
  188.0 26.5 %collective-permute-start.24 = (f32[128,8,256]{2,1,0:T(8,128)}, f32[128,8,256]{2,1,0:T(8,128)}, u32[]{:S(2)}, u32[]{:S(2)}) collective-permute-start(f32[128,8,256]{2,1,0:T(8,128)} %get-tuple-element.254.rise), channel_id=1, source_target_pairs={{1,3},{3,5},{5,7},{9,11},{11,13},{13,15},{17,19},{19,21},{21,23},{... | collective-permute-start | bytes 3145736 | tf_op jit(solution)/shard_map/ppermute | solution.py:268
  207.8 67.6 %collective-permute-start.29 = (f32[128,16,256]{2,1,0:T(8,128)}, f32[128,16,256]{2,1,0:T(8,128)S(1)}, u32[]{:S(2)}, u32[]{:S(2)}) collective-permute-start(f32[128,16,256]{2,1,0:T(8,128)} %maximum_maximum_fusion.2), channel_id=1, source_target_pairs={{2,0},{3,1},{4,2},{5,3},{6,4},{7,5},{10,8},{11,9},{12,10},{13,11},... | collective-permute-start | bytes 6291464 | tf_op jit(solution)/shard_map/ppermute | solution.py:265
  214.5 25.1 %collective-permute-start.28 = (f32[128,8,256]{2,1,0:T(8,128)}, f32[128,8,256]{2,1,0:T(8,128)}, u32[]{:S(2)}, u32[]{:S(2)}) collective-permute-start(f32[128,8,256]{2,1,0:T(8,128)} %get-tuple-element.267.rise), channel_id=1, source_target_pairs={{1,3},{3,5},{5,7},{9,11},{11,13},{13,15},{17,19},{19,21},{21,23},{... | collective-permute-start | bytes 3145736 | tf_op jit(solution)/shard_map/ppermute | solution.py:268
  230.2 52.5 %collective-permute-start.30 = (f32[128,8,256]{2,1,0:T(8,128)}, f32[128,8,256]{2,1,0:T(8,128)}, u32[]{:S(2)}, u32[]{:S(2)}) collective-permute-start(f32[128,8,256]{2,1,0:T(8,128)} %turn.19), channel_id=1, source_target_pairs={{0,1},{1,0},{2,3},{3,2},{4,5},{5,4},{6,7},{7,6},{8,9},{9,8},{10,11... | collective-permute-start | bytes 3145736 | tf_op jit(solution)/shard_map/ppermute | solution.py:271
  231.0 53.0 %collective-permute-start.27 = (f32[128,8,256]{2,1,0:T(8,128)}, f32[128,8,256]{2,1,0:T(8,128)}, u32[]{:S(2)}, u32[]{:S(2)}) collective-permute-start(f32[128,8,256]{2,1,0:T(8,128)} %get-tuple-element.266.refs_2_.here), channel_id=1, source_target_pairs={{0,16},{8,24},{16,0},{24,8},{1,17},{9,25},{17,1},{25,9},{2,18},{10... | collective-permute-start | bytes 3145736 | tf_op jit(solution)/shard_map/ppermute | solution.py:259
  239.6 48.0 %collective-permute-start.31 = (f32[128,8,256]{2,1,0:T(8,128)}, f32[128,8,256]{2,1,0:T(8,128)}, u32[]{:S(2)}, u32[]{:S(2)}) collective-permute-start(f32[128,8,256]{2,1,0:T(8,128)} %get-tuple-element.279.rise), channel_id=1, source_target_pairs={{1,3},{3,5},{5,7},{9,11},{11,13},{13,15},{17,19},{19,21},{21,23},{... | collective-permute-start | bytes 3145736 | tf_op jit(solution)/shard_map/ppermute | solution.py:268
  251.5 42.4 %collective-permute-start.26 = (f32[128,8,256]{2,1,0:T(8,128)S(1)}, f32[128,8,256]{2,1,0:T(8,128)}, u32[]{:S(2)}, u32[]{:S(2)}) collective-permute-start(f32[128,8,256]{2,1,0:T(8,128)S(1)} %get-tuple-element.264.refs_2_.here), channel_id=1, source_target_pairs={{0,16},{8,24},{16,0},{24,8},{1,17},{9,25},{17,1},{25,9},{2,18},{10... | collective-permute-start | bytes 3145736 | tf_op jit(solution)/shard_map/ppermute | solution.py:259
  275.4 94.7 %collective-permute-start.39 = (f32[64,64,256]{2,1,0:T(8,128)}, f32[64,64,256]{2,1,0:T(8,128)S(1)}, u32[]{:S(2)}, u32[]{:S(2)}) collective-permute-start(f32[64,64,256]{2,1,0:T(8,128)} %get-tuple-element.306), channel_id=1, source_target_pairs={{0,8},{8,0},{16,24},{24,16},{1,9},{9,1},{17,25},{25,17},{2,10},{10... | collective-permute-start | bytes 12582920 | tf_op jit(solution)/shard_map/ppermute | solution.py:262
  282.7 87.8 %collective-permute-start.40 = (f32[64,64,256]{2,1,0:T(8,128)}, f32[64,64,256]{2,1,0:T(8,128)}, u32[]{:S(2)}, u32[]{:S(2)}) collective-permute-start(f32[64,64,256]{2,1,0:T(8,128)} %get-tuple-element.307), channel_id=1, source_target_pairs={{0,8},{8,0},{16,24},{24,16},{1,9},{9,1},{17,25},{25,17},{2,10},{10... | collective-permute-start | bytes 12582920 | tf_op jit(solution)/shard_map/ppermute | solution.py:262
  284.0 25.0 %collective-permute-start.32 = (f32[128,8,256]{2,1,0:T(8,128)}, f32[128,8,256]{2,1,0:T(8,128)}, u32[]{:S(2)}, u32[]{:S(2)}) collective-permute-start(f32[128,8,256]{2,1,0:T(8,128)} %turn.20), channel_id=1, source_target_pairs={{0,1},{1,0},{2,3},{3,2},{4,5},{5,4},{6,7},{7,6},{8,9},{9,8},{10,11... | collective-permute-start | bytes 3145736 | tf_op jit(solution)/shard_map/ppermute | solution.py:271
  287.6 47.4 %collective-permute-start.33 = (f32[64,32,256]{2,1,0:T(8,128)}, f32[64,32,256]{2,1,0:T(8,128)}, u32[]{:S(2)}, u32[]{:S(2)}) collective-permute-start(f32[64,32,256]{2,1,0:T(8,128)} %get-tuple-element.284), channel_id=1, source_target_pairs={{0,8},{8,0},{16,24},{24,16},{1,9},{9,1},{17,25},{25,17},{2,10},{10... | collective-permute-start | bytes 6291464 | tf_op jit(solution)/shard_map/ppermute | solution.py:262
  293.9 63.2 %collective-permute-start.37 = (f32[128,16,256]{2,1,0:T(8,128)}, f32[128,16,256]{2,1,0:T(8,128)S(1)}, u32[]{:S(2)}, u32[]{:S(2)}) collective-permute-start(f32[128,16,256]{2,1,0:T(8,128)} %maximum_maximum_fusion.3), channel_id=1, source_target_pairs={{2,0},{3,1},{4,2},{5,3},{6,4},{7,5},{10,8},{11,9},{12,10},{13,11},... | collective-permute-start | bytes 6291464 | tf_op jit(solution)/shard_map/ppermute | solution.py:265
  309.0 26.0 %collective-permute-start.36 = (f32[128,8,256]{2,1,0:T(8,128)}, f32[128,8,256]{2,1,0:T(8,128)}, u32[]{:S(2)}, u32[]{:S(2)}) collective-permute-start(f32[128,8,256]{2,1,0:T(8,128)} %get-tuple-element.292.rise), channel_id=1, source_target_pairs={{1,3},{3,5},{5,7},{9,11},{11,13},{13,15},{17,19},{19,21},{21,23},{... | collective-permute-start | bytes 3145736 | tf_op jit(solution)/shard_map/ppermute | solution.py:268
  335.0 28.3 %collective-permute-start.38 = (f32[128,8,256]{2,1,0:T(8,128)}, f32[128,8,256]{2,1,0:T(8,128)}, u32[]{:S(2)}, u32[]{:S(2)}) collective-permute-start(f32[128,8,256]{2,1,0:T(8,128)} %turn.21), channel_id=1, source_target_pairs={{0,1},{1,0},{2,3},{3,2},{4,5},{5,4},{6,7},{7,6},{8,9},{9,8},{10,11... | collective-permute-start | bytes 3145736 | tf_op jit(solution)/shard_map/ppermute | solution.py:271
  335.1 29.2 %collective-permute-start.35 = (f32[128,8,256]{2,1,0:T(8,128)}, f32[128,8,256]{2,1,0:T(8,128)}, u32[]{:S(2)}, u32[]{:S(2)}) collective-permute-start(f32[128,8,256]{2,1,0:T(8,128)} %get-tuple-element.291.refs_2_.here), channel_id=1, source_target_pairs={{0,16},{8,24},{16,0},{24,8},{1,17},{9,25},{17,1},{25,9},{2,18},{10... | collective-permute-start | bytes 3145736 | tf_op jit(solution)/shard_map/ppermute | solution.py:259
  357.1 24.8 %collective-permute-start.41 = (f32[128,8,256]{2,1,0:T(8,128)}, f32[128,8,256]{2,1,0:T(8,128)}, u32[]{:S(2)}, u32[]{:S(2)}) collective-permute-start(f32[128,8,256]{2,1,0:T(8,128)} %get-tuple-element.309.rise), channel_id=1, source_target_pairs={{1,3},{3,5},{5,7},{9,11},{11,13},{13,15},{17,19},{19,21},{21,23},{... | collective-permute-start | bytes 3145736 | tf_op jit(solution)/shard_map/ppermute | solution.py:268
  363.4 25.2 %collective-permute-start.42 = (f32[128,8,256]{2,1,0:T(8,128)}, f32[128,8,256]{2,1,0:T(8,128)}, u32[]{:S(2)}, u32[]{:S(2)}) collective-permute-start(f32[128,8,256]{2,1,0:T(8,128)} %turn.22), channel_id=1, source_target_pairs={{0,1},{1,0},{2,3},{3,2},{4,5},{5,4},{6,7},{7,6},{8,9},{9,8},{10,11... | collective-permute-start | bytes 3145736 | tf_op jit(solution)/shard_map/ppermute | solution.py:271
  364.2 46.7 %collective-permute-start.46 = (f32[128,16,256]{2,1,0:T(8,128)}, f32[128,16,256]{2,1,0:T(8,128)S(1)}, u32[]{:S(2)}, u32[]{:S(2)}) collective-permute-start(f32[128,16,256]{2,1,0:T(8,128)} %maximum_maximum_fusion.4), channel_id=1, source_target_pairs={{2,0},{3,1},{4,2},{5,3},{6,4},{7,5},{10,8},{11,9},{12,10},{13,11},... | collective-permute-start | bytes 6291464 | tf_op jit(solution)/shard_map/ppermute | solution.py:265
  382.0 24.0 %collective-permute-start.45 = (f32[128,8,256]{2,1,0:T(8,128)}, f32[128,8,256]{2,1,0:T(8,128)}, u32[]{:S(2)}, u32[]{:S(2)}) collective-permute-start(f32[128,8,256]{2,1,0:T(8,128)} %get-tuple-element.322.rise), channel_id=1, source_target_pairs={{1,3},{3,5},{5,7},{9,11},{11,13},{13,15},{17,19},{19,21},{21,23},{... | collective-permute-start | bytes 3145736 | tf_op jit(solution)/shard_map/ppermute | solution.py:268
  388.6 27.7 %collective-permute-start.47 = (f32[128,8,256]{2,1,0:T(8,128)}, f32[128,8,256]{2,1,0:T(8,128)}, u32[]{:S(2)}, u32[]{:S(2)}) collective-permute-start(f32[128,8,256]{2,1,0:T(8,128)} %turn.23), channel_id=1, source_target_pairs={{0,1},{1,0},{2,3},{3,2},{4,5},{5,4},{6,7},{7,6},{8,9},{9,8},{10,11... | collective-permute-start | bytes 3145736 | tf_op jit(solution)/shard_map/ppermute | solution.py:271
  388.8 41.3 %collective-permute-start.44 = (f32[128,8,256]{2,1,0:T(8,128)S(1)}, f32[128,8,256]{2,1,0:T(8,128)}, u32[]{:S(2)}, u32[]{:S(2)}) collective-permute-start(f32[128,8,256]{2,1,0:T(8,128)S(1)} %get-tuple-element.321.refs_2_.here), channel_id=1, source_target_pairs={{0,16},{8,24},{16,0},{24,8},{1,17},{9,25},{17,1},{25,9},{2,18},{10... | collective-permute-start | bytes 3145736 | tf_op jit(solution)/shard_map/ppermute | solution.py:259
  419.7 45.5 %collective-permute-start.50 = (f32[64,32,256]{2,1,0:T(8,128)}, f32[64,32,256]{2,1,0:T(8,128)}, u32[]{:S(2)}, u32[]{:S(2)}) collective-permute-start(f32[64,32,256]{2,1,0:T(8,128)} %get-tuple-element.339), channel_id=1, source_target_pairs={{0,8},{8,0},{16,24},{24,16},{1,9},{9,1},{17,25},{25,17},{2,10},{10... | collective-permute-start | bytes 6291464 | tf_op jit(solution)/shard_map/ppermute | solution.py:262
  424.7 26.8 %collective-permute-start.48 = (f32[128,8,256]{2,1,0:T(8,128)S(1)}, f32[128,8,256]{2,1,0:T(8,128)S(1)}, u32[]{:S(2)}, u32[]{:S(2)}) collective-permute-start(f32[128,8,256]{2,1,0:T(8,128)S(1)} %copy-done.74), channel_id=1, source_target_pairs={{1,3},{3,5},{5,7},{9,11},{11,13},{13,15},{17,19},{19,21},{21,23},{... | collective-permute-start | bytes 3145736 | tf_op jit(solution)/shard_map/ppermute | solution.py:268
  426.6 53.3 %collective-permute-start.54 = (f32[128,16,256]{2,1,0:T(8,128)}, f32[128,16,256]{2,1,0:T(8,128)S(1)}, u32[]{:S(2)}, u32[]{:S(2)}) collective-permute-start(f32[128,16,256]{2,1,0:T(8,128)} %maximum_maximum_fusion.5), channel_id=1, source_target_pairs={{2,0},{3,1},{4,2},{5,3},{6,4},{7,5},{10,8},{11,9},{12,10},{13,11},... | collective-permute-start | bytes 6291464 | tf_op jit(solution)/shard_map/ppermute | solution.py:265
  430.0 28.7 %collective-permute-start.49 = (f32[128,8,256]{2,1,0:T(8,128)}, f32[128,8,256]{2,1,0:T(8,128)S(1)}, u32[]{:S(2)}, u32[]{:S(2)}) collective-permute-start(f32[128,8,256]{2,1,0:T(8,128)} %turn.24), channel_id=1, source_target_pairs={{0,1},{1,0},{2,3},{3,2},{4,5},{5,4},{6,7},{7,6},{8,9},{9,8},{10,11... | collective-permute-start | bytes 3145736 | tf_op jit(solution)/shard_map/ppermute | solution.py:271
  430.1 34.7 %collective-permute-start.43 = (f32[128,8,256]{2,1,0:T(8,128)S(1)}, f32[128,8,256]{2,1,0:T(8,128)}, u32[]{:S(2)}, u32[]{:S(2)}) collective-permute-start(f32[128,8,256]{2,1,0:T(8,128)S(1)} %get-tuple-element.319.refs_2_.here), channel_id=1, source_target_pairs={{0,16},{8,24},{16,0},{24,8},{1,17},{9,25},{17,1},{25,9},{2,18},{10... | collective-permute-start | bytes 3145736 | tf_op jit(solution)/shard_map/ppermute | solution.py:259
  452.5 27.5 %collective-permute-start.53 = (f32[128,8,256]{2,1,0:T(8,128)}, f32[128,8,256]{2,1,0:T(8,128)}, u32[]{:S(2)}, u32[]{:S(2)}) collective-permute-start(f32[128,8,256]{2,1,0:T(8,128)} %get-tuple-element.347.rise), channel_id=1, source_target_pairs={{1,3},{3,5},{5,7},{9,11},{11,13},{13,15},{17,19},{19,21},{21,23},{... | collective-permute-start | bytes 3145736 | tf_op jit(solution)/shard_map/ppermute | solution.py:268
  458.7 27.1 %collective-permute-start.55 = (f32[128,8,256]{2,1,0:T(8,128)}, f32[128,8,256]{2,1,0:T(8,128)}, u32[]{:S(2)}, u32[]{:S(2)}) collective-permute-start(f32[128,8,256]{2,1,0:T(8,128)} %turn.25), channel_id=1, source_target_pairs={{0,1},{1,0},{2,3},{3,2},{4,5},{5,4},{6,7},{7,6},{8,9},{9,8},{10,11... | collective-permute-start | bytes 3145736 | tf_op jit(solution)/shard_map/ppermute | solution.py:271
  464.8 29.1 %collective-permute-start.52 = (f32[128,8,256]{2,1,0:T(8,128)S(1)}, f32[128,8,256]{2,1,0:T(8,128)S(1)}, u32[]{:S(2)}, u32[]{:S(2)}) collective-permute-start(f32[128,8,256]{2,1,0:T(8,128)S(1)} %get-tuple-element.346.refs_2_.here), channel_id=1, source_target_pairs={{0,16},{8,24},{16,0},{24,8},{1,17},{9,25},{17,1},{25,9},{2,18},{10... | collective-permute-start | bytes 3145736 | tf_op jit(solution)/shard_map/ppermute | solution.py:259
  480.0 25.8 %collective-permute-start.56 = (f32[128,8,256]{2,1,0:T(8,128)}, f32[128,8,256]{2,1,0:T(8,128)S(1)}, u32[]{:S(2)}, u32[]{:S(2)}) collective-permute-start(f32[128,8,256]{2,1,0:T(8,128)} %get-tuple-element.359.rise), channel_id=1, source_target_pairs={{1,3},{3,5},{5,7},{9,11},{11,13},{13,15},{17,19},{19,21},{21,23},{... | collective-permute-start | bytes 3145736 | tf_op jit(solution)/shard_map/ppermute | solution.py:268
  485.8 27.3 %collective-permute-start.57 = (f32[128,8,256]{2,1,0:T(8,128)}, f32[128,8,256]{2,1,0:T(8,128)S(1)}, u32[]{:S(2)}, u32[]{:S(2)}) collective-permute-start(f32[128,8,256]{2,1,0:T(8,128)} %turn.26), channel_id=1, source_target_pairs={{0,1},{1,0},{2,3},{3,2},{4,5},{5,4},{6,7},{7,6},{8,9},{9,8},{10,11... | collective-permute-start | bytes 3145736 | tf_op jit(solution)/shard_map/ppermute | solution.py:271
  485.8 47.8 %collective-permute-start.61 = (f32[128,16,256]{2,1,0:T(8,128)}, f32[128,16,256]{2,1,0:T(8,128)S(1)}, u32[]{:S(2)}, u32[]{:S(2)}) collective-permute-start(f32[128,16,256]{2,1,0:T(8,128)} %maximum_maximum_fusion.6), channel_id=1, source_target_pairs={{2,0},{3,1},{4,2},{5,3},{6,4},{7,5},{10,8},{11,9},{12,10},{13,11},... | collective-permute-start | bytes 6291464 | tf_op jit(solution)/shard_map/ppermute | solution.py:265
  489.2 29.7 %collective-permute-start.51 = (f32[128,8,256]{2,1,0:T(8,128)S(1)}, f32[128,8,256]{2,1,0:T(8,128)}, u32[]{:S(2)}, u32[]{:S(2)}) collective-permute-start(f32[128,8,256]{2,1,0:T(8,128)S(1)} %get-tuple-element.344.refs_2_.here), channel_id=1, source_target_pairs={{0,16},{8,24},{16,0},{24,8},{1,17},{9,25},{17,1},{25,9},{2,18},{10... | collective-permute-start | bytes 3145736 | tf_op jit(solution)/shard_map/ppermute | solution.py:259
  506.7 25.1 %collective-permute-start.60 = (f32[128,8,256]{2,1,0:T(8,128)}, f32[128,8,256]{2,1,0:T(8,128)}, u32[]{:S(2)}, u32[]{:S(2)}) collective-permute-start(f32[128,8,256]{2,1,0:T(8,128)} %get-tuple-element.372.rise), channel_id=1, source_target_pairs={{1,3},{3,5},{5,7},{9,11},{11,13},{13,15},{17,19},{19,21},{21,23},{... | collective-permute-start | bytes 3145736 | tf_op jit(solution)/shard_map/ppermute | solution.py:268
  513.1 25.8 %collective-permute-start.62 = (f32[128,8,256]{2,1,0:T(8,128)}, f32[128,8,256]{2,1,0:T(8,128)}, u32[]{:S(2)}, u32[]{:S(2)}) collective-permute-start(f32[128,8,256]{2,1,0:T(8,128)} %turn.27), channel_id=1, source_target_pairs={{0,1},{1,0},{2,3},{3,2},{4,5},{5,4},{6,7},{7,6},{8,9},{9,8},{10,11... | collective-permute-start | bytes 3145736 | tf_op jit(solution)/shard_map/ppermute | solution.py:271
  514.2 38.4 %collective-permute-start.59 = (f32[128,8,256]{2,1,0:T(8,128)S(1)}, f32[128,8,256]{2,1,0:T(8,128)}, u32[]{:S(2)}, u32[]{:S(2)}) collective-permute-start(f32[128,8,256]{2,1,0:T(8,128)S(1)} %get-tuple-element.371.refs_2_.here), channel_id=1, source_target_pairs={{0,16},{8,24},{16,0},{24,8},{1,17},{9,25},{17,1},{25,9},{2,18},{10... | collective-permute-start | bytes 3145736 | tf_op jit(solution)/shard_map/ppermute | solution.py:259
  538.9 24.5 %collective-permute-start.63 = (f32[128,8,256]{2,1,0:T(8,128)}, f32[128,8,256]{2,1,0:T(8,128)}, u32[]{:S(2)}, u32[]{:S(2)}) collective-permute-start(f32[128,8,256]{2,1,0:T(8,128)} %get-tuple-element.384.rise), channel_id=1, source_target_pairs={{1,3},{3,5},{5,7},{9,11},{11,13},{13,15},{17,19},{19,21},{21,23},{... | collective-permute-start | bytes 3145736 | tf_op jit(solution)/shard_map/ppermute | solution.py:268
  544.2 33.3 %collective-permute-start.65 = (f32[64,32,256]{2,1,0:T(8,128)}, f32[64,32,256]{2,1,0:T(8,128)}, u32[]{:S(2)}, u32[]{:S(2)}) collective-permute-start(f32[64,32,256]{2,1,0:T(8,128)} %get-tuple-element.389), channel_id=1, source_target_pairs={{0,8},{8,0},{16,24},{24,16},{1,9},{9,1},{17,25},{25,17},{2,10},{10... | collective-permute-start | bytes 6291464 | tf_op jit(solution)/shard_map/ppermute | solution.py:262
  548.1 24.8 %collective-permute-start.64 = (f32[128,8,256]{2,1,0:T(8,128)S(1)}, f32[128,8,256]{2,1,0:T(8,128)S(1)}, u32[]{:S(2)}, u32[]{:S(2)}) collective-permute-start(f32[128,8,256]{2,1,0:T(8,128)S(1)} %copy-done.75), channel_id=1, source_target_pairs={{0,1},{1,0},{2,3},{3,2},{4,5},{5,4},{6,7},{7,6},{8,9},{9,8},{10,11... | collective-permute-start | bytes 3145736 | tf_op jit(solution)/shard_map/ppermute | solution.py:271
  549.3 49.0 %collective-permute-start.68 = (f32[128,16,256]{2,1,0:T(8,128)}, f32[128,16,256]{2,1,0:T(8,128)S(1)}, u32[]{:S(2)}, u32[]{:S(2)}) collective-permute-start(f32[128,16,256]{2,1,0:T(8,128)} %maximum_maximum_fusion.7), channel_id=1, source_target_pairs={{2,0},{3,1},{4,2},{5,3},{6,4},{7,5},{10,8},{11,9},{12,10},{13,11},... | collective-permute-start | bytes 6291464 | tf_op jit(solution)/shard_map/ppermute | solution.py:265
  552.7 24.8 %collective-permute-start.58 = (f32[128,8,256]{2,1,0:T(8,128)S(1)}, f32[128,8,256]{2,1,0:T(8,128)S(1)}, u32[]{:S(2)}, u32[]{:S(2)}) collective-permute-start(f32[128,8,256]{2,1,0:T(8,128)S(1)} %get-tuple-element.369.refs_2_.here), channel_id=1, source_target_pairs={{0,16},{8,24},{16,0},{24,8},{1,17},{9,25},{17,1},{25,9},{2,18},{10... | collective-permute-start | bytes 3145736 | tf_op jit(solution)/shard_map/ppermute | solution.py:259
  563.4 28.9 %collective-permute-start.66 = (f32[128,8,256]{2,1,0:T(8,128)}, f32[128,8,256]{2,1,0:T(8,128)S(1)}, u32[]{:S(2)}, u32[]{:S(2)}) collective-permute-start(f32[128,8,256]{2,1,0:T(8,128)} %get-tuple-element.396.rise), channel_id=1, source_target_pairs={{1,3},{3,5},{5,7},{9,11},{11,13},{13,15},{17,19},{19,21},{21,23},{... | collective-permute-start | bytes 3145736 | tf_op jit(solution)/shard_map/ppermute | solution.py:268
  572.9 30.7 %collective-permute-start.69 = (f32[128,8,256]{2,1,0:T(8,128)}, f32[128,8,256]{2,1,0:T(8,128)S(1)}, u32[]{:S(2)}, u32[]{:S(2)}) collective-permute-start(f32[128,8,256]{2,1,0:T(8,128)} %turn.29), channel_id=1, source_target_pairs={{0,1},{1,0},{2,3},{3,2},{4,5},{5,4},{6,7},{7,6},{8,9},{9,8},{10,11... | collective-permute-start | bytes 3145736 | tf_op jit(solution)/shard_map/ppermute | solution.py:271
  603.7 25.4 %collective-permute-start.67 = (f32[128,8,256]{2,1,0:T(8,128)S(1)}, f32[128,8,256]{2,1,0:T(8,128)S(1)}, u32[]{:S(2)}, u32[]{:S(2)}) collective-permute-start(f32[128,8,256]{2,1,0:T(8,128)S(1)} %copy-done.76), channel_id=1, source_target_pairs={{1,3},{3,5},{5,7},{9,11},{11,13},{13,15},{17,19},{19,21},{21,23},{... | collective-permute-start | bytes 3145736 | tf_op jit(solution)/shard_map/ppermute | solution.py:268
  605.6 28.4 %collective-permute-start.70 = (f32[128,8,256]{2,1,0:T(8,128)}, f32[128,8,256]{2,1,0:T(8,128)S(1)}, u32[]{:S(2)}, u32[]{:S(2)}) collective-permute-start(f32[128,8,256]{2,1,0:T(8,128)} %turn.31), channel_id=1, source_target_pairs={{0,1},{1,0},{2,3},{3,2},{4,5},{5,4},{6,7},{7,6},{8,9},{9,8},{10,11... | collective-permute-start | bytes 3145736 | tf_op jit(solution)/shard_map/ppermute | solution.py:271
  609.1 31.3 %collective-permute-start.72 = (f32[64,16,256]{2,1,0:T(8,128)}, f32[64,16,256]{2,1,0:T(8,128)S(1)}, u32[]{:S(2)}, u32[]{:S(2)}) collective-permute-start(f32[64,16,256]{2,1,0:T(8,128)} %get-tuple-element.407), channel_id=1, source_target_pairs={{0,8},{8,0},{16,24},{24,16},{1,9},{9,1},{17,25},{25,17},{2,10},{10... | collective-permute-start | bytes 3145736 | tf_op jit(solution)/shard_map/ppermute | solution.py:262
  638.3 26.0 %collective-permute-start.74 = (f32[64,8,256]{2,1,0:T(8,128)}, f32[64,8,256]{2,1,0:T(8,128)S(1)}, u32[]{:S(2)}, u32[]{:S(2)}) collective-permute-start(f32[64,8,256]{2,1,0:T(8,128)} %get-tuple-element.413), channel_id=1, source_target_pairs={{0,8},{8,0},{16,24},{24,16},{1,9},{9,1},{17,25},{25,17},{2,10},{10... | collective-permute-start | bytes 1572872 | tf_op jit(solution)/shard_map/ppermute | solution.py:262
  (98 other events, 941.9 us)

commit v4 on v3

v4 whole, which is shorter than its diff:
```python
import functools

import jax
import jax.numpy as jnp
from jax import lax
from jax.experimental import pallas as pl
from jax.experimental.pallas import tpu as pltpu
from jax.sharding import PartitionSpec as P

F32 = jnp.float32
BF16 = jnp.bfloat16
VMEM_LIMIT = 56 * 2**20
SPAN, LANES = 8, 128
LIGHT = pl.CostEstimate(flops=1000, transcendentals=0, bytes_accessed=1000)
PARAMS = pltpu.CompilerParams(vmem_limit_bytes=VMEM_LIMIT)
WHOLE = pl.BlockSpec(memory_space=pltpu.VMEM)


def gate(*values):
    return lax.optimization_barrier(values)


def flag(cond):
    return jnp.where(cond, 1.0, 0.0).astype(F32)


def halves(x):
    high = x.astype(BF16)
    low = (x - high.astype(F32)).astype(BF16)
    return high, low


def halves_outside(x):
    high = lax.reduce_precision(x, 8, 7)
    return high.astype(BF16), (x - high).astype(BF16)


def dot(a, b):
    return jnp.dot(a, b, preferred_element_type=F32)


def plan(rows, length):
    n = max(4, min(length // SPAN, rows // 4))
    size = length // n
    chunks = [(s * size, size) for s in range(n)]
    groups, at = [], 0
    while at < n:
        step = 4 if n - at > 4 else max(1, (n - at) // 2)
        groups.append((at, at + step))
        at += step
    return chunks, groups


def spans(*bounds):
    return list(zip(bounds[:-1], bounds[1:]))


def local_kernel(at, half, core, own_rows, occ, c_hi, c_lo, b_both, row_b, row_c, *outs):
    block, phases = occ.shape[0], occ.shape[2]
    size = outs[0].shape[2]
    first = pl.program_id(0) * block
    rows = [pl.ds(pl.multiple_of(core[n] * half + at, SPAN), size) for n in range(2)]
    y = jnp.concatenate([occ[i, r] for i in range(block) for r in rows], axis=0)
    y_hi, y_lo = halves(y)
    n_y = y.shape[0]
    by_c = dot(jnp.concatenate([y_hi, y_lo], axis=0), c_hi[...])
    by_c = by_c[:n_y] + by_c[n_y:] + dot(y_hi, c_lo[...])
    for i in range(block):
        x_hi, x_lo = halves(occ[i])
        by_b = dot(b_both[...], x_hi)
        by_b = by_b[: 4 * size] + by_b[4 * size :] + dot(b_both[: 4 * size], x_lo)
        here = slice(2 * size * i, 2 * size * (i + 1))
        left = row_c[...] - own_rows[first + i] - row_b[...]
        base = by_c[here, :phases] + by_b[: 2 * size] + y[here] * left
        rise = by_c[here, phases:] + by_b[2 * size :]
        mine, peer = outs
        for n, value in enumerate((base, rise)):
            mine[n, i] = value[:size]
            peer[n, i] = value[size:]


def local_terms(core, occ, own_rows, c_split, b_both, row_b, row_c, at, size):
    rows, mid, phases = occ.shape
    block = 8
    out = pl.BlockSpec((2, block, size, phases), lambda i, c: (0, i, 0, 0))
    return pl.pallas_call(
        functools.partial(local_kernel, at, mid // 2),
        grid_spec=pltpu.PrefetchScalarGridSpec(
            num_scalar_prefetch=1,
            grid=(rows // block,),
            in_specs=[
                pl.BlockSpec(memory_space=pltpu.SMEM),
                pl.BlockSpec((block, mid, phases), lambda i, c: (i, 0, 0)),
            ]
            + [WHOLE] * 5,
            out_specs=[out] * 2,
        ),
        out_shape=[jax.ShapeDtypeStruct((2, rows, size, phases), F32)] * 2,
        compiler_params=PARAMS,
        cost_estimate=LIGHT,
        name="local_terms",
    )(core, own_rows, occ, *c_split, b_both, row_b, row_c)


def first_kernel(n_slabs, n_deep, parity, fall, *refs):
    w_both, w_hi = refs[0], refs[1]
    slabs = refs[2 : 2 + n_slabs]
    deep = refs[2 + n_slabs : 2 + n_slabs + n_deep]
    mine, peer, stay_out, rise_out, swap_out = refs[2 + n_slabs + n_deep :]
    rows, span, lanes = stay_out.shape
    flat = [ref.reshape(ref.shape[0] * span, lanes) for ref in slabs]
    stay_flat = stay_out.reshape(rows * span, lanes)
    rise_flat = rise_out.reshape(rows * span, lanes)
    for b in range(0, span, 2):
        ats = [pl.ds(b, rows, stride=span), pl.ds(b + 1, rows, stride=span)]
        parts = []
        for ref in flat:
            picks = [pl.ds(b + n, ref.shape[0] // span, stride=span) for n in range(2)]
            parts.append(halves(jnp.concatenate([ref[pick, :] for pick in picks], axis=1)))
        g_hi = jnp.concatenate([p[0] for p in parts], axis=0)
        g_lo = jnp.concatenate([p[1] for p in parts], axis=0)
        both = dot(w_both[...], g_hi)
        out = both[: 2 * rows] + both[2 * rows :] + dot(w_hi[...], g_lo)
        for n, at in enumerate(ats):
            stay_flat[at, :] = out[:rows, n * lanes : (n + 1) * lanes]
            rise_flat[at, :] = out[rows:, n * lanes : (n + 1) * lanes]
    half = rows // 2
    once, twice = fall[0:1], fall[1:2]
    for which, near in enumerate((mine, peer)):
        part = slice(which * half, (which + 1) * half)
        far_down = deep[which][...] if n_deep == 2 else deep[0][part]
        stay_out[part] += near[0] + far_down * twice
        lift = rise_out[part] + near[1]
        rise_out[part] = lift

        @pl.when(parity[0] == 0)
        def _():
            swap_out[part] = lift + far_down * once

    @pl.when(parity[0] != 0)
    def _():
        at = 0
        for ref in slabs:
            if at < rows:
                swap_out[at : at + ref.shape[0]] = ref[...] * once
            at += ref.shape[0]


def first_terms(parity, fall, w_both, w_hi, slabs, deep, near, start):
    rows, size, phases = slabs[0].shape
    slab_specs = [pl.BlockSpec((v.shape[0], SPAN, LANES), lambda j, h: (0, j, h)) for v in [*slabs, *deep]]
    chunk = pl.BlockSpec((rows, SPAN, LANES), lambda j, h: (0, j, h))
    local_part = pl.BlockSpec((2, rows // 2, SPAN, LANES), lambda j, h: (0, 0, start // SPAN + j, h))
    return pl.pallas_call(
        functools.partial(first_kernel, len(slabs), len(deep)),
        grid=(size // SPAN, phases // LANES),
        in_specs=[pl.BlockSpec(memory_space=pltpu.SMEM), pl.BlockSpec((2, LANES), lambda j, h: (0, h)), WHOLE, WHOLE]
        + slab_specs
        + [local_part] * 2,
        out_specs=[chunk] * 3,
        out_shape=[jax.ShapeDtypeStruct((rows, size, phases), F32)] * 3,
        compiler_params=PARAMS,
        cost_estimate=LIGHT,
        name="first_terms",
    )(parity, fall, w_both, w_hi, *slabs, *deep, *near)


def turn_kernel(swap, lifted, out):
    out[...] = swap[...] + lifted[...]


def turn(swap, lifted):
    rows, size, phases = swap.shape
    block = max(8, rows // 2)
    chunk = pl.BlockSpec((block, SPAN, phases), lambda i, j: (i, j, 0))
    return pl.pallas_call(
        turn_kernel,
        grid=(rows // block, size // SPAN),
        in_specs=[chunk, chunk],
        out_specs=chunk,
        out_shape=jax.ShapeDtypeStruct(swap.shape, F32),
        compiler_params=PARAMS,
        cost_estimate=LIGHT,
        name="turn",
    )(swap, lifted)


def finish_kernel(n_alias, _, *refs):
    out, back = refs[4 + n_alias :]
    out[...] = refs[0][...] + refs[1][...]
    back[...] = refs[2][...] + refs[3][...]


def finish(core, out, back, shape, back_size, stay, risen, start, back_at):
    rows, size, phases = stay.shape
    half = rows // 2
    steps = shape[1] // 2 // SPAN
    args, specs = [core], []
    for which in range(2):
        for array in (stay, risen):
            args.append(array)
            specs.append(pl.BlockSpec((half, SPAN, LANES), lambda j, h, c, which=which: (which, j, h)))
    alias = {}
    for n, old in enumerate((out, back)):
        if old is not None:
            alias[len(args)] = n
            args.append(old)
            specs.append(pl.BlockSpec(memory_space=pl.ANY))
    return pl.pallas_call(
        functools.partial(finish_kernel, len(alias)),
        grid_spec=pltpu.PrefetchScalarGridSpec(
            num_scalar_prefetch=1,
            grid=(size // SPAN, phases // LANES),
            in_specs=specs,
            out_specs=[
                pl.BlockSpec((half, SPAN, LANES), lambda j, h, c: (0, c[0] * steps + start // SPAN + j, h)),
                pl.BlockSpec((half, SPAN, LANES), lambda j, h, c: (0, back_at // SPAN + j, h)),
            ],
        ),
        out_shape=[jax.ShapeDtypeStruct(shape, F32), jax.ShapeDtypeStruct((half, back_size, phases), F32)],
        input_output_aliases=alias,
        compiler_params=PARAMS,
        cost_estimate=LIGHT,
        name="finish",
    )(*args)


def put_kernel(core, piece, _, out):
    out[...] = piece[...]


def put(core, out, piece, start):
    rows, size, phases = piece.shape
    steps = out.shape[1] // 2 // SPAN
    return pl.pallas_call(
        put_kernel,
        grid_spec=pltpu.PrefetchScalarGridSpec(
            num_scalar_prefetch=1,
            grid=(size // SPAN,),
            in_specs=[
                pl.BlockSpec((rows, SPAN, phases), lambda j, c: (0, j, 0)),
                pl.BlockSpec(memory_space=pl.ANY),
            ],
            out_specs=pl.BlockSpec((rows, SPAN, phases), lambda j, c: (0, c[1] * steps + start // SPAN + j, 0)),
        ),
        out_shape=jax.ShapeDtypeStruct(out.shape, F32),
        input_output_aliases={2: 0},
        compiler_params=PARAMS,
        cost_estimate=LIGHT,
        name="put",
    )(core, piece, out)


def local(occupancy, rates, increments, draw, crusher_rate, bounds):
    n_cls, n_lvl = lax.axis_size("cls"), lax.axis_size("lvl")
    occ = occupancy[0]
    rows, mid, phases = occ.shape
    half = mid // 2
    level = lax.axis_index("lvl")
    place = lax.axis_index("cls")
    k = place % 2
    core = jnp.stack([k, 1 - k])
    even = level % 2 == 0
    bottom, top = bounds[0], bounds[1]

    def along_cls(v, by):
        return lax.ppermute(v, "cls", [(i, (i + by) % n_cls) for i in range(n_cls)])

    def other_core(v):
        return lax.ppermute(v, "cls", [(i, i ^ 1) for i in range(n_cls)])

    def two_down(v):
        return lax.ppermute(v, "lvl", [(i, i - 2) for i in range(2, n_lvl)])

    def two_up(v):
        return lax.ppermute(v, "lvl", [(i, i + 2) for i in range(1, n_lvl - 2, 2)])

    def pair_swap(v):
        return lax.ppermute(v, "lvl", [(i, i ^ 1) for i in range(n_lvl)])

    def cut(array, which, at, size):
        return lax.dynamic_slice_in_dim(array, core[which] * half + at, size, axis=1)

    chunks, groups = plan(rows, half)
    n = len(chunks)
    size = chunks[0][1]
    shifts = [2 * s for s in range(1, n_cls // 2)]
    sent = [None] * n
    tokens = []
    for lo, hi in spans(*sorted({0, n // 4, n})):
        at = chunks[lo][0]
        give = cut(occ, 1, at, (hi - lo) * size)
        if tokens:
            give, _ = gate(give, tokens[-1])
        got = other_core(give)
        tokens.append(got)
        for s in range(lo, hi):
            start = chunks[s][0]
            part = lax.slice_in_dim(got, start - at, start - at + size, axis=1)
            sent[s] = jnp.concatenate([cut(occ, 0, start, size), part], axis=0)

    far, deep = [None] * n, [None] * n

    def start_early(s):
        for by in shifts:
            straight = along_cls(cut(occ, 0, s * size, size), by)
            crossed = [(i, ((i + by) % n_cls) ^ 1) for i in range(n_cls)]
            cross = lax.ppermute(cut(occ, 1, s * size, size), "cls", crossed)
            far[s] = (far[s] or []) + [straight, cross]
        both = [(i * n_lvl + m, (i ^ 1) * n_lvl + m - 2) for i in range(n_cls) for m in range(2, n_lvl)]
        deep[s] = [two_down(cut(occ, 0, s * size, size)), lax.ppermute(cut(occ, 1, s * size, size), ("cls", "lvl"), both)]

    def start_far(s, *after):
        operand = gate(sent[s], *after)[0] if after else sent[s]
        far[s] = [along_cls(operand, by) for by in shifts]

    def start_deep(s, *after):
        operand = gate(sent[s], *after)[0] if after else sent[s]
        deep[s] = [two_down(operand)]

    start_early(0)

    row_total = jnp.sum(rates, axis=2)
    uniform_rate = jnp.sum(jnp.max(row_total, axis=1)) + jnp.max(crusher_rate)
    out_rows = row_total * flag((increments == 0) | (level + increments <= top))
    rise_ok = flag(level + 1 <= top)
    drop_here = crusher_rate * flag(level - draw >= bottom)
    drop_deep = crusher_rate * flag(level + 2 - draw >= bottom)
    scale = 1.0 / uniform_rate
    once = jnp.where(even, drop_deep, drop_here) * flag(draw == 1) * scale
    twice = drop_deep * flag(draw == 2) * scale
    fall_vec = jnp.stack([once, twice])
    parity = (level % 2)[None]

    stay_rows = rates * (flag(increments == 0) * scale)[:, :, None]
    rise_rows = rates * (flag(increments == 1) * (rise_ok * scale))[:, :, None]

    c_split = halves_outside(jnp.concatenate([stay_rows[2], rise_rows[2]], axis=1))
    lost = out_rows * scale
    own_rows = lax.dynamic_slice_in_dim(lost[0], place * rows, rows)
    row_c = (1.0 - lost[2] - drop_here * scale)[None, :]
    parts = []

    def start_part(lo, hi, begin):
        at, span = chunks[lo][0], (hi - lo) * size
        cat_b = jnp.concatenate([cut(r, w, at, span) for r in (stay_rows[1], rise_rows[1]) for w in range(2)], axis=1)
        row_b = jnp.concatenate([lax.dynamic_slice_in_dim(lost[1], core[w] * half + at, span) for w in range(2)])
        mine, give = local_terms(
            core,
            gate(occ, begin)[0],
            own_rows,
            c_split,
            jnp.concatenate(halves_outside(cat_b.T), axis=0),
            row_b[:, None],
            row_c,
            at,
            span,
        )
        return lo, hi, at, mine, give

    def send_part(part, *after):
        lo, hi, at, mine, give = part
        parts.append((lo, hi, at, (mine, other_core(gate(give, *after)[0]))))

    first_rows = 3 * n // 16 if n > 8 else n
    send_part(start_part(0, first_rows, tokens[0]), *far[0], *deep[0])
    waiting = {}
    later = {0: (first_rows, n // 2), n // 2 - 4: (n // 2, n)} if n > 8 else {}

    origin = [place, place ^ 1]
    for by in shifts:
        origin += [(place - by) % n_cls, ((place - by) % n_cls) ^ 1]
    mine = jnp.concatenate(
        [
            lax.dynamic_slice_in_dim(r, p * rows, rows, axis=1)
            for r in (stay_rows[0], rise_rows[0])
            for p in (place, place ^ 1)
        ],
        axis=1,
    ).T
    mine = jnp.concatenate([lax.dynamic_slice_in_dim(mine, o * rows, rows, axis=1) for o in origin], axis=1)
    a_hi, a_lo = halves_outside(mine)
    a_both = jnp.concatenate([a_hi, a_lo], axis=0)

    out = None
    stay, rise, swap, lifted, risen = ([None] * n for _ in range(5))
    back = [None] * len(groups)
    group_of = {s: g for g, (lo, hi) in enumerate(groups) for s in range(lo, hi)}

    for s in range(n + 4):
        if s < n:
            if s >= 3:
                far[s][0], risen[s - 3] = gate(far[s][0], risen[s - 3])
            if s >= 4:
                far[s][0], out = gate(far[s][0], out)
            if s + 1 < n:
                start_far(s + 1, far[s][0])
            if s + 1 < n:
                start_deep(s + 1, far[s][0], *deep[s])
            lo, hi, at, near = next(p for p in parts if p[0] <= s < p[1])
            stay[s], rise[s], swap[s] = first_terms(
                parity, fall_vec, a_both, a_hi, [sent[s]] + far[s], deep[s], near, chunks[s][0] - at
            )
            lift_me = rise[s]
            if s >= 1:
                lift_me, lifted[s - 1] = gate(lift_me, lifted[s - 1])
            lifted[s] = two_up(lift_me)
        if 1 <= s <= n:
            p = s - 1
            swap_me = turn(swap[p], lifted[p])
            if p in later:
                waiting[p + 2] = start_part(*later[p], swap_me)
            if p >= 1:
                swap_me, risen[p - 1] = gate(swap_me, risen[p - 1])
            risen[p] = pair_swap(swap_me)
            if s in waiting:
                send_part(waiting[s], *far[s], *deep[s], lifted[p], risen[p - 1])
        if 0 <= s - 2 < n:
            p = s - 2
            g = group_of[p]
            lo, hi = groups[g]
            out, back[g] = finish(
                core, out, back[g], occ.shape, (hi - lo) * size, stay[p], risen[p], chunks[p][0], (p - lo) * size
            )
            if p == hi - 1:
                back[g] = other_core(back[g])
        if 0 <= s - 3 < n:
            p = s - 3
            lo, hi = groups[group_of[p]]
            if p == hi - 1:
                out = put(core, out, back[group_of[p]], chunks[lo][0])
    return out[None]


def solution(mesh):
    in_specs = (P("lvl", "cls", None, None), P(), P(), P(), P(), P())
    out_specs = P("lvl", "cls", None, None)
    return jax.shard_map(local, mesh=mesh, in_specs=in_specs, out_specs=out_specs, check_vma=False)
```

time: 681 us -> 629 us (0.924)
  Pallas kernels: 313 us -> 242 us
  starting transfers between devices: 102 us -> 140 us
  other arithmetic: 33.1 us -> 15.3 us
    ppermute x16, waiting for transfers between devices: 106 us -> 23.5 us  [two_up(): return lax.ppermute(v, 'lvl', [(i, i + 2) for i in range(1, n_lvl - 2, 2)])]
    ppermute x8 -> x16, waiting for transfers between devices: 12.8 us -> 68.6 us  [two_down(): return lax.ppermute(v, 'lvl', [(i, i - 2) for i in range(2, n_lvl)])]
    ppermute x16, waiting for transfers between devices: 1.98 us -> 56.2 us  [along_cls(): return lax.ppermute(v, 'cls', [(i, (i + by) % n_cls) for i in range(n_cls)])]
    pallas_call x4 -> x3, Pallas kernels: 77.2 us -> 50.9 us  [local_terms(): pl.pallas_call(functools.partial(local_kernel, at, mid // 2), grid_spec=p...]
    pallas_call x16, Pallas kernels: 63.9 us -> 38.4 us  [turn(): pl.pallas_call(turn_kernel, grid=(rows // block, size // SPAN), in_specs=...]
    pallas_call x6, Pallas kernels: 44 us -> 21.1 us  [put(): pl.pallas_call(put_kernel, grid_spec=pltpu.PrefetchScalarGridSpec(num_sca...]
    ppermute x16, starting transfers between devices: 40.8 us -> 60.9 us  [two_up(): return lax.ppermute(v, 'lvl', [(i, i + 2) for i in range(1, n_lvl - 2, 2)])]
    ppermute x16, waiting for transfers between devices: 29.8 us -> 13.6 us  [pair_swap(): return lax.ppermute(v, 'lvl', [(i, i ^ 1) for i in range(n_lvl)])]
  transfers between devices with their start and end apart: 75 -> 77, of which waited for: 22 -> 33; matrix products, arithmetic and copies ran while one was open for 11% -> 7% of each run, Pallas kernels for 46% -> 38%
where the time goes in v4:
time: 629 us; the launch traced here: 624 us
  Pallas kernels  242 us (38%)
  waiting for transfers between devices  162 us (26%)
  starting transfers between devices  140 us (22%)
  local copies, waits for them, and re-layouts  61.7 us (10%)
  other arithmetic  15.3 us (2%)
    pallas_call x16, Pallas kernels, first_terms(): pl.pallas_call(functools.partial(first_kernel, len(slabs), len(deep)), gr...  81.9 us
    ppermute x16, waiting for transfers between devices, two_down(): return lax.ppermute(v, 'lvl', [(i, i - 2) for i in range(2, n_lvl)])  68.6 us
    ppermute x16, starting transfers between devices, two_up(): return lax.ppermute(v, 'lvl', [(i, i + 2) for i in range(1, n_lvl - 2, 2)])  60.9 us
    ppermute x16, waiting for transfers between devices, along_cls(): return lax.ppermute(v, 'cls', [(i, (i + by) % n_cls) for i in range(n_cls)])  56.2 us
    pallas_call x3, Pallas kernels, local_terms(): pl.pallas_call(functools.partial(local_kernel, at, mid // 2), grid_spec=p...  50.9 us
    pallas_call x16, Pallas kernels, finish(): pl.pallas_call(functools.partial(finish_kernel, len(alias)), grid_spec=pl...  49.4 us
    pallas_call x16, Pallas kernels, turn(): pl.pallas_call(turn_kernel, grid=(rows // block, size // SPAN), in_specs=...  38.4 us
    ppermute x16, starting transfers between devices, two_down(): return lax.ppermute(v, 'lvl', [(i, i - 2) for i in range(2, n_lvl)])  33.2 us
  transfers between devices with their start and end apart: 77, of which 33 were waited for; matrix products, arithmetic and copies ran while one was open for 7% of the time, Pallas kernels for 38%

profile of v4, /device:TPU:21, one launch (start us, length us, event | category | flops | bytes accessed | tf_op | source)
XLA Modules:
  0.0 624.0 jit_solution(1393324140207260730)
XLA Ops:
  0.0 7.0 %dynamic-slice_bitcast_fusion.2 = (f32[64,8,256]{2,1,0:T(8,128)}, f32[64,8,256]{2,1,0:T(8,128)}, f32[64,8,256]{2,1,0:T(8,128)}, f32[64,8,256]{2,1,0:T(8,128)}, f...) fusion(f32[1,64,256,256]{3,2,1,0:T(8,128)} %param.6, ...), kind=kLoop, calls=%fused_computation.22 | loop fusion | bytes 17825860 | tf_op jit(solution)/shard_map/dynamic_slice | solution.py:282
  13.2 3.2 dynamic-slice_bitcast_fusion.1
  29.9 13.7 %local_terms.3 = (f32[2,64,24,256]{3,2,1,0:T(8,128)}, f32[2,64,24,256]{3,2,1,0:T(8,128)}) custom-call(s32[2]{0:T(128)} %pad_add_fusion.core._, f32[64]{0:T(128)} %fusion.12.own_rows, f32[64,256,256]{2,1,0:T(8,128)} %bitcast.115, bf16[256,512]{1,0:T(8,128)(2,1)} %get-tuple-element.487.c_hi, bf16[256,512]{1,0:T(8,128)(2,1)} %get-tuple-element.486.c_lo, ...), custom_call_target="tpu_custom_call" | custom-call | flops 1000 | bytes 1000 | tf_op jit(solution)/shard_map/local_terms/pallas_call | solution.py:86
  54.5 5.1 first_terms.18
  59.6 4.5 collective-permute-start.12
  64.1 6.3 %dynamic-slice_bitcast_fusion = f32[64,96,256]{2,1,0:T(8,128)} fusion(f32[1,64,256,256]{3,2,1,0:T(8,128)} %param.6, s32[]{:T(128)S(6)} %select_n.168), kind=kLoop, calls=%fused_computation | loop fusion | bytes 12582916 | tf_op jit(solution)/shard_map/dynamic_slice | solution.py:282
  71.7 4.3 collective-permute-done.3.refs_3_
  81.0 5.1 first_terms.16
  86.1 4.0 collective-permute-start.13
  94.7 4.8 collective-permute-done.4.refs_3_
  99.5 4.3 collective-permute-done.11.refs_4_
  103.8 5.1 first_terms.17
  109.0 16.8 %local_terms.4 = (f32[2,64,40,256]{3,2,1,0:T(8,128)}, f32[2,64,40,256]{3,2,1,0:T(8,128)}) custom-call(s32[2]{0:T(128)} %pad_add_fusion.core._, f32[64]{0:T(128)} %fusion.12.own_rows, f32[64,256,256]{2,1,0:T(8,128)} %bitcast.116, bf16[256,512]{1,0:T(8,128)(2,1)} %get-tuple-element.487.c_hi, bf16[256,512]{1,0:T(8,128)(2,1)} %get-tuple-element.486.c_lo, ...), custom_call_target="tpu_custom_call" | custom-call | flops 1000 | bytes 1000 | tf_op jit(solution)/shard_map/local_terms/pallas_call | solution.py:86
  133.4 3.1 collective-permute-start.18
  136.5 19.3 %collective-permute-done.5.refs_3_ = f32[128,8,256]{2,1,0:T(8,128)} collective-permute-done((f32[128,8,256]{2,1,0:T(8,128)S(1)}, f32[128,8,256]{2,1,0:T(8,128)}, u32[]{:S(2)}, u32[]{:S(2)}) %collective-permute-start.5) | collective-permute-done | bytes 1048608 | tf_op jit(solution)/shard_map/ppermute | solution.py:267
  156.1 5.4 fusion.19
  167.6 5.1 first_terms.19
  172.6 4.1 collective-permute-start.22
  190.5 5.1 first_terms.20
  197.9 4.0 collective-permute-start.26
  205.3 3.1 finish.18
  214.8 5.1 first_terms.21
  222.1 4.0 collective-permute-start.30
  237.1 20.3 %local_terms.5 = (f32[2,64,64,256]{3,2,1,0:T(8,128)}, f32[2,64,64,256]{3,2,1,0:T(8,128)}) custom-call(s32[2]{0:T(128)} %pad_add_fusion.core._, f32[64]{0:T(128)} %fusion.12.own_rows, f32[64,256,256]{2,1,0:T(8,128)} %bitcast.117, bf16[256,512]{1,0:T(8,128)(2,1)} %get-tuple-element.487.c_hi, bf16[256,512]{1,0:T(8,128)(2,1)} %get-tuple-element.486.c_lo, ...), custom_call_target="tpu_custom_call" | custom-call | flops 1000 | bytes 1000 | tf_op jit(solution)/shard_map/local_terms/pallas_call | solution.py:86
  260.5 5.2 first_terms.22
  268.1 3.8 collective-permute-start.39
  275.1 4.4 collective-permute-start.35
  279.5 17.2 %collective-permute-done.28.refs_3_ = f32[128,8,256]{2,1,0:T(8,128)} collective-permute-done((f32[128,8,256]{2,1,0:T(8,128)S(1)}, f32[128,8,256]{2,1,0:T(8,128)}, u32[]{:S(2)}, u32[]{:S(2)}) %collective-permute-start.28) | collective-permute-done | bytes 1048608 | tf_op jit(solution)/shard_map/ppermute | solution.py:267
  301.5 4.5 put.6.refs_4_
  308.9 5.2 first_terms.23
  314.0 3.4 collective-permute-start.40
  325.2 4.1 collective-permute-done.33.refs_3_
  334.0 5.2 first_terms.24
  339.2 4.3 collective-permute-start.44
  352.6 3.2 collective-permute-done.43.refs_4_
  355.8 5.1 first_terms.25
  368.7 3.2 finish.23
  371.9 4.1 collective-permute-start.50
  377.9 3.4 collective-permute-start.48
  383.1 19.6 %collective-permute-done.47.refs_4_ = f32[128,8,256]{2,1,0:T(8,128)S(1)} collective-permute-done((f32[128,8,256]{2,1,0:T(8,128)S(1)}, f32[128,8,256]{2,1,0:T(8,128)S(1)}, u32[]{:S(2)}, u32[]{:S(2)}) %collective-permute-start.47) | collective-permute-done | bytes 1048608 | tf_op jit(solution)/shard_map/ppermute | solution.py:273
  405.9 5.1 first_terms.26
  411.0 4.1 collective-permute-start.53
  422.9 4.4 put.7.refs_4_
  432.1 5.1 first_terms.27
  437.2 3.9 collective-permute-start.57
  447.6 3.2 collective-permute-done.51.refs_3_
  451.4 3.5 collective-permute-done.56.refs_4_
  457.4 5.1 first_terms.28
  462.5 3.6 collective-permute-start.61
  474.0 4.9 collective-permute-done.60.refs_4_
  479.0 5.1 first_terms.29
  491.6 3.2 finish.27
  494.7 3.9 collective-permute-start.67
  500.5 3.4 collective-permute-start.65
  504.8 20.5 %collective-permute-done.64.refs_4_ = f32[128,8,256]{2,1,0:T(8,128)S(1)} collective-permute-done((f32[128,8,256]{2,1,0:T(8,128)S(1)}, f32[128,8,256]{2,1,0:T(8,128)S(1)}, u32[]{:S(2)}, u32[]{:S(2)}) %collective-permute-start.64) | collective-permute-done | bytes 1048608 | tf_op jit(solution)/shard_map/ppermute | solution.py:273
  528.3 5.1 first_terms.30
  533.4 3.4 collective-permute-start.69
  544.6 4.4 put.8.refs_4_
  553.1 5.1 first_terms.31
  559.2 3.3 collective-permute-start.70
  571.3 12.7 %collective-permute-done.70.lifted = f32[128,8,256]{2,1,0:T(8,128)S(1)} collective-permute-done((f32[128,8,256]{2,1,0:T(8,128)}, f32[128,8,256]{2,1,0:T(8,128)S(1)}, u32[]{:S(2)}, u32[]{:S(2)}) %collective-permute-start.70) | collective-permute-done | bytes 1048608 | tf_op jit(solution)/shard_map/ppermute | solution.py:276
  591.6 3.2 collective-permute-start.76
  598.5 10.7 %collective-permute-done.73.refs_1_.refs_3_ = f32[128,8,256]{2,1,0:T(8,128)S(1)} collective-permute-done((f32[128,8,256]{2,1,0:T(8,128)}, f32[128,8,256]{2,1,0:T(8,128)S(1)}, u32[]{:S(2)}, u32[]{:S(2)}) %collective-permute-start.73) | collective-permute-done | bytes 1048608 | tf_op jit(solution)/shard_map/ppermute | solution.py:279
  613.3 4.1 collective-permute-start.75
  (398 shorter events, 230.9 us)
Async XLA Ops:
  7.1 36.5 %collective-permute-start.9 = (f32[64,8,256]{2,1,0:T(8,128)}, f32[64,8,256]{2,1,0:T(8,128)}, u32[]{:S(2)}, u32[]{:S(2)}) collective-permute-start(f32[64,8,256]{2,1,0:T(8,128)} %get-tuple-element.445), channel_id=1, source_target_pairs={{0,24},{8,16},{16,8},{24,0},{1,25},{9,17},{17,9},{25,1},{2,26},{10... | collective-permute-start | bytes 1572872 | tf_op jit(solution)/shard_map/ppermute | solution.py:308
  8.9 34.7 %collective-permute-start.7 = (f32[64,8,256]{2,1,0:T(8,128)}, f32[64,8,256]{2,1,0:T(8,128)}, u32[]{:S(2)}, u32[]{:S(2)}) collective-permute-start(f32[64,8,256]{2,1,0:T(8,128)} %get-tuple-element.445), channel_id=1, source_target_pairs={{2,8},{3,9},{4,10},{5,11},{6,12},{7,13},{10,0},{11,1},{12,2},{13,3... | collective-permute-start | bytes 1572872 | tf_op jit(solution)/shard_map/ppermute | solution.py:311
  10.8 32.8 %collective-permute-start.6 = (f32[64,8,256]{2,1,0:T(8,128)}, f32[64,8,256]{2,1,0:T(8,128)}, u32[]{:S(2)}, u32[]{:S(2)}) collective-permute-start(f32[64,8,256]{2,1,0:T(8,128)} %get-tuple-element.446), channel_id=1, source_target_pairs={{2,0},{3,1},{4,2},{5,3},{6,4},{7,5},{10,8},{11,9},{12,10},{13,11},... | collective-permute-start | bytes 1572872 | tf_op jit(solution)/shard_map/ppermute | solution.py:273
  12.9 30.7 %collective-permute-start.2 = (f32[64,8,256]{2,1,0:T(8,128)}, f32[64,8,256]{2,1,0:T(8,128)}, u32[]{:S(2)}, u32[]{:S(2)}) collective-permute-start(f32[64,8,256]{2,1,0:T(8,128)} %get-tuple-element.446), channel_id=1, source_target_pairs={{0,16},{8,24},{16,0},{24,8},{1,17},{9,25},{17,1},{25,9},{2,18},{10... | collective-permute-start | bytes 1572872 | tf_op jit(solution)/shard_map/ppermute | solution.py:267
  51.4 24.6 %collective-permute-start.3 = (f32[128,8,256]{2,1,0:T(8,128)}, f32[128,8,256]{2,1,0:T(8,128)}, u32[]{:S(2)}, u32[]{:S(2)}) collective-permute-start(f32[128,8,256]{2,1,0:T(8,128)} %get-tuple-element.229.refs_2_), channel_id=1, source_target_pairs={{0,16},{8,24},{16,0},{24,8},{1,17},{9,25},{17,1},{25,9},{2,18},{10... | collective-permute-start | bytes 3145736 | tf_op jit(solution)/shard_map/ppermute | solution.py:267
  52.6 26.2 %collective-permute-start.8 = (f32[128,8,256]{2,1,0:T(8,128)}, f32[128,8,256]{2,1,0:T(8,128)}, u32[]{:S(2)}, u32[]{:S(2)}) collective-permute-start(f32[128,8,256]{2,1,0:T(8,128)} %get-tuple-element.229.refs_2_), channel_id=1, source_target_pairs={{2,0},{3,1},{4,2},{5,3},{6,4},{7,5},{10,8},{11,9},{12,10},{13,11},... | collective-permute-start | bytes 3145736 | tf_op jit(solution)/shard_map/ppermute | solution.py:273
  59.6 26.5 %collective-permute-start.12 = (f32[128,8,256]{2,1,0:T(8,128)}, f32[128,8,256]{2,1,0:T(8,128)}, u32[]{:S(2)}, u32[]{:S(2)}) collective-permute-start(f32[128,8,256]{2,1,0:T(8,128)} %get-tuple-element.238), channel_id=1, source_target_pairs={{1,3},{3,5},{5,7},{9,11},{11,13},{13,15},{17,19},{19,21},{21,23},{... | collective-permute-start | bytes 3145736 | tf_op jit(solution)/shard_map/ppermute | solution.py:276
  70.3 85.7 %collective-permute-start.1 = (f32[64,96,256]{2,1,0:T(8,128)}, f32[64,96,256]{2,1,0:T(8,128)}, u32[]{:S(2)}, u32[]{:S(2)}) collective-permute-start(f32[64,96,256]{2,1,0:T(8,128)} %dynamic-slice_bitcast_fusion), channel_id=1, source_target_pairs={{0,8},{8,0},{16,24},{24,16},{1,9},{9,1},{17,25},{25,17},{2,10},{10... | collective-permute-start | bytes 18874376 | tf_op jit(solution)/shard_map/ppermute | solution.py:270
  78.8 25.0 %collective-permute-start.11 = (f32[128,8,256]{2,1,0:T(8,128)S(1)}, f32[128,8,256]{2,1,0:T(8,128)}, u32[]{:S(2)}, u32[]{:S(2)}) collective-permute-start(f32[128,8,256]{2,1,0:T(8,128)S(1)} %pad_maximum_fusion.13.refs_2_), channel_id=1, source_target_pairs={{2,0},{3,1},{4,2},{5,3},{6,4},{7,5},{10,8},{11,9},{12,10},{13,11},... | collective-permute-start | bytes 3145736 | tf_op jit(solution)/shard_map/ppermute | solution.py:273
  86.1 39.7 %collective-permute-start.13 = (f32[128,8,256]{2,1,0:T(8,128)}, f32[128,8,256]{2,1,0:T(8,128)}, u32[]{:S(2)}, u32[]{:S(2)}) collective-permute-start(f32[128,8,256]{2,1,0:T(8,128)} %get-tuple-element.239), channel_id=1, source_target_pairs={{1,3},{3,5},{5,7},{9,11},{11,13},{13,15},{17,19},{19,21},{21,23},{... | collective-permute-start | bytes 3145736 | tf_op jit(solution)/shard_map/ppermute | solution.py:276
  92.5 35.6 %collective-permute-start.14 = (f32[128,8,256]{2,1,0:T(8,128)}, f32[128,8,256]{2,1,0:T(8,128)S(1)}, u32[]{:S(2)}, u32[]{:S(2)}) collective-permute-start(f32[128,8,256]{2,1,0:T(8,128)} %turn.17), channel_id=1, source_target_pairs={{0,1},{1,0},{2,3},{3,2},{4,5},{5,4},{6,7},{7,6},{8,9},{9,8},{10,11... | collective-permute-start | bytes 3145736 | tf_op jit(solution)/shard_map/ppermute | solution.py:279
  128.2 37.0 %collective-permute-start.17 = (f32[2,64,40,256]{3,2,1,0:T(8,128)}, f32[2,64,40,256]{3,2,1,0:T(8,128)S(1)}, u32[]{:S(2)}, u32[]{:S(2)}) collective-permute-start(f32[2,64,40,256]{3,2,1,0:T(8,128)} %get-tuple-element.251), channel_id=1, source_target_pairs={{0,8},{8,0},{16,24},{24,16},{1,9},{9,1},{17,25},{25,17},{2,10},{10... | collective-permute-start | bytes 15728648 | tf_op jit(solution)/shard_map/ppermute | solution.py:270
  130.9 24.9 %collective-permute-start.5 = (f32[128,8,256]{2,1,0:T(8,128)S(1)}, f32[128,8,256]{2,1,0:T(8,128)}, u32[]{:S(2)}, u32[]{:S(2)}) collective-permute-start(f32[128,8,256]{2,1,0:T(8,128)S(1)} %pad_maximum_fusion.12.refs_2_), channel_id=1, source_target_pairs={{0,16},{8,24},{16,0},{24,8},{1,17},{9,25},{17,1},{25,9},{2,18},{10... | collective-permute-start | bytes 3145736 | tf_op jit(solution)/shard_map/ppermute | solution.py:267
  131.2 31.9 %collective-permute-start.16 = (f32[128,8,256]{2,1,0:T(8,128)S(1)}, f32[128,8,256]{2,1,0:T(8,128)S(1)}, u32[]{:S(2)}, u32[]{:S(2)}) collective-permute-start(f32[128,8,256]{2,1,0:T(8,128)S(1)} %pad_maximum_fusion.12.refs_2_), channel_id=1, source_target_pairs={{2,0},{3,1},{4,2},{5,3},{6,4},{7,5},{10,8},{11,9},{12,10},{13,11},... | collective-permute-start | bytes 3145736 | tf_op jit(solution)/shard_map/ppermute | solution.py:273
  133.4 39.2 %collective-permute-start.18 = (f32[128,8,256]{2,1,0:T(8,128)}, f32[128,8,256]{2,1,0:T(8,128)}, u32[]{:S(2)}, u32[]{:S(2)}) collective-permute-start(f32[128,8,256]{2,1,0:T(8,128)} %get-tuple-element.253), channel_id=1, source_target_pairs={{1,3},{3,5},{5,7},{9,11},{11,13},{13,15},{17,19},{19,21},{21,23},{... | collective-permute-start | bytes 3145736 | tf_op jit(solution)/shard_map/ppermute | solution.py:276
  155.8 24.2 %collective-permute-start.19 = (f32[128,8,256]{2,1,0:T(8,128)}, f32[128,8,256]{2,1,0:T(8,128)S(1)}, u32[]{:S(2)}, u32[]{:S(2)}) collective-permute-start(f32[128,8,256]{2,1,0:T(8,128)} %turn.16), channel_id=1, source_target_pairs={{0,1},{1,0},{2,3},{3,2},{4,5},{5,4},{6,7},{7,6},{8,9},{9,8},{10,11... | collective-permute-start | bytes 3145736 | tf_op jit(solution)/shard_map/ppermute | solution.py:279
  162.5 24.0 %collective-permute-start.15 = (f32[128,8,256]{2,1,0:T(8,128)}, f32[128,8,256]{2,1,0:T(8,128)}, u32[]{:S(2)}, u32[]{:S(2)}) collective-permute-start(f32[128,8,256]{2,1,0:T(8,128)} %pad_maximum_fusion.11.refs_2_), channel_id=1, source_target_pairs={{0,16},{8,24},{16,0},{24,8},{1,17},{9,25},{17,1},{25,9},{2,18},{10... | collective-permute-start | bytes 3145736 | tf_op jit(solution)/shard_map/ppermute | solution.py:267
  163.1 25.5 %collective-permute-start.21 = (f32[128,8,256]{2,1,0:T(8,128)}, f32[128,8,256]{2,1,0:T(8,128)}, u32[]{:S(2)}, u32[]{:S(2)}) collective-permute-start(f32[128,8,256]{2,1,0:T(8,128)} %pad_maximum_fusion.11.refs_2_), channel_id=1, source_target_pairs={{2,0},{3,1},{4,2},{5,3},{6,4},{7,5},{10,8},{11,9},{12,10},{13,11},... | collective-permute-start | bytes 3145736 | tf_op jit(solution)/shard_map/ppermute | solution.py:273
  172.6 25.2 %collective-permute-start.22 = (f32[128,8,256]{2,1,0:T(8,128)}, f32[128,8,256]{2,1,0:T(8,128)S(1)}, u32[]{:S(2)}, u32[]{:S(2)}) collective-permute-start(f32[128,8,256]{2,1,0:T(8,128)} %get-tuple-element.268), channel_id=1, source_target_pairs={{1,3},{3,5},{5,7},{9,11},{11,13},{13,15},{17,19},{19,21},{21,23},{... | collective-permute-start | bytes 3145736 | tf_op jit(solution)/shard_map/ppermute | solution.py:276
  180.0 24.3 %collective-permute-start.23 = (f32[128,8,256]{2,1,0:T(8,128)}, f32[128,8,256]{2,1,0:T(8,128)S(1)}, u32[]{:S(2)}, u32[]{:S(2)}) collective-permute-start(f32[128,8,256]{2,1,0:T(8,128)} %turn.18), channel_id=1, source_target_pairs={{0,1},{1,0},{2,3},{3,2},{4,5},{5,4},{6,7},{7,6},{8,9},{9,8},{10,11... | collective-permute-start | bytes 3145736 | tf_op jit(solution)/shard_map/ppermute | solution.py:279
  188.5 24.3 %collective-permute-start.25 = (f32[128,8,256]{2,1,0:T(8,128)S(1)}, f32[128,8,256]{2,1,0:T(8,128)}, u32[]{:S(2)}, u32[]{:S(2)}) collective-permute-start(f32[128,8,256]{2,1,0:T(8,128)S(1)} %pad_maximum_fusion.10.refs_2_), channel_id=1, source_target_pairs={{2,0},{3,1},{4,2},{5,3},{6,4},{7,5},{10,8},{11,9},{12,10},{13,11},... | collective-permute-start | bytes 3145736 | tf_op jit(solution)/shard_map/ppermute | solution.py:273
  197.9 24.3 %collective-permute-start.26 = (f32[128,8,256]{2,1,0:T(8,128)}, f32[128,8,256]{2,1,0:T(8,128)}, u32[]{:S(2)}, u32[]{:S(2)}) collective-permute-start(f32[128,8,256]{2,1,0:T(8,128)} %get-tuple-element.282), channel_id=1, source_target_pairs={{1,3},{3,5},{5,7},{9,11},{11,13},{13,15},{17,19},{19,21},{21,23},{... | collective-permute-start | bytes 3145736 | tf_op jit(solution)/shard_map/ppermute | solution.py:276
  204.3 24.2 %collective-permute-start.27 = (f32[128,8,256]{2,1,0:T(8,128)}, f32[128,8,256]{2,1,0:T(8,128)S(1)}, u32[]{:S(2)}, u32[]{:S(2)}) collective-permute-start(f32[128,8,256]{2,1,0:T(8,128)} %turn.19), channel_id=1, source_target_pairs={{0,1},{1,0},{2,3},{3,2},{4,5},{5,4},{6,7},{7,6},{8,9},{9,8},{10,11... | collective-permute-start | bytes 3145736 | tf_op jit(solution)/shard_map/ppermute | solution.py:279
  209.4 51.0 %collective-permute-start.24 = (f32[128,8,256]{2,1,0:T(8,128)S(1)}, f32[128,8,256]{2,1,0:T(8,128)}, u32[]{:S(2)}, u32[]{:S(2)}) collective-permute-start(f32[128,8,256]{2,1,0:T(8,128)S(1)} %pad_maximum_fusion.9.refs_2_), channel_id=1, source_target_pairs={{0,16},{8,24},{16,0},{24,8},{1,17},{9,25},{17,1},{25,9},{2,18},{10... | collective-permute-start | bytes 3145736 | tf_op jit(solution)/shard_map/ppermute | solution.py:267
  212.9 47.6 %collective-permute-start.29 = (f32[128,8,256]{2,1,0:T(8,128)S(1)}, f32[128,8,256]{2,1,0:T(8,128)}, u32[]{:S(2)}, u32[]{:S(2)}) collective-permute-start(f32[128,8,256]{2,1,0:T(8,128)S(1)} %pad_maximum_fusion.9.refs_2_), channel_id=1, source_target_pairs={{2,0},{3,1},{4,2},{5,3},{6,4},{7,5},{10,8},{11,9},{12,10},{13,11},... | collective-permute-start | bytes 3145736 | tf_op jit(solution)/shard_map/ppermute | solution.py:273
  222.1 43.6 %collective-permute-start.30 = (f32[128,8,256]{2,1,0:T(8,128)}, f32[128,8,256]{2,1,0:T(8,128)}, u32[]{:S(2)}, u32[]{:S(2)}) collective-permute-start(f32[128,8,256]{2,1,0:T(8,128)} %get-tuple-element.296), channel_id=1, source_target_pairs={{1,3},{3,5},{5,7},{9,11},{11,13},{13,15},{17,19},{19,21},{21,23},{... | collective-permute-start | bytes 3145736 | tf_op jit(solution)/shard_map/ppermute | solution.py:276
  228.5 39.6 %collective-permute-start.31 = (f32[128,8,256]{2,1,0:T(8,128)}, f32[128,8,256]{2,1,0:T(8,128)S(1)}, u32[]{:S(2)}, u32[]{:S(2)}) collective-permute-start(f32[128,8,256]{2,1,0:T(8,128)} %turn.20), channel_id=1, source_target_pairs={{0,1},{1,0},{2,3},{3,2},{4,5},{5,4},{6,7},{7,6},{8,9},{9,8},{10,11... | collective-permute-start | bytes 3145736 | tf_op jit(solution)/shard_map/ppermute | solution.py:279
  268.1 65.8 %collective-permute-start.39 = (f32[2,64,64,256]{3,2,1,0:T(8,128)}, f32[2,64,64,256]{3,2,1,0:T(8,128)}, u32[]{:S(2)}, u32[]{:S(2)}) collective-permute-start(f32[2,64,64,256]{3,2,1,0:T(8,128)} %get-tuple-element.326), channel_id=1, source_target_pairs={{0,8},{8,0},{16,24},{24,16},{1,9},{9,1},{17,25},{25,17},{2,10},{10... | collective-permute-start | bytes 25165832 | tf_op jit(solution)/shard_map/ppermute | solution.py:270
  272.0 29.6 %collective-permute-start.32 = (f32[64,32,256]{2,1,0:T(8,128)S(1)}, f32[64,32,256]{2,1,0:T(8,128)}, u32[]{:S(2)}, u32[]{:S(2)}) collective-permute-start(f32[64,32,256]{2,1,0:T(8,128)S(1)} %copy-done.2), channel_id=1, source_target_pairs={{0,8},{8,0},{16,24},{24,16},{1,9},{9,1},{17,25},{25,17},{2,10},{10... | collective-permute-start | bytes 6291464 | tf_op jit(solution)/shard_map/ppermute | solution.py:270
  272.2 24.5 %collective-permute-start.28 = (f32[128,8,256]{2,1,0:T(8,128)S(1)}, f32[128,8,256]{2,1,0:T(8,128)}, u32[]{:S(2)}, u32[]{:S(2)}) collective-permute-start(f32[128,8,256]{2,1,0:T(8,128)S(1)} %pad_maximum_fusion.8.refs_2_), channel_id=1, source_target_pairs={{0,16},{8,24},{16,0},{24,8},{1,17},{9,25},{17,1},{25,9},{2,18},{10... | collective-permute-start | bytes 3145736 | tf_op jit(solution)/shard_map/ppermute | solution.py:267
  273.2 33.8 %collective-permute-start.34 = (f32[128,8,256]{2,1,0:T(8,128)S(1)}, f32[128,8,256]{2,1,0:T(8,128)}, u32[]{:S(2)}, u32[]{:S(2)}) collective-permute-start(f32[128,8,256]{2,1,0:T(8,128)S(1)} %pad_maximum_fusion.8.refs_2_), channel_id=1, source_target_pairs={{2,0},{3,1},{4,2},{5,3},{6,4},{7,5},{10,8},{11,9},{12,10},{13,11},... | collective-permute-start | bytes 3145736 | tf_op jit(solution)/shard_map/ppermute | solution.py:273
  275.1 39.0 %collective-permute-start.35 = (f32[128,8,256]{2,1,0:T(8,128)}, f32[128,8,256]{2,1,0:T(8,128)}, u32[]{:S(2)}, u32[]{:S(2)}) collective-permute-start(f32[128,8,256]{2,1,0:T(8,128)} %get-tuple-element.310), channel_id=1, source_target_pairs={{1,3},{3,5},{5,7},{9,11},{11,13},{13,15},{17,19},{19,21},{21,23},{... | collective-permute-start | bytes 3145736 | tf_op jit(solution)/shard_map/ppermute | solution.py:276
  296.6 24.1 %collective-permute-start.36 = (f32[128,8,256]{2,1,0:T(8,128)}, f32[128,8,256]{2,1,0:T(8,128)S(1)}, u32[]{:S(2)}, u32[]{:S(2)}) collective-permute-start(f32[128,8,256]{2,1,0:T(8,128)} %turn.21), channel_id=1, source_target_pairs={{0,1},{1,0},{2,3},{3,2},{4,5},{5,4},{6,7},{7,6},{8,9},{9,8},{10,11... | collective-permute-start | bytes 3145736 | tf_op jit(solution)/shard_map/ppermute | solution.py:279
  306.9 24.8 %collective-permute-start.38 = (f32[128,8,256]{2,1,0:T(8,128)S(1)}, f32[128,8,256]{2,1,0:T(8,128)S(1)}, u32[]{:S(2)}, u32[]{:S(2)}) collective-permute-start(f32[128,8,256]{2,1,0:T(8,128)S(1)} %pad_maximum_fusion.7.refs_2_), channel_id=1, source_target_pairs={{2,0},{3,1},{4,2},{5,3},{6,4},{7,5},{10,8},{11,9},{12,10},{13,11},... | collective-permute-start | bytes 3145736 | tf_op jit(solution)/shard_map/ppermute | solution.py:273
  314.0 25.2 %collective-permute-start.40 = (f32[128,8,256]{2,1,0:T(8,128)}, f32[128,8,256]{2,1,0:T(8,128)}, u32[]{:S(2)}, u32[]{:S(2)}) collective-permute-start(f32[128,8,256]{2,1,0:T(8,128)} %get-tuple-element.328), channel_id=1, source_target_pairs={{1,3},{3,5},{5,7},{9,11},{11,13},{13,15},{17,19},{19,21},{21,23},{... | collective-permute-start | bytes 3145736 | tf_op jit(solution)/shard_map/ppermute | solution.py:276
  320.8 25.1 %collective-permute-start.41 = (f32[128,8,256]{2,1,0:T(8,128)}, f32[128,8,256]{2,1,0:T(8,128)S(1)}, u32[]{:S(2)}, u32[]{:S(2)}) collective-permute-start(f32[128,8,256]{2,1,0:T(8,128)} %turn.22), channel_id=1, source_target_pairs={{0,1},{1,0},{2,3},{3,2},{4,5},{5,4},{6,7},{7,6},{8,9},{9,8},{10,11... | collective-permute-start | bytes 3145736 | tf_op jit(solution)/shard_map/ppermute | solution.py:279
  331.8 24.0 %collective-permute-start.43 = (f32[128,8,256]{2,1,0:T(8,128)S(1)}, f32[128,8,256]{2,1,0:T(8,128)}, u32[]{:S(2)}, u32[]{:S(2)}) collective-permute-start(f32[128,8,256]{2,1,0:T(8,128)S(1)} %pad_maximum_fusion.6.refs_2_), channel_id=1, source_target_pairs={{2,0},{3,1},{4,2},{5,3},{6,4},{7,5},{10,8},{11,9},{12,10},{13,11},... | collective-permute-start | bytes 3145736 | tf_op jit(solution)/shard_map/ppermute | solution.py:273
  339.2 24.1 %collective-permute-start.44 = (f32[128,8,256]{2,1,0:T(8,128)}, f32[128,8,256]{2,1,0:T(8,128)S(1)}, u32[]{:S(2)}, u32[]{:S(2)}) collective-permute-start(f32[128,8,256]{2,1,0:T(8,128)} %get-tuple-element.342), channel_id=1, source_target_pairs={{1,3},{3,5},{5,7},{9,11},{11,13},{13,15},{17,19},{19,21},{21,23},{... | collective-permute-start | bytes 3145736 | tf_op jit(solution)/shard_map/ppermute | solution.py:276
  351.6 29.9 %collective-permute-start.42 = (f32[128,8,256]{2,1,0:T(8,128)S(1)}, f32[128,8,256]{2,1,0:T(8,128)S(1)}, u32[]{:S(2)}, u32[]{:S(2)}) collective-permute-start(f32[128,8,256]{2,1,0:T(8,128)S(1)} %pad_maximum_fusion.5.refs_2_), channel_id=1, source_target_pairs={{0,16},{8,24},{16,0},{24,8},{1,17},{9,25},{17,1},{25,9},{2,18},{10... | collective-permute-start | bytes 3145736 | tf_op jit(solution)/shard_map/ppermute | solution.py:267
  371.9 49.6 %collective-permute-start.50 = (f32[64,32,256]{2,1,0:T(8,128)}, f32[64,32,256]{2,1,0:T(8,128)S(1)}, u32[]{:S(2)}, u32[]{:S(2)}) collective-permute-start(f32[64,32,256]{2,1,0:T(8,128)} %get-tuple-element.361), channel_id=1, source_target_pairs={{0,8},{8,0},{16,24},{24,16},{1,9},{9,1},{17,25},{25,17},{2,10},{10... | collective-permute-start | bytes 6291464 | tf_op jit(solution)/shard_map/ppermute | solution.py:270
  376.0 26.8 %collective-permute-start.47 = (f32[128,8,256]{2,1,0:T(8,128)S(1)}, f32[128,8,256]{2,1,0:T(8,128)S(1)}, u32[]{:S(2)}, u32[]{:S(2)}) collective-permute-start(f32[128,8,256]{2,1,0:T(8,128)S(1)} %pad_maximum_fusion.5.refs_2_), channel_id=1, source_target_pairs={{2,0},{3,1},{4,2},{5,3},{6,4},{7,5},{10,8},{11,9},{12,10},{13,11},... | collective-permute-start | bytes 3145736 | tf_op jit(solution)/shard_map/ppermute | solution.py:273
  377.9 33.0 %collective-permute-start.48 = (f32[128,8,256]{2,1,0:T(8,128)}, f32[128,8,256]{2,1,0:T(8,128)}, u32[]{:S(2)}, u32[]{:S(2)}) collective-permute-start(f32[128,8,256]{2,1,0:T(8,128)} %get-tuple-element.356), channel_id=1, source_target_pairs={{1,3},{3,5},{5,7},{9,11},{11,13},{13,15},{17,19},{19,21},{21,23},{... | collective-permute-start | bytes 3145736 | tf_op jit(solution)/shard_map/ppermute | solution.py:276
  381.4 36.1 %collective-permute-start.49 = (f32[128,8,256]{2,1,0:T(8,128)}, f32[128,8,256]{2,1,0:T(8,128)S(1)}, u32[]{:S(2)}, u32[]{:S(2)}) collective-permute-start(f32[128,8,256]{2,1,0:T(8,128)} %turn.24), channel_id=1, source_target_pairs={{0,1},{1,0},{2,3},{3,2},{4,5},{5,4},{6,7},{7,6},{8,9},{9,8},{10,11... | collective-permute-start | bytes 3145736 | tf_op jit(solution)/shard_map/ppermute | solution.py:279
  382.6 38.9 %collective-permute-start.46 = (f32[128,8,256]{2,1,0:T(8,128)S(1)}, f32[128,8,256]{2,1,0:T(8,128)}, u32[]{:S(2)}, u32[]{:S(2)}) collective-permute-start(f32[128,8,256]{2,1,0:T(8,128)S(1)} %pad_maximum_fusion.4.refs_2_), channel_id=1, source_target_pairs={{0,16},{8,24},{16,0},{24,8},{1,17},{9,25},{17,1},{25,9},{2,18},{10... | collective-permute-start | bytes 3145736 | tf_op jit(solution)/shard_map/ppermute | solution.py:267
  403.7 26.0 %collective-permute-start.52 = (f32[128,8,256]{2,1,0:T(8,128)S(1)}, f32[128,8,256]{2,1,0:T(8,128)}, u32[]{:S(2)}, u32[]{:S(2)}) collective-permute-start(f32[128,8,256]{2,1,0:T(8,128)S(1)} %pad_maximum_fusion.4.refs_2_), channel_id=1, source_target_pairs={{2,0},{3,1},{4,2},{5,3},{6,4},{7,5},{10,8},{11,9},{12,10},{13,11},... | collective-permute-start | bytes 3145736 | tf_op jit(solution)/shard_map/ppermute | solution.py:273
  411.0 26.2 %collective-permute-start.53 = (f32[128,8,256]{2,1,0:T(8,128)}, f32[128,8,256]{2,1,0:T(8,128)}, u32[]{:S(2)}, u32[]{:S(2)}) collective-permute-start(f32[128,8,256]{2,1,0:T(8,128)} %get-tuple-element.370), channel_id=1, source_target_pairs={{1,3},{3,5},{5,7},{9,11},{11,13},{13,15},{17,19},{19,21},{21,23},{... | collective-permute-start | bytes 3145736 | tf_op jit(solution)/shard_map/ppermute | solution.py:276
  417.5 26.0 %collective-permute-start.54 = (f32[128,8,256]{2,1,0:T(8,128)}, f32[128,8,256]{2,1,0:T(8,128)S(1)}, u32[]{:S(2)}, u32[]{:S(2)}) collective-permute-start(f32[128,8,256]{2,1,0:T(8,128)} %turn.25), channel_id=1, source_target_pairs={{0,1},{1,0},{2,3},{3,2},{4,5},{5,4},{6,7},{7,6},{8,9},{9,8},{10,11... | collective-permute-start | bytes 3145736 | tf_op jit(solution)/shard_map/ppermute | solution.py:279
  429.7 25.1 %collective-permute-start.56 = (f32[128,8,256]{2,1,0:T(8,128)S(1)}, f32[128,8,256]{2,1,0:T(8,128)}, u32[]{:S(2)}, u32[]{:S(2)}) collective-permute-start(f32[128,8,256]{2,1,0:T(8,128)S(1)} %pad_maximum_fusion.3.refs_2_), channel_id=1, source_target_pairs={{2,0},{3,1},{4,2},{5,3},{6,4},{7,5},{10,8},{11,9},{12,10},{13,11},... | collective-permute-start | bytes 3145736 | tf_op jit(solution)/shard_map/ppermute | solution.py:273
  437.2 25.3 %collective-permute-start.57 = (f32[128,8,256]{2,1,0:T(8,128)}, f32[128,8,256]{2,1,0:T(8,128)}, u32[]{:S(2)}, u32[]{:S(2)}) collective-permute-start(f32[128,8,256]{2,1,0:T(8,128)} %get-tuple-element.384), channel_id=1, source_target_pairs={{1,3},{3,5},{5,7},{9,11},{11,13},{13,15},{17,19},{19,21},{21,23},{... | collective-permute-start | bytes 3145736 | tf_op jit(solution)/shard_map/ppermute | solution.py:276
  443.5 25.1 %collective-permute-start.58 = (f32[128,8,256]{2,1,0:T(8,128)}, f32[128,8,256]{2,1,0:T(8,128)S(1)}, u32[]{:S(2)}, u32[]{:S(2)}) collective-permute-start(f32[128,8,256]{2,1,0:T(8,128)} %turn.26), channel_id=1, source_target_pairs={{0,1},{1,0},{2,3},{3,2},{4,5},{5,4},{6,7},{7,6},{8,9},{9,8},{10,11... | collective-permute-start | bytes 3145736 | tf_op jit(solution)/shard_map/ppermute | solution.py:279
  454.8 24.2 %collective-permute-start.60 = (f32[128,8,256]{2,1,0:T(8,128)S(1)}, f32[128,8,256]{2,1,0:T(8,128)}, u32[]{:S(2)}, u32[]{:S(2)}) collective-permute-start(f32[128,8,256]{2,1,0:T(8,128)S(1)} %pad_maximum_fusion.2.refs_2_), channel_id=1, source_target_pairs={{2,0},{3,1},{4,2},{5,3},{6,4},{7,5},{10,8},{11,9},{12,10},{13,11},... | collective-permute-start | bytes 3145736 | tf_op jit(solution)/shard_map/ppermute | solution.py:273
  462.5 24.3 %collective-permute-start.61 = (f32[128,8,256]{2,1,0:T(8,128)}, f32[128,8,256]{2,1,0:T(8,128)S(1)}, u32[]{:S(2)}, u32[]{:S(2)}) collective-permute-start(f32[128,8,256]{2,1,0:T(8,128)} %get-tuple-element.398), channel_id=1, source_target_pairs={{1,3},{3,5},{5,7},{9,11},{11,13},{13,15},{17,19},{19,21},{21,23},{... | collective-permute-start | bytes 3145736 | tf_op jit(solution)/shard_map/ppermute | solution.py:276
  473.5 30.6 %collective-permute-start.59 = (f32[128,8,256]{2,1,0:T(8,128)S(1)}, f32[128,8,256]{2,1,0:T(8,128)}, u32[]{:S(2)}, u32[]{:S(2)}) collective-permute-start(f32[128,8,256]{2,1,0:T(8,128)S(1)} %pad_maximum_fusion.1.refs_2_), channel_id=1, source_target_pairs={{0,16},{8,24},{16,0},{24,8},{1,17},{9,25},{17,1},{25,9},{2,18},{10... | collective-permute-start | bytes 3145736 | tf_op jit(solution)/shard_map/ppermute | solution.py:267
  494.7 48.5 %collective-permute-start.67 = (f32[64,32,256]{2,1,0:T(8,128)}, f32[64,32,256]{2,1,0:T(8,128)S(1)}, u32[]{:S(2)}, u32[]{:S(2)}) collective-permute-start(f32[64,32,256]{2,1,0:T(8,128)} %get-tuple-element.417), channel_id=1, source_target_pairs={{0,8},{8,0},{16,24},{24,16},{1,9},{9,1},{17,25},{25,17},{2,10},{10... | collective-permute-start | bytes 6291464 | tf_op jit(solution)/shard_map/ppermute | solution.py:270
  498.6 26.7 %collective-permute-start.64 = (f32[128,8,256]{2,1,0:T(8,128)S(1)}, f32[128,8,256]{2,1,0:T(8,128)S(1)}, u32[]{:S(2)}, u32[]{:S(2)}) collective-permute-start(f32[128,8,256]{2,1,0:T(8,128)S(1)} %pad_maximum_fusion.1.refs_2_), channel_id=1, source_target_pairs={{2,0},{3,1},{4,2},{5,3},{6,4},{7,5},{10,8},{11,9},{12,10},{13,11},... | collective-permute-start | bytes 3145736 | tf_op jit(solution)/shard_map/ppermute | solution.py:273
  500.5 32.8 %collective-permute-start.65 = (f32[128,8,256]{2,1,0:T(8,128)}, f32[128,8,256]{2,1,0:T(8,128)S(1)}, u32[]{:S(2)}, u32[]{:S(2)}) collective-permute-start(f32[128,8,256]{2,1,0:T(8,128)} %get-tuple-element.412), channel_id=1, source_target_pairs={{1,3},{3,5},{5,7},{9,11},{11,13},{13,15},{17,19},{19,21},{21,23},{... | collective-permute-start | bytes 3145736 | tf_op jit(solution)/shard_map/ppermute | solution.py:276
  504.0 35.2 %collective-permute-start.66 = (f32[128,8,256]{2,1,0:T(8,128)}, f32[128,8,256]{2,1,0:T(8,128)S(1)}, u32[]{:S(2)}, u32[]{:S(2)}) collective-permute-start(f32[128,8,256]{2,1,0:T(8,128)} %turn.28), channel_id=1, source_target_pairs={{0,1},{1,0},{2,3},{3,2},{4,5},{5,4},{6,7},{7,6},{8,9},{9,8},{10,11... | collective-permute-start | bytes 3145736 | tf_op jit(solution)/shard_map/ppermute | solution.py:279
  504.2 44.9 %collective-permute-start.63 = (f32[128,8,256]{2,1,0:T(8,128)S(1)}, f32[128,8,256]{2,1,0:T(8,128)S(1)}, u32[]{:S(2)}, u32[]{:S(2)}) collective-permute-start(f32[128,8,256]{2,1,0:T(8,128)S(1)} %pad_maximum_fusion.refs_2_), channel_id=1, source_target_pairs={{0,16},{8,24},{16,0},{24,8},{1,17},{9,25},{17,1},{25,9},{2,18},{10... | collective-permute-start | bytes 3145736 | tf_op jit(solution)/shard_map/ppermute | solution.py:267
  526.3 25.9 %collective-permute-start.68 = (f32[128,8,256]{2,1,0:T(8,128)S(1)}, f32[128,8,256]{2,1,0:T(8,128)S(1)}, u32[]{:S(2)}, u32[]{:S(2)}) collective-permute-start(f32[128,8,256]{2,1,0:T(8,128)S(1)} %pad_maximum_fusion.refs_2_), channel_id=1, source_target_pairs={{2,0},{3,1},{4,2},{5,3},{6,4},{7,5},{10,8},{11,9},{12,10},{13,11},... | collective-permute-start | bytes 3145736 | tf_op jit(solution)/shard_map/ppermute | solution.py:273
  533.4 25.9 %collective-permute-start.69 = (f32[128,8,256]{2,1,0:T(8,128)}, f32[128,8,256]{2,1,0:T(8,128)}, u32[]{:S(2)}, u32[]{:S(2)}) collective-permute-start(f32[128,8,256]{2,1,0:T(8,128)} %get-tuple-element.426), channel_id=1, source_target_pairs={{1,3},{3,5},{5,7},{9,11},{11,13},{13,15},{17,19},{19,21},{21,23},{... | collective-permute-start | bytes 3145736 | tf_op jit(solution)/shard_map/ppermute | solution.py:276
  539.2 25.8 %collective-permute-start.71 = (f32[128,8,256]{2,1,0:T(8,128)}, f32[128,8,256]{2,1,0:T(8,128)S(1)}, u32[]{:S(2)}, u32[]{:S(2)}) collective-permute-start(f32[128,8,256]{2,1,0:T(8,128)} %turn.29), channel_id=1, source_target_pairs={{0,1},{1,0},{2,3},{3,2},{4,5},{5,4},{6,7},{7,6},{8,9},{9,8},{10,11... | collective-permute-start | bytes 3145736 | tf_op jit(solution)/shard_map/ppermute | solution.py:279
  559.2 24.8 %collective-permute-start.70 = (f32[128,8,256]{2,1,0:T(8,128)}, f32[128,8,256]{2,1,0:T(8,128)S(1)}, u32[]{:S(2)}, u32[]{:S(2)}) collective-permute-start(f32[128,8,256]{2,1,0:T(8,128)} %get-tuple-element.427), channel_id=1, source_target_pairs={{1,3},{3,5},{5,7},{9,11},{11,13},{13,15},{17,19},{19,21},{21,23},{... | collective-permute-start | bytes 3145736 | tf_op jit(solution)/shard_map/ppermute | solution.py:276
  569.0 25.8 %collective-permute-start.74 = (f32[64,16,256]{2,1,0:T(8,128)}, f32[64,16,256]{2,1,0:T(8,128)S(1)}, u32[]{:S(2)}, u32[]{:S(2)}) collective-permute-start(f32[64,16,256]{2,1,0:T(8,128)} %get-tuple-element.437), channel_id=1, source_target_pairs={{0,8},{8,0},{16,24},{24,16},{1,9},{9,1},{17,25},{25,17},{2,10},{10... | collective-permute-start | bytes 3145736 | tf_op jit(solution)/shard_map/ppermute | solution.py:270
  591.6 25.8 %collective-permute-start.76 = (f32[64,8,256]{2,1,0:T(8,128)}, f32[64,8,256]{2,1,0:T(8,128)S(1)}, u32[]{:S(2)}, u32[]{:S(2)}) collective-permute-start(f32[64,8,256]{2,1,0:T(8,128)} %get-tuple-element.443), channel_id=1, source_target_pairs={{0,8},{8,0},{16,24},{24,16},{1,9},{9,1},{17,25},{25,17},{2,10},{10... | collective-permute-start | bytes 1572872 | tf_op jit(solution)/shard_map/ppermute | solution.py:270
  (100 other events, 1390.8 us)

commit v5 on v4

--- a/solution.py
+++ b/solution.py
@@ -40,15 +40,10 @@
 
 
 def plan(rows, length):
-    n = max(4, min(length // SPAN, rows // 4))
+    n = max(4, rows // 8)
     size = length // n
     chunks = [(s * size, size) for s in range(n)]
-    groups, at = [], 0
-    while at < n:
-        step = 4 if n - at > 4 else max(1, (n - at) // 2)
-        groups.append((at, at + step))
-        at += step
-    return chunks, groups
+    return chunks, [(0, n - 2), (n - 2, n - 1), (n - 1, n)]
 
 
 def spans(*bounds):
@@ -362,10 +357,10 @@
         lo, hi, at, mine, give = part
         parts.append((lo, hi, at, (mine, other_core(gate(give, *after)[0]))))
 
-    first_rows = 3 * n // 16 if n > 8 else n
+    first_rows = 3 if n > 4 else n
     send_part(start_part(0, first_rows, tokens[0]), *far[0], *deep[0])
     waiting = {}
-    later = {0: (first_rows, n // 2), n // 2 - 4: (n // 2, n)} if n > 8 else {}
+    later = {0: (first_rows, n)} if n > 4 else {}
 
     origin = [place, place ^ 1]
     for by in shifts:

time: 629 us -> 586 us (0.932)
  starting transfers between devices: 140 us -> 69.5 us
  waiting for transfers between devices: 162 us -> 224 us
  Pallas kernels: 242 us -> 201 us
  other arithmetic: 15.3 us -> 27.5 us
    ppermute x16 -> x8, waiting for transfers between devices: 56.2 us -> 113 us  [along_cls(): return lax.ppermute(v, 'cls', [(i, (i + by) % n_cls) for i in range(n_cls)])]
    ppermute x16 -> x8, waiting for transfers between devices: 68.6 us -> 28.4 us  [two_down(): return lax.ppermute(v, 'lvl', [(i, i - 2) for i in range(2, n_lvl)])]
    ppermute x16 -> x8, starting transfers between devices: 60.9 us -> 29.9 us  [two_up(): return lax.ppermute(v, 'lvl', [(i, i + 2) for i in range(1, n_lvl - 2, 2)])]
    ppermute x16 -> x8, waiting for transfers between devices: 23.5 us -> 51.6 us  [two_up(): return lax.ppermute(v, 'lvl', [(i, i + 2) for i in range(1, n_lvl - 2, 2)])]
    ppermute x16 -> x8, waiting for transfers between devices: 13.6 us -> 31.4 us  [pair_swap(): return lax.ppermute(v, 'lvl', [(i, i ^ 1) for i in range(n_lvl)])]
    unnamed x174 -> x56, local copies, waits for them, and re-layouts: 24.7 us -> 8.57 us
    ppermute x11 -> x7, starting transfers between devices: 26.6 us -> 11.9 us  [other_core(): return lax.ppermute(v, 'cls', [(i, i ^ 1) for i in range(n_cls)])]
    ppermute x16 -> x8, starting transfers between devices: 33.2 us -> 19.4 us  [two_down(): return lax.ppermute(v, 'lvl', [(i, i - 2) for i in range(2, n_lvl)])]
  transfers between devices with their start and end apart: 77 -> 41, of which waited for: 33 -> 18; matrix products, arithmetic and copies ran while one was open for 7% -> 12% of each run, Pallas kernels for 38% -> 33%
where the time goes in v5:
time: 586 us; the launch traced here: 582 us
  waiting for transfers between devices  224 us (38%)
  Pallas kernels  201 us (34%)
  starting transfers between devices  69.5 us (12%)
  local copies, waits for them, and re-layouts  57.5 us (10%)
  other arithmetic  27.5 us (5%)
    ppermute x8, waiting for transfers between devices, along_cls(): return lax.ppermute(v, 'cls', [(i, (i + by) % n_cls) for i in range(n_cls)])  113 us
    pallas_call x8, Pallas kernels, first_terms(): pl.pallas_call(functools.partial(first_kernel, len(slabs), len(deep)), gr...  71.1 us
    ppermute x8, waiting for transfers between devices, two_up(): return lax.ppermute(v, 'lvl', [(i, i + 2) for i in range(1, n_lvl - 2, 2)])  51.6 us
    pallas_call x2, Pallas kernels, local_terms(): pl.pallas_call(functools.partial(local_kernel, at, mid // 2), grid_spec=p...  40.6 us
    pallas_call x8, Pallas kernels, finish(): pl.pallas_call(functools.partial(finish_kernel, len(alias)), grid_spec=pl...  39.6 us
    pallas_call x8, Pallas kernels, turn(): pl.pallas_call(turn_kernel, grid=(rows // block, size // SPAN), in_specs=...  34.4 us
    ppermute x8, waiting for transfers between devices, pair_swap(): return lax.ppermute(v, 'lvl', [(i, i ^ 1) for i in range(n_lvl)])  31.4 us
    ppermute x8, starting transfers between devices, two_up(): return lax.ppermute(v, 'lvl', [(i, i + 2) for i in range(1, n_lvl - 2, 2)])  29.9 us
  transfers between devices with their start and end apart: 41, of which 18 were waited for; matrix products, arithmetic and copies ran while one was open for 12% of the time, Pallas kernels for 33%

profile of v5, /device:TPU:21, one launch (start us, length us, event | category | flops | bytes accessed | tf_op | source)
XLA Modules:
  0.0 582.1 jit_solution(14165010945734706140)
XLA Ops:
  0.0 7.2 %dynamic-slice_bitcast_fusion.2 = (f32[64,16,256]{2,1,0:T(8,128)}, f32[64,16,256]{2,1,0:T(8,128)S(1)}, f32[64,16,256]{2,1,0:T(8,128)S(1)}, f32[64,16,256]{2,1,0:...) fusion(f32[1,64,256,256]{3,2,1,0:T(8,128)} %param.6, ...), kind=kLoop, calls=%fused_computation.10 | loop fusion | bytes 18874404 | tf_op jit(solution)/shard_map/dynamic_slice | solution.py:277
  10.9 2.2 collective-permute-start.6
  13.4 3.2 dynamic-slice_bitcast_fusion.1
  41.2 17.6 %local_terms.2 = (f32[2,64,48,256]{3,2,1,0:T(8,128)}, f32[2,64,48,256]{3,2,1,0:T(8,128)}) custom-call(s32[2]{0:T(128)} %pad_add_fusion.core._, f32[64]{0:T(128)} %fusion.11.own_rows, f32[64,256,256]{2,1,0:T(8,128)} %bitcast.82, bf16[256,512]{1,0:T(8,128)(2,1)} %get-tuple-element.239.c_hi, bf16[256,512]{1,0:T(8,128)(2,1)} %get-tuple-element.238.c_lo, ...), custom_call_target="tpu_custom_call" | custom-call | flops 1000 | bytes 1000 | tf_op jit(solution)/shard_map/local_terms/pallas_call | solution.py:81
  58.9 6.3 %dynamic-slice_bitcast_fusion = f32[64,96,256]{2,1,0:T(8,128)} fusion(f32[1,64,256,256]{3,2,1,0:T(8,128)} %param.6, s32[]{:T(128)S(6)} %select_n.136), kind=kLoop, calls=%fused_computation | loop fusion | bytes 12582916 | tf_op jit(solution)/shard_map/dynamic_slice | solution.py:277
  83.1 9.0 %first_terms.10 = (f32[128,16,256]{2,1,0:T(8,128)}, f32[128,16,256]{2,1,0:T(8,128)}, f32[128,16,256]{2,1,0:T(8,128)}) custom-call(s32[1]{0:T(128)} %bitcast.2.parity, f32[2,256]{1,0:T(2,128)} %pad_maximum_fusion.14.fall, bf16[512,256]{1,0:T(8,128)(2,1)} %pad_maximum_fusion.12.refs_0_, bf16[256,256]{1,0:T(8,128)(2,1)} %copy-done, ...), custom_call_target="tpu_custom_call" | custom-call | flops 1000 | bytes 1000 | tf_op jit(solution)/shard_map/first_terms/pallas_call | solution.py:149
  92.1 4.9 collective-permute-start.12
  97.0 5.3 fusion.16
  102.5 24.9 %collective-permute-done.3.refs_3_ = f32[128,16,256]{2,1,0:T(8,128)} collective-permute-done((f32[128,16,256]{2,1,0:T(8,128)S(1)}, f32[128,16,256]{2,1,0:T(8,128)}, u32[]{:S(2)}, u32[]{:S(2)}) %collective-permute-start.3) | collective-permute-done | bytes 2097184 | tf_op jit(solution)/shard_map/ppermute | solution.py:262
  132.3 8.9 %first_terms.8 = (f32[128,16,256]{2,1,0:T(8,128)}, f32[128,16,256]{2,1,0:T(8,128)}, f32[128,16,256]{2,1,0:T(8,128)}) custom-call(s32[1]{0:T(128)} %bitcast.2.parity, f32[2,256]{1,0:T(2,128)} %pad_maximum_fusion.14.fall, bf16[512,256]{1,0:T(8,128)(2,1)} %pad_maximum_fusion.12.refs_0_, bf16[256,256]{1,0:T(8,128)(2,1)} %copy-done, f32[128,16,256]{2,1,0:T(8,128)} %copy-done.10, ...), custom_call_target="tpu_custom_call" | custom-call | flops 1000 | bytes 1000 | tf_op jit(solution)/shard_map/first_terms/pallas_call | solution.py:149
  141.8 4.3 collective-permute-start.13
  146.1 4.3 turn.9
  159.0 23.0 %local_terms.3 = (f32[2,64,80,256]{3,2,1,0:T(8,128)}, f32[2,64,80,256]{3,2,1,0:T(8,128)}) custom-call(s32[2]{0:T(128)} %pad_add_fusion.core._, f32[64]{0:T(128)} %fusion.11.own_rows, f32[64,256,256]{2,1,0:T(8,128)} %bitcast.83, bf16[256,512]{1,0:T(8,128)(2,1)} %get-tuple-element.239.c_hi, bf16[256,512]{1,0:T(8,128)(2,1)} %get-tuple-element.238.c_lo, ...), custom_call_target="tpu_custom_call" | custom-call | flops 1000 | bytes 1000 | tf_op jit(solution)/shard_map/local_terms/pallas_call | solution.py:81
  181.9 8.9 %first_terms.9 = (f32[128,16,256]{2,1,0:T(8,128)}, f32[128,16,256]{2,1,0:T(8,128)}, f32[128,16,256]{2,1,0:T(8,128)}) custom-call(s32[1]{0:T(128)} %bitcast.2.parity, f32[2,256]{1,0:T(2,128)} %pad_maximum_fusion.14.fall, bf16[512,256]{1,0:T(8,128)(2,1)} %pad_maximum_fusion.12.refs_0_, bf16[256,256]{1,0:T(8,128)(2,1)} %copy-done, f32[128,16,256]{2,1,0:T(8,128)} %copy-done.6, ...), custom_call_target="tpu_custom_call" | custom-call | flops 1000 | bytes 1000 | tf_op jit(solution)/shard_map/first_terms/pallas_call | solution.py:149
  190.8 4.4 turn.8
  196.2 2.5 collective-permute-start.17
  199.3 2.2 collective-permute-start.16
  201.5 3.5 collective-permute-start.18
  206.7 39.6 %collective-permute-done.5.refs_3_ = f32[128,16,256]{2,1,0:T(8,128)S(1)} collective-permute-done((f32[128,16,256]{2,1,0:T(8,128)S(1)}, f32[128,16,256]{2,1,0:T(8,128)S(1)}, u32[]{:S(2)}, u32[]{:S(2)}) %collective-permute-start.5) | collective-permute-done | bytes 2097184 | tf_op jit(solution)/shard_map/ppermute | solution.py:262
  248.5 2.2 collective-permute-start.21
  250.8 8.9 %first_terms.11 = (f32[128,16,256]{2,1,0:T(8,128)}, f32[128,16,256]{2,1,0:T(8,128)}, f32[128,16,256]{2,1,0:T(8,128)}) custom-call(s32[1]{0:T(128)} %bitcast.2.parity, f32[2,256]{1,0:T(2,128)} %pad_maximum_fusion.14.fall, bf16[512,256]{1,0:T(8,128)(2,1)} %pad_maximum_fusion.12.refs_0_, bf16[256,256]{1,0:T(8,128)(2,1)} %copy-done, f32[128,16,256]{2,1,0:T(8,128)} %copy-done.9, ...), custom_call_target="tpu_custom_call" | custom-call | flops 1000 | bytes 1000 | tf_op jit(solution)/shard_map/first_terms/pallas_call | solution.py:149
  259.7 4.4 collective-permute-start.22
  264.1 4.3 turn.10
  268.5 2.4 pad_maximum_fusion.2.refs_2_
  270.9 5.0 finish.8
  275.8 5.0 finish.9
  280.8 12.1 %collective-permute-done.15.refs_3_ = f32[128,16,256]{2,1,0:T(8,128)} collective-permute-done((f32[128,16,256]{2,1,0:T(8,128)}, f32[128,16,256]{2,1,0:T(8,128)}, u32[]{:S(2)}, u32[]{:S(2)}) %collective-permute-start.15) | collective-permute-done | bytes 2097184 | tf_op jit(solution)/shard_map/ppermute | solution.py:262
  293.2 3.7 collective-permute-done.21.refs_4_
  296.9 2.6 collective-permute-start.25
  299.5 8.9 %first_terms.12 = (f32[128,16,256]{2,1,0:T(8,128)}, f32[128,16,256]{2,1,0:T(8,128)}, f32[128,16,256]{2,1,0:T(8,128)}) custom-call(s32[1]{0:T(128)} %bitcast.2.parity, f32[2,256]{1,0:T(2,128)} %pad_maximum_fusion.14.fall, bf16[512,256]{1,0:T(8,128)(2,1)} %pad_maximum_fusion.12.refs_0_, bf16[256,256]{1,0:T(8,128)(2,1)} %copy-done, ...), custom_call_target="tpu_custom_call" | custom-call | flops 1000 | bytes 1000 | tf_op jit(solution)/shard_map/first_terms/pallas_call | solution.py:149
  308.4 4.0 collective-permute-start.26
  312.3 4.3 turn.11
  316.7 3.8 pad_maximum_fusion.1.refs_2_
  320.4 4.9 finish.10
  325.3 13.2 %collective-permute-done.20.refs_3_ = f32[128,16,256]{2,1,0:T(8,128)} collective-permute-done((f32[128,16,256]{2,1,0:T(8,128)S(1)}, f32[128,16,256]{2,1,0:T(8,128)}, u32[]{:S(2)}, u32[]{:S(2)}) %collective-permute-start.20) | collective-permute-done | bytes 2097184 | tf_op jit(solution)/shard_map/ppermute | solution.py:262
  338.7 5.4 collective-permute-done.25.refs_4_
  344.1 3.0 collective-permute-start.29
  347.1 8.8 %first_terms.13 = (f32[128,16,256]{2,1,0:T(8,128)}, f32[128,16,256]{2,1,0:T(8,128)}, f32[128,16,256]{2,1,0:T(8,128)}) custom-call(s32[1]{0:T(128)} %bitcast.2.parity, f32[2,256]{1,0:T(2,128)} %pad_maximum_fusion.14.fall, bf16[512,256]{1,0:T(8,128)(2,1)} %pad_maximum_fusion.12.refs_0_, bf16[256,256]{1,0:T(8,128)(2,1)} %copy-done, f32[128,16,256]{2,1,0:T(8,128)} %copy-done.7, ...), custom_call_target="tpu_custom_call" | custom-call | flops 1000 | bytes 1000 | tf_op jit(solution)/shard_map/first_terms/pallas_call | solution.py:149
  355.9 3.6 collective-permute-start.30
  359.5 4.3 turn.12
  363.9 2.1 pad_maximum_fusion.refs_2_
  366.0 4.9 finish.11
  371.0 12.3 %collective-permute-done.24.refs_3_ = f32[128,16,256]{2,1,0:T(8,128)} collective-permute-done((f32[128,16,256]{2,1,0:T(8,128)}, f32[128,16,256]{2,1,0:T(8,128)}, u32[]{:S(2)}, u32[]{:S(2)}) %collective-permute-start.24) | collective-permute-done | bytes 2097184 | tf_op jit(solution)/shard_map/ppermute | solution.py:262
  383.6 7.0 %collective-permute-done.29.refs_4_ = f32[128,16,256]{2,1,0:T(8,128)} collective-permute-done((f32[128,16,256]{2,1,0:T(8,128)}, f32[128,16,256]{2,1,0:T(8,128)}, u32[]{:S(2)}, u32[]{:S(2)}) %collective-permute-start.29) | collective-permute-done | bytes 2097184 | tf_op jit(solution)/shard_map/ppermute | solution.py:268
  390.6 3.3 collective-permute-start.32
  394.0 8.9 %first_terms.14 = (f32[128,16,256]{2,1,0:T(8,128)}, f32[128,16,256]{2,1,0:T(8,128)}, f32[128,16,256]{2,1,0:T(8,128)}) custom-call(s32[1]{0:T(128)} %bitcast.2.parity, f32[2,256]{1,0:T(2,128)} %pad_maximum_fusion.14.fall, bf16[512,256]{1,0:T(8,128)(2,1)} %pad_maximum_fusion.12.refs_0_, bf16[256,256]{1,0:T(8,128)(2,1)} %copy-done, ...), custom_call_target="tpu_custom_call" | custom-call | flops 1000 | bytes 1000 | tf_op jit(solution)/shard_map/first_terms/pallas_call | solution.py:149
  402.8 3.4 collective-permute-start.33
  406.3 4.3 turn.13
  411.9 5.0 finish.12
  416.9 10.6 %collective-permute-done.28.refs_3_ = f32[128,16,256]{2,1,0:T(8,128)} collective-permute-done((f32[128,16,256]{2,1,0:T(8,128)S(1)}, f32[128,16,256]{2,1,0:T(8,128)}, u32[]{:S(2)}, u32[]{:S(2)}) %collective-permute-start.28) | collective-permute-done | bytes 2097184 | tf_op jit(solution)/shard_map/ppermute | solution.py:262
  427.4 8.6 %collective-permute-done.32.refs_4_ = f32[128,16,256]{2,1,0:T(8,128)} collective-permute-done((f32[128,16,256]{2,1,0:T(8,128)S(1)}, f32[128,16,256]{2,1,0:T(8,128)}, u32[]{:S(2)}, u32[]{:S(2)}) %collective-permute-start.32) | collective-permute-done | bytes 2097184 | tf_op jit(solution)/shard_map/ppermute | solution.py:268
  436.0 8.8 %first_terms.15 = (f32[128,16,256]{2,1,0:T(8,128)}, f32[128,16,256]{2,1,0:T(8,128)}, f32[128,16,256]{2,1,0:T(8,128)}) custom-call(s32[1]{0:T(128)} %bitcast.2.parity, f32[2,256]{1,0:T(2,128)} %pad_maximum_fusion.14.fall, bf16[512,256]{1,0:T(8,128)(2,1)} %pad_maximum_fusion.12.refs_0_, bf16[256,256]{1,0:T(8,128)(2,1)} %copy-done, f32[128,16,256]{2,1,0:T(8,128)} %copy-done.8, ...), custom_call_target="tpu_custom_call" | custom-call | flops 1000 | bytes 1000 | tf_op jit(solution)/shard_map/first_terms/pallas_call | solution.py:149
  444.8 3.7 collective-permute-done.33.lifted
  448.5 4.3 turn.15
  455.0 5.0 finish.13
  460.0 5.2 collective-permute-start.38
  467.3 47.3 %collective-permute-done.34.lifted = f32[128,16,256]{2,1,0:T(8,128)S(1)} collective-permute-done((f32[128,16,256]{2,1,0:T(8,128)}, f32[128,16,256]{2,1,0:T(8,128)S(1)}, u32[]{:S(2)}, u32[]{:S(2)}) %collective-permute-start.34) | collective-permute-done | bytes 2097184 | tf_op jit(solution)/shard_map/ppermute | solution.py:271
  516.0 4.2 turn.14
  521.6 4.9 finish.14
  527.3 9.9 %put.3.refs_4_ = f32[64,256,256]{2,1,0:T(8,128)} custom-call(s32[2]{0:T(128)} %pad_add_fusion.core._, f32[64,96,256]{2,1,0:T(8,128)} %collective-permute-done.38.piece, f32[64,256,256]{2,1,0:T(8,128)} %get-tuple-element.209._), custom_call_target="tpu_custom_call", output_to_operand_aliasing={{}: (2, {})} | custom-call | flops 1000 | bytes 1000 | tf_op jit(solution)/shard_map/put/pallas_call | solution.py:230
  537.2 29.6 %collective-permute-done.37.refs_1_.refs_3_ = f32[128,16,256]{2,1,0:T(8,128)S(1)} collective-permute-done((f32[128,16,256]{2,1,0:T(8,128)}, f32[128,16,256]{2,1,0:T(8,128)S(1)}, u32[]{:S(2)}, u32[]{:S(2)}) %collective-permute-start.37) | collective-permute-done | bytes 2097184 | tf_op jit(solution)/shard_map/ppermute | solution.py:274
  568.2 4.9 finish.15
  575.7 2.7 put.4._
  579.4 2.7 put.5
  (161 shorter events, 79.3 us)
Async XLA Ops:
  7.2 51.7 %collective-permute-start.9 = (f32[64,16,256]{2,1,0:T(8,128)}, f32[64,16,256]{2,1,0:T(8,128)}, u32[]{:S(2)}, u32[]{:S(2)}) collective-permute-start(f32[64,16,256]{2,1,0:T(8,128)} %get-tuple-element.213), channel_id=1, source_target_pairs={{0,24},{8,16},{16,8},{24,0},{1,25},{9,17},{17,9},{25,1},{2,26},{10... | collective-permute-start | bytes 3145736 | tf_op jit(solution)/shard_map/ppermute | solution.py:303
  8.9 49.9 %collective-permute-start.7 = (f32[64,16,256]{2,1,0:T(8,128)}, f32[64,16,256]{2,1,0:T(8,128)}, u32[]{:S(2)}, u32[]{:S(2)}) collective-permute-start(f32[64,16,256]{2,1,0:T(8,128)} %get-tuple-element.213), channel_id=1, source_target_pairs={{2,8},{3,9},{4,10},{5,11},{6,12},{7,13},{10,0},{11,1},{12,2},{13,3... | collective-permute-start | bytes 3145736 | tf_op jit(solution)/shard_map/ppermute | solution.py:306
  10.9 6.9 %copy-start.27 = (s32[2]{0:T(128)S(1)}, s32[2]{0:T(128)}, u32[]{:S(2)}) copy-start(s32[2]{0:T(128)} %param.11) | copy-start | bytes 28
  10.9 7.5 %copy-start.25 = (f32[256]{0:T(256)S(1)}, f32[256]{0:T(256)}, u32[]{:S(2)}) copy-start(f32[256]{0:T(256)} %param.10) | copy-start | bytes 3076
  10.9 12.0 %copy-start.26 = (s32[3,256]{1,0:T(4,128)S(1)}, s32[3,256]{1,0:T(4,128)}, u32[]{:S(2)}) copy-start(s32[3,256]{1,0:T(4,128)} %param.8) | copy-start | bytes 9220
  10.9 47.9 %collective-permute-start.6 = (f32[64,16,256]{2,1,0:T(8,128)S(1)}, f32[64,16,256]{2,1,0:T(8,128)}, u32[]{:S(2)}, u32[]{:S(2)}) collective-permute-start(f32[64,16,256]{2,1,0:T(8,128)S(1)} %get-tuple-element.214), channel_id=1, source_target_pairs={{2,0},{3,1},{4,2},{5,3},{6,4},{7,5},{10,8},{11,9},{12,10},{13,11},... | collective-permute-start | bytes 3145736 | tf_op jit(solution)/shard_map/ppermute | solution.py:268
  13.1 45.7 %collective-permute-start.2 = (f32[64,16,256]{2,1,0:T(8,128)S(1)}, f32[64,16,256]{2,1,0:T(8,128)}, u32[]{:S(2)}, u32[]{:S(2)}) collective-permute-start(f32[64,16,256]{2,1,0:T(8,128)S(1)} %get-tuple-element.214), channel_id=1, source_target_pairs={{0,16},{8,24},{16,0},{24,8},{1,17},{9,25},{17,1},{25,9},{2,18},{10... | collective-permute-start | bytes 3145736 | tf_op jit(solution)/shard_map/ppermute | solution.py:262
  16.6 24.6 %collective-permute-start = (f32[64,32,256]{2,1,0:T(8,128)}, f32[64,32,256]{2,1,0:T(8,128)}, u32[]{:S(2)}, u32[]{:S(2)}) collective-permute-start(f32[64,32,256]{2,1,0:T(8,128)} %dynamic-slice_bitcast_fusion.1), channel_id=1, source_target_pairs={{0,8},{8,0},{16,24},{24,16},{1,9},{9,1},{17,25},{25,17},{2,10},{10... | collective-permute-start | bytes 6291464 | tf_op jit(solution)/shard_map/ppermute | solution.py:265
  58.9 24.3 %collective-permute-start.10 = (f32[2,64,48,256]{3,2,1,0:T(8,128)}, f32[2,64,48,256]{3,2,1,0:T(8,128)}, u32[]{:S(2)}, u32[]{:S(2)}) collective-permute-start(f32[2,64,48,256]{3,2,1,0:T(8,128)} %get-tuple-element.117), channel_id=1, source_target_pairs={{0,8},{8,0},{16,24},{24,16},{1,9},{9,1},{17,25},{25,17},{2,10},{10... | collective-permute-start | bytes 18874376 | tf_op jit(solution)/shard_map/ppermute | solution.py:265
  65.2 31.8 %collective-permute-start.1 = (f32[64,96,256]{2,1,0:T(8,128)}, f32[64,96,256]{2,1,0:T(8,128)}, u32[]{:S(2)}, u32[]{:S(2)}) collective-permute-start(f32[64,96,256]{2,1,0:T(8,128)} %dynamic-slice_bitcast_fusion), channel_id=1, source_target_pairs={{0,8},{8,0},{16,24},{24,16},{1,9},{9,1},{17,25},{25,17},{2,10},{10... | collective-permute-start | bytes 18874376 | tf_op jit(solution)/shard_map/ppermute | solution.py:265
  75.7 2.5 copy-start
  80.0 12.1 %copy-start.10 = (f32[128,16,256]{2,1,0:T(8,128)}, f32[128,16,256]{2,1,0:T(8,128)S(1)}, u32[]{:S(2)}) copy-start(f32[128,16,256]{2,1,0:T(8,128)S(1)} %get-tuple-element.113.refs_2_) | copy-start | bytes 6291460
  80.0 47.3 %collective-permute-start.3 = (f32[128,16,256]{2,1,0:T(8,128)S(1)}, f32[128,16,256]{2,1,0:T(8,128)}, u32[]{:S(2)}, u32[]{:S(2)}) collective-permute-start(f32[128,16,256]{2,1,0:T(8,128)S(1)} %get-tuple-element.113.refs_2_), channel_id=1, source_target_pairs={{0,16},{8,24},{16,0},{24,8},{1,17},{9,25},{17,1},{25,9},{2,18},{10... | collective-permute-start | bytes 6291464 | tf_op jit(solution)/shard_map/ppermute | solution.py:262
  81.2 49.1 %collective-permute-start.8 = (f32[128,16,256]{2,1,0:T(8,128)S(1)}, f32[128,16,256]{2,1,0:T(8,128)}, u32[]{:S(2)}, u32[]{:S(2)}) collective-permute-start(f32[128,16,256]{2,1,0:T(8,128)S(1)} %get-tuple-element.113.refs_2_), channel_id=1, source_target_pairs={{2,0},{3,1},{4,2},{5,3},{6,4},{7,5},{10,8},{11,9},{12,10},{13,11},... | collective-permute-start | bytes 6291464 | tf_op jit(solution)/shard_map/ppermute | solution.py:268
  92.1 10.2 %copy-start.15 = (f32[64,16,256]{2,1,0:T(8,128)S(1)}, f32[64,16,256]{2,1,0:T(8,128)}, u32[]{:S(2)}) copy-start(f32[64,16,256]{2,1,0:T(8,128)} %get-tuple-element.216) | copy-start | bytes 3145732
  92.1 49.7 %collective-permute-start.12 = (f32[128,16,256]{2,1,0:T(8,128)}, f32[128,16,256]{2,1,0:T(8,128)}, u32[]{:S(2)}, u32[]{:S(2)}) collective-permute-start(f32[128,16,256]{2,1,0:T(8,128)} %get-tuple-element.122), channel_id=1, source_target_pairs={{1,3},{3,5},{5,7},{9,11},{11,13},{13,15},{17,19},{19,21},{21,23},{... | collective-permute-start | bytes 6291464 | tf_op jit(solution)/shard_map/ppermute | solution.py:271
  102.5 38.8 %copy-start.6 = (f32[128,16,256]{2,1,0:T(8,128)}, f32[128,16,256]{2,1,0:T(8,128)S(1)}, u32[]{:S(2)}) copy-start(f32[128,16,256]{2,1,0:T(8,128)S(1)} %pad_maximum_fusion.5.refs_2_) | copy-start | bytes 6291460
  127.3 54.6 %collective-permute-start.4 = (f32[128,16,256]{2,1,0:T(8,128)S(1)}, f32[128,16,256]{2,1,0:T(8,128)}, u32[]{:S(2)}, u32[]{:S(2)}) collective-permute-start(f32[128,16,256]{2,1,0:T(8,128)S(1)} %pad_maximum_fusion.5.refs_2_), channel_id=1, source_target_pairs={{0,16},{8,24},{16,0},{24,8},{1,17},{9,25},{17,1},{25,9},{2,18},{10... | collective-permute-start | bytes 6291464 | tf_op jit(solution)/shard_map/ppermute | solution.py:262
  130.3 51.6 %collective-permute-start.11 = (f32[128,16,256]{2,1,0:T(8,128)S(1)}, f32[128,16,256]{2,1,0:T(8,128)}, u32[]{:S(2)}, u32[]{:S(2)}) collective-permute-start(f32[128,16,256]{2,1,0:T(8,128)S(1)} %pad_maximum_fusion.5.refs_2_), channel_id=1, source_target_pairs={{2,0},{3,1},{4,2},{5,3},{6,4},{7,5},{10,8},{11,9},{12,10},{13,11},... | collective-permute-start | bytes 6291464 | tf_op jit(solution)/shard_map/ppermute | solution.py:268
  141.8 49.0 %collective-permute-start.13 = (f32[128,16,256]{2,1,0:T(8,128)}, f32[128,16,256]{2,1,0:T(8,128)}, u32[]{:S(2)}, u32[]{:S(2)}) collective-permute-start(f32[128,16,256]{2,1,0:T(8,128)} %get-tuple-element.123), channel_id=1, source_target_pairs={{1,3},{3,5},{5,7},{9,11},{11,13},{13,15},{17,19},{19,21},{21,23},{... | collective-permute-start | bytes 6291464 | tf_op jit(solution)/shard_map/ppermute | solution.py:271
  150.4 45.8 %collective-permute-start.14 = (f32[128,16,256]{2,1,0:T(8,128)}, f32[128,16,256]{2,1,0:T(8,128)}, u32[]{:S(2)}, u32[]{:S(2)}) collective-permute-start(f32[128,16,256]{2,1,0:T(8,128)} %turn.9), channel_id=1, source_target_pairs={{0,1},{1,0},{2,3},{3,2},{4,5},{5,4},{6,7},{7,6},{8,9},{9,8},{10,11... | collective-permute-start | bytes 6291464 | tf_op jit(solution)/shard_map/ppermute | solution.py:274
  190.8 7.9 %copy-start.14 = (f32[64,16,256]{2,1,0:T(8,128)S(1)}, f32[64,16,256]{2,1,0:T(8,128)}, u32[]{:S(2)}) copy-start(f32[64,16,256]{2,1,0:T(8,128)} %get-tuple-element.217) | copy-start | bytes 3145732
  190.8 7.9 %copy-start.17 = (f32[64,16,256]{2,1,0:T(8,128)S(1)}, f32[64,16,256]{2,1,0:T(8,128)}, u32[]{:S(2)}) copy-start(f32[64,16,256]{2,1,0:T(8,128)} %get-tuple-element.223) | copy-start | bytes 3145732
  196.2 54.5 %collective-permute-start.17 = (f32[2,64,80,256]{3,2,1,0:T(8,128)}, f32[2,64,80,256]{3,2,1,0:T(8,128)}, u32[]{:S(2)}, u32[]{:S(2)}) collective-permute-start(f32[2,64,80,256]{3,2,1,0:T(8,128)} %get-tuple-element.135), channel_id=1, source_target_pairs={{0,8},{8,0},{16,24},{24,16},{1,9},{9,1},{17,25},{25,17},{2,10},{10... | collective-permute-start | bytes 31457288 | tf_op jit(solution)/shard_map/ppermute | solution.py:265
  198.8 6.3 %copy-start.13 = (f32[64,16,256]{2,1,0:T(8,128)S(1)}, f32[64,16,256]{2,1,0:T(8,128)}, u32[]{:S(2)}) copy-start(f32[64,16,256]{2,1,0:T(8,128)} %get-tuple-element.218) | copy-start | bytes 3145732
  198.8 6.3 %copy-start.16 = (f32[64,16,256]{2,1,0:T(8,128)S(1)}, f32[64,16,256]{2,1,0:T(8,128)}, u32[]{:S(2)}) copy-start(f32[64,16,256]{2,1,0:T(8,128)} %get-tuple-element.224) | copy-start | bytes 3145732
  199.0 7.7 %copy-start.9 = (f32[128,16,256]{2,1,0:T(8,128)}, f32[128,16,256]{2,1,0:T(8,128)S(1)}, u32[]{:S(2)}) copy-start(f32[128,16,256]{2,1,0:T(8,128)S(1)} %pad_maximum_fusion.4.refs_2_) | copy-start | bytes 6291460
  199.0 47.3 %collective-permute-start.5 = (f32[128,16,256]{2,1,0:T(8,128)S(1)}, f32[128,16,256]{2,1,0:T(8,128)S(1)}, u32[]{:S(2)}, u32[]{:S(2)}) collective-permute-start(f32[128,16,256]{2,1,0:T(8,128)S(1)} %pad_maximum_fusion.4.refs_2_), channel_id=1, source_target_pairs={{0,16},{8,24},{16,0},{24,8},{1,17},{9,25},{17,1},{25,9},{2,18},{10... | collective-permute-start | bytes 6291464 | tf_op jit(solution)/shard_map/ppermute | solution.py:262
  199.3 49.2 %collective-permute-start.16 = (f32[128,16,256]{2,1,0:T(8,128)S(1)}, f32[128,16,256]{2,1,0:T(8,128)S(1)}, u32[]{:S(2)}, u32[]{:S(2)}) collective-permute-start(f32[128,16,256]{2,1,0:T(8,128)S(1)} %pad_maximum_fusion.4.refs_2_), channel_id=1, source_target_pairs={{2,0},{3,1},{4,2},{5,3},{6,4},{7,5},{10,8},{11,9},{12,10},{13,11},... | collective-permute-start | bytes 6291464 | tf_op jit(solution)/shard_map/ppermute | solution.py:268
  201.5 58.2 %collective-permute-start.18 = (f32[128,16,256]{2,1,0:T(8,128)}, f32[128,16,256]{2,1,0:T(8,128)S(1)}, u32[]{:S(2)}, u32[]{:S(2)}) collective-permute-start(f32[128,16,256]{2,1,0:T(8,128)} %get-tuple-element.137), channel_id=1, source_target_pairs={{1,3},{3,5},{5,7},{9,11},{11,13},{13,15},{17,19},{19,21},{21,23},{... | collective-permute-start | bytes 6291464 | tf_op jit(solution)/shard_map/ppermute | solution.py:271
  205.0 63.4 %collective-permute-start.19 = (f32[128,16,256]{2,1,0:T(8,128)}, f32[128,16,256]{2,1,0:T(8,128)S(1)}, u32[]{:S(2)}, u32[]{:S(2)}) collective-permute-start(f32[128,16,256]{2,1,0:T(8,128)} %turn.8), channel_id=1, source_target_pairs={{0,1},{1,0},{2,3},{3,2},{4,5},{5,4},{6,7},{7,6},{8,9},{9,8},{10,11... | collective-permute-start | bytes 6291464 | tf_op jit(solution)/shard_map/ppermute | solution.py:274
  246.3 2.2 copy-start.19
  246.3 46.7 %collective-permute-start.15 = (f32[128,16,256]{2,1,0:T(8,128)}, f32[128,16,256]{2,1,0:T(8,128)}, u32[]{:S(2)}, u32[]{:S(2)}) collective-permute-start(f32[128,16,256]{2,1,0:T(8,128)} %pad_maximum_fusion.3.refs_2_), channel_id=1, source_target_pairs={{0,16},{8,24},{16,0},{24,8},{1,17},{9,25},{17,1},{25,9},{2,18},{10... | collective-permute-start | bytes 6291464 | tf_op jit(solution)/shard_map/ppermute | solution.py:262
  248.5 2.2 copy-start.20
  248.5 48.4 %collective-permute-start.21 = (f32[128,16,256]{2,1,0:T(8,128)}, f32[128,16,256]{2,1,0:T(8,128)}, u32[]{:S(2)}, u32[]{:S(2)}) collective-permute-start(f32[128,16,256]{2,1,0:T(8,128)} %pad_maximum_fusion.3.refs_2_), channel_id=1, source_target_pairs={{2,0},{3,1},{4,2},{5,3},{6,4},{7,5},{10,8},{11,9},{12,10},{13,11},... | collective-permute-start | bytes 6291464 | tf_op jit(solution)/shard_map/ppermute | solution.py:268
  259.7 4.4 copy-start.18
  259.7 48.7 %collective-permute-start.22 = (f32[128,16,256]{2,1,0:T(8,128)}, f32[128,16,256]{2,1,0:T(8,128)}, u32[]{:S(2)}, u32[]{:S(2)}) collective-permute-start(f32[128,16,256]{2,1,0:T(8,128)} %get-tuple-element.152), channel_id=1, source_target_pairs={{1,3},{3,5},{5,7},{9,11},{11,13},{13,15},{17,19},{19,21},{21,23},{... | collective-permute-start | bytes 6291464 | tf_op jit(solution)/shard_map/ppermute | solution.py:271
  268.4 2.5 copy-start.2
  268.4 48.2 %collective-permute-start.23 = (f32[128,16,256]{2,1,0:T(8,128)}, f32[128,16,256]{2,1,0:T(8,128)S(1)}, u32[]{:S(2)}, u32[]{:S(2)}) collective-permute-start(f32[128,16,256]{2,1,0:T(8,128)} %turn.10), channel_id=1, source_target_pairs={{0,1},{1,0},{2,3},{3,2},{4,5},{5,4},{6,7},{7,6},{8,9},{9,8},{10,11... | collective-permute-start | bytes 6291464 | tf_op jit(solution)/shard_map/ppermute | solution.py:274
  270.9 26.0 %copy-start.7 = (f32[128,16,256]{2,1,0:T(8,128)}, f32[128,16,256]{2,1,0:T(8,128)S(1)}, u32[]{:S(2)}) copy-start(f32[128,16,256]{2,1,0:T(8,128)S(1)} %pad_maximum_fusion.2.refs_2_) | copy-start | bytes 6291460
  292.9 45.5 %collective-permute-start.20 = (f32[128,16,256]{2,1,0:T(8,128)S(1)}, f32[128,16,256]{2,1,0:T(8,128)}, u32[]{:S(2)}, u32[]{:S(2)}) collective-permute-start(f32[128,16,256]{2,1,0:T(8,128)S(1)} %pad_maximum_fusion.2.refs_2_), channel_id=1, source_target_pairs={{0,16},{8,24},{16,0},{24,8},{1,17},{9,25},{17,1},{25,9},{2,18},{10... | collective-permute-start | bytes 6291464 | tf_op jit(solution)/shard_map/ppermute | solution.py:262
  296.9 47.2 %collective-permute-start.25 = (f32[128,16,256]{2,1,0:T(8,128)S(1)}, f32[128,16,256]{2,1,0:T(8,128)}, u32[]{:S(2)}, u32[]{:S(2)}) collective-permute-start(f32[128,16,256]{2,1,0:T(8,128)S(1)} %pad_maximum_fusion.2.refs_2_), channel_id=1, source_target_pairs={{2,0},{3,1},{4,2},{5,3},{6,4},{7,5},{10,8},{11,9},{12,10},{13,11},... | collective-permute-start | bytes 6291464 | tf_op jit(solution)/shard_map/ppermute | solution.py:268
  308.4 47.6 %collective-permute-start.26 = (f32[128,16,256]{2,1,0:T(8,128)}, f32[128,16,256]{2,1,0:T(8,128)}, u32[]{:S(2)}, u32[]{:S(2)}) collective-permute-start(f32[128,16,256]{2,1,0:T(8,128)} %get-tuple-element.166), channel_id=1, source_target_pairs={{1,3},{3,5},{5,7},{9,11},{11,13},{13,15},{17,19},{19,21},{21,23},{... | collective-permute-start | bytes 6291464 | tf_op jit(solution)/shard_map/ppermute | solution.py:271
  316.6 3.8 copy-start.1
  316.6 47.2 %collective-permute-start.27 = (f32[128,16,256]{2,1,0:T(8,128)}, f32[128,16,256]{2,1,0:T(8,128)S(1)}, u32[]{:S(2)}, u32[]{:S(2)}) collective-permute-start(f32[128,16,256]{2,1,0:T(8,128)} %turn.11), channel_id=1, source_target_pairs={{0,1},{1,0},{2,3},{3,2},{4,5},{5,4},{6,7},{7,6},{8,9},{9,8},{10,11... | collective-permute-start | bytes 6291464 | tf_op jit(solution)/shard_map/ppermute | solution.py:274
  338.5 44.8 %collective-permute-start.24 = (f32[128,16,256]{2,1,0:T(8,128)}, f32[128,16,256]{2,1,0:T(8,128)}, u32[]{:S(2)}, u32[]{:S(2)}) collective-permute-start(f32[128,16,256]{2,1,0:T(8,128)} %pad_maximum_fusion.1.refs_2_), channel_id=1, source_target_pairs={{0,16},{8,24},{16,0},{24,8},{1,17},{9,25},{17,1},{25,9},{2,18},{10... | collective-permute-start | bytes 6291464 | tf_op jit(solution)/shard_map/ppermute | solution.py:262
  344.1 46.5 %collective-permute-start.29 = (f32[128,16,256]{2,1,0:T(8,128)}, f32[128,16,256]{2,1,0:T(8,128)}, u32[]{:S(2)}, u32[]{:S(2)}) collective-permute-start(f32[128,16,256]{2,1,0:T(8,128)} %pad_maximum_fusion.1.refs_2_), channel_id=1, source_target_pairs={{2,0},{3,1},{4,2},{5,3},{6,4},{7,5},{10,8},{11,9},{12,10},{13,11},... | collective-permute-start | bytes 6291464 | tf_op jit(solution)/shard_map/ppermute | solution.py:268
  355.9 46.9 %collective-permute-start.30 = (f32[128,16,256]{2,1,0:T(8,128)}, f32[128,16,256]{2,1,0:T(8,128)}, u32[]{:S(2)}, u32[]{:S(2)}) collective-permute-start(f32[128,16,256]{2,1,0:T(8,128)} %get-tuple-element.180), channel_id=1, source_target_pairs={{1,3},{3,5},{5,7},{9,11},{11,13},{13,15},{17,19},{19,21},{21,23},{... | collective-permute-start | bytes 6291464 | tf_op jit(solution)/shard_map/ppermute | solution.py:271
  363.9 2.2 copy-start.3
  363.9 46.7 %collective-permute-start.31 = (f32[128,16,256]{2,1,0:T(8,128)}, f32[128,16,256]{2,1,0:T(8,128)S(1)}, u32[]{:S(2)}, u32[]{:S(2)}) collective-permute-start(f32[128,16,256]{2,1,0:T(8,128)} %turn.12), channel_id=1, source_target_pairs={{0,1},{1,0},{2,3},{3,2},{4,5},{5,4},{6,7},{7,6},{8,9},{9,8},{10,11... | collective-permute-start | bytes 6291464 | tf_op jit(solution)/shard_map/ppermute | solution.py:274
  366.0 24.6 %copy-start.8 = (f32[128,16,256]{2,1,0:T(8,128)}, f32[128,16,256]{2,1,0:T(8,128)S(1)}, u32[]{:S(2)}) copy-start(f32[128,16,256]{2,1,0:T(8,128)S(1)} %pad_maximum_fusion.refs_2_) | copy-start | bytes 6291460
  383.3 44.1 %collective-permute-start.28 = (f32[128,16,256]{2,1,0:T(8,128)S(1)}, f32[128,16,256]{2,1,0:T(8,128)}, u32[]{:S(2)}, u32[]{:S(2)}) collective-permute-start(f32[128,16,256]{2,1,0:T(8,128)S(1)} %pad_maximum_fusion.refs_2_), channel_id=1, source_target_pairs={{0,16},{8,24},{16,0},{24,8},{1,17},{9,25},{17,1},{25,9},{2,18},{10... | collective-permute-start | bytes 6291464 | tf_op jit(solution)/shard_map/ppermute | solution.py:262
  390.6 45.4 %collective-permute-start.32 = (f32[128,16,256]{2,1,0:T(8,128)S(1)}, f32[128,16,256]{2,1,0:T(8,128)}, u32[]{:S(2)}, u32[]{:S(2)}) collective-permute-start(f32[128,16,256]{2,1,0:T(8,128)S(1)} %pad_maximum_fusion.refs_2_), channel_id=1, source_target_pairs={{2,0},{3,1},{4,2},{5,3},{6,4},{7,5},{10,8},{11,9},{12,10},{13,11},... | collective-permute-start | bytes 6291464 | tf_op jit(solution)/shard_map/ppermute | solution.py:268
  402.8 45.7 %collective-permute-start.33 = (f32[128,16,256]{2,1,0:T(8,128)}, f32[128,16,256]{2,1,0:T(8,128)}, u32[]{:S(2)}, u32[]{:S(2)}) collective-permute-start(f32[128,16,256]{2,1,0:T(8,128)} %get-tuple-element.194), channel_id=1, source_target_pairs={{1,3},{3,5},{5,7},{9,11},{11,13},{13,15},{17,19},{19,21},{21,23},{... | collective-permute-start | bytes 6291464 | tf_op jit(solution)/shard_map/ppermute | solution.py:271
  410.6 43.1 %collective-permute-start.35 = (f32[128,16,256]{2,1,0:T(8,128)}, f32[128,16,256]{2,1,0:T(8,128)S(1)}, u32[]{:S(2)}, u32[]{:S(2)}) collective-permute-start(f32[128,16,256]{2,1,0:T(8,128)} %turn.13), channel_id=1, source_target_pairs={{0,1},{1,0},{2,3},{3,2},{4,5},{5,4},{6,7},{7,6},{8,9},{9,8},{10,11... | collective-permute-start | bytes 6291464 | tf_op jit(solution)/shard_map/ppermute | solution.py:274
  455.0 12.2 %copy-start.21 = (f32[128,16,256]{2,1,0:T(8,128)S(1)}, f32[128,16,256]{2,1,0:T(8,128)}, u32[]{:S(2)}) copy-start(f32[128,16,256]{2,1,0:T(8,128)} %turn.15) | copy-start | bytes 6291460
  460.0 67.3 %collective-permute-start.38 = (f32[64,96,256]{2,1,0:T(8,128)}, f32[64,96,256]{2,1,0:T(8,128)}, u32[]{:S(2)}, u32[]{:S(2)}) collective-permute-start(f32[64,96,256]{2,1,0:T(8,128)} %get-tuple-element.205), channel_id=1, source_target_pairs={{0,8},{8,0},{16,24},{24,16},{1,9},{9,1},{17,25},{25,17},{2,10},{10... | collective-permute-start | bytes 18874376 | tf_op jit(solution)/shard_map/ppermute | solution.py:265
  465.3 49.3 %collective-permute-start.34 = (f32[128,16,256]{2,1,0:T(8,128)}, f32[128,16,256]{2,1,0:T(8,128)S(1)}, u32[]{:S(2)}, u32[]{:S(2)}) collective-permute-start(f32[128,16,256]{2,1,0:T(8,128)} %get-tuple-element.195), channel_id=1, source_target_pairs={{1,3},{3,5},{5,7},{9,11},{11,13},{13,15},{17,19},{19,21},{21,23},{... | collective-permute-start | bytes 6291464 | tf_op jit(solution)/shard_map/ppermute | solution.py:271
  467.2 53.0 %collective-permute-start.36 = (f32[128,16,256]{2,1,0:T(8,128)S(1)}, f32[128,16,256]{2,1,0:T(8,128)S(1)}, u32[]{:S(2)}, u32[]{:S(2)}) collective-permute-start(f32[128,16,256]{2,1,0:T(8,128)S(1)} %copy-done.21), channel_id=1, source_target_pairs={{0,1},{1,0},{2,3},{3,2},{4,5},{5,4},{6,7},{7,6},{8,9},{9,8},{10,11... | collective-permute-start | bytes 6291464 | tf_op jit(solution)/shard_map/ppermute | solution.py:274
  514.6 1.4 copy-start.22
  520.2 1.4 copy-start.12
  520.2 46.6 %collective-permute-start.37 = (f32[128,16,256]{2,1,0:T(8,128)}, f32[128,16,256]{2,1,0:T(8,128)S(1)}, u32[]{:S(2)}, u32[]{:S(2)}) collective-permute-start(f32[128,16,256]{2,1,0:T(8,128)} %turn.14), channel_id=1, source_target_pairs={{0,1},{1,0},{2,3},{3,2},{4,5},{5,4},{6,7},{7,6},{8,9},{9,8},{10,11... | collective-permute-start | bytes 6291464 | tf_op jit(solution)/shard_map/ppermute | solution.py:274
  526.5 48.3 %collective-permute-start.40 = (f32[64,16,256]{2,1,0:T(8,128)}, f32[64,16,256]{2,1,0:T(8,128)S(1)}, u32[]{:S(2)}, u32[]{:S(2)}) collective-permute-start(f32[64,16,256]{2,1,0:T(8,128)} %get-tuple-element.211), channel_id=1, source_target_pairs={{0,8},{8,0},{16,24},{24,16},{1,9},{9,1},{17,25},{25,17},{2,10},{10... | collective-permute-start | bytes 3145736 | tf_op jit(solution)/shard_map/ppermute | solution.py:265
  573.1 5.4 collective-permute-start.39
  (5 other events, 5.9 us)

commit v6 on v5

--- a/solution.py
+++ b/solution.py
@@ -11,6 +11,7 @@
 BF16 = jnp.bfloat16
 VMEM_LIMIT = 56 * 2**20
 SPAN, LANES = 8, 128
+FIRST_ROWS = 1
 LIGHT = pl.CostEstimate(flops=1000, transcendentals=0, bytes_accessed=1000)
 PARAMS = pltpu.CompilerParams(vmem_limit_bytes=VMEM_LIMIT)
 WHOLE = pl.BlockSpec(memory_space=pltpu.VMEM)
@@ -50,11 +51,93 @@
     return list(zip(bounds[:-1], bounds[1:]))
 
 
-def local_kernel(at, half, core, own_rows, occ, c_hi, c_lo, b_both, row_b, row_c, *outs):
+def prepare_kernel(rows, where, bounds, rates, inc_rows, inc_cols, draw, crusher, a_out, c_hi, c_lo, b_hi, b_lo, lost_a, lost_b,
+                   left_c, fall, flip):
+    level = where[2]
+    top, bottom = bounds[1], bounds[0]
+    phases = rates.shape[1]
+    totals = [jnp.sum(rates[c], axis=1, keepdims=True) for c in range(3)]
+    uniform = jnp.max(crusher[...], axis=1, keepdims=True)
+    for total in totals:
+        uniform = uniform + jnp.max(total, axis=0, keepdims=True)
+    scale = 1.0 / uniform
+    rise_ok = jnp.where(level + 1 <= top, 1.0, 0.0)
+
+    def opened(inc):
+        return jnp.where((inc == 0) | (level + inc <= top), 1.0, 0.0)
+
+    def masks(inc):
+        return [jnp.where(inc == 0, 1.0, 0.0) * scale, jnp.where(inc == 1, 1.0, 0.0) * (rise_ok * scale)]
+
+    lost_a[...] = totals[0] * opened(inc_cols[0]) * scale
+    lost_b[...] = totals[1] * opened(inc_cols[1]) * scale
+    total_c = jnp.sum(jnp.transpose(rates[2]), axis=0, keepdims=True)
+    here = crusher[...] * jnp.where(level - draw[...] >= bottom, 1.0, 0.0)
+    deep = crusher[...] * jnp.where(level + 2 - draw[...] >= bottom, 1.0, 0.0)
+    left_c[...] = 1.0 - total_c * opened(inc_rows[2:3]) * scale - here * scale
+    fall[0:1] = jnp.where(level % 2 == 0, deep, here) * jnp.where(draw[...] == 1, 1.0, 0.0) * scale
+    fall[1:2] = deep * jnp.where(draw[...] == 2, 1.0, 0.0) * scale
+    for n, mask in enumerate(masks(inc_cols[2])):
+        high, low = halves(rates[2] * mask)
+        c_hi[:, n * phases : (n + 1) * phases] = high
+        c_lo[:, n * phases : (n + 1) * phases] = low
+    for n, mask in enumerate(masks(inc_cols[1])):
+        high, low = halves(jnp.transpose(rates[1] * mask))
+        b_hi[n] = high
+        b_lo[n] = low
+    spots = [pl.ds(pl.multiple_of(where[3 + n] * rows, 8), rows) for n in range(phases // rows)]
+    ordered = jnp.concatenate([rates[0, spot] for spot in spots], axis=0)
+    inc = jnp.concatenate([inc_cols[0, spot] for spot in spots], axis=0)
+    for n, mask in enumerate(masks(inc)):
+        flip[...] = jnp.transpose(ordered * mask)
+        for which in range(2):
+            at = (2 * n + which) * rows
+            high, low = halves(flip[spots[which]])
+            a_out[at : at + rows] = high
+            a_out[4 * rows + at : 5 * rows + at] = low
+
+
+def prepare(where, bounds, rates, increments, draw, crusher_rate, rows):
+    phases = rates.shape[1]
+    smem = pl.BlockSpec(memory_space=pltpu.SMEM)
+    shapes = [
+        ((8 * rows, phases), BF16),
+        ((phases, 2 * phases), BF16),
+        ((phases, 2 * phases), BF16),
+        ((2, phases, phases), BF16),
+        ((2, phases, phases), BF16),
+        ((phases, 1), F32),
+        ((phases, 1), F32),
+        ((1, phases), F32),
+        ((2, phases), F32),
+    ]
+    return pl.pallas_call(
+        functools.partial(prepare_kernel, rows),
+        in_specs=[smem, smem] + [WHOLE] * 5,
+        out_specs=[WHOLE] * len(shapes),
+        out_shape=[jax.ShapeDtypeStruct(*v) for v in shapes],
+        scratch_shapes=[pltpu.VMEM((phases, phases), F32)],
+        compiler_params=PARAMS,
+        cost_estimate=LIGHT,
+        name="prepare",
+    )(where, bounds, rates, increments, increments[:, :, None], draw[None], crusher_rate[None])
+
+
+def local_kernel(at, half, where, lost_a, occ, c_hi, c_lo, b_hi, b_lo, lost_b, left_c, mine, peer, b_both, left_b):
     block, phases = occ.shape[0], occ.shape[2]
-    size = outs[0].shape[2]
-    first = pl.program_id(0) * block
-    rows = [pl.ds(pl.multiple_of(core[n] * half + at, SPAN), size) for n in range(2)]
+    size = mine.shape[2]
+    rows = [pl.ds(pl.multiple_of(where[n] * half + at, 16), size) for n in range(2)]
+
+    @pl.when(pl.program_id(0) == 0)
+    def _():
+        for n in range(2):
+            left_b[n * size : (n + 1) * size] = lost_b[rows[n]]
+            for m in range(2):
+                spot = (2 * m + n) * size
+                b_both[spot : spot + size] = b_hi[m, rows[n]]
+                b_both[4 * size + spot : 5 * size + spot] = b_lo[m, rows[n]]
+
+    first = where[3] * (pl.num_programs(0) * block) + pl.program_id(0) * block
     y = jnp.concatenate([occ[i, r] for i in range(block) for r in rows], axis=0)
     y_hi, y_lo = halves(y)
     n_y = y.shape[0]
@@ -65,16 +148,15 @@
         by_b = dot(b_both[...], x_hi)
         by_b = by_b[: 4 * size] + by_b[4 * size :] + dot(b_both[: 4 * size], x_lo)
         here = slice(2 * size * i, 2 * size * (i + 1))
-        left = row_c[...] - own_rows[first + i] - row_b[...]
+        left = left_c[...] - lost_a[pl.ds(first + i, 1)] - left_b[...]
         base = by_c[here, :phases] + by_b[: 2 * size] + y[here] * left
         rise = by_c[here, phases:] + by_b[2 * size :]
-        mine, peer = outs
         for n, value in enumerate((base, rise)):
             mine[n, i] = value[:size]
             peer[n, i] = value[size:]
 
 
-def local_terms(core, occ, own_rows, c_split, b_both, row_b, row_c, at, size):
+def local_terms(where, occ, lost_a, factors, at, size):
     rows, mid, phases = occ.shape
     block = 8
     out = pl.BlockSpec((2, block, size, phases), lambda i, c: (0, i, 0, 0))
@@ -83,25 +165,22 @@
         grid_spec=pltpu.PrefetchScalarGridSpec(
             num_scalar_prefetch=1,
             grid=(rows // block,),
-            in_specs=[
-                pl.BlockSpec(memory_space=pltpu.SMEM),
-                pl.BlockSpec((block, mid, phases), lambda i, c: (i, 0, 0)),
-            ]
-            + [WHOLE] * 5,
+            in_specs=[WHOLE, pl.BlockSpec((block, mid, phases), lambda i, c: (i, 0, 0))] + [WHOLE] * len(factors),
             out_specs=[out] * 2,
+            scratch_shapes=[pltpu.VMEM((8 * size, mid), BF16), pltpu.VMEM((2 * size, 1), F32)],
         ),
         out_shape=[jax.ShapeDtypeStruct((2, rows, size, phases), F32)] * 2,
         compiler_params=PARAMS,
         cost_estimate=LIGHT,
         name="local_terms",
-    )(core, own_rows, occ, *c_split, b_both, row_b, row_c)
-
-
-def first_kernel(n_slabs, n_deep, parity, fall, *refs):
-    w_both, w_hi = refs[0], refs[1]
-    slabs = refs[2 : 2 + n_slabs]
-    deep = refs[2 + n_slabs : 2 + n_slabs + n_deep]
-    mine, peer, stay_out, rise_out, swap_out = refs[2 + n_slabs + n_deep :]
+    )(where, lost_a, occ, *factors)
+
+
+def first_kernel(n_slabs, n_deep, where, fall, *refs):
+    w_both = refs[0]
+    slabs = refs[1 : 1 + n_slabs]
+    deep = refs[1 + n_slabs : 1 + n_slabs + n_deep]
+    mine, peer, stay_out, rise_out, swap_out = refs[1 + n_slabs + n_deep :]
     rows, span, lanes = stay_out.shape
     flat = [ref.reshape(ref.shape[0] * span, lanes) for ref in slabs]
     stay_flat = stay_out.reshape(rows * span, lanes)
@@ -115,7 +194,7 @@
         g_hi = jnp.concatenate([p[0] for p in parts], axis=0)
         g_lo = jnp.concatenate([p[1] for p in parts], axis=0)
         both = dot(w_both[...], g_hi)
-        out = both[: 2 * rows] + both[2 * rows :] + dot(w_hi[...], g_lo)
+        out = both[: 2 * rows] + both[2 * rows :] + dot(w_both[: 2 * rows], g_lo)
         for n, at in enumerate(ats):
             stay_flat[at, :] = out[:rows, n * lanes : (n + 1) * lanes]
             rise_flat[at, :] = out[rows:, n * lanes : (n + 1) * lanes]
@@ -128,11 +207,11 @@
         lift = rise_out[part] + near[1]
         rise_out[part] = lift
 
-        @pl.when(parity[0] == 0)
+        @pl.when(where[2] % 2 == 0)
         def _():
             swap_out[part] = lift + far_down * once
 
-    @pl.when(parity[0] != 0)
+    @pl.when(where[2] % 2 != 0)
     def _():
         at = 0
         for ref in slabs:
@@ -141,7 +220,7 @@
             at += ref.shape[0]
 
 
-def first_terms(parity, fall, w_both, w_hi, slabs, deep, near, start):
+def first_terms(where, fall, w_both, slabs, deep, near, start):
     rows, size, phases = slabs[0].shape
     slab_specs = [pl.BlockSpec((v.shape[0], SPAN, LANES), lambda j, h: (0, j, h)) for v in [*slabs, *deep]]
     chunk = pl.BlockSpec((rows, SPAN, LANES), lambda j, h: (0, j, h))
@@ -149,7 +228,7 @@
     return pl.pallas_call(
         functools.partial(first_kernel, len(slabs), len(deep)),
         grid=(size // SPAN, phases // LANES),
-        in_specs=[pl.BlockSpec(memory_space=pltpu.SMEM), pl.BlockSpec((2, LANES), lambda j, h: (0, h)), WHOLE, WHOLE]
+        in_specs=[pl.BlockSpec(memory_space=pltpu.SMEM), pl.BlockSpec((2, LANES), lambda j, h: (0, h)), WHOLE]
         + slab_specs
         + [local_part] * 2,
         out_specs=[chunk] * 3,
@@ -157,7 +236,7 @@
         compiler_params=PARAMS,
         cost_estimate=LIGHT,
         name="first_terms",
-    )(parity, fall, w_both, w_hi, *slabs, *deep, *near)
+    )(where, fall, w_both, *slabs, *deep, *near)
 
 
 def turn_kernel(swap, lifted, out):
@@ -254,9 +333,11 @@
     level = lax.axis_index("lvl")
     place = lax.axis_index("cls")
     k = place % 2
-    core = jnp.stack([k, 1 - k])
-    even = level % 2 == 0
-    bottom, top = bounds[0], bounds[1]
+    core = (k, 1 - k)
+    origin = [place, place ^ 1]
+    for by in range(2, n_cls, 2):
+        origin += [(place - by) % n_cls, ((place - by) % n_cls) ^ 1]
+    where = jnp.stack([*core, level, *origin])
 
     def along_cls(v, by):
         return lax.ppermute(v, "cls", [(i, (i + by) % n_cls) for i in range(n_cls)])
@@ -315,67 +396,26 @@
 
     start_early(0)
 
-    row_total = jnp.sum(rates, axis=2)
-    uniform_rate = jnp.sum(jnp.max(row_total, axis=1)) + jnp.max(crusher_rate)
-    out_rows = row_total * flag((increments == 0) | (level + increments <= top))
-    rise_ok = flag(level + 1 <= top)
-    drop_here = crusher_rate * flag(level - draw >= bottom)
-    drop_deep = crusher_rate * flag(level + 2 - draw >= bottom)
-    scale = 1.0 / uniform_rate
-    once = jnp.where(even, drop_deep, drop_here) * flag(draw == 1) * scale
-    twice = drop_deep * flag(draw == 2) * scale
-    fall_vec = jnp.stack([once, twice])
-    parity = (level % 2)[None]
-
-    stay_rows = rates * (flag(increments == 0) * scale)[:, :, None]
-    rise_rows = rates * (flag(increments == 1) * (rise_ok * scale))[:, :, None]
-
-    c_split = halves_outside(jnp.concatenate([stay_rows[2], rise_rows[2]], axis=1))
-    lost = out_rows * scale
-    own_rows = lax.dynamic_slice_in_dim(lost[0], place * rows, rows)
-    row_c = (1.0 - lost[2] - drop_here * scale)[None, :]
+    a_both, *factors = prepare(where, bounds, rates, increments, draw, crusher_rate, rows)
+    *factors, fall_vec = factors
+    lost_a = factors.pop(4)
+
     parts = []
 
     def start_part(lo, hi, begin):
         at, span = chunks[lo][0], (hi - lo) * size
-        cat_b = jnp.concatenate([cut(r, w, at, span) for r in (stay_rows[1], rise_rows[1]) for w in range(2)], axis=1)
-        row_b = jnp.concatenate([lax.dynamic_slice_in_dim(lost[1], core[w] * half + at, span) for w in range(2)])
-        mine, give = local_terms(
-            core,
-            gate(occ, begin)[0],
-            own_rows,
-            c_split,
-            jnp.concatenate(halves_outside(cat_b.T), axis=0),
-            row_b[:, None],
-            row_c,
-            at,
-            span,
-        )
+        mine, give = local_terms(where, gate(occ, begin)[0], lost_a, factors, at, span)
         return lo, hi, at, mine, give
 
     def send_part(part, *after):
         lo, hi, at, mine, give = part
         parts.append((lo, hi, at, (mine, other_core(gate(give, *after)[0]))))
 
-    first_rows = 3 if n > 4 else n
-    send_part(start_part(0, first_rows, tokens[0]), *far[0], *deep[0])
-    waiting = {}
-    later = {0: (first_rows, n)} if n > 4 else {}
-
-    origin = [place, place ^ 1]
-    for by in shifts:
-        origin += [(place - by) % n_cls, ((place - by) % n_cls) ^ 1]
-    mine = jnp.concatenate(
-        [
-            lax.dynamic_slice_in_dim(r, p * rows, rows, axis=1)
-            for r in (stay_rows[0], rise_rows[0])
-            for p in (place, place ^ 1)
-        ],
-        axis=1,
-    ).T
-    mine = jnp.concatenate([lax.dynamic_slice_in_dim(mine, o * rows, rows, axis=1) for o in origin], axis=1)
-    a_hi, a_lo = halves_outside(mine)
-    a_both = jnp.concatenate([a_hi, a_lo], axis=0)
+    part = start_part(0, FIRST_ROWS, tokens[0])
+    rest = start_part(FIRST_ROWS, n, part[3])
+    far[0][0], _ = gate(far[0][0], rest[3])
+    send_part(part, *far[0], *deep[0])
+    send_part(rest, parts[0][3][1])
 
     out = None
     stay, rise, swap, lifted, risen = ([None] * n for _ in range(5))
@@ -390,11 +430,13 @@
                 far[s][0], out = gate(far[s][0], out)
             if s + 1 < n:
                 start_far(s + 1, far[s][0])
-            if s + 1 < n:
-                start_deep(s + 1, far[s][0], *deep[s])
+            if s == 0:
+                start_deep(1, far[0][0])
+            if s + 2 < n:
+                start_deep(s + 2, *deep[s])
             lo, hi, at, near = next(p for p in parts if p[0] <= s < p[1])
             stay[s], rise[s], swap[s] = first_terms(
-                parity, fall_vec, a_both, a_hi, [sent[s]] + far[s], deep[s], near, chunks[s][0] - at
+                where, fall_vec, a_both, [sent[s]] + far[s], deep[s], near, chunks[s][0] - at
             )
             lift_me = rise[s]
             if s >= 1:
@@ -403,19 +445,15 @@
         if 1 <= s <= n:
             p = s - 1
             swap_me = turn(swap[p], lifted[p])
-            if p in later:
-                waiting[p + 2] = start_part(*later[p], swap_me)
             if p >= 1:
                 swap_me, risen[p - 1] = gate(swap_me, risen[p - 1])
             risen[p] = pair_swap(swap_me)
-            if s in waiting:
-                send_part(waiting[s], *far[s], *deep[s], lifted[p], risen[p - 1])
         if 0 <= s - 2 < n:
             p = s - 2
             g = group_of[p]
             lo, hi = groups[g]
             out, back[g] = finish(
-                core, out, back[g], occ.shape, (hi - lo) * size, stay[p], risen[p], chunks[p][0], (p - lo) * size
+                where, out, back[g], occ.shape, (hi - lo) * size, stay[p], risen[p], chunks[p][0], (p - lo) * size
             )
             if p == hi - 1:
                 back[g] = other_core(back[g])
@@ -423,7 +461,7 @@
             p = s - 3
             lo, hi = groups[group_of[p]]
             if p == hi - 1:
-                out = put(core, out, back[group_of[p]], chunks[lo][0])
+                out = put(where, out, back[group_of[p]], chunks[lo][0])
     return out[None]
 
 

time: 586 us -> 555 us (0.947)
  local copies, waits for them, and re-layouts: 57.5 us -> 33.5 us
  other arithmetic: 27.5 us -> 16.9 us
    ppermute x8, waiting for transfers between devices: 51.6 us -> 112 us  [two_up(): return lax.ppermute(v, 'lvl', [(i, i + 2) for i in range(1, n_lvl - 2, 2)])]
    ppermute x8, waiting for transfers between devices: 113 us -> 71 us  [along_cls(): return lax.ppermute(v, 'cls', [(i, (i + by) % n_cls) for i in range(n_cls)])]
    ppermute x8, waiting for transfers between devices: 28.4 us -> 3.22 us  [two_down(): return lax.ppermute(v, 'lvl', [(i, i - 2) for i in range(2, n_lvl)])]
    dynamic_slice x15 -> x3, local copies, waits for them, and re-layouts: 29.6 us -> 16.5 us  [cut(): lax.dynamic_slice_in_dim(array, core[which] * half + at, size, axis=1)]
    dynamic_slice x10 -> x0, local copies, waits for them, and re-layouts: 9.13 us -> none  [the longest x6 8.12 us: local(): lax.dynamic_slice_in_dim(r, p * rows, rows, axis=1)]
    ppermute x7, waiting for transfers between devices: 0.02 us -> 7.41 us  [other_core(): return lax.ppermute(v, 'cls', [(i, i ^ 1) for i in range(n_cls)])]
    concatenate x7 -> x8, other arithmetic: 11.9 us -> 16.9 us  [local(): sent[s] = jnp.concatenate([cut(occ, 0, start, size), part], axis=0)]
  transfers between devices with their start and end apart: 41 -> 41, of which waited for: 18 -> 21; matrix products, arithmetic and copies ran while one was open for 12% -> 7% of each run, Pallas kernels for 33% -> 36%
where the time goes in v6:
time: 555 us; the launch traced here: 552 us
  waiting for transfers between devices  225 us (41%)
  Pallas kernels  205 us (37%)
  starting transfers between devices  71 us (13%)
  local copies, waits for them, and re-layouts  33.5 us (6%)
  other arithmetic  16.9 us (3%)
    ppermute x8, waiting for transfers between devices, two_up(): return lax.ppermute(v, 'lvl', [(i, i + 2) for i in range(1, n_lvl - 2, 2)])  112 us
    pallas_call x8, Pallas kernels, first_terms(): pl.pallas_call(functools.partial(first_kernel, len(slabs), len(deep)), gr...  71.3 us
    ppermute x8, waiting for transfers between devices, along_cls(): return lax.ppermute(v, 'cls', [(i, (i + by) % n_cls) for i in range(n_cls)])  71 us
    pallas_call x2, Pallas kernels, local_terms(): pl.pallas_call(functools.partial(local_kernel, at, mid // 2), grid_spec=p...  42 us
    pallas_call x8, Pallas kernels, finish(): pl.pallas_call(functools.partial(finish_kernel, len(alias)), grid_spec=pl...  39.6 us
    pallas_call x8, Pallas kernels, turn(): pl.pallas_call(turn_kernel, grid=(rows // block, size // SPAN), in_specs=...  34.1 us
    ppermute x8, waiting for transfers between devices, pair_swap(): return lax.ppermute(v, 'lvl', [(i, i ^ 1) for i in range(n_lvl)])  31.6 us
    ppermute x8, starting transfers between devices, two_up(): return lax.ppermute(v, 'lvl', [(i, i + 2) for i in range(1, n_lvl - 2, 2)])  31.4 us
  transfers between devices with their start and end apart: 41, of which 21 were waited for; matrix products, arithmetic and copies ran while one was open for 7% of the time, Pallas kernels for 36%

profile of v6, /device:TPU:21, one launch (start us, length us, event | category | flops | bytes accessed | tf_op | source)
XLA Modules:
  0.0 552.4 jit_solution(15551067082277586084)
XLA Ops:
  0.0 3.2 dynamic-slice_bitcast_fusion.1
  3.8 7.2 %dynamic-slice_bitcast_fusion.2 = (f32[64,16,256]{2,1,0:T(8,128)}, f32[64,16,256]{2,1,0:T(8,128)}, f32[64,16,256]{2,1,0:T(8,128)}, f32[64,16,256]{2,1,0:T(8,128)...) fusion(f32[1,64,256,256]{3,2,1,0:T(8,128)} %param.6, ...), kind=kLoop, calls=%fused_computation.10 | loop fusion | bytes 18874404 | tf_op jit(solution)/shard_map/dynamic_slice | solution.py:358
  18.7 3.0 prepare.1
  21.7 12.8 %local_terms.2 = (f32[2,64,16,256]{3,2,1,0:T(8,128)}, f32[2,64,16,256]{3,2,1,0:T(8,128)}) custom-call(s32[7]{0:T(128)} %stack.31.where._.core, f32[256,1]{1,0:T(8,128)} %get-tuple-element.121.lost_a, f32[64,256,256]{2,1,0:T(8,128)} %bitcast.34, bf16[256,512]{1,0:T(8,128)(2,1)} %get-tuple-element.123.c_hi, bf16[256,512]{1,0:T(8,128)(2,1)} %get-tuple-element.124.c_lo, ...), custom_call_target="tpu_custom_call" | custom-call | flops 1000 | bytes 1000 | tf_op jit(solution)/shard_map/local_terms/pallas_call | solution.py:163
  34.5 29.2 %local_terms.3 = (f32[2,64,112,256]{3,2,1,0:T(8,128)}, f32[2,64,112,256]{3,2,1,0:T(8,128)}) custom-call(s32[7]{0:T(128)} %stack.31.where._.core, f32[256,1]{1,0:T(8,128)} %get-tuple-element.121.lost_a, f32[64,256,256]{2,1,0:T(8,128)} %bitcast.35, bf16[256,512]{1,0:T(8,128)(2,1)} %get-tuple-element.123.c_hi, bf16[256,512]{1,0:T(8,128)(2,1)} %get-tuple-element.124.c_lo, ...), custom_call_target="tpu_custom_call" | custom-call | flops 1000 | bytes 1000 | tf_op jit(solution)/shard_map/local_terms/pallas_call | solution.py:163
  63.8 4.3 collective-permute-done.10.refs_7_
  68.2 6.2 %dynamic-slice_bitcast_fusion = f32[64,96,256]{2,1,0:T(8,128)} fusion(f32[1,64,256,256]{3,2,1,0:T(8,128)} %param.6, s32[]{:T(128)S(6)} %select_n.50), kind=kLoop, calls=%fused_computation | loop fusion | bytes 12582916 | tf_op jit(solution)/shard_map/dynamic_slice | solution.py:358
  80.0 2.7 pad_maximum_fusion.7.refs_1_
  82.7 8.9 %first_terms.10 = (f32[128,16,256]{2,1,0:T(8,128)}, f32[128,16,256]{2,1,0:T(8,128)}, f32[128,16,256]{2,1,0:T(8,128)}) custom-call(s32[7]{0:T(128)} %stack.31.where._.core, f32[2,256]{1,0:T(2,128)} %get-tuple-element.118.fall, bf16[512,256]{1,0:T(8,128)(2,1)} %get-tuple-element.119.refs_0_, f32[128,16,256]{2,1,0:T(8,128)} %pad_maximum_fusion.7.refs_1_, ...), custom_call_target="tpu_custom_call" | custom-call | flops 1000 | bytes 1000 | tf_op jit(solution)/shard_map/first_terms/pallas_call | solution.py:228
  91.6 4.9 collective-permute-start.13
  96.5 3.1 collective-permute-done.1
  99.6 5.2 fusion
  105.0 19.0 %collective-permute-done.3.refs_2_ = f32[128,16,256]{2,1,0:T(8,128)} collective-permute-done((f32[128,16,256]{2,1,0:T(8,128)S(1)}, f32[128,16,256]{2,1,0:T(8,128)}, u32[]{:S(2)}, u32[]{:S(2)}) %collective-permute-start.3) | collective-permute-done | bytes 2097184 | tf_op jit(solution)/shard_map/ppermute | solution.py:343
  127.3 8.9 %first_terms.8 = (f32[128,16,256]{2,1,0:T(8,128)}, f32[128,16,256]{2,1,0:T(8,128)}, f32[128,16,256]{2,1,0:T(8,128)}) custom-call(s32[7]{0:T(128)} %stack.31.where._.core, f32[2,256]{1,0:T(2,128)} %get-tuple-element.118.fall, bf16[512,256]{1,0:T(8,128)(2,1)} %get-tuple-element.119.refs_0_, f32[128,16,256]{2,1,0:T(8,128)} %copy-done.7, ...), custom_call_target="tpu_custom_call" | custom-call | flops 1000 | bytes 1000 | tf_op jit(solution)/shard_map/first_terms/pallas_call | solution.py:228
  136.2 5.1 collective-permute-done.13.lifted
  141.2 4.1 collective-permute-start.14
  145.3 4.3 turn.9
  151.4 18.8 %collective-permute-done.4.refs_2_ = f32[128,16,256]{2,1,0:T(8,128)} collective-permute-done((f32[128,16,256]{2,1,0:T(8,128)S(1)}, f32[128,16,256]{2,1,0:T(8,128)}, u32[]{:S(2)}, u32[]{:S(2)}) %collective-permute-start.4) | collective-permute-done | bytes 2097184 | tf_op jit(solution)/shard_map/ppermute | solution.py:343
  173.5 8.9 %first_terms.9 = (f32[128,16,256]{2,1,0:T(8,128)}, f32[128,16,256]{2,1,0:T(8,128)}, f32[128,16,256]{2,1,0:T(8,128)}) custom-call(s32[7]{0:T(128)} %stack.31.where._.core, f32[2,256]{1,0:T(2,128)} %get-tuple-element.118.fall, bf16[512,256]{1,0:T(8,128)(2,1)} %get-tuple-element.119.refs_0_, f32[128,16,256]{2,1,0:T(8,128)} %copy-done.8, ...), custom_call_target="tpu_custom_call" | custom-call | flops 1000 | bytes 1000 | tf_op jit(solution)/shard_map/first_terms/pallas_call | solution.py:228
  182.4 6.8 %collective-permute-done.14.lifted = f32[128,16,256]{2,1,0:T(8,128)} collective-permute-done((f32[128,16,256]{2,1,0:T(8,128)}, f32[128,16,256]{2,1,0:T(8,128)}, u32[]{:S(2)}, u32[]{:S(2)}) %collective-permute-start.14) | collective-permute-done | bytes 2097184 | tf_op jit(solution)/shard_map/ppermute | solution.py:352
  189.2 4.1 collective-permute-start.18
  193.3 4.2 turn.8
  197.6 3.7 pad_maximum_fusion.3.refs_1_
  201.3 14.2 %collective-permute-done.5.refs_2_ = f32[128,16,256]{2,1,0:T(8,128)} collective-permute-done((f32[128,16,256]{2,1,0:T(8,128)S(1)}, f32[128,16,256]{2,1,0:T(8,128)}, u32[]{:S(2)}, u32[]{:S(2)}) %collective-permute-start.5) | collective-permute-done | bytes 2097184 | tf_op jit(solution)/shard_map/ppermute | solution.py:343
  218.6 9.0 %first_terms.11 = (f32[128,16,256]{2,1,0:T(8,128)}, f32[128,16,256]{2,1,0:T(8,128)}, f32[128,16,256]{2,1,0:T(8,128)}) custom-call(s32[7]{0:T(128)} %stack.31.where._.core, f32[2,256]{1,0:T(2,128)} %get-tuple-element.118.fall, bf16[512,256]{1,0:T(8,128)(2,1)} %get-tuple-element.119.refs_0_, f32[128,16,256]{2,1,0:T(8,128)} %copy-done.9, ...), custom_call_target="tpu_custom_call" | custom-call | flops 1000 | bytes 1000 | tf_op jit(solution)/shard_map/first_terms/pallas_call | solution.py:228
  227.6 8.6 %collective-permute-done.18.lifted = f32[128,16,256]{2,1,0:T(8,128)} collective-permute-done((f32[128,16,256]{2,1,0:T(8,128)}, f32[128,16,256]{2,1,0:T(8,128)}, u32[]{:S(2)}, u32[]{:S(2)}) %collective-permute-start.18) | collective-permute-done | bytes 2097184 | tf_op jit(solution)/shard_map/ppermute | solution.py:352
  236.2 4.1 collective-permute-start.22
  240.3 4.3 turn.10
  247.1 5.0 finish.8
  252.1 4.9 finish.9
  257.1 3.0 collective-permute-done.16.refs_2_
  263.2 8.9 %first_terms.12 = (f32[128,16,256]{2,1,0:T(8,128)}, f32[128,16,256]{2,1,0:T(8,128)}, f32[128,16,256]{2,1,0:T(8,128)}) custom-call(s32[7]{0:T(128)} %stack.31.where._.core, f32[2,256]{1,0:T(2,128)} %get-tuple-element.118.fall, bf16[512,256]{1,0:T(8,128)(2,1)} %get-tuple-element.119.refs_0_, f32[128,16,256]{2,1,0:T(8,128)} %pad_maximum_fusion.3.refs_1_, ...), custom_call_target="tpu_custom_call" | custom-call | flops 1000 | bytes 1000 | tf_op jit(solution)/shard_map/first_terms/pallas_call | solution.py:228
  272.1 10.2 %collective-permute-done.22.lifted = f32[128,16,256]{2,1,0:T(8,128)} collective-permute-done((f32[128,16,256]{2,1,0:T(8,128)}, f32[128,16,256]{2,1,0:T(8,128)}, u32[]{:S(2)}, u32[]{:S(2)}) %collective-permute-start.22) | collective-permute-done | bytes 2097184 | tf_op jit(solution)/shard_map/ppermute | solution.py:352
  282.3 4.1 collective-permute-start.26
  286.4 4.3 turn.11
  290.8 3.7 pad_maximum_fusion.1.refs_1_
  294.5 4.9 finish.10
  299.4 4.7 collective-permute-done.20.refs_2_
  307.3 8.9 %first_terms.13 = (f32[128,16,256]{2,1,0:T(8,128)}, f32[128,16,256]{2,1,0:T(8,128)}, f32[128,16,256]{2,1,0:T(8,128)}) custom-call(s32[7]{0:T(128)} %stack.31.where._.core, f32[2,256]{1,0:T(2,128)} %get-tuple-element.118.fall, bf16[512,256]{1,0:T(8,128)(2,1)} %get-tuple-element.119.refs_0_, f32[128,16,256]{2,1,0:T(8,128)} %copy-done.5, ...), custom_call_target="tpu_custom_call" | custom-call | flops 1000 | bytes 1000 | tf_op jit(solution)/shard_map/first_terms/pallas_call | solution.py:228
  316.2 11.2 %collective-permute-done.26.lifted = f32[128,16,256]{2,1,0:T(8,128)} collective-permute-done((f32[128,16,256]{2,1,0:T(8,128)}, f32[128,16,256]{2,1,0:T(8,128)}, u32[]{:S(2)}, u32[]{:S(2)}) %collective-permute-start.26) | collective-permute-done | bytes 2097184 | tf_op jit(solution)/shard_map/ppermute | solution.py:352
  327.5 4.1 collective-permute-start.30
  331.6 4.2 turn.12
  338.0 4.9 finish.11
  342.9 5.3 collective-permute-done.24.refs_2_
  351.4 9.0 %first_terms.14 = (f32[128,16,256]{2,1,0:T(8,128)}, f32[128,16,256]{2,1,0:T(8,128)}, f32[128,16,256]{2,1,0:T(8,128)}) custom-call(s32[7]{0:T(128)} %stack.31.where._.core, f32[2,256]{1,0:T(2,128)} %get-tuple-element.118.fall, bf16[512,256]{1,0:T(8,128)(2,1)} %get-tuple-element.119.refs_0_, f32[128,16,256]{2,1,0:T(8,128)} %pad_maximum_fusion.1.refs_1_, ...), custom_call_target="tpu_custom_call" | custom-call | flops 1000 | bytes 1000 | tf_op jit(solution)/shard_map/first_terms/pallas_call | solution.py:228
  360.4 11.4 %collective-permute-done.30.lifted = f32[128,16,256]{2,1,0:T(8,128)} collective-permute-done((f32[128,16,256]{2,1,0:T(8,128)}, f32[128,16,256]{2,1,0:T(8,128)}, u32[]{:S(2)}, u32[]{:S(2)}) %collective-permute-start.30) | collective-permute-done | bytes 2097184 | tf_op jit(solution)/shard_map/ppermute | solution.py:352
  371.7 4.1 collective-permute-start.33
  375.8 4.3 turn.13
  381.4 5.0 finish.12
  386.4 5.9 %collective-permute-done.28.refs_2_ = f32[128,16,256]{2,1,0:T(8,128)} collective-permute-done((f32[128,16,256]{2,1,0:T(8,128)S(1)}, f32[128,16,256]{2,1,0:T(8,128)}, u32[]{:S(2)}, u32[]{:S(2)}) %collective-permute-start.28) | collective-permute-done | bytes 2097184 | tf_op jit(solution)/shard_map/ppermute | solution.py:343
  392.3 3.0 collective-permute-done.32.refs_3_
  395.4 8.9 %first_terms.15 = (f32[128,16,256]{2,1,0:T(8,128)}, f32[128,16,256]{2,1,0:T(8,128)}, f32[128,16,256]{2,1,0:T(8,128)}) custom-call(s32[7]{0:T(128)} %stack.31.where._.core, f32[2,256]{1,0:T(2,128)} %get-tuple-element.118.fall, bf16[512,256]{1,0:T(8,128)(2,1)} %get-tuple-element.119.refs_0_, f32[128,16,256]{2,1,0:T(8,128)} %copy-done.6, ...), custom_call_target="tpu_custom_call" | custom-call | flops 1000 | bytes 1000 | tf_op jit(solution)/shard_map/first_terms/pallas_call | solution.py:228
  404.3 11.6 %collective-permute-done.33.lifted = f32[128,16,256]{2,1,0:T(8,128)} collective-permute-done((f32[128,16,256]{2,1,0:T(8,128)}, f32[128,16,256]{2,1,0:T(8,128)}, u32[]{:S(2)}, u32[]{:S(2)}) %collective-permute-start.33) | collective-permute-done | bytes 2097184 | tf_op jit(solution)/shard_map/ppermute | solution.py:352
  415.8 4.2 turn.15
  423.3 5.1 finish.13
  428.4 7.1 %collective-permute-start.38 = (f32[64,96,256]{2,1,0:T(8,128)}, f32[64,96,256]{2,1,0:T(8,128)}, u32[]{:S(2)}, u32[]{:S(2)}) collective-permute-start(f32[64,96,256]{2,1,0:T(8,128)} %get-tuple-element.223), channel_id=1, source_target_pairs={{0,8},{8,0},{16,24},{24,16},{1,9},{9,1},{17,25},{25,17},{2,10},{10... | collective-permute-start | bytes 18874376 | tf_op jit(solution)/shard_map/ppermute | solution.py:346
  437.5 47.3 %collective-permute-done.34.lifted = f32[128,16,256]{2,1,0:T(8,128)S(1)} collective-permute-done((f32[128,16,256]{2,1,0:T(8,128)}, f32[128,16,256]{2,1,0:T(8,128)S(1)}, u32[]{:S(2)}, u32[]{:S(2)}) %collective-permute-start.34) | collective-permute-done | bytes 2097184 | tf_op jit(solution)/shard_map/ppermute | solution.py:352
  486.2 4.3 turn.14
  491.8 4.9 finish.14
  497.5 9.9 %put.3.refs_4_ = f32[64,256,256]{2,1,0:T(8,128)} custom-call(s32[7]{0:T(128)} %stack.31.where._.core, f32[64,96,256]{2,1,0:T(8,128)} %collective-permute-done.38.piece, f32[64,256,256]{2,1,0:T(8,128)} %get-tuple-element.227._), custom_call_target="tpu_custom_call", output_to_operand_aliasing={{}: (2, {})} | custom-call | flops 1000 | bytes 1000 | tf_op jit(solution)/shard_map/put/pallas_call | solution.py:309
  507.4 29.7 %collective-permute-done.37.refs_1_.refs_3_ = f32[128,16,256]{2,1,0:T(8,128)S(1)} collective-permute-done((f32[128,16,256]{2,1,0:T(8,128)}, f32[128,16,256]{2,1,0:T(8,128)S(1)}, u32[]{:S(2)}, u32[]{:S(2)}) %collective-permute-start.37) | collective-permute-done | bytes 2097184 | tf_op jit(solution)/shard_map/ppermute | solution.py:355
  538.4 4.9 finish.15
  546.0 2.7 put.4._
  549.7 2.7 put.5
  (103 shorter events, 55.1 us)
Async XLA Ops:
  3.2 18.6 %collective-permute-start = (f32[64,32,256]{2,1,0:T(8,128)}, f32[64,32,256]{2,1,0:T(8,128)}, u32[]{:S(2)}, u32[]{:S(2)}) collective-permute-start(f32[64,32,256]{2,1,0:T(8,128)} %dynamic-slice_bitcast_fusion.1), channel_id=1, source_target_pairs={{0,8},{8,0},{16,24},{24,16},{1,9},{9,1},{17,25},{25,17},{2,10},{10... | collective-permute-start | bytes 6291464 | tf_op jit(solution)/shard_map/ppermute | solution.py:346
  3.8 13.4 %copy-start.18 = (s32[3,256]{1,0:T(4,128)S(1)}, s32[3,256]{1,0:T(4,128)}, u32[]{:S(2)}) copy-start(s32[3,256]{1,0:T(4,128)} %inc_rows.1) | copy-start | bytes 9220
  11.0 52.7 %collective-permute-start.2 = (f32[64,16,256]{2,1,0:T(8,128)}, f32[64,16,256]{2,1,0:T(8,128)}, u32[]{:S(2)}, u32[]{:S(2)}) collective-permute-start(f32[64,16,256]{2,1,0:T(8,128)} %get-tuple-element.232), channel_id=1, source_target_pairs={{0,16},{8,24},{16,0},{24,8},{1,17},{9,25},{17,1},{25,9},{2,18},{10... | collective-permute-start | bytes 3145736 | tf_op jit(solution)/shard_map/ppermute | solution.py:343
  12.2 51.5 %collective-permute-start.7 = (f32[64,16,256]{2,1,0:T(8,128)}, f32[64,16,256]{2,1,0:T(8,128)}, u32[]{:S(2)}, u32[]{:S(2)}) collective-permute-start(f32[64,16,256]{2,1,0:T(8,128)} %get-tuple-element.231), channel_id=1, source_target_pairs={{0,24},{8,16},{16,8},{24,0},{1,25},{9,17},{17,9},{25,1},{2,26},{10... | collective-permute-start | bytes 3145736 | tf_op jit(solution)/shard_map/ppermute | solution.py:384
  12.6 51.1 %collective-permute-start.8 = (f32[64,16,256]{2,1,0:T(8,128)}, f32[64,16,256]{2,1,0:T(8,128)}, u32[]{:S(2)}, u32[]{:S(2)}) collective-permute-start(f32[64,16,256]{2,1,0:T(8,128)} %get-tuple-element.232), channel_id=1, source_target_pairs={{2,0},{3,1},{4,2},{5,3},{6,4},{7,5},{10,8},{11,9},{12,10},{13,11},... | collective-permute-start | bytes 3145736 | tf_op jit(solution)/shard_map/ppermute | solution.py:349
  14.7 49.0 %collective-permute-start.9 = (f32[64,16,256]{2,1,0:T(8,128)}, f32[64,16,256]{2,1,0:T(8,128)}, u32[]{:S(2)}, u32[]{:S(2)}) collective-permute-start(f32[64,16,256]{2,1,0:T(8,128)} %get-tuple-element.231), channel_id=1, source_target_pairs={{2,8},{3,9},{4,10},{5,11},{6,12},{7,13},{10,0},{11,1},{12,2},{13,3... | collective-permute-start | bytes 3145736 | tf_op jit(solution)/shard_map/ppermute | solution.py:387
  34.5 29.2 %copy-start.19 = (f32[2,64,16,256]{3,2,1,0:T(8,128)S(1)}, f32[2,64,16,256]{3,2,1,0:T(8,128)}, u32[]{:S(2)}) copy-start(f32[2,64,16,256]{3,2,1,0:T(8,128)} %get-tuple-element.138) | copy-start | bytes 6291460
  63.7 4.4 collective-permute-start.10
  68.1 59.2 %collective-permute-start.11 = (f32[2,64,112,256]{3,2,1,0:T(8,128)}, f32[2,64,112,256]{3,2,1,0:T(8,128)}, u32[]{:S(2)}, u32[]{:S(2)}) collective-permute-start(f32[2,64,112,256]{3,2,1,0:T(8,128)} %get-tuple-element.139), channel_id=1, source_target_pairs={{0,8},{8,0},{16,24},{24,16},{1,9},{9,1},{17,25},{25,17},{2,10},{10... | collective-permute-start | bytes 44040200 | tf_op jit(solution)/shard_map/ppermute | solution.py:346
  74.4 2.1 copy-start.13
  74.4 25.2 %collective-permute-start.1 = (f32[64,96,256]{2,1,0:T(8,128)}, f32[64,96,256]{2,1,0:T(8,128)}, u32[]{:S(2)}, u32[]{:S(2)}) collective-permute-start(f32[64,96,256]{2,1,0:T(8,128)} %dynamic-slice_bitcast_fusion), channel_id=1, source_target_pairs={{0,8},{8,0},{16,24},{24,16},{1,9},{9,1},{17,25},{25,17},{2,10},{10... | collective-permute-start | bytes 18874376 | tf_op jit(solution)/shard_map/ppermute | solution.py:346
  76.8 5.9 %copy-start.7 = (f32[128,16,256]{2,1,0:T(8,128)}, f32[128,16,256]{2,1,0:T(8,128)S(1)}, u32[]{:S(2)}) copy-start(f32[128,16,256]{2,1,0:T(8,128)S(1)} %pad_maximum_fusion.6.refs_1_) | copy-start | bytes 6291460
  76.8 47.2 %collective-permute-start.3 = (f32[128,16,256]{2,1,0:T(8,128)S(1)}, f32[128,16,256]{2,1,0:T(8,128)}, u32[]{:S(2)}, u32[]{:S(2)}) collective-permute-start(f32[128,16,256]{2,1,0:T(8,128)S(1)} %pad_maximum_fusion.6.refs_1_), channel_id=1, source_target_pairs={{0,16},{8,24},{16,0},{24,8},{1,17},{9,25},{17,1},{25,9},{2,18},{10... | collective-permute-start | bytes 6291464 | tf_op jit(solution)/shard_map/ppermute | solution.py:343
  78.1 49.2 %collective-permute-start.6 = (f32[128,16,256]{2,1,0:T(8,128)S(1)}, f32[128,16,256]{2,1,0:T(8,128)}, u32[]{:S(2)}, u32[]{:S(2)}) collective-permute-start(f32[128,16,256]{2,1,0:T(8,128)S(1)} %pad_maximum_fusion.6.refs_1_), channel_id=1, source_target_pairs={{2,0},{3,1},{4,2},{5,3},{6,4},{7,5},{10,8},{11,9},{12,10},{13,11},... | collective-permute-start | bytes 6291464 | tf_op jit(solution)/shard_map/ppermute | solution.py:349
  91.6 49.7 %collective-permute-start.13 = (f32[128,16,256]{2,1,0:T(8,128)}, f32[128,16,256]{2,1,0:T(8,128)}, u32[]{:S(2)}, u32[]{:S(2)}) collective-permute-start(f32[128,16,256]{2,1,0:T(8,128)} %get-tuple-element.144), channel_id=1, source_target_pairs={{1,3},{3,5},{5,7},{9,11},{11,13},{13,15},{17,19},{19,21},{21,23},{... | collective-permute-start | bytes 6291464 | tf_op jit(solution)/shard_map/ppermute | solution.py:352
  105.0 31.2 %copy-start.8 = (f32[128,16,256]{2,1,0:T(8,128)}, f32[128,16,256]{2,1,0:T(8,128)S(1)}, u32[]{:S(2)}) copy-start(f32[128,16,256]{2,1,0:T(8,128)S(1)} %pad_maximum_fusion.5.refs_1_) | copy-start | bytes 6291460
  124.0 46.2 %collective-permute-start.4 = (f32[128,16,256]{2,1,0:T(8,128)S(1)}, f32[128,16,256]{2,1,0:T(8,128)}, u32[]{:S(2)}, u32[]{:S(2)}) collective-permute-start(f32[128,16,256]{2,1,0:T(8,128)S(1)} %pad_maximum_fusion.5.refs_1_), channel_id=1, source_target_pairs={{0,16},{8,24},{16,0},{24,8},{1,17},{9,25},{17,1},{25,9},{2,18},{10... | collective-permute-start | bytes 6291464 | tf_op jit(solution)/shard_map/ppermute | solution.py:343
  125.2 48.3 %collective-permute-start.12 = (f32[128,16,256]{2,1,0:T(8,128)S(1)}, f32[128,16,256]{2,1,0:T(8,128)}, u32[]{:S(2)}, u32[]{:S(2)}) collective-permute-start(f32[128,16,256]{2,1,0:T(8,128)S(1)} %pad_maximum_fusion.5.refs_1_), channel_id=1, source_target_pairs={{2,0},{3,1},{4,2},{5,3},{6,4},{7,5},{10,8},{11,9},{12,10},{13,11},... | collective-permute-start | bytes 6291464 | tf_op jit(solution)/shard_map/ppermute | solution.py:349
  141.2 47.9 %collective-permute-start.14 = (f32[128,16,256]{2,1,0:T(8,128)}, f32[128,16,256]{2,1,0:T(8,128)}, u32[]{:S(2)}, u32[]{:S(2)}) collective-permute-start(f32[128,16,256]{2,1,0:T(8,128)} %get-tuple-element.145), channel_id=1, source_target_pairs={{1,3},{3,5},{5,7},{9,11},{11,13},{13,15},{17,19},{19,21},{21,23},{... | collective-permute-start | bytes 6291464 | tf_op jit(solution)/shard_map/ppermute | solution.py:352
  149.6 47.8 %collective-permute-start.15 = (f32[128,16,256]{2,1,0:T(8,128)}, f32[128,16,256]{2,1,0:T(8,128)S(1)}, u32[]{:S(2)}, u32[]{:S(2)}) collective-permute-start(f32[128,16,256]{2,1,0:T(8,128)} %turn.9), channel_id=1, source_target_pairs={{0,1},{1,0},{2,3},{3,2},{4,5},{5,4},{6,7},{7,6},{8,9},{9,8},{10,11... | collective-permute-start | bytes 6291464 | tf_op jit(solution)/shard_map/ppermute | solution.py:355
  151.4 31.0 %copy-start.9 = (f32[128,16,256]{2,1,0:T(8,128)}, f32[128,16,256]{2,1,0:T(8,128)S(1)}, u32[]{:S(2)}) copy-start(f32[128,16,256]{2,1,0:T(8,128)S(1)} %pad_maximum_fusion.4.refs_1_) | copy-start | bytes 6291460
  170.2 45.3 %collective-permute-start.5 = (f32[128,16,256]{2,1,0:T(8,128)S(1)}, f32[128,16,256]{2,1,0:T(8,128)}, u32[]{:S(2)}, u32[]{:S(2)}) collective-permute-start(f32[128,16,256]{2,1,0:T(8,128)S(1)} %pad_maximum_fusion.4.refs_1_), channel_id=1, source_target_pairs={{0,16},{8,24},{16,0},{24,8},{1,17},{9,25},{17,1},{25,9},{2,18},{10... | collective-permute-start | bytes 6291464 | tf_op jit(solution)/shard_map/ppermute | solution.py:343
  171.4 47.2 %collective-permute-start.17 = (f32[128,16,256]{2,1,0:T(8,128)S(1)}, f32[128,16,256]{2,1,0:T(8,128)}, u32[]{:S(2)}, u32[]{:S(2)}) collective-permute-start(f32[128,16,256]{2,1,0:T(8,128)S(1)} %pad_maximum_fusion.4.refs_1_), channel_id=1, source_target_pairs={{2,0},{3,1},{4,2},{5,3},{6,4},{7,5},{10,8},{11,9},{12,10},{13,11},... | collective-permute-start | bytes 6291464 | tf_op jit(solution)/shard_map/ppermute | solution.py:349
  189.2 47.0 %collective-permute-start.18 = (f32[128,16,256]{2,1,0:T(8,128)}, f32[128,16,256]{2,1,0:T(8,128)}, u32[]{:S(2)}, u32[]{:S(2)}) collective-permute-start(f32[128,16,256]{2,1,0:T(8,128)} %get-tuple-element.155), channel_id=1, source_target_pairs={{1,3},{3,5},{5,7},{9,11},{11,13},{13,15},{17,19},{19,21},{21,23},{... | collective-permute-start | bytes 6291464 | tf_op jit(solution)/shard_map/ppermute | solution.py:352
  197.5 3.8 copy-start.10
  197.5 47.1 %collective-permute-start.19 = (f32[128,16,256]{2,1,0:T(8,128)}, f32[128,16,256]{2,1,0:T(8,128)S(1)}, u32[]{:S(2)}, u32[]{:S(2)}) collective-permute-start(f32[128,16,256]{2,1,0:T(8,128)} %turn.8), channel_id=1, source_target_pairs={{0,1},{1,0},{2,3},{3,2},{4,5},{5,4},{6,7},{7,6},{8,9},{9,8},{10,11... | collective-permute-start | bytes 6291464 | tf_op jit(solution)/shard_map/ppermute | solution.py:355
  215.5 44.6 %collective-permute-start.16 = (f32[128,16,256]{2,1,0:T(8,128)}, f32[128,16,256]{2,1,0:T(8,128)}, u32[]{:S(2)}, u32[]{:S(2)}) collective-permute-start(f32[128,16,256]{2,1,0:T(8,128)} %pad_maximum_fusion.3.refs_1_), channel_id=1, source_target_pairs={{0,16},{8,24},{16,0},{24,8},{1,17},{9,25},{17,1},{25,9},{2,18},{10... | collective-permute-start | bytes 6291464 | tf_op jit(solution)/shard_map/ppermute | solution.py:343
  216.7 46.5 %collective-permute-start.21 = (f32[128,16,256]{2,1,0:T(8,128)}, f32[128,16,256]{2,1,0:T(8,128)}, u32[]{:S(2)}, u32[]{:S(2)}) collective-permute-start(f32[128,16,256]{2,1,0:T(8,128)} %pad_maximum_fusion.3.refs_1_), channel_id=1, source_target_pairs={{2,0},{3,1},{4,2},{5,3},{6,4},{7,5},{10,8},{11,9},{12,10},{13,11},... | collective-permute-start | bytes 6291464 | tf_op jit(solution)/shard_map/ppermute | solution.py:349
  236.2 46.1 %collective-permute-start.22 = (f32[128,16,256]{2,1,0:T(8,128)}, f32[128,16,256]{2,1,0:T(8,128)}, u32[]{:S(2)}, u32[]{:S(2)}) collective-permute-start(f32[128,16,256]{2,1,0:T(8,128)} %get-tuple-element.170), channel_id=1, source_target_pairs={{1,3},{3,5},{5,7},{9,11},{11,13},{13,15},{17,19},{19,21},{21,23},{... | collective-permute-start | bytes 6291464 | tf_op jit(solution)/shard_map/ppermute | solution.py:352
  244.6 2.5 copy-start.3
  244.6 46.1 %collective-permute-start.23 = (f32[128,16,256]{2,1,0:T(8,128)}, f32[128,16,256]{2,1,0:T(8,128)S(1)}, u32[]{:S(2)}, u32[]{:S(2)}) collective-permute-start(f32[128,16,256]{2,1,0:T(8,128)} %turn.10), channel_id=1, source_target_pairs={{0,1},{1,0},{2,3},{3,2},{4,5},{5,4},{6,7},{7,6},{8,9},{9,8},{10,11... | collective-permute-start | bytes 6291464 | tf_op jit(solution)/shard_map/ppermute | solution.py:355
  247.1 14.1 %copy-start.5 = (f32[128,16,256]{2,1,0:T(8,128)}, f32[128,16,256]{2,1,0:T(8,128)S(1)}, u32[]{:S(2)}) copy-start(f32[128,16,256]{2,1,0:T(8,128)S(1)} %pad_maximum_fusion.2.refs_1_) | copy-start | bytes 6291460
  260.1 44.1 %collective-permute-start.20 = (f32[128,16,256]{2,1,0:T(8,128)S(1)}, f32[128,16,256]{2,1,0:T(8,128)}, u32[]{:S(2)}, u32[]{:S(2)}) collective-permute-start(f32[128,16,256]{2,1,0:T(8,128)S(1)} %pad_maximum_fusion.2.refs_1_), channel_id=1, source_target_pairs={{0,16},{8,24},{16,0},{24,8},{1,17},{9,25},{17,1},{25,9},{2,18},{10... | collective-permute-start | bytes 6291464 | tf_op jit(solution)/shard_map/ppermute | solution.py:343
  261.3 46.0 %collective-permute-start.25 = (f32[128,16,256]{2,1,0:T(8,128)S(1)}, f32[128,16,256]{2,1,0:T(8,128)}, u32[]{:S(2)}, u32[]{:S(2)}) collective-permute-start(f32[128,16,256]{2,1,0:T(8,128)S(1)} %pad_maximum_fusion.2.refs_1_), channel_id=1, source_target_pairs={{2,0},{3,1},{4,2},{5,3},{6,4},{7,5},{10,8},{11,9},{12,10},{13,11},... | collective-permute-start | bytes 6291464 | tf_op jit(solution)/shard_map/ppermute | solution.py:349
  282.3 45.2 %collective-permute-start.26 = (f32[128,16,256]{2,1,0:T(8,128)}, f32[128,16,256]{2,1,0:T(8,128)}, u32[]{:S(2)}, u32[]{:S(2)}) collective-permute-start(f32[128,16,256]{2,1,0:T(8,128)} %get-tuple-element.184), channel_id=1, source_target_pairs={{1,3},{3,5},{5,7},{9,11},{11,13},{13,15},{17,19},{19,21},{21,23},{... | collective-permute-start | bytes 6291464 | tf_op jit(solution)/shard_map/ppermute | solution.py:352
  290.7 3.8 copy-start
  290.7 45.1 %collective-permute-start.27 = (f32[128,16,256]{2,1,0:T(8,128)}, f32[128,16,256]{2,1,0:T(8,128)S(1)}, u32[]{:S(2)}, u32[]{:S(2)}) collective-permute-start(f32[128,16,256]{2,1,0:T(8,128)} %turn.11), channel_id=1, source_target_pairs={{0,1},{1,0},{2,3},{3,2},{4,5},{5,4},{6,7},{7,6},{8,9},{9,8},{10,11... | collective-permute-start | bytes 6291464 | tf_op jit(solution)/shard_map/ppermute | solution.py:355
  304.2 44.1 %collective-permute-start.24 = (f32[128,16,256]{2,1,0:T(8,128)}, f32[128,16,256]{2,1,0:T(8,128)}, u32[]{:S(2)}, u32[]{:S(2)}) collective-permute-start(f32[128,16,256]{2,1,0:T(8,128)} %pad_maximum_fusion.1.refs_1_), channel_id=1, source_target_pairs={{0,16},{8,24},{16,0},{24,8},{1,17},{9,25},{17,1},{25,9},{2,18},{10... | collective-permute-start | bytes 6291464 | tf_op jit(solution)/shard_map/ppermute | solution.py:343
  305.4 46.0 %collective-permute-start.29 = (f32[128,16,256]{2,1,0:T(8,128)}, f32[128,16,256]{2,1,0:T(8,128)}, u32[]{:S(2)}, u32[]{:S(2)}) collective-permute-start(f32[128,16,256]{2,1,0:T(8,128)} %pad_maximum_fusion.1.refs_1_), channel_id=1, source_target_pairs={{2,0},{3,1},{4,2},{5,3},{6,4},{7,5},{10,8},{11,9},{12,10},{13,11},... | collective-permute-start | bytes 6291464 | tf_op jit(solution)/shard_map/ppermute | solution.py:349
  327.5 44.3 %collective-permute-start.30 = (f32[128,16,256]{2,1,0:T(8,128)}, f32[128,16,256]{2,1,0:T(8,128)}, u32[]{:S(2)}, u32[]{:S(2)}) collective-permute-start(f32[128,16,256]{2,1,0:T(8,128)} %get-tuple-element.198), channel_id=1, source_target_pairs={{1,3},{3,5},{5,7},{9,11},{11,13},{13,15},{17,19},{19,21},{21,23},{... | collective-permute-start | bytes 6291464 | tf_op jit(solution)/shard_map/ppermute | solution.py:352
  335.8 2.2 copy-start.1
  335.8 44.3 %collective-permute-start.31 = (f32[128,16,256]{2,1,0:T(8,128)}, f32[128,16,256]{2,1,0:T(8,128)S(1)}, u32[]{:S(2)}, u32[]{:S(2)}) collective-permute-start(f32[128,16,256]{2,1,0:T(8,128)} %turn.12), channel_id=1, source_target_pairs={{0,1},{1,0},{2,3},{3,2},{4,5},{5,4},{6,7},{7,6},{8,9},{9,8},{10,11... | collective-permute-start | bytes 6291464 | tf_op jit(solution)/shard_map/ppermute | solution.py:355
  338.0 11.5 %copy-start.6 = (f32[128,16,256]{2,1,0:T(8,128)}, f32[128,16,256]{2,1,0:T(8,128)S(1)}, u32[]{:S(2)}) copy-start(f32[128,16,256]{2,1,0:T(8,128)S(1)} %pad_maximum_fusion.refs_1_) | copy-start | bytes 6291460
  348.2 44.1 %collective-permute-start.28 = (f32[128,16,256]{2,1,0:T(8,128)S(1)}, f32[128,16,256]{2,1,0:T(8,128)}, u32[]{:S(2)}, u32[]{:S(2)}) collective-permute-start(f32[128,16,256]{2,1,0:T(8,128)S(1)} %pad_maximum_fusion.refs_1_), channel_id=1, source_target_pairs={{0,16},{8,24},{16,0},{24,8},{1,17},{9,25},{17,1},{25,9},{2,18},{10... | collective-permute-start | bytes 6291464 | tf_op jit(solution)/shard_map/ppermute | solution.py:343
  349.5 45.9 %collective-permute-start.32 = (f32[128,16,256]{2,1,0:T(8,128)S(1)}, f32[128,16,256]{2,1,0:T(8,128)}, u32[]{:S(2)}, u32[]{:S(2)}) collective-permute-start(f32[128,16,256]{2,1,0:T(8,128)S(1)} %pad_maximum_fusion.refs_1_), channel_id=1, source_target_pairs={{2,0},{3,1},{4,2},{5,3},{6,4},{7,5},{10,8},{11,9},{12,10},{13,11},... | collective-permute-start | bytes 6291464 | tf_op jit(solution)/shard_map/ppermute | solution.py:349
  371.7 44.1 %collective-permute-start.33 = (f32[128,16,256]{2,1,0:T(8,128)}, f32[128,16,256]{2,1,0:T(8,128)}, u32[]{:S(2)}, u32[]{:S(2)}) collective-permute-start(f32[128,16,256]{2,1,0:T(8,128)} %get-tuple-element.212), channel_id=1, source_target_pairs={{1,3},{3,5},{5,7},{9,11},{11,13},{13,15},{17,19},{19,21},{21,23},{... | collective-permute-start | bytes 6291464 | tf_op jit(solution)/shard_map/ppermute | solution.py:352
  380.1 1.3 copy-start.2
  380.1 41.9 %collective-permute-start.35 = (f32[128,16,256]{2,1,0:T(8,128)}, f32[128,16,256]{2,1,0:T(8,128)S(1)}, u32[]{:S(2)}, u32[]{:S(2)}) collective-permute-start(f32[128,16,256]{2,1,0:T(8,128)} %turn.13), channel_id=1, source_target_pairs={{0,1},{1,0},{2,3},{3,2},{4,5},{5,4},{6,7},{7,6},{8,9},{9,8},{10,11... | collective-permute-start | bytes 6291464 | tf_op jit(solution)/shard_map/ppermute | solution.py:355
  422.0 1.3 copy-start.4
  423.3 14.1 %copy-start.14 = (f32[128,16,256]{2,1,0:T(8,128)S(1)}, f32[128,16,256]{2,1,0:T(8,128)}, u32[]{:S(2)}) copy-start(f32[128,16,256]{2,1,0:T(8,128)} %turn.15) | copy-start | bytes 6291460
  428.4 69.1 %collective-permute-start.38 = (f32[64,96,256]{2,1,0:T(8,128)}, f32[64,96,256]{2,1,0:T(8,128)}, u32[]{:S(2)}, u32[]{:S(2)}) collective-permute-start(f32[64,96,256]{2,1,0:T(8,128)} %get-tuple-element.223), channel_id=1, source_target_pairs={{0,8},{8,0},{16,24},{24,16},{1,9},{9,1},{17,25},{25,17},{2,10},{10... | collective-permute-start | bytes 18874376 | tf_op jit(solution)/shard_map/ppermute | solution.py:346
  435.4 49.3 %collective-permute-start.34 = (f32[128,16,256]{2,1,0:T(8,128)}, f32[128,16,256]{2,1,0:T(8,128)S(1)}, u32[]{:S(2)}, u32[]{:S(2)}) collective-permute-start(f32[128,16,256]{2,1,0:T(8,128)} %get-tuple-element.213), channel_id=1, source_target_pairs={{1,3},{3,5},{5,7},{9,11},{11,13},{13,15},{17,19},{19,21},{21,23},{... | collective-permute-start | bytes 6291464 | tf_op jit(solution)/shard_map/ppermute | solution.py:352
  437.4 53.0 %collective-permute-start.36 = (f32[128,16,256]{2,1,0:T(8,128)S(1)}, f32[128,16,256]{2,1,0:T(8,128)S(1)}, u32[]{:S(2)}, u32[]{:S(2)}) collective-permute-start(f32[128,16,256]{2,1,0:T(8,128)S(1)} %copy-done.14), channel_id=1, source_target_pairs={{0,1},{1,0},{2,3},{3,2},{4,5},{5,4},{6,7},{7,6},{8,9},{9,8},{10,11... | collective-permute-start | bytes 6291464 | tf_op jit(solution)/shard_map/ppermute | solution.py:355
  484.8 1.4 copy-start.15
  490.4 1.4 copy-start.12
  490.4 46.6 %collective-permute-start.37 = (f32[128,16,256]{2,1,0:T(8,128)}, f32[128,16,256]{2,1,0:T(8,128)S(1)}, u32[]{:S(2)}, u32[]{:S(2)}) collective-permute-start(f32[128,16,256]{2,1,0:T(8,128)} %turn.14), channel_id=1, source_target_pairs={{0,1},{1,0},{2,3},{3,2},{4,5},{5,4},{6,7},{7,6},{8,9},{9,8},{10,11... | collective-permute-start | bytes 6291464 | tf_op jit(solution)/shard_map/ppermute | solution.py:355
  496.7 48.3 %collective-permute-start.40 = (f32[64,16,256]{2,1,0:T(8,128)}, f32[64,16,256]{2,1,0:T(8,128)S(1)}, u32[]{:S(2)}, u32[]{:S(2)}) collective-permute-start(f32[64,16,256]{2,1,0:T(8,128)} %get-tuple-element.229), channel_id=1, source_target_pairs={{0,8},{8,0},{16,24},{24,16},{1,9},{9,1},{17,25},{25,17},{2,10},{10... | collective-permute-start | bytes 3145736 | tf_op jit(solution)/shard_map/ppermute | solution.py:346
  537.1 1.3 copy-start.11
  543.3 5.4 collective-permute-start.39
  545.0 1.0 copy-start.16
  548.7 1.0 copy-start.17

commit v7 on v6

--- a/solution.py
+++ b/solution.py
@@ -11,7 +11,7 @@
 BF16 = jnp.bfloat16
 VMEM_LIMIT = 56 * 2**20
 SPAN, LANES = 8, 128
-FIRST_ROWS = 1
+FIRST_ROWS = 2
 LIGHT = pl.CostEstimate(flops=1000, transcendentals=0, bytes_accessed=1000)
 PARAMS = pltpu.CompilerParams(vmem_limit_bytes=VMEM_LIMIT)
 WHOLE = pl.BlockSpec(memory_space=pltpu.VMEM)
@@ -41,7 +41,7 @@
 
 
 def plan(rows, length):
-    n = max(4, rows // 8)
+    n = max(4, rows // 4)
     size = length // n
     chunks = [(s * size, size) for s in range(n)]
     return chunks, [(0, n - 2), (n - 2, n - 1), (n - 1, n)]
@@ -362,12 +362,13 @@
     size = chunks[0][1]
     shifts = [2 * s for s in range(1, n_cls // 2)]
     sent = [None] * n
-    tokens = []
+    tokens, gives = [], []
     for lo, hi in spans(*sorted({0, n // 4, n})):
         at = chunks[lo][0]
         give = cut(occ, 1, at, (hi - lo) * size)
         if tokens:
-            give, _ = gate(give, tokens[-1])
+            give, _ = gate(give, sent[0])
+        gives.append(give)
         got = other_core(give)
         tokens.append(got)
         for s in range(lo, hi):
@@ -402,9 +403,9 @@
 
     parts = []
 
-    def start_part(lo, hi, begin):
+    def start_part(lo, hi, *begin):
         at, span = chunks[lo][0], (hi - lo) * size
-        mine, give = local_terms(where, gate(occ, begin)[0], lost_a, factors, at, span)
+        mine, give = local_terms(where, gate(occ, *begin)[0], lost_a, factors, at, span)
         return lo, hi, at, mine, give
 
     def send_part(part, *after):
@@ -412,7 +413,7 @@
         parts.append((lo, hi, at, (mine, other_core(gate(give, *after)[0]))))
 
     part = start_part(0, FIRST_ROWS, tokens[0])
-    rest = start_part(FIRST_ROWS, n, part[3])
+    rest = start_part(FIRST_ROWS, n, part[3], gives[1], sent[0], sent[1])
     far[0][0], _ = gate(far[0][0], rest[3])
     send_part(part, *far[0], *deep[0])
     send_part(rest, parts[0][3][1])

time: 555 us -> 520 us (0.937)
  waiting for transfers between devices: 225 us -> 110 us
  starting transfers between devices: 71 us -> 133 us
  Pallas kernels: 205 us -> 231 us
  other arithmetic: 16.9 us -> 4.61 us
    ppermute x8 -> x16, waiting for transfers between devices: 112 us -> 53.8 us  [two_up(): return lax.ppermute(v, 'lvl', [(i, i + 2) for i in range(1, n_lvl - 2, 2)])]
    ppermute x8 -> x16, waiting for transfers between devices: 71 us -> 30.5 us  [along_cls(): return lax.ppermute(v, 'cls', [(i, (i + by) % n_cls) for i in range(n_cls)])]
    ppermute x8 -> x16, starting transfers between devices: 15.6 us -> 47.7 us  [two_down(): return lax.ppermute(v, 'lvl', [(i, i - 2) for i in range(2, n_lvl)])]
    ppermute x8 -> x16, starting transfers between devices: 31.4 us -> 51.8 us  [two_up(): return lax.ppermute(v, 'lvl', [(i, i + 2) for i in range(1, n_lvl - 2, 2)])]
    ppermute x8 -> x16, waiting for transfers between devices: 31.6 us -> 13.2 us  [pair_swap(): return lax.ppermute(v, 'lvl', [(i, i ^ 1) for i in range(n_lvl)])]
    concatenate x8 -> x15, other arithmetic: 16.9 us -> 4.61 us  [local(): sent[s] = jnp.concatenate([cut(occ, 0, start, size), part], axis=0)]
    pallas_call x8 -> x16, Pallas kernels: 71.3 us -> 81.8 us  [first_terms(): pl.pallas_call(functools.partial(first_kernel, len(slabs), len(deep)), gr...]
    pallas_call x8 -> x16, Pallas kernels: 39.6 us -> 49.9 us  [finish(): pl.pallas_call(functools.partial(finish_kernel, len(alias)), grid_spec=pl...]
  transfers between devices with their start and end apart: 41 -> 73, of which waited for: 21 -> 34; matrix products, arithmetic and copies ran while one was open for 7% -> 5% of each run, Pallas kernels for 36% -> 44%
where the time goes in v7:
time: 520 us; the launch traced here: 517 us
  Pallas kernels  231 us (44%)
  starting transfers between devices  133 us (26%)
  waiting for transfers between devices  110 us (21%)
  local copies, waits for them, and re-layouts  36.8 us (7%)
    pallas_call x16, Pallas kernels, first_terms(): pl.pallas_call(functools.partial(first_kernel, len(slabs), len(deep)), gr...  81.8 us
    ppermute x16, waiting for transfers between devices, two_up(): return lax.ppermute(v, 'lvl', [(i, i + 2) for i in range(1, n_lvl - 2, 2)])  53.8 us
    ppermute x16, starting transfers between devices, two_up(): return lax.ppermute(v, 'lvl', [(i, i + 2) for i in range(1, n_lvl - 2, 2)])  51.8 us
    pallas_call x16, Pallas kernels, finish(): pl.pallas_call(functools.partial(finish_kernel, len(alias)), grid_spec=pl...  49.9 us
    ppermute x16, starting transfers between devices, two_down(): return lax.ppermute(v, 'lvl', [(i, i - 2) for i in range(2, n_lvl)])  47.7 us
    pallas_call x2, Pallas kernels, local_terms(): pl.pallas_call(functools.partial(local_kernel, at, mid // 2), grid_spec=p...  41.9 us
    pallas_call x16, Pallas kernels, turn(): pl.pallas_call(turn_kernel, grid=(rows // block, size // SPAN), in_specs=...  38.1 us
    ppermute x16, waiting for transfers between devices, along_cls(): return lax.ppermute(v, 'cls', [(i, (i + by) % n_cls) for i in range(n_cls)])  30.5 us
  transfers between devices with their start and end apart: 73, of which 34 were waited for; matrix products, arithmetic and copies ran while one was open for 5% of the time, Pallas kernels for 44%

profile of v7, /device:TPU:21, one launch (start us, length us, event | category | flops | bytes accessed | tf_op | source)
XLA Modules:
  0.0 516.6 jit_solution(11060390123195442186)
XLA Ops:
  0.0 3.2 dynamic-slice_bitcast_fusion.1
  3.8 6.7 %dynamic-slice_bitcast_fusion.2 = (f32[64,8,256]{2,1,0:T(8,128)}, f32[64,8,256]{2,1,0:T(8,128)}, f32[64,8,256]{2,1,0:T(8,128)}, f32[64,8,256]{2,1,0:T(8,128)}, f...) fusion(f32[1,64,256,256]{3,2,1,0:T(8,128)} %param.6, ...), kind=kLoop, calls=%fused_computation.18 | loop fusion | bytes 17825860 | tf_op jit(solution)/shard_map/dynamic_slice | solution.py:358
  16.6 6.1 %dynamic-slice_bitcast_fusion = f32[64,96,256]{2,1,0:T(8,128)} fusion(f32[1,64,256,256]{3,2,1,0:T(8,128)} %param.6, s32[]{:T(128)S(6)} %select_n.74), kind=kLoop, calls=%fused_computation | loop fusion | bytes 12582916 | tf_op jit(solution)/shard_map/dynamic_slice | solution.py:358
  27.4 12.8 %local_terms.2 = (f32[2,64,16,256]{3,2,1,0:T(8,128)}, f32[2,64,16,256]{3,2,1,0:T(8,128)}) custom-call(s32[7]{0:T(128)} %stack.31.where._.core, f32[256,1]{1,0:T(8,128)} %get-tuple-element.233.lost_a, f32[64,256,256]{2,1,0:T(8,128)} %bitcast.50, bf16[256,512]{1,0:T(8,128)(2,1)} %get-tuple-element.235.c_hi, bf16[256,512]{1,0:T(8,128)(2,1)} %get-tuple-element.236.c_lo, ...), custom_call_target="tpu_custom_call" | custom-call | flops 1000 | bytes 1000 | tf_op jit(solution)/shard_map/local_terms/pallas_call | solution.py:163
  43.5 29.1 %local_terms.3 = (f32[2,64,112,256]{3,2,1,0:T(8,128)}, f32[2,64,112,256]{3,2,1,0:T(8,128)}) custom-call(s32[7]{0:T(128)} %stack.31.where._.core, f32[256,1]{1,0:T(8,128)} %get-tuple-element.233.lost_a, f32[64,256,256]{2,1,0:T(8,128)} %bitcast.51, bf16[256,512]{1,0:T(8,128)(2,1)} %get-tuple-element.235.c_hi, bf16[256,512]{1,0:T(8,128)(2,1)} %get-tuple-element.236.c_lo, ...), custom_call_target="tpu_custom_call" | custom-call | flops 1000 | bytes 1000 | tf_op jit(solution)/shard_map/local_terms/pallas_call | solution.py:163
  73.2 4.0 collective-permute-done.10.refs_5_.refs_7_
  80.9 5.1 first_terms.18
  86.0 4.3 collective-permute-start.13
  90.4 11.8 %collective-permute-done.3.refs_2_ = f32[128,8,256]{2,1,0:T(8,128)} collective-permute-done((f32[128,8,256]{2,1,0:T(8,128)S(1)}, f32[128,8,256]{2,1,0:T(8,128)}, u32[]{:S(2)}, u32[]{:S(2)}) %collective-permute-start.3) | collective-permute-done | bytes 1048608 | tf_op jit(solution)/shard_map/ppermute | solution.py:343
  107.2 5.2 %first_terms.16 = (f32[128,8,256]{2,1,0:T(8,128)}, f32[128,8,256]{2,1,0:T(8,128)}, f32[128,8,256]{2,1,0:T(8,128)}) custom-call(s32[7]{0:T(128)} %stack.31.where._.core, f32[2,256]{1,0:T(2,128)} %get-tuple-element.230.fall, bf16[512,256]{1,0:T(8,128)(2,1)} %get-tuple-element.231.refs_0_, f32[128,8,256]{2,1,0:T(8,128)} %copy-done.17, ...), custom_call_target="tpu_custom_call" | custom-call | flops 1000 | bytes 1000 | tf_op jit(solution)/shard_map/first_terms/pallas_call | solution.py:228
  112.4 3.9 collective-permute-start.14
  118.7 7.1 %collective-permute-done.4.refs_2_ = f32[128,8,256]{2,1,0:T(8,128)S(1)} collective-permute-done((f32[128,8,256]{2,1,0:T(8,128)S(1)}, f32[128,8,256]{2,1,0:T(8,128)S(1)}, u32[]{:S(2)}, u32[]{:S(2)}) %collective-permute-start.4) | collective-permute-done | bytes 1048608 | tf_op jit(solution)/shard_map/ppermute | solution.py:343
  126.3 3.8 collective-permute-done.11.refs_3_
  132.9 5.1 first_terms.17
  138.0 4.0 collective-permute-start.18
  144.3 4.4 collective-permute-done.15.refs_1_.refs_3_
  149.3 4.9 fusion
  158.2 5.1 first_terms.19
  163.3 3.6 collective-permute-start.22
  171.7 3.1 finish.16
  181.3 5.1 first_terms.20
  187.0 3.4 collective-permute-start.26
  193.8 3.1 finish.18
  198.9 3.4 collective-permute-start.29
  202.3 5.1 first_terms.21
  209.8 3.1 collective-permute-start.30
  216.9 3.2 finish.19
  220.5 3.4 collective-permute-start.33
  224.0 5.2 %first_terms.22 = (f32[128,8,256]{2,1,0:T(8,128)}, f32[128,8,256]{2,1,0:T(8,128)}, f32[128,8,256]{2,1,0:T(8,128)}) custom-call(s32[7]{0:T(128)} %stack.31.where._.core, f32[2,256]{1,0:T(2,128)} %get-tuple-element.230.fall, bf16[512,256]{1,0:T(8,128)(2,1)} %get-tuple-element.231.refs_0_, f32[128,8,256]{2,1,0:T(8,128)} %copy-done.6, ...), custom_call_target="tpu_custom_call" | custom-call | flops 1000 | bytes 1000 | tf_op jit(solution)/shard_map/first_terms/pallas_call | solution.py:228
  237.9 3.1 finish.20
  242.2 3.4 collective-permute-start.37
  245.6 5.1 first_terms.23
  259.6 3.1 finish.21
  263.8 3.4 collective-permute-start.41
  267.2 5.1 first_terms.24
  281.2 3.2 finish.22
  285.4 3.4 collective-permute-start.45
  288.8 5.1 first_terms.25
  302.8 3.1 finish.23
  307.0 3.4 collective-permute-start.49
  310.4 5.1 first_terms.26
  318.1 3.1 collective-permute-start.50
  324.6 3.2 finish.24
  328.7 3.4 collective-permute-start.53
  332.2 5.1 first_terms.27
  346.0 3.2 finish.25
  350.3 3.4 collective-permute-start.57
  353.8 5.1 first_terms.28
  367.6 3.2 finish.26
  372.2 3.3 collective-permute-start.61
  375.5 5.1 first_terms.29
  383.2 3.1 collective-permute-start.62
  397.6 5.1 first_terms.30
  402.7 3.2 collective-permute-done.62.lifted
  405.9 3.3 collective-permute-start.65
  412.6 3.1 finish.28
  421.2 5.1 first_terms.31
  434.8 3.1 finish.29
  437.9 13.7 %collective-permute-start.70 = (f32[64,112,256]{2,1,0:T(8,128)}, f32[64,112,256]{2,1,0:T(8,128)S(1)}, u32[]{:S(2)}, u32[]{:S(2)}) collective-permute-start(f32[64,112,256]{2,1,0:T(8,128)} %get-tuple-element.447), channel_id=1, source_target_pairs={{0,8},{8,0},{16,24},{24,16},{1,9},{9,1},{17,25},{25,17},{2,10},{10... | collective-permute-start | bytes 22020104 | tf_op jit(solution)/shard_map/ppermute | solution.py:346
  454.2 24.4 %collective-permute-done.66.lifted = f32[128,8,256]{2,1,0:T(8,128)} collective-permute-done((f32[128,8,256]{2,1,0:T(8,128)}, f32[128,8,256]{2,1,0:T(8,128)}, u32[]{:S(2)}, u32[]{:S(2)}) %collective-permute-start.66) | collective-permute-done | bytes 1048608 | tf_op jit(solution)/shard_map/ppermute | solution.py:352
  481.0 3.1 finish.30
  487.8 11.2 %put.3.refs_4_ = f32[64,256,256]{2,1,0:T(8,128)} custom-call(s32[7]{0:T(128)} %stack.31.where._.core, f32[64,112,256]{2,1,0:T(8,128)} %copy-done.1, f32[64,256,256]{2,1,0:T(8,128)} %get-tuple-element.451._), custom_call_target="tpu_custom_call", output_to_operand_aliasing={{}: (2, {})} | custom-call | flops 1000 | bytes 1000 | tf_op jit(solution)/shard_map/put/pallas_call | solution.py:309
  499.0 6.2 %collective-permute-done.69.refs_1_.refs_3_ = f32[128,8,256]{2,1,0:T(8,128)} collective-permute-done((f32[128,8,256]{2,1,0:T(8,128)}, f32[128,8,256]{2,1,0:T(8,128)}, u32[]{:S(2)}, u32[]{:S(2)}) %collective-permute-start.69) | collective-permute-done | bytes 1048608 | tf_op jit(solution)/shard_map/ppermute | solution.py:355
  505.2 3.1 finish.31
  (286 shorter events, 175.1 us)
Async XLA Ops:
  3.2 24.2 %collective-permute-start = (f32[64,32,256]{2,1,0:T(8,128)}, f32[64,32,256]{2,1,0:T(8,128)S(1)}, u32[]{:S(2)}, u32[]{:S(2)}) collective-permute-start(f32[64,32,256]{2,1,0:T(8,128)} %dynamic-slice_bitcast_fusion.1), channel_id=1, source_target_pairs={{0,8},{8,0},{16,24},{24,16},{1,9},{9,1},{17,25},{25,17},{2,10},{10... | collective-permute-start | bytes 6291464 | tf_op jit(solution)/shard_map/ppermute | solution.py:346
  10.6 62.0 %collective-permute-start.2 = (f32[64,8,256]{2,1,0:T(8,128)}, f32[64,8,256]{2,1,0:T(8,128)}, u32[]{:S(2)}, u32[]{:S(2)}) collective-permute-start(f32[64,8,256]{2,1,0:T(8,128)} %get-tuple-element.470), channel_id=1, source_target_pairs={{0,16},{8,24},{16,0},{24,8},{1,17},{9,25},{17,1},{25,9},{2,18},{10... | collective-permute-start | bytes 1572872 | tf_op jit(solution)/shard_map/ppermute | solution.py:343
  11.8 60.7 %collective-permute-start.8 = (f32[64,8,256]{2,1,0:T(8,128)}, f32[64,8,256]{2,1,0:T(8,128)}, u32[]{:S(2)}, u32[]{:S(2)}) collective-permute-start(f32[64,8,256]{2,1,0:T(8,128)} %get-tuple-element.470), channel_id=1, source_target_pairs={{2,0},{3,1},{4,2},{5,3},{6,4},{7,5},{10,8},{11,9},{12,10},{13,11},... | collective-permute-start | bytes 1572872 | tf_op jit(solution)/shard_map/ppermute | solution.py:349
  13.9 58.7 %collective-permute-start.7 = (f32[64,8,256]{2,1,0:T(8,128)}, f32[64,8,256]{2,1,0:T(8,128)}, u32[]{:S(2)}, u32[]{:S(2)}) collective-permute-start(f32[64,8,256]{2,1,0:T(8,128)} %get-tuple-element.455), channel_id=1, source_target_pairs={{0,24},{8,16},{16,8},{24,0},{1,25},{9,17},{17,9},{25,1},{2,26},{10... | collective-permute-start | bytes 1572872 | tf_op jit(solution)/shard_map/ppermute | solution.py:385
  14.7 57.9 %collective-permute-start.9 = (f32[64,8,256]{2,1,0:T(8,128)}, f32[64,8,256]{2,1,0:T(8,128)}, u32[]{:S(2)}, u32[]{:S(2)}) collective-permute-start(f32[64,8,256]{2,1,0:T(8,128)} %get-tuple-element.455), channel_id=1, source_target_pairs={{2,8},{3,9},{4,10},{5,11},{6,12},{7,13},{10,0},{11,1},{12,2},{13,3... | collective-permute-start | bytes 1572872 | tf_op jit(solution)/shard_map/ppermute | solution.py:388
  77.2 53.2 %collective-permute-start.12 = (f32[2,64,112,256]{3,2,1,0:T(8,128)}, f32[2,64,112,256]{3,2,1,0:T(8,128)}, u32[]{:S(2)}, u32[]{:S(2)}) collective-permute-start(f32[2,64,112,256]{3,2,1,0:T(8,128)} %get-tuple-element.253), channel_id=1, source_target_pairs={{0,8},{8,0},{16,24},{24,16},{1,9},{9,1},{17,25},{25,17},{2,10},{10... | collective-permute-start | bytes 44040200 | tf_op jit(solution)/shard_map/ppermute | solution.py:346
  77.6 71.7 %collective-permute-start.1 = (f32[64,96,256]{2,1,0:T(8,128)}, f32[64,96,256]{2,1,0:T(8,128)}, u32[]{:S(2)}, u32[]{:S(2)}) collective-permute-start(f32[64,96,256]{2,1,0:T(8,128)} %dynamic-slice_bitcast_fusion), channel_id=1, source_target_pairs={{0,8},{8,0},{16,24},{24,16},{1,9},{9,1},{17,25},{25,17},{2,10},{10... | collective-permute-start | bytes 18874376 | tf_op jit(solution)/shard_map/ppermute | solution.py:346
  77.7 24.5 %collective-permute-start.3 = (f32[128,8,256]{2,1,0:T(8,128)S(1)}, f32[128,8,256]{2,1,0:T(8,128)}, u32[]{:S(2)}, u32[]{:S(2)}) collective-permute-start(f32[128,8,256]{2,1,0:T(8,128)S(1)} %get-tuple-element.245.refs_1_), channel_id=1, source_target_pairs={{0,16},{8,24},{16,0},{24,8},{1,17},{9,25},{17,1},{25,9},{2,18},{10... | collective-permute-start | bytes 3145736 | tf_op jit(solution)/shard_map/ppermute | solution.py:343
  78.9 26.1 %collective-permute-start.6 = (f32[128,8,256]{2,1,0:T(8,128)S(1)}, f32[128,8,256]{2,1,0:T(8,128)}, u32[]{:S(2)}, u32[]{:S(2)}) collective-permute-start(f32[128,8,256]{2,1,0:T(8,128)S(1)} %get-tuple-element.245.refs_1_), channel_id=1, source_target_pairs={{2,0},{3,1},{4,2},{5,3},{6,4},{7,5},{10,8},{11,9},{12,10},{13,11},... | collective-permute-start | bytes 3145736 | tf_op jit(solution)/shard_map/ppermute | solution.py:349
  86.0 26.4 %collective-permute-start.13 = (f32[128,8,256]{2,1,0:T(8,128)}, f32[128,8,256]{2,1,0:T(8,128)}, u32[]{:S(2)}, u32[]{:S(2)}) collective-permute-start(f32[128,8,256]{2,1,0:T(8,128)} %get-tuple-element.256), channel_id=1, source_target_pairs={{1,3},{3,5},{5,7},{9,11},{11,13},{13,15},{17,19},{19,21},{21,23},{... | collective-permute-start | bytes 3145736 | tf_op jit(solution)/shard_map/ppermute | solution.py:352
  102.2 23.6 %collective-permute-start.4 = (f32[128,8,256]{2,1,0:T(8,128)S(1)}, f32[128,8,256]{2,1,0:T(8,128)S(1)}, u32[]{:S(2)}, u32[]{:S(2)}) collective-permute-start(f32[128,8,256]{2,1,0:T(8,128)S(1)} %pad_maximum_fusion.14.refs_1_), channel_id=1, source_target_pairs={{0,16},{8,24},{16,0},{24,8},{1,17},{9,25},{17,1},{25,9},{2,18},{10... | collective-permute-start | bytes 3145736 | tf_op jit(solution)/shard_map/ppermute | solution.py:343
  105.0 25.1 %collective-permute-start.11 = (f32[128,8,256]{2,1,0:T(8,128)S(1)}, f32[128,8,256]{2,1,0:T(8,128)S(1)}, u32[]{:S(2)}, u32[]{:S(2)}) collective-permute-start(f32[128,8,256]{2,1,0:T(8,128)S(1)} %pad_maximum_fusion.14.refs_1_), channel_id=1, source_target_pairs={{2,0},{3,1},{4,2},{5,3},{6,4},{7,5},{10,8},{11,9},{12,10},{13,11},... | collective-permute-start | bytes 3145736 | tf_op jit(solution)/shard_map/ppermute | solution.py:349
  112.4 25.6 %collective-permute-start.14 = (f32[128,8,256]{2,1,0:T(8,128)}, f32[128,8,256]{2,1,0:T(8,128)}, u32[]{:S(2)}, u32[]{:S(2)}) collective-permute-start(f32[128,8,256]{2,1,0:T(8,128)} %get-tuple-element.257), channel_id=1, source_target_pairs={{1,3},{3,5},{5,7},{9,11},{11,13},{13,15},{17,19},{19,21},{21,23},{... | collective-permute-start | bytes 3145736 | tf_op jit(solution)/shard_map/ppermute | solution.py:352
  125.8 22.9 %collective-permute-start.15 = (f32[128,8,256]{2,1,0:T(8,128)}, f32[128,8,256]{2,1,0:T(8,128)S(1)}, u32[]{:S(2)}, u32[]{:S(2)}) collective-permute-start(f32[128,8,256]{2,1,0:T(8,128)} %turn.17), channel_id=1, source_target_pairs={{0,1},{1,0},{2,3},{3,2},{4,5},{5,4},{6,7},{7,6},{8,9},{9,8},{10,11... | collective-permute-start | bytes 3145736 | tf_op jit(solution)/shard_map/ppermute | solution.py:355
  130.1 24.2 %collective-permute-start.5 = (f32[128,8,256]{2,1,0:T(8,128)S(1)}, f32[128,8,256]{2,1,0:T(8,128)}, u32[]{:S(2)}, u32[]{:S(2)}) collective-permute-start(f32[128,8,256]{2,1,0:T(8,128)S(1)} %pad_maximum_fusion.13.refs_1_), channel_id=1, source_target_pairs={{0,16},{8,24},{16,0},{24,8},{1,17},{9,25},{17,1},{25,9},{2,18},{10... | collective-permute-start | bytes 3145736 | tf_op jit(solution)/shard_map/ppermute | solution.py:343
  130.4 27.8 %collective-permute-start.17 = (f32[128,8,256]{2,1,0:T(8,128)S(1)}, f32[128,8,256]{2,1,0:T(8,128)}, u32[]{:S(2)}, u32[]{:S(2)}) collective-permute-start(f32[128,8,256]{2,1,0:T(8,128)S(1)} %pad_maximum_fusion.13.refs_1_), channel_id=1, source_target_pairs={{2,0},{3,1},{4,2},{5,3},{6,4},{7,5},{10,8},{11,9},{12,10},{13,11},... | collective-permute-start | bytes 3145736 | tf_op jit(solution)/shard_map/ppermute | solution.py:349
  138.0 25.4 %collective-permute-start.18 = (f32[128,8,256]{2,1,0:T(8,128)}, f32[128,8,256]{2,1,0:T(8,128)}, u32[]{:S(2)}, u32[]{:S(2)}) collective-permute-start(f32[128,8,256]{2,1,0:T(8,128)} %get-tuple-element.267), channel_id=1, source_target_pairs={{1,3},{3,5},{5,7},{9,11},{11,13},{13,15},{17,19},{19,21},{21,23},{... | collective-permute-start | bytes 3145736 | tf_op jit(solution)/shard_map/ppermute | solution.py:352
  148.7 22.1 %collective-permute-start.19 = (f32[128,8,256]{2,1,0:T(8,128)}, f32[128,8,256]{2,1,0:T(8,128)S(1)}, u32[]{:S(2)}, u32[]{:S(2)}) collective-permute-start(f32[128,8,256]{2,1,0:T(8,128)} %turn.16), channel_id=1, source_target_pairs={{0,1},{1,0},{2,3},{3,2},{4,5},{5,4},{6,7},{7,6},{8,9},{9,8},{10,11... | collective-permute-start | bytes 3145736 | tf_op jit(solution)/shard_map/ppermute | solution.py:355
  154.3 23.5 %collective-permute-start.16 = (f32[128,8,256]{2,1,0:T(8,128)S(1)}, f32[128,8,256]{2,1,0:T(8,128)}, u32[]{:S(2)}, u32[]{:S(2)}) collective-permute-start(f32[128,8,256]{2,1,0:T(8,128)S(1)} %pad_maximum_fusion.12.refs_1_), channel_id=1, source_target_pairs={{0,16},{8,24},{16,0},{24,8},{1,17},{9,25},{17,1},{25,9},{2,18},{10... | collective-permute-start | bytes 3145736 | tf_op jit(solution)/shard_map/ppermute | solution.py:343
  155.4 25.9 %collective-permute-start.21 = (f32[128,8,256]{2,1,0:T(8,128)S(1)}, f32[128,8,256]{2,1,0:T(8,128)}, u32[]{:S(2)}, u32[]{:S(2)}) collective-permute-start(f32[128,8,256]{2,1,0:T(8,128)S(1)} %pad_maximum_fusion.12.refs_1_), channel_id=1, source_target_pairs={{2,0},{3,1},{4,2},{5,3},{6,4},{7,5},{10,8},{11,9},{12,10},{13,11},... | collective-permute-start | bytes 3145736 | tf_op jit(solution)/shard_map/ppermute | solution.py:349
  163.3 23.7 %collective-permute-start.22 = (f32[128,8,256]{2,1,0:T(8,128)}, f32[128,8,256]{2,1,0:T(8,128)}, u32[]{:S(2)}, u32[]{:S(2)}) collective-permute-start(f32[128,8,256]{2,1,0:T(8,128)} %get-tuple-element.282), channel_id=1, source_target_pairs={{1,3},{3,5},{5,7},{9,11},{11,13},{13,15},{17,19},{19,21},{21,23},{... | collective-permute-start | bytes 3145736 | tf_op jit(solution)/shard_map/ppermute | solution.py:352
  170.9 22.0 %collective-permute-start.23 = (f32[128,8,256]{2,1,0:T(8,128)}, f32[128,8,256]{2,1,0:T(8,128)S(1)}, u32[]{:S(2)}, u32[]{:S(2)}) collective-permute-start(f32[128,8,256]{2,1,0:T(8,128)} %turn.18), channel_id=1, source_target_pairs={{0,1},{1,0},{2,3},{3,2},{4,5},{5,4},{6,7},{7,6},{8,9},{9,8},{10,11... | collective-permute-start | bytes 3145736 | tf_op jit(solution)/shard_map/ppermute | solution.py:355
  178.4 24.0 %collective-permute-start.25 = (f32[128,8,256]{2,1,0:T(8,128)S(1)}, f32[128,8,256]{2,1,0:T(8,128)}, u32[]{:S(2)}, u32[]{:S(2)}) collective-permute-start(f32[128,8,256]{2,1,0:T(8,128)S(1)} %pad_maximum_fusion.11.refs_1_), channel_id=1, source_target_pairs={{2,0},{3,1},{4,2},{5,3},{6,4},{7,5},{10,8},{11,9},{12,10},{13,11},... | collective-permute-start | bytes 3145736 | tf_op jit(solution)/shard_map/ppermute | solution.py:349
  187.0 22.8 %collective-permute-start.26 = (f32[128,8,256]{2,1,0:T(8,128)}, f32[128,8,256]{2,1,0:T(8,128)}, u32[]{:S(2)}, u32[]{:S(2)}) collective-permute-start(f32[128,8,256]{2,1,0:T(8,128)} %get-tuple-element.296), channel_id=1, source_target_pairs={{1,3},{3,5},{5,7},{9,11},{11,13},{13,15},{17,19},{19,21},{21,23},{... | collective-permute-start | bytes 3145736 | tf_op jit(solution)/shard_map/ppermute | solution.py:352
  192.8 22.5 %collective-permute-start.27 = (f32[128,8,256]{2,1,0:T(8,128)}, f32[128,8,256]{2,1,0:T(8,128)S(1)}, u32[]{:S(2)}, u32[]{:S(2)}) collective-permute-start(f32[128,8,256]{2,1,0:T(8,128)} %turn.19), channel_id=1, source_target_pairs={{0,1},{1,0},{2,3},{3,2},{4,5},{5,4},{6,7},{7,6},{8,9},{9,8},{10,11... | collective-permute-start | bytes 3145736 | tf_op jit(solution)/shard_map/ppermute | solution.py:355
  198.9 25.0 %collective-permute-start.29 = (f32[128,8,256]{2,1,0:T(8,128)S(1)}, f32[128,8,256]{2,1,0:T(8,128)}, u32[]{:S(2)}, u32[]{:S(2)}) collective-permute-start(f32[128,8,256]{2,1,0:T(8,128)S(1)} %pad_maximum_fusion.10.refs_1_), channel_id=1, source_target_pairs={{2,0},{3,1},{4,2},{5,3},{6,4},{7,5},{10,8},{11,9},{12,10},{13,11},... | collective-permute-start | bytes 3145736 | tf_op jit(solution)/shard_map/ppermute | solution.py:349
  209.8 21.7 %collective-permute-start.30 = (f32[128,8,256]{2,1,0:T(8,128)}, f32[128,8,256]{2,1,0:T(8,128)S(1)}, u32[]{:S(2)}, u32[]{:S(2)}) collective-permute-start(f32[128,8,256]{2,1,0:T(8,128)} %get-tuple-element.310), channel_id=1, source_target_pairs={{1,3},{3,5},{5,7},{9,11},{11,13},{13,15},{17,19},{19,21},{21,23},{... | collective-permute-start | bytes 3145736 | tf_op jit(solution)/shard_map/ppermute | solution.py:352
  220.4 21.6 %collective-permute-start.28 = (f32[128,8,256]{2,1,0:T(8,128)S(1)}, f32[128,8,256]{2,1,0:T(8,128)}, u32[]{:S(2)}, u32[]{:S(2)}) collective-permute-start(f32[128,8,256]{2,1,0:T(8,128)S(1)} %pad_maximum_fusion.9.refs_1_), channel_id=1, source_target_pairs={{0,16},{8,24},{16,0},{24,8},{1,17},{9,25},{17,1},{25,9},{2,18},{10... | collective-permute-start | bytes 3145736 | tf_op jit(solution)/shard_map/ppermute | solution.py:343
  220.5 25.0 %collective-permute-start.33 = (f32[128,8,256]{2,1,0:T(8,128)S(1)}, f32[128,8,256]{2,1,0:T(8,128)}, u32[]{:S(2)}, u32[]{:S(2)}) collective-permute-start(f32[128,8,256]{2,1,0:T(8,128)S(1)} %pad_maximum_fusion.9.refs_1_), channel_id=1, source_target_pairs={{2,0},{3,1},{4,2},{5,3},{6,4},{7,5},{10,8},{11,9},{12,10},{13,11},... | collective-permute-start | bytes 3145736 | tf_op jit(solution)/shard_map/ppermute | solution.py:349
  231.5 21.7 %collective-permute-start.34 = (f32[128,8,256]{2,1,0:T(8,128)}, f32[128,8,256]{2,1,0:T(8,128)}, u32[]{:S(2)}, u32[]{:S(2)}) collective-permute-start(f32[128,8,256]{2,1,0:T(8,128)} %get-tuple-element.324), channel_id=1, source_target_pairs={{1,3},{3,5},{5,7},{9,11},{11,13},{13,15},{17,19},{19,21},{21,23},{... | collective-permute-start | bytes 3145736 | tf_op jit(solution)/shard_map/ppermute | solution.py:352
  236.9 21.7 %collective-permute-start.35 = (f32[128,8,256]{2,1,0:T(8,128)}, f32[128,8,256]{2,1,0:T(8,128)S(1)}, u32[]{:S(2)}, u32[]{:S(2)}) collective-permute-start(f32[128,8,256]{2,1,0:T(8,128)} %turn.21), channel_id=1, source_target_pairs={{0,1},{1,0},{2,3},{3,2},{4,5},{5,4},{6,7},{7,6},{8,9},{9,8},{10,11... | collective-permute-start | bytes 3145736 | tf_op jit(solution)/shard_map/ppermute | solution.py:355
  242.0 21.6 %collective-permute-start.32 = (f32[128,8,256]{2,1,0:T(8,128)S(1)}, f32[128,8,256]{2,1,0:T(8,128)}, u32[]{:S(2)}, u32[]{:S(2)}) collective-permute-start(f32[128,8,256]{2,1,0:T(8,128)S(1)} %pad_maximum_fusion.8.refs_1_), channel_id=1, source_target_pairs={{0,16},{8,24},{16,0},{24,8},{1,17},{9,25},{17,1},{25,9},{2,18},{10... | collective-permute-start | bytes 3145736 | tf_op jit(solution)/shard_map/ppermute | solution.py:343
  242.2 25.0 %collective-permute-start.37 = (f32[128,8,256]{2,1,0:T(8,128)S(1)}, f32[128,8,256]{2,1,0:T(8,128)}, u32[]{:S(2)}, u32[]{:S(2)}) collective-permute-start(f32[128,8,256]{2,1,0:T(8,128)S(1)} %pad_maximum_fusion.8.refs_1_), channel_id=1, source_target_pairs={{2,0},{3,1},{4,2},{5,3},{6,4},{7,5},{10,8},{11,9},{12,10},{13,11},... | collective-permute-start | bytes 3145736 | tf_op jit(solution)/shard_map/ppermute | solution.py:349
  253.3 21.6 %collective-permute-start.38 = (f32[128,8,256]{2,1,0:T(8,128)}, f32[128,8,256]{2,1,0:T(8,128)}, u32[]{:S(2)}, u32[]{:S(2)}) collective-permute-start(f32[128,8,256]{2,1,0:T(8,128)} %get-tuple-element.338), channel_id=1, source_target_pairs={{1,3},{3,5},{5,7},{9,11},{11,13},{13,15},{17,19},{19,21},{21,23},{... | collective-permute-start | bytes 3145736 | tf_op jit(solution)/shard_map/ppermute | solution.py:352
  258.6 21.6 %collective-permute-start.39 = (f32[128,8,256]{2,1,0:T(8,128)}, f32[128,8,256]{2,1,0:T(8,128)S(1)}, u32[]{:S(2)}, u32[]{:S(2)}) collective-permute-start(f32[128,8,256]{2,1,0:T(8,128)} %turn.22), channel_id=1, source_target_pairs={{0,1},{1,0},{2,3},{3,2},{4,5},{5,4},{6,7},{7,6},{8,9},{9,8},{10,11... | collective-permute-start | bytes 3145736 | tf_op jit(solution)/shard_map/ppermute | solution.py:355
  263.6 21.6 %collective-permute-start.36 = (f32[128,8,256]{2,1,0:T(8,128)S(1)}, f32[128,8,256]{2,1,0:T(8,128)}, u32[]{:S(2)}, u32[]{:S(2)}) collective-permute-start(f32[128,8,256]{2,1,0:T(8,128)S(1)} %pad_maximum_fusion.7.refs_1_), channel_id=1, source_target_pairs={{0,16},{8,24},{16,0},{24,8},{1,17},{9,25},{17,1},{25,9},{2,18},{10... | collective-permute-start | bytes 3145736 | tf_op jit(solution)/shard_map/ppermute | solution.py:343
  263.8 25.0 %collective-permute-start.41 = (f32[128,8,256]{2,1,0:T(8,128)S(1)}, f32[128,8,256]{2,1,0:T(8,128)}, u32[]{:S(2)}, u32[]{:S(2)}) collective-permute-start(f32[128,8,256]{2,1,0:T(8,128)S(1)} %pad_maximum_fusion.7.refs_1_), channel_id=1, source_target_pairs={{2,0},{3,1},{4,2},{5,3},{6,4},{7,5},{10,8},{11,9},{12,10},{13,11},... | collective-permute-start | bytes 3145736 | tf_op jit(solution)/shard_map/ppermute | solution.py:349
  274.9 21.6 %collective-permute-start.42 = (f32[128,8,256]{2,1,0:T(8,128)}, f32[128,8,256]{2,1,0:T(8,128)}, u32[]{:S(2)}, u32[]{:S(2)}) collective-permute-start(f32[128,8,256]{2,1,0:T(8,128)} %get-tuple-element.352), channel_id=1, source_target_pairs={{1,3},{3,5},{5,7},{9,11},{11,13},{13,15},{17,19},{19,21},{21,23},{... | collective-permute-start | bytes 3145736 | tf_op jit(solution)/shard_map/ppermute | solution.py:352
  285.2 21.6 %collective-permute-start.40 = (f32[128,8,256]{2,1,0:T(8,128)S(1)}, f32[128,8,256]{2,1,0:T(8,128)S(1)}, u32[]{:S(2)}, u32[]{:S(2)}) collective-permute-start(f32[128,8,256]{2,1,0:T(8,128)S(1)} %pad_maximum_fusion.6.refs_1_), channel_id=1, source_target_pairs={{0,16},{8,24},{16,0},{24,8},{1,17},{9,25},{17,1},{25,9},{2,18},{10... | collective-permute-start | bytes 3145736 | tf_op jit(solution)/shard_map/ppermute | solution.py:343
  285.4 25.0 %collective-permute-start.45 = (f32[128,8,256]{2,1,0:T(8,128)S(1)}, f32[128,8,256]{2,1,0:T(8,128)}, u32[]{:S(2)}, u32[]{:S(2)}) collective-permute-start(f32[128,8,256]{2,1,0:T(8,128)S(1)} %pad_maximum_fusion.6.refs_1_), channel_id=1, source_target_pairs={{2,0},{3,1},{4,2},{5,3},{6,4},{7,5},{10,8},{11,9},{12,10},{13,11},... | collective-permute-start | bytes 3145736 | tf_op jit(solution)/shard_map/ppermute | solution.py:349
  296.5 21.6 %collective-permute-start.46 = (f32[128,8,256]{2,1,0:T(8,128)}, f32[128,8,256]{2,1,0:T(8,128)}, u32[]{:S(2)}, u32[]{:S(2)}) collective-permute-start(f32[128,8,256]{2,1,0:T(8,128)} %get-tuple-element.366), channel_id=1, source_target_pairs={{1,3},{3,5},{5,7},{9,11},{11,13},{13,15},{17,19},{19,21},{21,23},{... | collective-permute-start | bytes 3145736 | tf_op jit(solution)/shard_map/ppermute | solution.py:352
  301.8 21.9 %collective-permute-start.47 = (f32[128,8,256]{2,1,0:T(8,128)}, f32[128,8,256]{2,1,0:T(8,128)S(1)}, u32[]{:S(2)}, u32[]{:S(2)}) collective-permute-start(f32[128,8,256]{2,1,0:T(8,128)} %turn.24), channel_id=1, source_target_pairs={{0,1},{1,0},{2,3},{3,2},{4,5},{5,4},{6,7},{7,6},{8,9},{9,8},{10,11... | collective-permute-start | bytes 3145736 | tf_op jit(solution)/shard_map/ppermute | solution.py:355
  306.9 21.7 %collective-permute-start.44 = (f32[128,8,256]{2,1,0:T(8,128)S(1)}, f32[128,8,256]{2,1,0:T(8,128)}, u32[]{:S(2)}, u32[]{:S(2)}) collective-permute-start(f32[128,8,256]{2,1,0:T(8,128)S(1)} %pad_maximum_fusion.5.refs_1_), channel_id=1, source_target_pairs={{0,16},{8,24},{16,0},{24,8},{1,17},{9,25},{17,1},{25,9},{2,18},{10... | collective-permute-start | bytes 3145736 | tf_op jit(solution)/shard_map/ppermute | solution.py:343
  307.0 25.1 %collective-permute-start.49 = (f32[128,8,256]{2,1,0:T(8,128)S(1)}, f32[128,8,256]{2,1,0:T(8,128)}, u32[]{:S(2)}, u32[]{:S(2)}) collective-permute-start(f32[128,8,256]{2,1,0:T(8,128)S(1)} %pad_maximum_fusion.5.refs_1_), channel_id=1, source_target_pairs={{2,0},{3,1},{4,2},{5,3},{6,4},{7,5},{10,8},{11,9},{12,10},{13,11},... | collective-permute-start | bytes 3145736 | tf_op jit(solution)/shard_map/ppermute | solution.py:349
  328.6 21.6 %collective-permute-start.48 = (f32[128,8,256]{2,1,0:T(8,128)S(1)}, f32[128,8,256]{2,1,0:T(8,128)S(1)}, u32[]{:S(2)}, u32[]{:S(2)}) collective-permute-start(f32[128,8,256]{2,1,0:T(8,128)S(1)} %pad_maximum_fusion.4.refs_1_), channel_id=1, source_target_pairs={{0,16},{8,24},{16,0},{24,8},{1,17},{9,25},{17,1},{25,9},{2,18},{10... | collective-permute-start | bytes 3145736 | tf_op jit(solution)/shard_map/ppermute | solution.py:343
  328.7 25.0 %collective-permute-start.53 = (f32[128,8,256]{2,1,0:T(8,128)S(1)}, f32[128,8,256]{2,1,0:T(8,128)}, u32[]{:S(2)}, u32[]{:S(2)}) collective-permute-start(f32[128,8,256]{2,1,0:T(8,128)S(1)} %pad_maximum_fusion.4.refs_1_), channel_id=1, source_target_pairs={{2,0},{3,1},{4,2},{5,3},{6,4},{7,5},{10,8},{11,9},{12,10},{13,11},... | collective-permute-start | bytes 3145736 | tf_op jit(solution)/shard_map/ppermute | solution.py:349
  339.7 21.6 %collective-permute-start.54 = (f32[128,8,256]{2,1,0:T(8,128)}, f32[128,8,256]{2,1,0:T(8,128)}, u32[]{:S(2)}, u32[]{:S(2)}) collective-permute-start(f32[128,8,256]{2,1,0:T(8,128)} %get-tuple-element.394), channel_id=1, source_target_pairs={{1,3},{3,5},{5,7},{9,11},{11,13},{13,15},{17,19},{19,21},{21,23},{... | collective-permute-start | bytes 3145736 | tf_op jit(solution)/shard_map/ppermute | solution.py:352
  350.2 21.7 %collective-permute-start.52 = (f32[128,8,256]{2,1,0:T(8,128)S(1)}, f32[128,8,256]{2,1,0:T(8,128)}, u32[]{:S(2)}, u32[]{:S(2)}) collective-permute-start(f32[128,8,256]{2,1,0:T(8,128)S(1)} %pad_maximum_fusion.3.refs_1_), channel_id=1, source_target_pairs={{0,16},{8,24},{16,0},{24,8},{1,17},{9,25},{17,1},{25,9},{2,18},{10... | collective-permute-start | bytes 3145736 | tf_op jit(solution)/shard_map/ppermute | solution.py:343
  350.3 25.1 %collective-permute-start.57 = (f32[128,8,256]{2,1,0:T(8,128)S(1)}, f32[128,8,256]{2,1,0:T(8,128)}, u32[]{:S(2)}, u32[]{:S(2)}) collective-permute-start(f32[128,8,256]{2,1,0:T(8,128)S(1)} %pad_maximum_fusion.3.refs_1_), channel_id=1, source_target_pairs={{2,0},{3,1},{4,2},{5,3},{6,4},{7,5},{10,8},{11,9},{12,10},{13,11},... | collective-permute-start | bytes 3145736 | tf_op jit(solution)/shard_map/ppermute | solution.py:349
  361.3 21.9 %collective-permute-start.58 = (f32[128,8,256]{2,1,0:T(8,128)}, f32[128,8,256]{2,1,0:T(8,128)}, u32[]{:S(2)}, u32[]{:S(2)}) collective-permute-start(f32[128,8,256]{2,1,0:T(8,128)} %get-tuple-element.408), channel_id=1, source_target_pairs={{1,3},{3,5},{5,7},{9,11},{11,13},{13,15},{17,19},{19,21},{21,23},{... | collective-permute-start | bytes 3145736 | tf_op jit(solution)/shard_map/ppermute | solution.py:352
  366.6 22.2 %collective-permute-start.59 = (f32[128,8,256]{2,1,0:T(8,128)}, f32[128,8,256]{2,1,0:T(8,128)S(1)}, u32[]{:S(2)}, u32[]{:S(2)}) collective-permute-start(f32[128,8,256]{2,1,0:T(8,128)} %turn.27), channel_id=1, source_target_pairs={{0,1},{1,0},{2,3},{3,2},{4,5},{5,4},{6,7},{7,6},{8,9},{9,8},{10,11... | collective-permute-start | bytes 3145736 | tf_op jit(solution)/shard_map/ppermute | solution.py:355
  371.9 22.3 %collective-permute-start.56 = (f32[128,8,256]{2,1,0:T(8,128)S(1)}, f32[128,8,256]{2,1,0:T(8,128)S(1)}, u32[]{:S(2)}, u32[]{:S(2)}) collective-permute-start(f32[128,8,256]{2,1,0:T(8,128)S(1)} %pad_maximum_fusion.2.refs_1_), channel_id=1, source_target_pairs={{0,16},{8,24},{16,0},{24,8},{1,17},{9,25},{17,1},{25,9},{2,18},{10... | collective-permute-start | bytes 3145736 | tf_op jit(solution)/shard_map/ppermute | solution.py:343
  372.2 25.4 %collective-permute-start.61 = (f32[128,8,256]{2,1,0:T(8,128)S(1)}, f32[128,8,256]{2,1,0:T(8,128)}, u32[]{:S(2)}, u32[]{:S(2)}) collective-permute-start(f32[128,8,256]{2,1,0:T(8,128)S(1)} %pad_maximum_fusion.2.refs_1_), channel_id=1, source_target_pairs={{2,0},{3,1},{4,2},{5,3},{6,4},{7,5},{10,8},{11,9},{12,10},{13,11},... | collective-permute-start | bytes 3145736 | tf_op jit(solution)/shard_map/ppermute | solution.py:349
  383.2 22.7 %collective-permute-start.62 = (f32[128,8,256]{2,1,0:T(8,128)}, f32[128,8,256]{2,1,0:T(8,128)}, u32[]{:S(2)}, u32[]{:S(2)}) collective-permute-start(f32[128,8,256]{2,1,0:T(8,128)} %get-tuple-element.422), channel_id=1, source_target_pairs={{1,3},{3,5},{5,7},{9,11},{11,13},{13,15},{17,19},{19,21},{21,23},{... | collective-permute-start | bytes 3145736 | tf_op jit(solution)/shard_map/ppermute | solution.py:352
  388.8 22.8 %collective-permute-start.63 = (f32[128,8,256]{2,1,0:T(8,128)}, f32[128,8,256]{2,1,0:T(8,128)S(1)}, u32[]{:S(2)}, u32[]{:S(2)}) collective-permute-start(f32[128,8,256]{2,1,0:T(8,128)} %turn.28), channel_id=1, source_target_pairs={{0,1},{1,0},{2,3},{3,2},{4,5},{5,4},{6,7},{7,6},{8,9},{9,8},{10,11... | collective-permute-start | bytes 3145736 | tf_op jit(solution)/shard_map/ppermute | solution.py:355
  394.2 23.0 %collective-permute-start.60 = (f32[128,8,256]{2,1,0:T(8,128)S(1)}, f32[128,8,256]{2,1,0:T(8,128)S(1)}, u32[]{:S(2)}, u32[]{:S(2)}) collective-permute-start(f32[128,8,256]{2,1,0:T(8,128)S(1)} %pad_maximum_fusion.1.refs_1_), channel_id=1, source_target_pairs={{0,16},{8,24},{16,0},{24,8},{1,17},{9,25},{17,1},{25,9},{2,18},{10... | collective-permute-start | bytes 3145736 | tf_op jit(solution)/shard_map/ppermute | solution.py:343
  394.7 25.5 %collective-permute-start.64 = (f32[128,8,256]{2,1,0:T(8,128)S(1)}, f32[128,8,256]{2,1,0:T(8,128)S(1)}, u32[]{:S(2)}, u32[]{:S(2)}) collective-permute-start(f32[128,8,256]{2,1,0:T(8,128)S(1)} %pad_maximum_fusion.1.refs_1_), channel_id=1, source_target_pairs={{2,0},{3,1},{4,2},{5,3},{6,4},{7,5},{10,8},{11,9},{12,10},{13,11},... | collective-permute-start | bytes 3145736 | tf_op jit(solution)/shard_map/ppermute | solution.py:349
  405.9 23.4 %collective-permute-start.65 = (f32[128,8,256]{2,1,0:T(8,128)}, f32[128,8,256]{2,1,0:T(8,128)S(1)}, u32[]{:S(2)}, u32[]{:S(2)}) collective-permute-start(f32[128,8,256]{2,1,0:T(8,128)} %get-tuple-element.436), channel_id=1, source_target_pairs={{1,3},{3,5},{5,7},{9,11},{11,13},{13,15},{17,19},{19,21},{21,23},{... | collective-permute-start | bytes 3145736 | tf_op jit(solution)/shard_map/ppermute | solution.py:352
  411.6 22.2 %collective-permute-start.67 = (f32[128,8,256]{2,1,0:T(8,128)}, f32[128,8,256]{2,1,0:T(8,128)S(1)}, u32[]{:S(2)}, u32[]{:S(2)}) collective-permute-start(f32[128,8,256]{2,1,0:T(8,128)} %turn.29), channel_id=1, source_target_pairs={{0,1},{1,0},{2,3},{3,2},{4,5},{5,4},{6,7},{7,6},{8,9},{9,8},{10,11... | collective-permute-start | bytes 3145736 | tf_op jit(solution)/shard_map/ppermute | solution.py:355
  437.9 47.0 %collective-permute-start.70 = (f32[64,112,256]{2,1,0:T(8,128)}, f32[64,112,256]{2,1,0:T(8,128)S(1)}, u32[]{:S(2)}, u32[]{:S(2)}) collective-permute-start(f32[64,112,256]{2,1,0:T(8,128)} %get-tuple-element.447), channel_id=1, source_target_pairs={{0,8},{8,0},{16,24},{24,16},{1,9},{9,1},{17,25},{25,17},{2,10},{10... | collective-permute-start | bytes 22020104 | tf_op jit(solution)/shard_map/ppermute | solution.py:346
  451.6 27.0 %collective-permute-start.66 = (f32[128,8,256]{2,1,0:T(8,128)}, f32[128,8,256]{2,1,0:T(8,128)}, u32[]{:S(2)}, u32[]{:S(2)}) collective-permute-start(f32[128,8,256]{2,1,0:T(8,128)} %get-tuple-element.437), channel_id=1, source_target_pairs={{1,3},{3,5},{5,7},{9,11},{11,13},{13,15},{17,19},{19,21},{21,23},{... | collective-permute-start | bytes 3145736 | tf_op jit(solution)/shard_map/ppermute | solution.py:352
  454.1 26.9 %collective-permute-start.68 = (f32[128,8,256]{2,1,0:T(8,128)}, f32[128,8,256]{2,1,0:T(8,128)}, u32[]{:S(2)}, u32[]{:S(2)}) collective-permute-start(f32[128,8,256]{2,1,0:T(8,128)} %turn.31), channel_id=1, source_target_pairs={{0,1},{1,0},{2,3},{3,2},{4,5},{5,4},{6,7},{7,6},{8,9},{9,8},{10,11... | collective-permute-start | bytes 3145736 | tf_op jit(solution)/shard_map/ppermute | solution.py:355
  481.0 24.2 %collective-permute-start.69 = (f32[128,8,256]{2,1,0:T(8,128)}, f32[128,8,256]{2,1,0:T(8,128)}, u32[]{:S(2)}, u32[]{:S(2)}) collective-permute-start(f32[128,8,256]{2,1,0:T(8,128)} %turn.30), channel_id=1, source_target_pairs={{0,1},{1,0},{2,3},{3,2},{4,5},{5,4},{6,7},{7,6},{8,9},{9,8},{10,11... | collective-permute-start | bytes 3145736 | tf_op jit(solution)/shard_map/ppermute | solution.py:355
  484.1 25.8 %collective-permute-start.72 = (f32[64,8,256]{2,1,0:T(8,128)}, f32[64,8,256]{2,1,0:T(8,128)S(1)}, u32[]{:S(2)}, u32[]{:S(2)}) collective-permute-start(f32[64,8,256]{2,1,0:T(8,128)} %get-tuple-element.453), channel_id=1, source_target_pairs={{0,8},{8,0},{16,24},{24,16},{1,9},{9,1},{17,25},{25,17},{2,10},{10... | collective-permute-start | bytes 1572872 | tf_op jit(solution)/shard_map/ppermute | solution.py:346
  (73 other events, 1028.0 us)

commit v8 on v7

--- a/solution.py
+++ b/solution.py
@@ -11,7 +11,6 @@
 BF16 = jnp.bfloat16
 VMEM_LIMIT = 56 * 2**20
 SPAN, LANES = 8, 128
-FIRST_ROWS = 2
 LIGHT = pl.CostEstimate(flops=1000, transcendentals=0, bytes_accessed=1000)
 PARAMS = pltpu.CompilerParams(vmem_limit_bytes=VMEM_LIMIT)
 WHOLE = pl.BlockSpec(memory_space=pltpu.VMEM)
@@ -123,10 +122,11 @@
     )(where, bounds, rates, increments, increments[:, :, None], draw[None], crusher_rate[None])
 
 
-def local_kernel(at, half, where, lost_a, occ, c_hi, c_lo, b_hi, b_lo, lost_b, left_c, mine, peer, b_both, left_b):
+def local_kernel(half, where, lost_a, occ, c_hi, c_lo, b_hi, b_lo, lost_b, left_c, *outs):
     block, phases = occ.shape[0], occ.shape[2]
-    size = mine.shape[2]
-    rows = [pl.ds(pl.multiple_of(where[n] * half + at, 16), size) for n in range(2)]
+    mine, peer, mine_rest, peer_rest, b_both, left_b = outs
+    size, cut = half, mine.shape[2]
+    rows = [pl.ds(pl.multiple_of(where[n] * half, 16), size) for n in range(2)]
 
     @pl.when(pl.program_id(0) == 0)
     def _():
@@ -152,24 +152,26 @@
         base = by_c[here, :phases] + by_b[: 2 * size] + y[here] * left
         rise = by_c[here, phases:] + by_b[2 * size :]
         for n, value in enumerate((base, rise)):
-            mine[n, i] = value[:size]
-            peer[n, i] = value[size:]
-
-
-def local_terms(where, occ, lost_a, factors, at, size):
+            mine[n, i] = value[:cut]
+            mine_rest[n, i] = value[cut:size]
+            peer[n, i] = value[size : size + cut]
+            peer_rest[n, i] = value[size + cut :]
+
+
+def local_terms(where, occ, lost_a, factors, first):
     rows, mid, phases = occ.shape
-    block = 8
-    out = pl.BlockSpec((2, block, size, phases), lambda i, c: (0, i, 0, 0))
-    return pl.pallas_call(
-        functools.partial(local_kernel, at, mid // 2),
+    block, size = 8, mid // 2
+    sizes = [first, first, size - first, size - first]
+    return pl.pallas_call(
+        functools.partial(local_kernel, size),
         grid_spec=pltpu.PrefetchScalarGridSpec(
             num_scalar_prefetch=1,
             grid=(rows // block,),
             in_specs=[WHOLE, pl.BlockSpec((block, mid, phases), lambda i, c: (i, 0, 0))] + [WHOLE] * len(factors),
-            out_specs=[out] * 2,
+            out_specs=[pl.BlockSpec((2, block, v, phases), lambda i, c: (0, i, 0, 0)) for v in sizes],
             scratch_shapes=[pltpu.VMEM((8 * size, mid), BF16), pltpu.VMEM((2 * size, 1), F32)],
         ),
-        out_shape=[jax.ShapeDtypeStruct((2, rows, size, phases), F32)] * 2,
+        out_shape=[jax.ShapeDtypeStruct((2, rows, v, phases), F32) for v in sizes],
         compiler_params=PARAMS,
         cost_estimate=LIGHT,
         name="local_terms",
@@ -220,9 +222,11 @@
             at += ref.shape[0]
 
 
-def first_terms(where, fall, w_both, slabs, deep, near, start):
-    rows, size, phases = slabs[0].shape
-    slab_specs = [pl.BlockSpec((v.shape[0], SPAN, LANES), lambda j, h: (0, j, h)) for v in [*slabs, *deep]]
+def first_terms(where, fall, w_both, slabs, deep, near, start, size):
+    rows, _, phases = slabs[0][0].shape
+    slab_specs = [
+        pl.BlockSpec((v.shape[0], SPAN, LANES), lambda j, h, at=at: (0, at // SPAN + j, h)) for v, at in [*slabs, *deep]
+    ]
     chunk = pl.BlockSpec((rows, SPAN, LANES), lambda j, h: (0, j, h))
     local_part = pl.BlockSpec((2, rows // 2, SPAN, LANES), lambda j, h: (0, 0, start // SPAN + j, h))
     return pl.pallas_call(
@@ -236,7 +240,7 @@
         compiler_params=PARAMS,
         cost_estimate=LIGHT,
         name="first_terms",
-    )(where, fall, w_both, *slabs, *deep, *near)
+    )(where, fall, w_both, *[v for v, _ in [*slabs, *deep]], *near)
 
 
 def turn_kernel(swap, lifted, out):
@@ -362,30 +366,34 @@
     size = chunks[0][1]
     shifts = [2 * s for s in range(1, n_cls // 2)]
     sent = [None] * n
-    tokens, gives = [], []
-    for lo, hi in spans(*sorted({0, n // 4, n})):
+
+    def exchange(lo, hi, *after):
         at = chunks[lo][0]
         give = cut(occ, 1, at, (hi - lo) * size)
-        if tokens:
-            give, _ = gate(give, sent[0])
-        gives.append(give)
+        if after:
+            give = gate(give, *after)[0]
         got = other_core(give)
-        tokens.append(got)
         for s in range(lo, hi):
             start = chunks[s][0]
             part = lax.slice_in_dim(got, start - at, start - at + size, axis=1)
             sent[s] = jnp.concatenate([cut(occ, 0, start, size), part], axis=0)
+        return give, got
+
+    quarter = max(3, n // 4)
+    _, token = exchange(0, quarter)
 
     far, deep = [None] * n, [None] * n
 
-    def start_early(s):
+    def start_early():
+        own, other = cut(occ, 0, 0, 2 * size), cut(occ, 1, 0, 2 * size)
+        got = []
         for by in shifts:
-            straight = along_cls(cut(occ, 0, s * size, size), by)
             crossed = [(i, ((i + by) % n_cls) ^ 1) for i in range(n_cls)]
-            cross = lax.ppermute(cut(occ, 1, s * size, size), "cls", crossed)
-            far[s] = (far[s] or []) + [straight, cross]
+            got += [along_cls(own, by), lax.ppermute(other, "cls", crossed)]
+        far[0], far[1] = list(got), list(got)
         both = [(i * n_lvl + m, (i ^ 1) * n_lvl + m - 2) for i in range(n_cls) for m in range(2, n_lvl)]
-        deep[s] = [two_down(cut(occ, 0, s * size, size)), lax.ppermute(cut(occ, 1, s * size, size), ("cls", "lvl"), both)]
+        got = [two_down(own), lax.ppermute(other, ("cls", "lvl"), both)]
+        deep[0], deep[1] = list(got), list(got)
 
     def start_far(s, *after):
         operand = gate(sent[s], *after)[0] if after else sent[s]
@@ -395,29 +403,20 @@
         operand = gate(sent[s], *after)[0] if after else sent[s]
         deep[s] = [two_down(operand)]
 
-    start_early(0)
+    start_early()
 
     a_both, *factors = prepare(where, bounds, rates, increments, draw, crusher_rate, rows)
     *factors, fall_vec = factors
     lost_a = factors.pop(4)
 
-    parts = []
-
-    def start_part(lo, hi, *begin):
-        at, span = chunks[lo][0], (hi - lo) * size
-        mine, give = local_terms(where, gate(occ, *begin)[0], lost_a, factors, at, span)
-        return lo, hi, at, mine, give
-
-    def send_part(part, *after):
-        lo, hi, at, mine, give = part
-        parts.append((lo, hi, at, (mine, other_core(gate(give, *after)[0]))))
-
-    part = start_part(0, FIRST_ROWS, tokens[0])
-    rest = start_part(FIRST_ROWS, n, part[3], gives[1], sent[0], sent[1])
-    far[0][0], _ = gate(far[0][0], rest[3])
-    send_part(part, *far[0], *deep[0])
-    send_part(rest, parts[0][3][1])
-
+    first = quarter * size
+    mine, peer, mine_rest, peer_rest = local_terms(where, gate(occ, token, sent[0], sent[2])[0], lost_a, factors, first)
+    _, got_rest = exchange(quarter, n, mine)
+    far[0][0], _ = gate(far[0][0], mine)
+    parts = [(0, quarter, 0, (mine, other_core(gate(peer, *far[0], *deep[0])[0])))]
+
+    parts.append((quarter, n, first, (mine_rest, other_core(gate(peer_rest, parts[0][3][1])[0]))))
+    offset = {1: size}
     out = None
     stay, rise, swap, lifted, risen = ([None] * n for _ in range(5))
     back = [None] * len(groups)
@@ -425,19 +424,29 @@
 
     for s in range(n + 4):
         if s < n:
+            if s == 2:
+                far[2][0], _, _ = gate(far[2][0], got_rest, parts[1][3][1])
             if s >= 3:
                 far[s][0], risen[s - 3] = gate(far[s][0], risen[s - 3])
             if s >= 4:
                 far[s][0], out = gate(far[s][0], out)
-            if s + 1 < n:
+            if s == 0:
+                start_far(2, *far[0])
+                start_deep(2, *far[0])
+            elif 3 <= s + 1 < n and s != 1:
                 start_far(s + 1, far[s][0])
-            if s == 0:
-                start_deep(1, far[0][0])
-            if s + 2 < n:
+            if 3 <= s + 2 < n:
                 start_deep(s + 2, *deep[s])
             lo, hi, at, near = next(p for p in parts if p[0] <= s < p[1])
             stay[s], rise[s], swap[s] = first_terms(
-                where, fall_vec, a_both, [sent[s]] + far[s], deep[s], near, chunks[s][0] - at
+                where,
+                fall_vec,
+                a_both,
+                [(sent[s], 0)] + [(v, offset.get(s, 0)) for v in far[s]],
+                [(v, offset.get(s, 0)) for v in deep[s]],
+                near,
+                chunks[s][0] - at,
+                size,
             )
             lift_me = rise[s]
             if s >= 1:

time: 520 us -> 514 us (0.988)
  Pallas kernels: 231 us -> 222 us
    ppermute x16, waiting for transfers between devices: 53.8 us -> 89.2 us  [two_up(): return lax.ppermute(v, 'lvl', [(i, i + 2) for i in range(1, n_lvl - 2, 2)])]
    ppermute x16 -> x15, waiting for transfers between devices: 30.5 us -> 1 us  [along_cls(): return lax.ppermute(v, 'cls', [(i, (i + by) % n_cls) for i in range(n_cls)])]
    ppermute x16 -> x15, starting transfers between devices: 47.7 us -> 29 us  [two_down(): return lax.ppermute(v, 'lvl', [(i, i - 2) for i in range(2, n_lvl)])]
    ppermute x16 -> x15, starting transfers between devices: 7.58 us -> 18.5 us  [along_cls(): return lax.ppermute(v, 'cls', [(i, (i + by) % n_cls) for i in range(n_cls)])]
    ppermute x16, starting transfers between devices: 51.8 us -> 61.2 us  [two_up(): return lax.ppermute(v, 'lvl', [(i, i + 2) for i in range(1, n_lvl - 2, 2)])]
    pallas_call x2 -> x1, Pallas kernels: 41.9 us -> 32.7 us  [local_terms(): pl.pallas_call(functools.partial(local_kernel, size), grid_spec=pltpu.Pre...]
    ppermute x16 -> x15, waiting for transfers between devices: 8.38 us -> 2.39 us  [two_down(): return lax.ppermute(v, 'lvl', [(i, i - 2) for i in range(2, n_lvl)])]
    ppermute x16, waiting for transfers between devices: 13.2 us -> 7.58 us  [pair_swap(): return lax.ppermute(v, 'lvl', [(i, i ^ 1) for i in range(n_lvl)])]
  transfers between devices with their start and end apart: 73 -> 71, of which waited for: 34 -> 21; matrix products, arithmetic and copies ran while one was open for 5% -> 6% of each run, Pallas kernels for 44% -> 42%
where the time goes in v8:
time: 514 us; the launch traced here: 511 us
  Pallas kernels  222 us (43%)
  starting transfers between devices  129 us (25%)
  waiting for transfers between devices  108 us (21%)
  local copies, waits for them, and re-layouts  41.8 us (8%)
  other arithmetic  9.48 us (2%)
    ppermute x16, waiting for transfers between devices, two_up(): return lax.ppermute(v, 'lvl', [(i, i + 2) for i in range(1, n_lvl - 2, 2)])  89.2 us
    pallas_call x16, Pallas kernels, first_terms(): pl.pallas_call(functools.partial(first_kernel, len(slabs), len(deep)), gr...  81.9 us
    ppermute x16, starting transfers between devices, two_up(): return lax.ppermute(v, 'lvl', [(i, i + 2) for i in range(1, n_lvl - 2, 2)])  61.2 us
    pallas_call x16, Pallas kernels, finish(): pl.pallas_call(functools.partial(finish_kernel, len(alias)), grid_spec=pl...  50 us
    pallas_call x16, Pallas kernels, turn(): pl.pallas_call(turn_kernel, grid=(rows // block, size // SPAN), in_specs=...  38.4 us
    pallas_call x1, Pallas kernels, local_terms(): pl.pallas_call(functools.partial(local_kernel, size), grid_spec=pltpu.Pre...  32.7 us
    ppermute x15, starting transfers between devices, two_down(): return lax.ppermute(v, 'lvl', [(i, i - 2) for i in range(2, n_lvl)])  29 us
    dynamic_slice x4, local copies, waits for them, and re-layouts, cut(): lax.dynamic_slice_in_dim(array, core[which] * half + at, size, axis=1)  18.8 us
  transfers between devices with their start and end apart: 71, of which 21 were waited for; matrix products, arithmetic and copies ran while one was open for 6% of the time, Pallas kernels for 42%

profile of v8, /device:TPU:21, one launch (start us, length us, event | category | flops | bytes accessed | tf_op | source)
XLA Modules:
  0.0 511.4 jit_solution(3339941565647831207)
XLA Ops:
  0.0 3.2 dynamic-slice_bitcast_fusion.1
  3.8 3.0 dynamic-slice_bitcast_fusion.2
  18.4 6.5 %dynamic-slice_bitcast_fusion.4 = (f32[64,8,256]{2,1,0:T(8,128)}, f32[64,8,256]{2,1,0:T(8,128)}, f32[64,8,256]{2,1,0:T(8,128)}, f32[64,8,256]{2,1,0:T(8,128)}, f...) fusion(f32[1,64,256,256]{3,2,1,0:T(8,128)} %param.6, ...), kind=kLoop, calls=%fused_computation.20 | loop fusion | bytes 16777280 | tf_op jit(solution)/shard_map/dynamic_slice | solution.py:362
  29.5 32.7 %local_terms.1 = (f32[2,64,32,256]{3,2,1,0:T(8,128)}, f32[2,64,32,256]{3,2,1,0:T(8,128)}, f32[2,64,96,256]{3,2,1,0:T(8,128)}, f32[2,64,96,256]{3,2,1,0:T(8,128)}) custom-call(s32[7]{0:T(128)} %stack.31.where._.core, f32[256,1]{1,0:T(8,128)} %get-tuple-element.230.lost_a, f32[64,256,256]{2,1,0:T(8,128)} %bitcast.52, ...), custom_call_target="tpu_custom_call" | custom-call | flops 1000 | bytes 1000 | tf_op jit(solution)/shard_map/local_terms/pallas_call | solution.py:165
  62.3 7.5 %collective-permute-done.7.refs_7_.refs_5_ = f32[2,64,32,256]{3,2,1,0:T(8,128)} collective-permute-done((f32[2,64,32,256]{3,2,1,0:T(8,128)}, f32[2,64,32,256]{3,2,1,0:T(8,128)}, u32[]{:S(2)}, u32[]{:S(2)}) %collective-permute-start.7) | collective-permute-done | bytes 4194336 | tf_op jit(solution)/shard_map/ppermute | solution.py:350
  70.0 6.1 %dynamic-slice_bitcast_fusion = f32[64,96,256]{2,1,0:T(8,128)} fusion(f32[1,64,256,256]{3,2,1,0:T(8,128)} %param.6, s32[]{:T(128)S(6)} %select_n.72), kind=kLoop, calls=%fused_computation | loop fusion | bytes 12582916 | tf_op jit(solution)/shard_map/dynamic_slice | solution.py:362
  76.5 5.1 %first_terms.18 = (f32[128,8,256]{2,1,0:T(8,128)}, f32[128,8,256]{2,1,0:T(8,128)}, f32[128,8,256]{2,1,0:T(8,128)}) custom-call(s32[7]{0:T(128)} %stack.31.where._.core, f32[2,256]{1,0:T(2,128)} %get-tuple-element.228.fall, bf16[512,256]{1,0:T(8,128)(2,1)} %get-tuple-element.229.refs_0_, f32[128,8,256]{2,1,0:T(8,128)} %pad_maximum_fusion.refs_1_, ...), custom_call_target="tpu_custom_call" | custom-call | flops 1000 | bytes 1000 | tf_op jit(solution)/shard_map/first_terms/pallas_call | solution.py:232
  81.6 4.2 collective-permute-start.11
  91.2 5.2 %first_terms.16 = (f32[128,8,256]{2,1,0:T(8,128)}, f32[128,8,256]{2,1,0:T(8,128)}, f32[128,8,256]{2,1,0:T(8,128)}) custom-call(s32[7]{0:T(128)} %stack.31.where._.core, f32[2,256]{1,0:T(2,128)} %get-tuple-element.228.fall, bf16[512,256]{1,0:T(8,128)(2,1)} %get-tuple-element.229.refs_0_, f32[128,8,256]{2,1,0:T(8,128)} %pad_maximum_fusion.15.refs_1_, ...), custom_call_target="tpu_custom_call" | custom-call | flops 1000 | bytes 1000 | tf_op jit(solution)/shard_map/first_terms/pallas_call | solution.py:232
  96.4 12.0 %collective-permute-done.11.lifted = f32[128,8,256]{2,1,0:T(8,128)S(1)} collective-permute-done((f32[128,8,256]{2,1,0:T(8,128)}, f32[128,8,256]{2,1,0:T(8,128)S(1)}, u32[]{:S(2)}, u32[]{:S(2)}) %collective-permute-start.11) | collective-permute-done | bytes 1048608 | tf_op jit(solution)/shard_map/ppermute | solution.py:356
  108.4 4.0 collective-permute-start.12
  120.1 5.1 first_terms.17
  125.2 9.1 %collective-permute-done.12.lifted = f32[128,8,256]{2,1,0:T(8,128)} collective-permute-done((f32[128,8,256]{2,1,0:T(8,128)}, f32[128,8,256]{2,1,0:T(8,128)}, u32[]{:S(2)}, u32[]{:S(2)}) %collective-permute-start.12) | collective-permute-done | bytes 1048608 | tf_op jit(solution)/shard_map/ppermute | solution.py:356
  134.3 4.0 collective-permute-start.16
  147.9 5.0 first_terms.19
  152.9 6.3 %collective-permute-done.16.lifted = f32[128,8,256]{2,1,0:T(8,128)} collective-permute-done((f32[128,8,256]{2,1,0:T(8,128)}, f32[128,8,256]{2,1,0:T(8,128)}, u32[]{:S(2)}, u32[]{:S(2)}) %collective-permute-start.16) | collective-permute-done | bytes 1048608 | tf_op jit(solution)/shard_map/ppermute | solution.py:356
  159.2 3.9 collective-permute-start.20
  166.7 3.1 finish.16
  169.8 3.1 finish.17
  176.1 5.1 %first_terms.20 = (f32[128,8,256]{2,1,0:T(8,128)}, f32[128,8,256]{2,1,0:T(8,128)}, f32[128,8,256]{2,1,0:T(8,128)}) custom-call(s32[7]{0:T(128)} %stack.31.where._.core, f32[2,256]{1,0:T(2,128)} %get-tuple-element.228.fall, bf16[512,256]{1,0:T(8,128)(2,1)} %get-tuple-element.229.refs_0_, f32[128,8,256]{2,1,0:T(8,128)} %copy-done.6, ...), custom_call_target="tpu_custom_call" | custom-call | flops 1000 | bytes 1000 | tf_op jit(solution)/shard_map/first_terms/pallas_call | solution.py:232
  183.2 3.9 collective-permute-start.24
  190.5 3.1 finish.18
  197.7 5.1 %first_terms.21 = (f32[128,8,256]{2,1,0:T(8,128)}, f32[128,8,256]{2,1,0:T(8,128)}, f32[128,8,256]{2,1,0:T(8,128)}) custom-call(s32[7]{0:T(128)} %stack.31.where._.core, f32[2,256]{1,0:T(2,128)} %get-tuple-element.228.fall, bf16[512,256]{1,0:T(8,128)(2,1)} %get-tuple-element.229.refs_0_, f32[128,8,256]{2,1,0:T(8,128)} %copy-done.4, ...), custom_call_target="tpu_custom_call" | custom-call | flops 1000 | bytes 1000 | tf_op jit(solution)/shard_map/first_terms/pallas_call | solution.py:232
  202.8 3.6 collective-permute-done.24.lifted
  206.4 3.9 collective-permute-start.28
  213.7 3.3 finish.19
  220.2 5.1 first_terms.22
  225.2 3.5 collective-permute-done.28.lifted
  228.8 3.9 collective-permute-start.32
  236.1 3.2 finish.20
  242.5 5.2 %first_terms.23 = (f32[128,8,256]{2,1,0:T(8,128)}, f32[128,8,256]{2,1,0:T(8,128)}, f32[128,8,256]{2,1,0:T(8,128)}) custom-call(s32[7]{0:T(128)} %stack.31.where._.core, f32[2,256]{1,0:T(2,128)} %get-tuple-element.228.fall, bf16[512,256]{1,0:T(8,128)(2,1)} %get-tuple-element.229.refs_0_, f32[128,8,256]{2,1,0:T(8,128)} %copy-done.8, ...), custom_call_target="tpu_custom_call" | custom-call | flops 1000 | bytes 1000 | tf_op jit(solution)/shard_map/first_terms/pallas_call | solution.py:232
  250.4 3.9 collective-permute-start.36
  257.7 3.2 finish.21
  264.1 5.2 %first_terms.24 = (f32[128,8,256]{2,1,0:T(8,128)}, f32[128,8,256]{2,1,0:T(8,128)}, f32[128,8,256]{2,1,0:T(8,128)}) custom-call(s32[7]{0:T(128)} %stack.31.where._.core, f32[2,256]{1,0:T(2,128)} %get-tuple-element.228.fall, bf16[512,256]{1,0:T(8,128)(2,1)} %get-tuple-element.229.refs_0_, f32[128,8,256]{2,1,0:T(8,128)} %copy-done.9, ...), custom_call_target="tpu_custom_call" | custom-call | flops 1000 | bytes 1000 | tf_op jit(solution)/shard_map/first_terms/pallas_call | solution.py:232
  272.1 3.9 collective-permute-start.40
  279.4 3.2 finish.22
  285.8 5.1 first_terms.25
  293.7 3.9 collective-permute-start.44
  301.0 3.2 finish.23
  307.4 5.1 first_terms.26
  315.4 4.1 collective-permute-start.48
  322.9 3.1 finish.24
  329.2 5.1 first_terms.27
  337.0 3.8 collective-permute-start.52
  344.2 3.2 finish.25
  350.6 5.1 first_terms.28
  358.7 3.7 collective-permute-start.56
  365.8 3.2 finish.26
  372.2 5.2 %first_terms.29 = (f32[128,8,256]{2,1,0:T(8,128)}, f32[128,8,256]{2,1,0:T(8,128)}, f32[128,8,256]{2,1,0:T(8,128)}) custom-call(s32[7]{0:T(128)} %stack.31.where._.core, f32[2,256]{1,0:T(2,128)} %get-tuple-element.228.fall, bf16[512,256]{1,0:T(8,128)(2,1)} %get-tuple-element.229.refs_0_, f32[128,8,256]{2,1,0:T(8,128)} %copy-done.14, ...), custom_call_target="tpu_custom_call" | custom-call | flops 1000 | bytes 1000 | tf_op jit(solution)/shard_map/first_terms/pallas_call | solution.py:232
  380.3 3.8 collective-permute-start.60
  387.6 3.1 finish.27
  393.8 5.1 first_terms.30
  398.9 3.4 collective-permute-done.60.lifted
  402.3 3.8 collective-permute-start.63
  409.5 3.0 finish.28
  414.9 5.2 %first_terms.31 = (f32[128,8,256]{2,1,0:T(8,128)}, f32[128,8,256]{2,1,0:T(8,128)}, f32[128,8,256]{2,1,0:T(8,128)}) custom-call(s32[7]{0:T(128)} %stack.31.where._.core, f32[2,256]{1,0:T(2,128)} %get-tuple-element.228.fall, bf16[512,256]{1,0:T(8,128)(2,1)} %get-tuple-element.229.refs_0_, f32[128,8,256]{2,1,0:T(8,128)} %copy-done.15, ...), custom_call_target="tpu_custom_call" | custom-call | flops 1000 | bytes 1000 | tf_op jit(solution)/shard_map/first_terms/pallas_call | solution.py:232
  420.1 4.8 collective-permute-done.63.lifted
  430.7 3.0 finish.29
  433.7 12.7 %collective-permute-start.68 = (f32[64,112,256]{2,1,0:T(8,128)}, f32[64,112,256]{2,1,0:T(8,128)S(1)}, u32[]{:S(2)}, u32[]{:S(2)}) collective-permute-start(f32[64,112,256]{2,1,0:T(8,128)} %get-tuple-element.443), channel_id=1, source_target_pairs={{0,8},{8,0},{16,24},{24,16},{1,9},{9,1},{17,25},{25,17},{2,10},{10... | collective-permute-start | bytes 22020104 | tf_op jit(solution)/shard_map/ppermute | solution.py:350
  449.0 24.4 %collective-permute-done.64.lifted = f32[128,8,256]{2,1,0:T(8,128)} collective-permute-done((f32[128,8,256]{2,1,0:T(8,128)}, f32[128,8,256]{2,1,0:T(8,128)}, u32[]{:S(2)}, u32[]{:S(2)}) %collective-permute-start.64) | collective-permute-done | bytes 1048608 | tf_op jit(solution)/shard_map/ppermute | solution.py:356
  475.8 3.0 finish.30
  482.6 11.2 %put.3.refs_4_ = f32[64,256,256]{2,1,0:T(8,128)} custom-call(s32[7]{0:T(128)} %stack.31.where._.core, f32[64,112,256]{2,1,0:T(8,128)} %copy-done, f32[64,256,256]{2,1,0:T(8,128)} %get-tuple-element.447._), custom_call_target="tpu_custom_call", output_to_operand_aliasing={{}: (2, {})} | custom-call | flops 1000 | bytes 1000 | tf_op jit(solution)/shard_map/put/pallas_call | solution.py:313
  493.9 6.1 %collective-permute-done.67.refs_1_.refs_3_ = f32[128,8,256]{2,1,0:T(8,128)} collective-permute-done((f32[128,8,256]{2,1,0:T(8,128)}, f32[128,8,256]{2,1,0:T(8,128)}, u32[]{:S(2)}, u32[]{:S(2)}) %collective-permute-start.67) | collective-permute-done | bytes 1048608 | tf_op jit(solution)/shard_map/ppermute | solution.py:359
  500.0 3.1 finish.31
  (281 shorter events, 163.4 us)
Async XLA Ops:
  3.2 21.7 %collective-permute-start = (f32[64,32,256]{2,1,0:T(8,128)}, f32[64,32,256]{2,1,0:T(8,128)}, u32[]{:S(2)}, u32[]{:S(2)}) collective-permute-start(f32[64,32,256]{2,1,0:T(8,128)} %dynamic-slice_bitcast_fusion.1), channel_id=1, source_target_pairs={{0,8},{8,0},{16,24},{24,16},{1,9},{9,1},{17,25},{25,17},{2,10},{10... | collective-permute-start | bytes 6291464 | tf_op jit(solution)/shard_map/ppermute | solution.py:350
  6.9 55.3 %collective-permute-start.2 = (f32[64,16,256]{2,1,0:T(8,128)}, f32[64,16,256]{2,1,0:T(8,128)S(1)}, u32[]{:S(2)}, u32[]{:S(2)}) collective-permute-start(f32[64,16,256]{2,1,0:T(8,128)} %get-tuple-element.468), channel_id=1, source_target_pairs={{0,16},{8,24},{16,0},{24,8},{1,17},{9,25},{17,1},{25,9},{2,18},{10... | collective-permute-start | bytes 3145736 | tf_op jit(solution)/shard_map/ppermute | solution.py:347
  8.1 54.1 %collective-permute-start.3 = (f32[64,16,256]{2,1,0:T(8,128)}, f32[64,16,256]{2,1,0:T(8,128)S(1)}, u32[]{:S(2)}, u32[]{:S(2)}) collective-permute-start(f32[64,16,256]{2,1,0:T(8,128)} %get-tuple-element.467), channel_id=1, source_target_pairs={{0,24},{8,16},{16,8},{24,0},{1,25},{9,17},{17,9},{25,1},{2,26},{10... | collective-permute-start | bytes 3145736 | tf_op jit(solution)/shard_map/ppermute | solution.py:392
  8.5 53.7 %collective-permute-start.5 = (f32[64,16,256]{2,1,0:T(8,128)}, f32[64,16,256]{2,1,0:T(8,128)}, u32[]{:S(2)}, u32[]{:S(2)}) collective-permute-start(f32[64,16,256]{2,1,0:T(8,128)} %get-tuple-element.468), channel_id=1, source_target_pairs={{2,0},{3,1},{4,2},{5,3},{6,4},{7,5},{10,8},{11,9},{12,10},{13,11},... | collective-permute-start | bytes 3145736 | tf_op jit(solution)/shard_map/ppermute | solution.py:353
  10.6 51.7 %collective-permute-start.6 = (f32[64,16,256]{2,1,0:T(8,128)}, f32[64,16,256]{2,1,0:T(8,128)}, u32[]{:S(2)}, u32[]{:S(2)}) collective-permute-start(f32[64,16,256]{2,1,0:T(8,128)} %get-tuple-element.467), channel_id=1, source_target_pairs={{2,8},{3,9},{4,10},{5,11},{6,12},{7,13},{10,0},{11,1},{12,2},{13,3... | collective-permute-start | bytes 3145736 | tf_op jit(solution)/shard_map/ppermute | solution.py:395
  69.8 47.1 %collective-permute-start.8 = (f32[2,64,96,256]{3,2,1,0:T(8,128)}, f32[2,64,96,256]{3,2,1,0:T(8,128)}, u32[]{:S(2)}, u32[]{:S(2)}) collective-permute-start(f32[2,64,96,256]{3,2,1,0:T(8,128)} %get-tuple-element.245), channel_id=1, source_target_pairs={{0,8},{8,0},{16,24},{24,16},{1,9},{9,1},{17,25},{25,17},{2,10},{10... | collective-permute-start | bytes 37748744 | tf_op jit(solution)/shard_map/ppermute | solution.py:350
  76.1 40.8 %collective-permute-start.1 = (f32[64,96,256]{2,1,0:T(8,128)}, f32[64,96,256]{2,1,0:T(8,128)S(1)}, u32[]{:S(2)}, u32[]{:S(2)}) collective-permute-start(f32[64,96,256]{2,1,0:T(8,128)} %dynamic-slice_bitcast_fusion), channel_id=1, source_target_pairs={{0,8},{8,0},{16,24},{24,16},{1,9},{9,1},{17,25},{25,17},{2,10},{10... | collective-permute-start | bytes 18874376 | tf_op jit(solution)/shard_map/ppermute | solution.py:350
  81.6 26.8 %collective-permute-start.11 = (f32[128,8,256]{2,1,0:T(8,128)}, f32[128,8,256]{2,1,0:T(8,128)S(1)}, u32[]{:S(2)}, u32[]{:S(2)}) collective-permute-start(f32[128,8,256]{2,1,0:T(8,128)} %get-tuple-element.251), channel_id=1, source_target_pairs={{1,3},{3,5},{5,7},{9,11},{11,13},{13,15},{17,19},{19,21},{21,23},{... | collective-permute-start | bytes 3145736 | tf_op jit(solution)/shard_map/ppermute | solution.py:356
  85.8 29.1 %collective-permute-start.4 = (f32[128,8,256]{2,1,0:T(8,128)}, f32[128,8,256]{2,1,0:T(8,128)}, u32[]{:S(2)}, u32[]{:S(2)}) collective-permute-start(f32[128,8,256]{2,1,0:T(8,128)} %pad_maximum_fusion.1.refs_1_), channel_id=1, source_target_pairs={{0,16},{8,24},{16,0},{24,8},{1,17},{9,25},{17,1},{25,9},{2,18},{10... | collective-permute-start | bytes 3145736 | tf_op jit(solution)/shard_map/ppermute | solution.py:347
  89.3 30.8 %collective-permute-start.10 = (f32[128,8,256]{2,1,0:T(8,128)}, f32[128,8,256]{2,1,0:T(8,128)}, u32[]{:S(2)}, u32[]{:S(2)}) collective-permute-start(f32[128,8,256]{2,1,0:T(8,128)} %pad_maximum_fusion.1.refs_1_), channel_id=1, source_target_pairs={{2,0},{3,1},{4,2},{5,3},{6,4},{7,5},{10,8},{11,9},{12,10},{13,11},... | collective-permute-start | bytes 3145736 | tf_op jit(solution)/shard_map/ppermute | solution.py:353
  108.4 25.8 %collective-permute-start.12 = (f32[128,8,256]{2,1,0:T(8,128)}, f32[128,8,256]{2,1,0:T(8,128)}, u32[]{:S(2)}, u32[]{:S(2)}) collective-permute-start(f32[128,8,256]{2,1,0:T(8,128)} %get-tuple-element.252), channel_id=1, source_target_pairs={{1,3},{3,5},{5,7},{9,11},{11,13},{13,15},{17,19},{19,21},{21,23},{... | collective-permute-start | bytes 3145736 | tf_op jit(solution)/shard_map/ppermute | solution.py:356
  114.9 25.8 %collective-permute-start.13 = (f32[128,8,256]{2,1,0:T(8,128)}, f32[128,8,256]{2,1,0:T(8,128)S(1)}, u32[]{:S(2)}, u32[]{:S(2)}) collective-permute-start(f32[128,8,256]{2,1,0:T(8,128)} %turn.17), channel_id=1, source_target_pairs={{0,1},{1,0},{2,3},{3,2},{4,5},{5,4},{6,7},{7,6},{8,9},{9,8},{10,11... | collective-permute-start | bytes 3145736 | tf_op jit(solution)/shard_map/ppermute | solution.py:359
  116.9 27.6 %collective-permute-start.9 = (f32[128,8,256]{2,1,0:T(8,128)}, f32[128,8,256]{2,1,0:T(8,128)}, u32[]{:S(2)}, u32[]{:S(2)}) collective-permute-start(f32[128,8,256]{2,1,0:T(8,128)} %pad_maximum_fusion.14.refs_1_), channel_id=1, source_target_pairs={{0,16},{8,24},{16,0},{24,8},{1,17},{9,25},{17,1},{25,9},{2,18},{10... | collective-permute-start | bytes 3145736 | tf_op jit(solution)/shard_map/ppermute | solution.py:347
  118.2 29.7 %collective-permute-start.15 = (f32[128,8,256]{2,1,0:T(8,128)}, f32[128,8,256]{2,1,0:T(8,128)}, u32[]{:S(2)}, u32[]{:S(2)}) collective-permute-start(f32[128,8,256]{2,1,0:T(8,128)} %pad_maximum_fusion.14.refs_1_), channel_id=1, source_target_pairs={{2,0},{3,1},{4,2},{5,3},{6,4},{7,5},{10,8},{11,9},{12,10},{13,11},... | collective-permute-start | bytes 3145736 | tf_op jit(solution)/shard_map/ppermute | solution.py:353
  134.3 24.9 %collective-permute-start.16 = (f32[128,8,256]{2,1,0:T(8,128)}, f32[128,8,256]{2,1,0:T(8,128)}, u32[]{:S(2)}, u32[]{:S(2)}) collective-permute-start(f32[128,8,256]{2,1,0:T(8,128)} %get-tuple-element.262), channel_id=1, source_target_pairs={{1,3},{3,5},{5,7},{9,11},{11,13},{13,15},{17,19},{19,21},{21,23},{... | collective-permute-start | bytes 3145736 | tf_op jit(solution)/shard_map/ppermute | solution.py:356
  140.7 24.9 %collective-permute-start.17 = (f32[128,8,256]{2,1,0:T(8,128)}, f32[128,8,256]{2,1,0:T(8,128)}, u32[]{:S(2)}, u32[]{:S(2)}) collective-permute-start(f32[128,8,256]{2,1,0:T(8,128)} %turn.16), channel_id=1, source_target_pairs={{0,1},{1,0},{2,3},{3,2},{4,5},{5,4},{6,7},{7,6},{8,9},{9,8},{10,11... | collective-permute-start | bytes 3145736 | tf_op jit(solution)/shard_map/ppermute | solution.py:359
  144.5 28.3 %collective-permute-start.14 = (f32[128,8,256]{2,1,0:T(8,128)S(1)}, f32[128,8,256]{2,1,0:T(8,128)S(1)}, u32[]{:S(2)}, u32[]{:S(2)}) collective-permute-start(f32[128,8,256]{2,1,0:T(8,128)S(1)} %pad_maximum_fusion.13.refs_1_), channel_id=1, source_target_pairs={{0,16},{8,24},{16,0},{24,8},{1,17},{9,25},{17,1},{25,9},{2,18},{10... | collective-permute-start | bytes 3145736 | tf_op jit(solution)/shard_map/ppermute | solution.py:347
  145.8 30.3 %collective-permute-start.19 = (f32[128,8,256]{2,1,0:T(8,128)S(1)}, f32[128,8,256]{2,1,0:T(8,128)}, u32[]{:S(2)}, u32[]{:S(2)}) collective-permute-start(f32[128,8,256]{2,1,0:T(8,128)S(1)} %pad_maximum_fusion.13.refs_1_), channel_id=1, source_target_pairs={{2,0},{3,1},{4,2},{5,3},{6,4},{7,5},{10,8},{11,9},{12,10},{13,11},... | collective-permute-start | bytes 3145736 | tf_op jit(solution)/shard_map/ppermute | solution.py:353
  159.2 24.0 %collective-permute-start.20 = (f32[128,8,256]{2,1,0:T(8,128)}, f32[128,8,256]{2,1,0:T(8,128)S(1)}, u32[]{:S(2)}, u32[]{:S(2)}) collective-permute-start(f32[128,8,256]{2,1,0:T(8,128)} %get-tuple-element.278), channel_id=1, source_target_pairs={{1,3},{3,5},{5,7},{9,11},{11,13},{13,15},{17,19},{19,21},{21,23},{... | collective-permute-start | bytes 3145736 | tf_op jit(solution)/shard_map/ppermute | solution.py:356
  165.6 24.0 %collective-permute-start.21 = (f32[128,8,256]{2,1,0:T(8,128)}, f32[128,8,256]{2,1,0:T(8,128)S(1)}, u32[]{:S(2)}, u32[]{:S(2)}) collective-permute-start(f32[128,8,256]{2,1,0:T(8,128)} %turn.18), channel_id=1, source_target_pairs={{0,1},{1,0},{2,3},{3,2},{4,5},{5,4},{6,7},{7,6},{8,9},{9,8},{10,11... | collective-permute-start | bytes 3145736 | tf_op jit(solution)/shard_map/ppermute | solution.py:359
  172.9 21.7 %collective-permute-start.18 = (f32[128,8,256]{2,1,0:T(8,128)S(1)}, f32[128,8,256]{2,1,0:T(8,128)}, u32[]{:S(2)}, u32[]{:S(2)}) collective-permute-start(f32[128,8,256]{2,1,0:T(8,128)S(1)} %pad_maximum_fusion.12.refs_1_), channel_id=1, source_target_pairs={{0,16},{8,24},{16,0},{24,8},{1,17},{9,25},{17,1},{25,9},{2,18},{10... | collective-permute-start | bytes 3145736 | tf_op jit(solution)/shard_map/ppermute | solution.py:347
  174.1 23.5 %collective-permute-start.23 = (f32[128,8,256]{2,1,0:T(8,128)S(1)}, f32[128,8,256]{2,1,0:T(8,128)}, u32[]{:S(2)}, u32[]{:S(2)}) collective-permute-start(f32[128,8,256]{2,1,0:T(8,128)S(1)} %pad_maximum_fusion.12.refs_1_), channel_id=1, source_target_pairs={{2,0},{3,1},{4,2},{5,3},{6,4},{7,5},{10,8},{11,9},{12,10},{13,11},... | collective-permute-start | bytes 3145736 | tf_op jit(solution)/shard_map/ppermute | solution.py:353
  183.2 23.2 %collective-permute-start.24 = (f32[128,8,256]{2,1,0:T(8,128)}, f32[128,8,256]{2,1,0:T(8,128)S(1)}, u32[]{:S(2)}, u32[]{:S(2)}) collective-permute-start(f32[128,8,256]{2,1,0:T(8,128)} %get-tuple-element.292), channel_id=1, source_target_pairs={{1,3},{3,5},{5,7},{9,11},{11,13},{13,15},{17,19},{19,21},{21,23},{... | collective-permute-start | bytes 3145736 | tf_op jit(solution)/shard_map/ppermute | solution.py:356
  189.5 23.2 %collective-permute-start.25 = (f32[128,8,256]{2,1,0:T(8,128)}, f32[128,8,256]{2,1,0:T(8,128)S(1)}, u32[]{:S(2)}, u32[]{:S(2)}) collective-permute-start(f32[128,8,256]{2,1,0:T(8,128)} %turn.19), channel_id=1, source_target_pairs={{0,1},{1,0},{2,3},{3,2},{4,5},{5,4},{6,7},{7,6},{8,9},{9,8},{10,11... | collective-permute-start | bytes 3145736 | tf_op jit(solution)/shard_map/ppermute | solution.py:359
  194.6 22.4 %collective-permute-start.22 = (f32[128,8,256]{2,1,0:T(8,128)S(1)}, f32[128,8,256]{2,1,0:T(8,128)}, u32[]{:S(2)}, u32[]{:S(2)}) collective-permute-start(f32[128,8,256]{2,1,0:T(8,128)S(1)} %pad_maximum_fusion.11.refs_1_), channel_id=1, source_target_pairs={{0,16},{8,24},{16,0},{24,8},{1,17},{9,25},{17,1},{25,9},{2,18},{10... | collective-permute-start | bytes 3145736 | tf_op jit(solution)/shard_map/ppermute | solution.py:347
  195.7 24.4 %collective-permute-start.27 = (f32[128,8,256]{2,1,0:T(8,128)S(1)}, f32[128,8,256]{2,1,0:T(8,128)}, u32[]{:S(2)}, u32[]{:S(2)}) collective-permute-start(f32[128,8,256]{2,1,0:T(8,128)S(1)} %pad_maximum_fusion.11.refs_1_), channel_id=1, source_target_pairs={{2,0},{3,1},{4,2},{5,3},{6,4},{7,5},{10,8},{11,9},{12,10},{13,11},... | collective-permute-start | bytes 3145736 | tf_op jit(solution)/shard_map/ppermute | solution.py:353
  206.4 22.4 %collective-permute-start.28 = (f32[128,8,256]{2,1,0:T(8,128)}, f32[128,8,256]{2,1,0:T(8,128)}, u32[]{:S(2)}, u32[]{:S(2)}) collective-permute-start(f32[128,8,256]{2,1,0:T(8,128)} %get-tuple-element.306), channel_id=1, source_target_pairs={{1,3},{3,5},{5,7},{9,11},{11,13},{13,15},{17,19},{19,21},{21,23},{... | collective-permute-start | bytes 3145736 | tf_op jit(solution)/shard_map/ppermute | solution.py:356
  212.7 22.3 %collective-permute-start.29 = (f32[128,8,256]{2,1,0:T(8,128)}, f32[128,8,256]{2,1,0:T(8,128)S(1)}, u32[]{:S(2)}, u32[]{:S(2)}) collective-permute-start(f32[128,8,256]{2,1,0:T(8,128)} %turn.20), channel_id=1, source_target_pairs={{0,1},{1,0},{2,3},{3,2},{4,5},{5,4},{6,7},{7,6},{8,9},{9,8},{10,11... | collective-permute-start | bytes 3145736 | tf_op jit(solution)/shard_map/ppermute | solution.py:359
  217.0 22.3 %collective-permute-start.26 = (f32[128,8,256]{2,1,0:T(8,128)S(1)}, f32[128,8,256]{2,1,0:T(8,128)}, u32[]{:S(2)}, u32[]{:S(2)}) collective-permute-start(f32[128,8,256]{2,1,0:T(8,128)S(1)} %pad_maximum_fusion.10.refs_1_), channel_id=1, source_target_pairs={{0,16},{8,24},{16,0},{24,8},{1,17},{9,25},{17,1},{25,9},{2,18},{10... | collective-permute-start | bytes 3145736 | tf_op jit(solution)/shard_map/ppermute | solution.py:347
  218.2 24.2 %collective-permute-start.31 = (f32[128,8,256]{2,1,0:T(8,128)S(1)}, f32[128,8,256]{2,1,0:T(8,128)}, u32[]{:S(2)}, u32[]{:S(2)}) collective-permute-start(f32[128,8,256]{2,1,0:T(8,128)S(1)} %pad_maximum_fusion.10.refs_1_), channel_id=1, source_target_pairs={{2,0},{3,1},{4,2},{5,3},{6,4},{7,5},{10,8},{11,9},{12,10},{13,11},... | collective-permute-start | bytes 3145736 | tf_op jit(solution)/shard_map/ppermute | solution.py:353
  228.8 21.6 %collective-permute-start.32 = (f32[128,8,256]{2,1,0:T(8,128)}, f32[128,8,256]{2,1,0:T(8,128)S(1)}, u32[]{:S(2)}, u32[]{:S(2)}) collective-permute-start(f32[128,8,256]{2,1,0:T(8,128)} %get-tuple-element.320), channel_id=1, source_target_pairs={{1,3},{3,5},{5,7},{9,11},{11,13},{13,15},{17,19},{19,21},{21,23},{... | collective-permute-start | bytes 3145736 | tf_op jit(solution)/shard_map/ppermute | solution.py:356
  235.1 21.6 %collective-permute-start.33 = (f32[128,8,256]{2,1,0:T(8,128)}, f32[128,8,256]{2,1,0:T(8,128)S(1)}, u32[]{:S(2)}, u32[]{:S(2)}) collective-permute-start(f32[128,8,256]{2,1,0:T(8,128)} %turn.21), channel_id=1, source_target_pairs={{0,1},{1,0},{2,3},{3,2},{4,5},{5,4},{6,7},{7,6},{8,9},{9,8},{10,11... | collective-permute-start | bytes 3145736 | tf_op jit(solution)/shard_map/ppermute | solution.py:359
  239.3 21.6 %collective-permute-start.30 = (f32[128,8,256]{2,1,0:T(8,128)S(1)}, f32[128,8,256]{2,1,0:T(8,128)}, u32[]{:S(2)}, u32[]{:S(2)}) collective-permute-start(f32[128,8,256]{2,1,0:T(8,128)S(1)} %pad_maximum_fusion.9.refs_1_), channel_id=1, source_target_pairs={{0,16},{8,24},{16,0},{24,8},{1,17},{9,25},{17,1},{25,9},{2,18},{10... | collective-permute-start | bytes 3145736 | tf_op jit(solution)/shard_map/ppermute | solution.py:347
  240.5 23.5 %collective-permute-start.35 = (f32[128,8,256]{2,1,0:T(8,128)S(1)}, f32[128,8,256]{2,1,0:T(8,128)}, u32[]{:S(2)}, u32[]{:S(2)}) collective-permute-start(f32[128,8,256]{2,1,0:T(8,128)S(1)} %pad_maximum_fusion.9.refs_1_), channel_id=1, source_target_pairs={{2,0},{3,1},{4,2},{5,3},{6,4},{7,5},{10,8},{11,9},{12,10},{13,11},... | collective-permute-start | bytes 3145736 | tf_op jit(solution)/shard_map/ppermute | solution.py:353
  250.4 21.7 %collective-permute-start.36 = (f32[128,8,256]{2,1,0:T(8,128)}, f32[128,8,256]{2,1,0:T(8,128)}, u32[]{:S(2)}, u32[]{:S(2)}) collective-permute-start(f32[128,8,256]{2,1,0:T(8,128)} %get-tuple-element.334), channel_id=1, source_target_pairs={{1,3},{3,5},{5,7},{9,11},{11,13},{13,15},{17,19},{19,21},{21,23},{... | collective-permute-start | bytes 3145736 | tf_op jit(solution)/shard_map/ppermute | solution.py:356
  256.7 21.7 %collective-permute-start.37 = (f32[128,8,256]{2,1,0:T(8,128)}, f32[128,8,256]{2,1,0:T(8,128)S(1)}, u32[]{:S(2)}, u32[]{:S(2)}) collective-permute-start(f32[128,8,256]{2,1,0:T(8,128)} %turn.22), channel_id=1, source_target_pairs={{0,1},{1,0},{2,3},{3,2},{4,5},{5,4},{6,7},{7,6},{8,9},{9,8},{10,11... | collective-permute-start | bytes 3145736 | tf_op jit(solution)/shard_map/ppermute | solution.py:359
  260.9 21.7 %collective-permute-start.34 = (f32[128,8,256]{2,1,0:T(8,128)S(1)}, f32[128,8,256]{2,1,0:T(8,128)}, u32[]{:S(2)}, u32[]{:S(2)}) collective-permute-start(f32[128,8,256]{2,1,0:T(8,128)S(1)} %pad_maximum_fusion.8.refs_1_), channel_id=1, source_target_pairs={{0,16},{8,24},{16,0},{24,8},{1,17},{9,25},{17,1},{25,9},{2,18},{10... | collective-permute-start | bytes 3145736 | tf_op jit(solution)/shard_map/ppermute | solution.py:347
  262.1 23.6 %collective-permute-start.39 = (f32[128,8,256]{2,1,0:T(8,128)S(1)}, f32[128,8,256]{2,1,0:T(8,128)}, u32[]{:S(2)}, u32[]{:S(2)}) collective-permute-start(f32[128,8,256]{2,1,0:T(8,128)S(1)} %pad_maximum_fusion.8.refs_1_), channel_id=1, source_target_pairs={{2,0},{3,1},{4,2},{5,3},{6,4},{7,5},{10,8},{11,9},{12,10},{13,11},... | collective-permute-start | bytes 3145736 | tf_op jit(solution)/shard_map/ppermute | solution.py:353
  272.1 21.6 %collective-permute-start.40 = (f32[128,8,256]{2,1,0:T(8,128)}, f32[128,8,256]{2,1,0:T(8,128)S(1)}, u32[]{:S(2)}, u32[]{:S(2)}) collective-permute-start(f32[128,8,256]{2,1,0:T(8,128)} %get-tuple-element.348), channel_id=1, source_target_pairs={{1,3},{3,5},{5,7},{9,11},{11,13},{13,15},{17,19},{19,21},{21,23},{... | collective-permute-start | bytes 3145736 | tf_op jit(solution)/shard_map/ppermute | solution.py:356
  278.4 21.6 %collective-permute-start.41 = (f32[128,8,256]{2,1,0:T(8,128)}, f32[128,8,256]{2,1,0:T(8,128)S(1)}, u32[]{:S(2)}, u32[]{:S(2)}) collective-permute-start(f32[128,8,256]{2,1,0:T(8,128)} %turn.23), channel_id=1, source_target_pairs={{0,1},{1,0},{2,3},{3,2},{4,5},{5,4},{6,7},{7,6},{8,9},{9,8},{10,11... | collective-permute-start | bytes 3145736 | tf_op jit(solution)/shard_map/ppermute | solution.py:359
  282.6 21.6 %collective-permute-start.38 = (f32[128,8,256]{2,1,0:T(8,128)S(1)}, f32[128,8,256]{2,1,0:T(8,128)}, u32[]{:S(2)}, u32[]{:S(2)}) collective-permute-start(f32[128,8,256]{2,1,0:T(8,128)S(1)} %pad_maximum_fusion.7.refs_1_), channel_id=1, source_target_pairs={{0,16},{8,24},{16,0},{24,8},{1,17},{9,25},{17,1},{25,9},{2,18},{10... | collective-permute-start | bytes 3145736 | tf_op jit(solution)/shard_map/ppermute | solution.py:347
  283.8 23.5 %collective-permute-start.43 = (f32[128,8,256]{2,1,0:T(8,128)S(1)}, f32[128,8,256]{2,1,0:T(8,128)}, u32[]{:S(2)}, u32[]{:S(2)}) collective-permute-start(f32[128,8,256]{2,1,0:T(8,128)S(1)} %pad_maximum_fusion.7.refs_1_), channel_id=1, source_target_pairs={{2,0},{3,1},{4,2},{5,3},{6,4},{7,5},{10,8},{11,9},{12,10},{13,11},... | collective-permute-start | bytes 3145736 | tf_op jit(solution)/shard_map/ppermute | solution.py:353
  293.7 21.7 %collective-permute-start.44 = (f32[128,8,256]{2,1,0:T(8,128)}, f32[128,8,256]{2,1,0:T(8,128)}, u32[]{:S(2)}, u32[]{:S(2)}) collective-permute-start(f32[128,8,256]{2,1,0:T(8,128)} %get-tuple-element.362), channel_id=1, source_target_pairs={{1,3},{3,5},{5,7},{9,11},{11,13},{13,15},{17,19},{19,21},{21,23},{... | collective-permute-start | bytes 3145736 | tf_op jit(solution)/shard_map/ppermute | solution.py:356
  300.0 22.0 %collective-permute-start.45 = (f32[128,8,256]{2,1,0:T(8,128)}, f32[128,8,256]{2,1,0:T(8,128)S(1)}, u32[]{:S(2)}, u32[]{:S(2)}) collective-permute-start(f32[128,8,256]{2,1,0:T(8,128)} %turn.24), channel_id=1, source_target_pairs={{0,1},{1,0},{2,3},{3,2},{4,5},{5,4},{6,7},{7,6},{8,9},{9,8},{10,11... | collective-permute-start | bytes 3145736 | tf_op jit(solution)/shard_map/ppermute | solution.py:359
  304.2 21.8 %collective-permute-start.42 = (f32[128,8,256]{2,1,0:T(8,128)S(1)}, f32[128,8,256]{2,1,0:T(8,128)}, u32[]{:S(2)}, u32[]{:S(2)}) collective-permute-start(f32[128,8,256]{2,1,0:T(8,128)S(1)} %pad_maximum_fusion.6.refs_1_), channel_id=1, source_target_pairs={{0,16},{8,24},{16,0},{24,8},{1,17},{9,25},{17,1},{25,9},{2,18},{10... | collective-permute-start | bytes 3145736 | tf_op jit(solution)/shard_map/ppermute | solution.py:347
  305.4 23.7 %collective-permute-start.47 = (f32[128,8,256]{2,1,0:T(8,128)S(1)}, f32[128,8,256]{2,1,0:T(8,128)}, u32[]{:S(2)}, u32[]{:S(2)}) collective-permute-start(f32[128,8,256]{2,1,0:T(8,128)S(1)} %pad_maximum_fusion.6.refs_1_), channel_id=1, source_target_pairs={{2,0},{3,1},{4,2},{5,3},{6,4},{7,5},{10,8},{11,9},{12,10},{13,11},... | collective-permute-start | bytes 3145736 | tf_op jit(solution)/shard_map/ppermute | solution.py:353
  315.4 21.6 %collective-permute-start.48 = (f32[128,8,256]{2,1,0:T(8,128)}, f32[128,8,256]{2,1,0:T(8,128)S(1)}, u32[]{:S(2)}, u32[]{:S(2)}) collective-permute-start(f32[128,8,256]{2,1,0:T(8,128)} %get-tuple-element.376), channel_id=1, source_target_pairs={{1,3},{3,5},{5,7},{9,11},{11,13},{13,15},{17,19},{19,21},{21,23},{... | collective-permute-start | bytes 3145736 | tf_op jit(solution)/shard_map/ppermute | solution.py:356
  327.2 23.4 %collective-permute-start.51 = (f32[128,8,256]{2,1,0:T(8,128)S(1)}, f32[128,8,256]{2,1,0:T(8,128)}, u32[]{:S(2)}, u32[]{:S(2)}) collective-permute-start(f32[128,8,256]{2,1,0:T(8,128)S(1)} %pad_maximum_fusion.5.refs_1_), channel_id=1, source_target_pairs={{2,0},{3,1},{4,2},{5,3},{6,4},{7,5},{10,8},{11,9},{12,10},{13,11},... | collective-permute-start | bytes 3145736 | tf_op jit(solution)/shard_map/ppermute | solution.py:353
  337.0 21.7 %collective-permute-start.52 = (f32[128,8,256]{2,1,0:T(8,128)}, f32[128,8,256]{2,1,0:T(8,128)S(1)}, u32[]{:S(2)}, u32[]{:S(2)}) collective-permute-start(f32[128,8,256]{2,1,0:T(8,128)} %get-tuple-element.390), channel_id=1, source_target_pairs={{1,3},{3,5},{5,7},{9,11},{11,13},{13,15},{17,19},{19,21},{21,23},{... | collective-permute-start | bytes 3145736 | tf_op jit(solution)/shard_map/ppermute | solution.py:356
  348.7 23.5 %collective-permute-start.55 = (f32[128,8,256]{2,1,0:T(8,128)S(1)}, f32[128,8,256]{2,1,0:T(8,128)}, u32[]{:S(2)}, u32[]{:S(2)}) collective-permute-start(f32[128,8,256]{2,1,0:T(8,128)S(1)} %pad_maximum_fusion.4.refs_1_), channel_id=1, source_target_pairs={{2,0},{3,1},{4,2},{5,3},{6,4},{7,5},{10,8},{11,9},{12,10},{13,11},... | collective-permute-start | bytes 3145736 | tf_op jit(solution)/shard_map/ppermute | solution.py:353
  358.7 21.6 %collective-permute-start.56 = (f32[128,8,256]{2,1,0:T(8,128)}, f32[128,8,256]{2,1,0:T(8,128)S(1)}, u32[]{:S(2)}, u32[]{:S(2)}) collective-permute-start(f32[128,8,256]{2,1,0:T(8,128)} %get-tuple-element.404), channel_id=1, source_target_pairs={{1,3},{3,5},{5,7},{9,11},{11,13},{13,15},{17,19},{19,21},{21,23},{... | collective-permute-start | bytes 3145736 | tf_op jit(solution)/shard_map/ppermute | solution.py:356
  364.9 21.7 %collective-permute-start.57 = (f32[128,8,256]{2,1,0:T(8,128)}, f32[128,8,256]{2,1,0:T(8,128)S(1)}, u32[]{:S(2)}, u32[]{:S(2)}) collective-permute-start(f32[128,8,256]{2,1,0:T(8,128)} %turn.27), channel_id=1, source_target_pairs={{0,1},{1,0},{2,3},{3,2},{4,5},{5,4},{6,7},{7,6},{8,9},{9,8},{10,11... | collective-permute-start | bytes 3145736 | tf_op jit(solution)/shard_map/ppermute | solution.py:359
  369.0 21.6 %collective-permute-start.54 = (f32[128,8,256]{2,1,0:T(8,128)S(1)}, f32[128,8,256]{2,1,0:T(8,128)S(1)}, u32[]{:S(2)}, u32[]{:S(2)}) collective-permute-start(f32[128,8,256]{2,1,0:T(8,128)S(1)} %pad_maximum_fusion.3.refs_1_), channel_id=1, source_target_pairs={{0,16},{8,24},{16,0},{24,8},{1,17},{9,25},{17,1},{25,9},{2,18},{10... | collective-permute-start | bytes 3145736 | tf_op jit(solution)/shard_map/ppermute | solution.py:347
  370.3 23.5 %collective-permute-start.59 = (f32[128,8,256]{2,1,0:T(8,128)S(1)}, f32[128,8,256]{2,1,0:T(8,128)}, u32[]{:S(2)}, u32[]{:S(2)}) collective-permute-start(f32[128,8,256]{2,1,0:T(8,128)S(1)} %pad_maximum_fusion.3.refs_1_), channel_id=1, source_target_pairs={{2,0},{3,1},{4,2},{5,3},{6,4},{7,5},{10,8},{11,9},{12,10},{13,11},... | collective-permute-start | bytes 3145736 | tf_op jit(solution)/shard_map/ppermute | solution.py:353
  380.3 22.0 %collective-permute-start.60 = (f32[128,8,256]{2,1,0:T(8,128)}, f32[128,8,256]{2,1,0:T(8,128)S(1)}, u32[]{:S(2)}, u32[]{:S(2)}) collective-permute-start(f32[128,8,256]{2,1,0:T(8,128)} %get-tuple-element.418), channel_id=1, source_target_pairs={{1,3},{3,5},{5,7},{9,11},{11,13},{13,15},{17,19},{19,21},{21,23},{... | collective-permute-start | bytes 3145736 | tf_op jit(solution)/shard_map/ppermute | solution.py:356
  386.6 21.9 %collective-permute-start.61 = (f32[128,8,256]{2,1,0:T(8,128)}, f32[128,8,256]{2,1,0:T(8,128)S(1)}, u32[]{:S(2)}, u32[]{:S(2)}) collective-permute-start(f32[128,8,256]{2,1,0:T(8,128)} %turn.28), channel_id=1, source_target_pairs={{0,1},{1,0},{2,3},{3,2},{4,5},{5,4},{6,7},{7,6},{8,9},{9,8},{10,11... | collective-permute-start | bytes 3145736 | tf_op jit(solution)/shard_map/ppermute | solution.py:359
  390.7 21.9 %collective-permute-start.58 = (f32[128,8,256]{2,1,0:T(8,128)S(1)}, f32[128,8,256]{2,1,0:T(8,128)S(1)}, u32[]{:S(2)}, u32[]{:S(2)}) collective-permute-start(f32[128,8,256]{2,1,0:T(8,128)S(1)} %pad_maximum_fusion.2.refs_1_), channel_id=1, source_target_pairs={{0,16},{8,24},{16,0},{24,8},{1,17},{9,25},{17,1},{25,9},{2,18},{10... | collective-permute-start | bytes 3145736 | tf_op jit(solution)/shard_map/ppermute | solution.py:347
  391.9 23.0 %collective-permute-start.62 = (f32[128,8,256]{2,1,0:T(8,128)S(1)}, f32[128,8,256]{2,1,0:T(8,128)}, u32[]{:S(2)}, u32[]{:S(2)}) collective-permute-start(f32[128,8,256]{2,1,0:T(8,128)S(1)} %pad_maximum_fusion.2.refs_1_), channel_id=1, source_target_pairs={{2,0},{3,1},{4,2},{5,3},{6,4},{7,5},{10,8},{11,9},{12,10},{13,11},... | collective-permute-start | bytes 3145736 | tf_op jit(solution)/shard_map/ppermute | solution.py:353
  402.3 22.6 %collective-permute-start.63 = (f32[128,8,256]{2,1,0:T(8,128)}, f32[128,8,256]{2,1,0:T(8,128)S(1)}, u32[]{:S(2)}, u32[]{:S(2)}) collective-permute-start(f32[128,8,256]{2,1,0:T(8,128)} %get-tuple-element.432), channel_id=1, source_target_pairs={{1,3},{3,5},{5,7},{9,11},{11,13},{13,15},{17,19},{19,21},{21,23},{... | collective-permute-start | bytes 3145736 | tf_op jit(solution)/shard_map/ppermute | solution.py:356
  433.7 45.9 %collective-permute-start.68 = (f32[64,112,256]{2,1,0:T(8,128)}, f32[64,112,256]{2,1,0:T(8,128)S(1)}, u32[]{:S(2)}, u32[]{:S(2)}) collective-permute-start(f32[64,112,256]{2,1,0:T(8,128)} %get-tuple-element.443), channel_id=1, source_target_pairs={{0,8},{8,0},{16,24},{24,16},{1,9},{9,1},{17,25},{25,17},{2,10},{10... | collective-permute-start | bytes 22020104 | tf_op jit(solution)/shard_map/ppermute | solution.py:350
  446.4 27.0 %collective-permute-start.64 = (f32[128,8,256]{2,1,0:T(8,128)}, f32[128,8,256]{2,1,0:T(8,128)}, u32[]{:S(2)}, u32[]{:S(2)}) collective-permute-start(f32[128,8,256]{2,1,0:T(8,128)} %get-tuple-element.433), channel_id=1, source_target_pairs={{1,3},{3,5},{5,7},{9,11},{11,13},{13,15},{17,19},{19,21},{21,23},{... | collective-permute-start | bytes 3145736 | tf_op jit(solution)/shard_map/ppermute | solution.py:356
  448.9 26.9 %collective-permute-start.66 = (f32[128,8,256]{2,1,0:T(8,128)}, f32[128,8,256]{2,1,0:T(8,128)}, u32[]{:S(2)}, u32[]{:S(2)}) collective-permute-start(f32[128,8,256]{2,1,0:T(8,128)} %turn.31), channel_id=1, source_target_pairs={{0,1},{1,0},{2,3},{3,2},{4,5},{5,4},{6,7},{7,6},{8,9},{9,8},{10,11... | collective-permute-start | bytes 3145736 | tf_op jit(solution)/shard_map/ppermute | solution.py:359
  475.8 24.2 %collective-permute-start.67 = (f32[128,8,256]{2,1,0:T(8,128)}, f32[128,8,256]{2,1,0:T(8,128)}, u32[]{:S(2)}, u32[]{:S(2)}) collective-permute-start(f32[128,8,256]{2,1,0:T(8,128)} %turn.30), channel_id=1, source_target_pairs={{0,1},{1,0},{2,3},{3,2},{4,5},{5,4},{6,7},{7,6},{8,9},{9,8},{10,11... | collective-permute-start | bytes 3145736 | tf_op jit(solution)/shard_map/ppermute | solution.py:359
  478.8 25.9 %collective-permute-start.70 = (f32[64,8,256]{2,1,0:T(8,128)}, f32[64,8,256]{2,1,0:T(8,128)S(1)}, u32[]{:S(2)}, u32[]{:S(2)}) collective-permute-start(f32[64,8,256]{2,1,0:T(8,128)} %get-tuple-element.449), channel_id=1, source_target_pairs={{0,8},{8,0},{16,24},{24,16},{1,9},{9,1},{17,25},{25,17},{2,10},{10... | collective-permute-start | bytes 1572872 | tf_op jit(solution)/shard_map/ppermute | solution.py:350
  (70 other events, 716.0 us)

commit v9 on v8

--- a/solution.py
+++ b/solution.py
@@ -381,6 +381,7 @@
 
     quarter = max(3, n // 4)
     _, token = exchange(0, quarter)
+    give_rest, got_rest = exchange(quarter, n, sent[0])
 
     far, deep = [None] * n, [None] * n
 
@@ -410,8 +411,7 @@
     lost_a = factors.pop(4)
 
     first = quarter * size
-    mine, peer, mine_rest, peer_rest = local_terms(where, gate(occ, token, sent[0], sent[2])[0], lost_a, factors, first)
-    _, got_rest = exchange(quarter, n, mine)
+    mine, peer, mine_rest, peer_rest = local_terms(where, gate(occ, token, sent[0], sent[2], give_rest)[0], lost_a, factors, first)
     far[0][0], _ = gate(far[0][0], mine)
     parts = [(0, quarter, 0, (mine, other_core(gate(peer, *far[0], *deep[0])[0])))]
 

time: 514 us -> 516 us (level)
    unnamed x126 -> x124, local copies, waits for them, and re-layouts: 15.7 us -> 16.9 us
  transfers between devices with their start and end apart: 71 -> 71, of which waited for: 21 -> 27; matrix products, arithmetic and copies ran while one was open for 6% -> 7% of each run, Pallas kernels for 42% -> 42%
where the time goes in v9:
time: 516 us; the launch traced here: 513 us
  Pallas kernels  222 us (43%)
  starting transfers between devices  131 us (25%)
  waiting for transfers between devices  104 us (20%)
  local copies, waits for them, and re-layouts  45.3 us (9%)
  other arithmetic  9.33 us (2%)
    ppermute x16, waiting for transfers between devices, two_up(): return lax.ppermute(v, 'lvl', [(i, i + 2) for i in range(1, n_lvl - 2, 2)])  84.5 us
    pallas_call x16, Pallas kernels, first_terms(): pl.pallas_call(functools.partial(first_kernel, len(slabs), len(deep)), gr...  82.3 us
    ppermute x16, starting transfers between devices, two_up(): return lax.ppermute(v, 'lvl', [(i, i + 2) for i in range(1, n_lvl - 2, 2)])  62.6 us
    pallas_call x16, Pallas kernels, finish(): pl.pallas_call(functools.partial(finish_kernel, len(alias)), grid_spec=pl...  49.4 us
    pallas_call x16, Pallas kernels, turn(): pl.pallas_call(turn_kernel, grid=(rows // block, size // SPAN), in_specs=...  38.4 us
    pallas_call x1, Pallas kernels, local_terms(): pl.pallas_call(functools.partial(local_kernel, size), grid_spec=pltpu.Pre...  32.7 us
    ppermute x15, starting transfers between devices, two_down(): return lax.ppermute(v, 'lvl', [(i, i - 2) for i in range(2, n_lvl)])  29 us
    dynamic_slice x4, local copies, waits for them, and re-layouts, cut(): lax.dynamic_slice_in_dim(array, core[which] * half + at, size, axis=1)  18.8 us
  transfers between devices with their start and end apart: 71, of which 27 were waited for; matrix products, arithmetic and copies ran while one was open for 7% of the time, Pallas kernels for 42%

profile of v9, /device:TPU:21, one launch (start us, length us, event | category | flops | bytes accessed | tf_op | source)
XLA Modules:
  0.0 513.1 jit_solution(15852112278996349269)
XLA Ops:
  0.0 3.2 dynamic-slice_bitcast_fusion.1
  3.8 3.0 dynamic-slice_bitcast_fusion.2
  18.2 6.2 %dynamic-slice_bitcast_fusion = f32[64,96,256]{2,1,0:T(8,128)} fusion(f32[1,64,256,256]{3,2,1,0:T(8,128)} %param.6, s32[]{:T(128)S(6)} %select_n.72), kind=kLoop, calls=%fused_computation | loop fusion | bytes 12582916 | tf_op jit(solution)/shard_map/dynamic_slice | solution.py:362
  24.4 6.4 %dynamic-slice_bitcast_fusion.4 = (f32[64,8,256]{2,1,0:T(8,128)}, f32[64,8,256]{2,1,0:T(8,128)S(1)}, f32[64,8,256]{2,1,0:T(8,128)}, f32[64,8,256]{2,1,0:T(8,128)...) fusion(f32[1,64,256,256]{3,2,1,0:T(8,128)} %param.6, ...), kind=kLoop, calls=%fused_computation.20 | loop fusion | bytes 16777280 | tf_op jit(solution)/shard_map/dynamic_slice | solution.py:362
  35.4 32.7 %local_terms.1 = (f32[2,64,32,256]{3,2,1,0:T(8,128)}, f32[2,64,32,256]{3,2,1,0:T(8,128)}, f32[2,64,96,256]{3,2,1,0:T(8,128)}, f32[2,64,96,256]{3,2,1,0:T(8,128)}) custom-call(s32[7]{0:T(128)} %stack.31.where._.core, f32[256,1]{1,0:T(8,128)} %get-tuple-element.231.lost_a, f32[64,256,256]{2,1,0:T(8,128)} %bitcast.52, ...), custom_call_target="tpu_custom_call" | custom-call | flops 1000 | bytes 1000 | tf_op jit(solution)/shard_map/local_terms/pallas_call | solution.py:165
  68.7 7.0 %collective-permute-done.7.refs_7_.refs_5_ = f32[2,64,32,256]{3,2,1,0:T(8,128)S(1)} collective-permute-done((f32[2,64,32,256]{3,2,1,0:T(8,128)}, f32[2,64,32,256]{3,2,1,0:T(8,128)S(1)}, u32[]{:S(2)}, u32[]{:S(2)}) %collective-permute-start.7) | collective-permute-done | bytes 4194336 | tf_op jit(solution)/shard_map/ppermute | solution.py:350
  77.8 5.1 first_terms.18
  82.9 4.3 collective-permute-start.11
  92.7 5.2 %first_terms.16 = (f32[128,8,256]{2,1,0:T(8,128)}, f32[128,8,256]{2,1,0:T(8,128)}, f32[128,8,256]{2,1,0:T(8,128)}) custom-call(s32[7]{0:T(128)} %stack.31.where._.core, f32[2,256]{1,0:T(2,128)} %get-tuple-element.228.fall, bf16[512,256]{1,0:T(8,128)(2,1)} %get-tuple-element.229.refs_0_, f32[128,8,256]{2,1,0:T(8,128)} %pad_maximum_fusion.15.refs_1_, ...), custom_call_target="tpu_custom_call" | custom-call | flops 1000 | bytes 1000 | tf_op jit(solution)/shard_map/first_terms/pallas_call | solution.py:232
  97.8 11.9 %collective-permute-done.11.lifted = f32[128,8,256]{2,1,0:T(8,128)S(1)} collective-permute-done((f32[128,8,256]{2,1,0:T(8,128)}, f32[128,8,256]{2,1,0:T(8,128)S(1)}, u32[]{:S(2)}, u32[]{:S(2)}) %collective-permute-start.11) | collective-permute-done | bytes 1048608 | tf_op jit(solution)/shard_map/ppermute | solution.py:356
  109.7 4.0 collective-permute-start.12
  120.5 5.1 first_terms.17
  125.6 9.7 %collective-permute-done.12.lifted = f32[128,8,256]{2,1,0:T(8,128)S(1)} collective-permute-done((f32[128,8,256]{2,1,0:T(8,128)}, f32[128,8,256]{2,1,0:T(8,128)S(1)}, u32[]{:S(2)}, u32[]{:S(2)}) %collective-permute-start.12) | collective-permute-done | bytes 1048608 | tf_op jit(solution)/shard_map/ppermute | solution.py:356
  135.4 4.0 collective-permute-start.16
  141.9 4.9 fusion
  150.2 5.1 first_terms.19
  155.4 4.8 collective-permute-done.16.lifted
  160.2 4.0 collective-permute-start.20
  168.1 3.0 finish.16
  171.2 3.0 finish.17
  177.4 5.2 %first_terms.20 = (f32[128,8,256]{2,1,0:T(8,128)}, f32[128,8,256]{2,1,0:T(8,128)}, f32[128,8,256]{2,1,0:T(8,128)}) custom-call(s32[7]{0:T(128)} %stack.31.where._.core, f32[2,256]{1,0:T(2,128)} %get-tuple-element.228.fall, bf16[512,256]{1,0:T(8,128)(2,1)} %get-tuple-element.229.refs_0_, f32[128,8,256]{2,1,0:T(8,128)} %copy-done.9, ...), custom_call_target="tpu_custom_call" | custom-call | flops 1000 | bytes 1000 | tf_op jit(solution)/shard_map/first_terms/pallas_call | solution.py:232
  184.1 4.0 collective-permute-start.24
  191.5 3.1 finish.18
  199.0 5.2 %first_terms.21 = (f32[128,8,256]{2,1,0:T(8,128)}, f32[128,8,256]{2,1,0:T(8,128)}, f32[128,8,256]{2,1,0:T(8,128)}) custom-call(s32[7]{0:T(128)} %stack.31.where._.core, f32[2,256]{1,0:T(2,128)} %get-tuple-element.228.fall, bf16[512,256]{1,0:T(8,128)(2,1)} %get-tuple-element.229.refs_0_, f32[128,8,256]{2,1,0:T(8,128)} %copy-done.7, ...), custom_call_target="tpu_custom_call" | custom-call | flops 1000 | bytes 1000 | tf_op jit(solution)/shard_map/first_terms/pallas_call | solution.py:232
  207.1 4.0 collective-permute-start.28
  215.1 3.2 finish.19
  221.5 5.1 first_terms.22
  229.1 4.0 collective-permute-start.32
  236.6 3.1 finish.20
  242.9 5.1 first_terms.23
  250.8 4.0 collective-permute-start.36
  258.2 3.1 finish.21
  264.5 5.2 %first_terms.24 = (f32[128,8,256]{2,1,0:T(8,128)}, f32[128,8,256]{2,1,0:T(8,128)}, f32[128,8,256]{2,1,0:T(8,128)}) custom-call(s32[7]{0:T(128)} %stack.31.where._.core, f32[2,256]{1,0:T(2,128)} %get-tuple-element.228.fall, bf16[512,256]{1,0:T(8,128)(2,1)} %get-tuple-element.229.refs_0_, f32[128,8,256]{2,1,0:T(8,128)} %copy-done.12, ...), custom_call_target="tpu_custom_call" | custom-call | flops 1000 | bytes 1000 | tf_op jit(solution)/shard_map/first_terms/pallas_call | solution.py:232
  272.4 4.0 collective-permute-start.40
  279.8 3.1 finish.22
  286.2 5.1 first_terms.25
  294.0 4.0 collective-permute-start.44
  301.4 3.1 finish.23
  307.8 5.1 %first_terms.26 = (f32[128,8,256]{2,1,0:T(8,128)}, f32[128,8,256]{2,1,0:T(8,128)}, f32[128,8,256]{2,1,0:T(8,128)}) custom-call(s32[7]{0:T(128)} %stack.31.where._.core, f32[2,256]{1,0:T(2,128)} %get-tuple-element.228.fall, bf16[512,256]{1,0:T(8,128)(2,1)} %get-tuple-element.229.refs_0_, f32[128,8,256]{2,1,0:T(8,128)} %copy-done.14, ...), custom_call_target="tpu_custom_call" | custom-call | flops 1000 | bytes 1000 | tf_op jit(solution)/shard_map/first_terms/pallas_call | solution.py:232
  315.6 4.2 collective-permute-start.48
  323.2 3.1 finish.24
  329.5 5.3 %first_terms.27 = (f32[128,8,256]{2,1,0:T(8,128)}, f32[128,8,256]{2,1,0:T(8,128)}, f32[128,8,256]{2,1,0:T(8,128)}) custom-call(s32[7]{0:T(128)} %stack.31.where._.core, f32[2,256]{1,0:T(2,128)} %get-tuple-element.228.fall, bf16[512,256]{1,0:T(8,128)(2,1)} %get-tuple-element.229.refs_0_, f32[128,8,256]{2,1,0:T(8,128)} %copy-done.15, ...), custom_call_target="tpu_custom_call" | custom-call | flops 1000 | bytes 1000 | tf_op jit(solution)/shard_map/first_terms/pallas_call | solution.py:232
  337.2 3.9 collective-permute-start.52
  345.1 3.1 finish.25
  351.4 5.1 first_terms.28
  358.8 3.9 collective-permute-start.56
  366.2 3.2 finish.26
  372.7 5.2 %first_terms.29 = (f32[128,8,256]{2,1,0:T(8,128)}, f32[128,8,256]{2,1,0:T(8,128)}, f32[128,8,256]{2,1,0:T(8,128)}) custom-call(s32[7]{0:T(128)} %stack.31.where._.core, f32[2,256]{1,0:T(2,128)} %get-tuple-element.228.fall, bf16[512,256]{1,0:T(8,128)(2,1)} %get-tuple-element.229.refs_0_, f32[128,8,256]{2,1,0:T(8,128)} %copy-done.17, ...), custom_call_target="tpu_custom_call" | custom-call | flops 1000 | bytes 1000 | tf_op jit(solution)/shard_map/first_terms/pallas_call | solution.py:232
  380.5 4.0 collective-permute-start.60
  387.9 3.1 finish.27
  394.3 5.1 first_terms.30
  399.4 3.6 collective-permute-done.60.lifted
  403.0 3.9 collective-permute-start.63
  410.3 3.1 finish.28
  416.0 5.2 %first_terms.31 = (f32[128,8,256]{2,1,0:T(8,128)}, f32[128,8,256]{2,1,0:T(8,128)}, f32[128,8,256]{2,1,0:T(8,128)}) custom-call(s32[7]{0:T(128)} %stack.31.where._.core, f32[2,256]{1,0:T(2,128)} %get-tuple-element.228.fall, bf16[512,256]{1,0:T(8,128)(2,1)} %get-tuple-element.229.refs_0_, f32[128,8,256]{2,1,0:T(8,128)} %copy-done.18, ...), custom_call_target="tpu_custom_call" | custom-call | flops 1000 | bytes 1000 | tf_op jit(solution)/shard_map/first_terms/pallas_call | solution.py:232
  421.2 4.9 collective-permute-done.63.lifted
  431.9 3.1 finish.29
  435.0 13.1 %collective-permute-start.68 = (f32[64,112,256]{2,1,0:T(8,128)}, f32[64,112,256]{2,1,0:T(8,128)S(1)}, u32[]{:S(2)}, u32[]{:S(2)}) collective-permute-start(f32[64,112,256]{2,1,0:T(8,128)} %get-tuple-element.443), channel_id=1, source_target_pairs={{0,8},{8,0},{16,24},{24,16},{1,9},{9,1},{17,25},{25,17},{2,10},{10... | collective-permute-start | bytes 22020104 | tf_op jit(solution)/shard_map/ppermute | solution.py:350
  450.7 24.4 %collective-permute-done.64.lifted = f32[128,8,256]{2,1,0:T(8,128)} collective-permute-done((f32[128,8,256]{2,1,0:T(8,128)}, f32[128,8,256]{2,1,0:T(8,128)}, u32[]{:S(2)}, u32[]{:S(2)}) %collective-permute-start.64) | collective-permute-done | bytes 1048608 | tf_op jit(solution)/shard_map/ppermute | solution.py:356
  477.4 3.1 finish.30
  481.3 3.0 copy-done.1
  484.3 11.2 %put.3.refs_4_ = f32[64,256,256]{2,1,0:T(8,128)} custom-call(s32[7]{0:T(128)} %stack.31.where._.core, f32[64,112,256]{2,1,0:T(8,128)} %copy-done.1, f32[64,256,256]{2,1,0:T(8,128)} %get-tuple-element.447._), custom_call_target="tpu_custom_call", output_to_operand_aliasing={{}: (2, {})} | custom-call | flops 1000 | bytes 1000 | tf_op jit(solution)/shard_map/put/pallas_call | solution.py:313
  495.5 6.1 %collective-permute-done.67.refs_1_.refs_3_ = f32[128,8,256]{2,1,0:T(8,128)} collective-permute-done((f32[128,8,256]{2,1,0:T(8,128)}, f32[128,8,256]{2,1,0:T(8,128)}, u32[]{:S(2)}, u32[]{:S(2)}) %collective-permute-start.67) | collective-permute-done | bytes 1048608 | tf_op jit(solution)/shard_map/ppermute | solution.py:359
  501.6 3.1 finish.31
  (279 shorter events, 163.8 us)
Async XLA Ops:
  3.2 27.6 %collective-permute-start = (f32[64,32,256]{2,1,0:T(8,128)}, f32[64,32,256]{2,1,0:T(8,128)}, u32[]{:S(2)}, u32[]{:S(2)}) collective-permute-start(f32[64,32,256]{2,1,0:T(8,128)} %dynamic-slice_bitcast_fusion.1), channel_id=1, source_target_pairs={{0,8},{8,0},{16,24},{24,16},{1,9},{9,1},{17,25},{25,17},{2,10},{10... | collective-permute-start | bytes 6291464 | tf_op jit(solution)/shard_map/ppermute | solution.py:350
  6.9 61.2 %collective-permute-start.2 = (f32[64,16,256]{2,1,0:T(8,128)}, f32[64,16,256]{2,1,0:T(8,128)S(1)}, u32[]{:S(2)}, u32[]{:S(2)}) collective-permute-start(f32[64,16,256]{2,1,0:T(8,128)} %get-tuple-element.468), channel_id=1, source_target_pairs={{0,16},{8,24},{16,0},{24,8},{1,17},{9,25},{17,1},{25,9},{2,18},{10... | collective-permute-start | bytes 3145736 | tf_op jit(solution)/shard_map/ppermute | solution.py:347
  8.1 60.0 %collective-permute-start.5 = (f32[64,16,256]{2,1,0:T(8,128)}, f32[64,16,256]{2,1,0:T(8,128)S(1)}, u32[]{:S(2)}, u32[]{:S(2)}) collective-permute-start(f32[64,16,256]{2,1,0:T(8,128)} %get-tuple-element.468), channel_id=1, source_target_pairs={{2,0},{3,1},{4,2},{5,3},{6,4},{7,5},{10,8},{11,9},{12,10},{13,11},... | collective-permute-start | bytes 3145736 | tf_op jit(solution)/shard_map/ppermute | solution.py:353
  10.2 57.9 %collective-permute-start.3 = (f32[64,16,256]{2,1,0:T(8,128)}, f32[64,16,256]{2,1,0:T(8,128)S(1)}, u32[]{:S(2)}, u32[]{:S(2)}) collective-permute-start(f32[64,16,256]{2,1,0:T(8,128)} %get-tuple-element.467), channel_id=1, source_target_pairs={{0,24},{8,16},{16,8},{24,0},{1,25},{9,17},{17,9},{25,1},{2,26},{10... | collective-permute-start | bytes 3145736 | tf_op jit(solution)/shard_map/ppermute | solution.py:393
  10.9 57.2 %collective-permute-start.6 = (f32[64,16,256]{2,1,0:T(8,128)}, f32[64,16,256]{2,1,0:T(8,128)}, u32[]{:S(2)}, u32[]{:S(2)}) collective-permute-start(f32[64,16,256]{2,1,0:T(8,128)} %get-tuple-element.467), channel_id=1, source_target_pairs={{2,8},{3,9},{4,10},{5,11},{6,12},{7,13},{10,0},{11,1},{12,2},{13,3... | collective-permute-start | bytes 3145736 | tf_op jit(solution)/shard_map/ppermute | solution.py:396
  75.7 40.6 %collective-permute-start.8 = (f32[2,64,96,256]{3,2,1,0:T(8,128)}, f32[2,64,96,256]{3,2,1,0:T(8,128)}, u32[]{:S(2)}, u32[]{:S(2)}) collective-permute-start(f32[2,64,96,256]{3,2,1,0:T(8,128)} %get-tuple-element.245), channel_id=1, source_target_pairs={{0,8},{8,0},{16,24},{24,16},{1,9},{9,1},{17,25},{25,17},{2,10},{10... | collective-permute-start | bytes 37748744 | tf_op jit(solution)/shard_map/ppermute | solution.py:350
  76.1 40.2 %collective-permute-start.1 = (f32[64,96,256]{2,1,0:T(8,128)}, f32[64,96,256]{2,1,0:T(8,128)}, u32[]{:S(2)}, u32[]{:S(2)}) collective-permute-start(f32[64,96,256]{2,1,0:T(8,128)} %dynamic-slice_bitcast_fusion), channel_id=1, source_target_pairs={{0,8},{8,0},{16,24},{24,16},{1,9},{9,1},{17,25},{25,17},{2,10},{10... | collective-permute-start | bytes 18874376 | tf_op jit(solution)/shard_map/ppermute | solution.py:350
  82.9 26.8 %collective-permute-start.11 = (f32[128,8,256]{2,1,0:T(8,128)}, f32[128,8,256]{2,1,0:T(8,128)S(1)}, u32[]{:S(2)}, u32[]{:S(2)}) collective-permute-start(f32[128,8,256]{2,1,0:T(8,128)} %get-tuple-element.251), channel_id=1, source_target_pairs={{1,3},{3,5},{5,7},{9,11},{11,13},{13,15},{17,19},{19,21},{21,23},{... | collective-permute-start | bytes 3145736 | tf_op jit(solution)/shard_map/ppermute | solution.py:356
  87.3 28.9 %collective-permute-start.4 = (f32[128,8,256]{2,1,0:T(8,128)}, f32[128,8,256]{2,1,0:T(8,128)S(1)}, u32[]{:S(2)}, u32[]{:S(2)}) collective-permute-start(f32[128,8,256]{2,1,0:T(8,128)} %pad_maximum_fusion.14.refs_1_), channel_id=1, source_target_pairs={{0,16},{8,24},{16,0},{24,8},{1,17},{9,25},{17,1},{25,9},{2,18},{10... | collective-permute-start | bytes 3145736 | tf_op jit(solution)/shard_map/ppermute | solution.py:347
  90.8 28.8 %collective-permute-start.10 = (f32[128,8,256]{2,1,0:T(8,128)}, f32[128,8,256]{2,1,0:T(8,128)S(1)}, u32[]{:S(2)}, u32[]{:S(2)}) collective-permute-start(f32[128,8,256]{2,1,0:T(8,128)} %pad_maximum_fusion.14.refs_1_), channel_id=1, source_target_pairs={{2,0},{3,1},{4,2},{5,3},{6,4},{7,5},{10,8},{11,9},{12,10},{13,11},... | collective-permute-start | bytes 3145736 | tf_op jit(solution)/shard_map/ppermute | solution.py:353
  109.7 25.6 %collective-permute-start.12 = (f32[128,8,256]{2,1,0:T(8,128)}, f32[128,8,256]{2,1,0:T(8,128)S(1)}, u32[]{:S(2)}, u32[]{:S(2)}) collective-permute-start(f32[128,8,256]{2,1,0:T(8,128)} %get-tuple-element.252), channel_id=1, source_target_pairs={{1,3},{3,5},{5,7},{9,11},{11,13},{13,15},{17,19},{19,21},{21,23},{... | collective-permute-start | bytes 3145736 | tf_op jit(solution)/shard_map/ppermute | solution.py:356
  116.2 25.6 %collective-permute-start.13 = (f32[128,8,256]{2,1,0:T(8,128)}, f32[128,8,256]{2,1,0:T(8,128)S(1)}, u32[]{:S(2)}, u32[]{:S(2)}) collective-permute-start(f32[128,8,256]{2,1,0:T(8,128)} %turn.17), channel_id=1, source_target_pairs={{0,1},{1,0},{2,3},{3,2},{4,5},{5,4},{6,7},{7,6},{8,9},{9,8},{10,11... | collective-permute-start | bytes 3145736 | tf_op jit(solution)/shard_map/ppermute | solution.py:359
  116.4 30.5 %collective-permute-start.9 = (f32[128,8,256]{2,1,0:T(8,128)S(1)}, f32[128,8,256]{2,1,0:T(8,128)}, u32[]{:S(2)}, u32[]{:S(2)}) collective-permute-start(f32[128,8,256]{2,1,0:T(8,128)S(1)} %pad_maximum_fusion.13.refs_1_), channel_id=1, source_target_pairs={{0,16},{8,24},{16,0},{24,8},{1,17},{9,25},{17,1},{25,9},{2,18},{10... | collective-permute-start | bytes 3145736 | tf_op jit(solution)/shard_map/ppermute | solution.py:347
  117.6 32.6 %collective-permute-start.15 = (f32[128,8,256]{2,1,0:T(8,128)S(1)}, f32[128,8,256]{2,1,0:T(8,128)}, u32[]{:S(2)}, u32[]{:S(2)}) collective-permute-start(f32[128,8,256]{2,1,0:T(8,128)S(1)} %pad_maximum_fusion.13.refs_1_), channel_id=1, source_target_pairs={{2,0},{3,1},{4,2},{5,3},{6,4},{7,5},{10,8},{11,9},{12,10},{13,11},... | collective-permute-start | bytes 3145736 | tf_op jit(solution)/shard_map/ppermute | solution.py:353
  135.4 24.8 %collective-permute-start.16 = (f32[128,8,256]{2,1,0:T(8,128)}, f32[128,8,256]{2,1,0:T(8,128)}, u32[]{:S(2)}, u32[]{:S(2)}) collective-permute-start(f32[128,8,256]{2,1,0:T(8,128)} %get-tuple-element.262), channel_id=1, source_target_pairs={{1,3},{3,5},{5,7},{9,11},{11,13},{13,15},{17,19},{19,21},{21,23},{... | collective-permute-start | bytes 3145736 | tf_op jit(solution)/shard_map/ppermute | solution.py:356
  141.8 24.8 %collective-permute-start.17 = (f32[128,8,256]{2,1,0:T(8,128)}, f32[128,8,256]{2,1,0:T(8,128)S(1)}, u32[]{:S(2)}, u32[]{:S(2)}) collective-permute-start(f32[128,8,256]{2,1,0:T(8,128)} %turn.16), channel_id=1, source_target_pairs={{0,1},{1,0},{2,3},{3,2},{4,5},{5,4},{6,7},{7,6},{8,9},{9,8},{10,11... | collective-permute-start | bytes 3145736 | tf_op jit(solution)/shard_map/ppermute | solution.py:359
  146.8 27.4 %collective-permute-start.14 = (f32[128,8,256]{2,1,0:T(8,128)S(1)}, f32[128,8,256]{2,1,0:T(8,128)}, u32[]{:S(2)}, u32[]{:S(2)}) collective-permute-start(f32[128,8,256]{2,1,0:T(8,128)S(1)} %pad_maximum_fusion.12.refs_1_), channel_id=1, source_target_pairs={{0,16},{8,24},{16,0},{24,8},{1,17},{9,25},{17,1},{25,9},{2,18},{10... | collective-permute-start | bytes 3145736 | tf_op jit(solution)/shard_map/ppermute | solution.py:347
  148.1 29.3 %collective-permute-start.19 = (f32[128,8,256]{2,1,0:T(8,128)S(1)}, f32[128,8,256]{2,1,0:T(8,128)}, u32[]{:S(2)}, u32[]{:S(2)}) collective-permute-start(f32[128,8,256]{2,1,0:T(8,128)S(1)} %pad_maximum_fusion.12.refs_1_), channel_id=1, source_target_pairs={{2,0},{3,1},{4,2},{5,3},{6,4},{7,5},{10,8},{11,9},{12,10},{13,11},... | collective-permute-start | bytes 3145736 | tf_op jit(solution)/shard_map/ppermute | solution.py:353
  160.2 23.9 %collective-permute-start.20 = (f32[128,8,256]{2,1,0:T(8,128)}, f32[128,8,256]{2,1,0:T(8,128)}, u32[]{:S(2)}, u32[]{:S(2)}) collective-permute-start(f32[128,8,256]{2,1,0:T(8,128)} %get-tuple-element.278), channel_id=1, source_target_pairs={{1,3},{3,5},{5,7},{9,11},{11,13},{13,15},{17,19},{19,21},{21,23},{... | collective-permute-start | bytes 3145736 | tf_op jit(solution)/shard_map/ppermute | solution.py:356
  166.6 23.9 %collective-permute-start.21 = (f32[128,8,256]{2,1,0:T(8,128)}, f32[128,8,256]{2,1,0:T(8,128)S(1)}, u32[]{:S(2)}, u32[]{:S(2)}) collective-permute-start(f32[128,8,256]{2,1,0:T(8,128)} %turn.18), channel_id=1, source_target_pairs={{0,1},{1,0},{2,3},{3,2},{4,5},{5,4},{6,7},{7,6},{8,9},{9,8},{10,11... | collective-permute-start | bytes 3145736 | tf_op jit(solution)/shard_map/ppermute | solution.py:359
  175.5 23.5 %collective-permute-start.23 = (f32[128,8,256]{2,1,0:T(8,128)S(1)}, f32[128,8,256]{2,1,0:T(8,128)}, u32[]{:S(2)}, u32[]{:S(2)}) collective-permute-start(f32[128,8,256]{2,1,0:T(8,128)S(1)} %pad_maximum_fusion.11.refs_1_), channel_id=1, source_target_pairs={{2,0},{3,1},{4,2},{5,3},{6,4},{7,5},{10,8},{11,9},{12,10},{13,11},... | collective-permute-start | bytes 3145736 | tf_op jit(solution)/shard_map/ppermute | solution.py:353
  184.1 23.0 %collective-permute-start.24 = (f32[128,8,256]{2,1,0:T(8,128)}, f32[128,8,256]{2,1,0:T(8,128)}, u32[]{:S(2)}, u32[]{:S(2)}) collective-permute-start(f32[128,8,256]{2,1,0:T(8,128)} %get-tuple-element.292), channel_id=1, source_target_pairs={{1,3},{3,5},{5,7},{9,11},{11,13},{13,15},{17,19},{19,21},{21,23},{... | collective-permute-start | bytes 3145736 | tf_op jit(solution)/shard_map/ppermute | solution.py:356
  190.5 23.0 %collective-permute-start.25 = (f32[128,8,256]{2,1,0:T(8,128)}, f32[128,8,256]{2,1,0:T(8,128)S(1)}, u32[]{:S(2)}, u32[]{:S(2)}) collective-permute-start(f32[128,8,256]{2,1,0:T(8,128)} %turn.19), channel_id=1, source_target_pairs={{0,1},{1,0},{2,3},{3,2},{4,5},{5,4},{6,7},{7,6},{8,9},{9,8},{10,11... | collective-permute-start | bytes 3145736 | tf_op jit(solution)/shard_map/ppermute | solution.py:359
  195.8 22.5 %collective-permute-start.22 = (f32[128,8,256]{2,1,0:T(8,128)S(1)}, f32[128,8,256]{2,1,0:T(8,128)}, u32[]{:S(2)}, u32[]{:S(2)}) collective-permute-start(f32[128,8,256]{2,1,0:T(8,128)S(1)} %pad_maximum_fusion.10.refs_1_), channel_id=1, source_target_pairs={{0,16},{8,24},{16,0},{24,8},{1,17},{9,25},{17,1},{25,9},{2,18},{10... | collective-permute-start | bytes 3145736 | tf_op jit(solution)/shard_map/ppermute | solution.py:347
  197.0 24.5 %collective-permute-start.27 = (f32[128,8,256]{2,1,0:T(8,128)S(1)}, f32[128,8,256]{2,1,0:T(8,128)}, u32[]{:S(2)}, u32[]{:S(2)}) collective-permute-start(f32[128,8,256]{2,1,0:T(8,128)S(1)} %pad_maximum_fusion.10.refs_1_), channel_id=1, source_target_pairs={{2,0},{3,1},{4,2},{5,3},{6,4},{7,5},{10,8},{11,9},{12,10},{13,11},... | collective-permute-start | bytes 3145736 | tf_op jit(solution)/shard_map/ppermute | solution.py:353
  207.1 22.1 %collective-permute-start.28 = (f32[128,8,256]{2,1,0:T(8,128)}, f32[128,8,256]{2,1,0:T(8,128)}, u32[]{:S(2)}, u32[]{:S(2)}) collective-permute-start(f32[128,8,256]{2,1,0:T(8,128)} %get-tuple-element.306), channel_id=1, source_target_pairs={{1,3},{3,5},{5,7},{9,11},{11,13},{13,15},{17,19},{19,21},{21,23},{... | collective-permute-start | bytes 3145736 | tf_op jit(solution)/shard_map/ppermute | solution.py:356
  213.5 22.0 %collective-permute-start.29 = (f32[128,8,256]{2,1,0:T(8,128)}, f32[128,8,256]{2,1,0:T(8,128)S(1)}, u32[]{:S(2)}, u32[]{:S(2)}) collective-permute-start(f32[128,8,256]{2,1,0:T(8,128)} %turn.20), channel_id=1, source_target_pairs={{0,1},{1,0},{2,3},{3,2},{4,5},{5,4},{6,7},{7,6},{8,9},{9,8},{10,11... | collective-permute-start | bytes 3145736 | tf_op jit(solution)/shard_map/ppermute | solution.py:359
  219.6 23.4 %collective-permute-start.31 = (f32[128,8,256]{2,1,0:T(8,128)S(1)}, f32[128,8,256]{2,1,0:T(8,128)}, u32[]{:S(2)}, u32[]{:S(2)}) collective-permute-start(f32[128,8,256]{2,1,0:T(8,128)S(1)} %pad_maximum_fusion.9.refs_1_), channel_id=1, source_target_pairs={{2,0},{3,1},{4,2},{5,3},{6,4},{7,5},{10,8},{11,9},{12,10},{13,11},... | collective-permute-start | bytes 3145736 | tf_op jit(solution)/shard_map/ppermute | solution.py:353
  229.1 21.6 %collective-permute-start.32 = (f32[128,8,256]{2,1,0:T(8,128)}, f32[128,8,256]{2,1,0:T(8,128)}, u32[]{:S(2)}, u32[]{:S(2)}) collective-permute-start(f32[128,8,256]{2,1,0:T(8,128)} %get-tuple-element.320), channel_id=1, source_target_pairs={{1,3},{3,5},{5,7},{9,11},{11,13},{13,15},{17,19},{19,21},{21,23},{... | collective-permute-start | bytes 3145736 | tf_op jit(solution)/shard_map/ppermute | solution.py:356
  235.6 21.6 %collective-permute-start.33 = (f32[128,8,256]{2,1,0:T(8,128)}, f32[128,8,256]{2,1,0:T(8,128)S(1)}, u32[]{:S(2)}, u32[]{:S(2)}) collective-permute-start(f32[128,8,256]{2,1,0:T(8,128)} %turn.21), channel_id=1, source_target_pairs={{0,1},{1,0},{2,3},{3,2},{4,5},{5,4},{6,7},{7,6},{8,9},{9,8},{10,11... | collective-permute-start | bytes 3145736 | tf_op jit(solution)/shard_map/ppermute | solution.py:359
  239.8 21.6 %collective-permute-start.30 = (f32[128,8,256]{2,1,0:T(8,128)S(1)}, f32[128,8,256]{2,1,0:T(8,128)}, u32[]{:S(2)}, u32[]{:S(2)}) collective-permute-start(f32[128,8,256]{2,1,0:T(8,128)S(1)} %pad_maximum_fusion.8.refs_1_), channel_id=1, source_target_pairs={{0,16},{8,24},{16,0},{24,8},{1,17},{9,25},{17,1},{25,9},{2,18},{10... | collective-permute-start | bytes 3145736 | tf_op jit(solution)/shard_map/ppermute | solution.py:347
  241.0 23.5 %collective-permute-start.35 = (f32[128,8,256]{2,1,0:T(8,128)S(1)}, f32[128,8,256]{2,1,0:T(8,128)}, u32[]{:S(2)}, u32[]{:S(2)}) collective-permute-start(f32[128,8,256]{2,1,0:T(8,128)S(1)} %pad_maximum_fusion.8.refs_1_), channel_id=1, source_target_pairs={{2,0},{3,1},{4,2},{5,3},{6,4},{7,5},{10,8},{11,9},{12,10},{13,11},... | collective-permute-start | bytes 3145736 | tf_op jit(solution)/shard_map/ppermute | solution.py:353
  250.8 21.6 %collective-permute-start.36 = (f32[128,8,256]{2,1,0:T(8,128)}, f32[128,8,256]{2,1,0:T(8,128)}, u32[]{:S(2)}, u32[]{:S(2)}) collective-permute-start(f32[128,8,256]{2,1,0:T(8,128)} %get-tuple-element.334), channel_id=1, source_target_pairs={{1,3},{3,5},{5,7},{9,11},{11,13},{13,15},{17,19},{19,21},{21,23},{... | collective-permute-start | bytes 3145736 | tf_op jit(solution)/shard_map/ppermute | solution.py:356
  257.2 21.6 %collective-permute-start.37 = (f32[128,8,256]{2,1,0:T(8,128)}, f32[128,8,256]{2,1,0:T(8,128)S(1)}, u32[]{:S(2)}, u32[]{:S(2)}) collective-permute-start(f32[128,8,256]{2,1,0:T(8,128)} %turn.22), channel_id=1, source_target_pairs={{0,1},{1,0},{2,3},{3,2},{4,5},{5,4},{6,7},{7,6},{8,9},{9,8},{10,11... | collective-permute-start | bytes 3145736 | tf_op jit(solution)/shard_map/ppermute | solution.py:359
  261.4 21.6 %collective-permute-start.34 = (f32[128,8,256]{2,1,0:T(8,128)S(1)}, f32[128,8,256]{2,1,0:T(8,128)}, u32[]{:S(2)}, u32[]{:S(2)}) collective-permute-start(f32[128,8,256]{2,1,0:T(8,128)S(1)} %pad_maximum_fusion.7.refs_1_), channel_id=1, source_target_pairs={{0,16},{8,24},{16,0},{24,8},{1,17},{9,25},{17,1},{25,9},{2,18},{10... | collective-permute-start | bytes 3145736 | tf_op jit(solution)/shard_map/ppermute | solution.py:347
  262.6 23.5 %collective-permute-start.39 = (f32[128,8,256]{2,1,0:T(8,128)S(1)}, f32[128,8,256]{2,1,0:T(8,128)}, u32[]{:S(2)}, u32[]{:S(2)}) collective-permute-start(f32[128,8,256]{2,1,0:T(8,128)S(1)} %pad_maximum_fusion.7.refs_1_), channel_id=1, source_target_pairs={{2,0},{3,1},{4,2},{5,3},{6,4},{7,5},{10,8},{11,9},{12,10},{13,11},... | collective-permute-start | bytes 3145736 | tf_op jit(solution)/shard_map/ppermute | solution.py:353
  272.4 21.6 %collective-permute-start.40 = (f32[128,8,256]{2,1,0:T(8,128)}, f32[128,8,256]{2,1,0:T(8,128)}, u32[]{:S(2)}, u32[]{:S(2)}) collective-permute-start(f32[128,8,256]{2,1,0:T(8,128)} %get-tuple-element.348), channel_id=1, source_target_pairs={{1,3},{3,5},{5,7},{9,11},{11,13},{13,15},{17,19},{19,21},{21,23},{... | collective-permute-start | bytes 3145736 | tf_op jit(solution)/shard_map/ppermute | solution.py:356
  278.8 21.6 %collective-permute-start.41 = (f32[128,8,256]{2,1,0:T(8,128)}, f32[128,8,256]{2,1,0:T(8,128)S(1)}, u32[]{:S(2)}, u32[]{:S(2)}) collective-permute-start(f32[128,8,256]{2,1,0:T(8,128)} %turn.23), channel_id=1, source_target_pairs={{0,1},{1,0},{2,3},{3,2},{4,5},{5,4},{6,7},{7,6},{8,9},{9,8},{10,11... | collective-permute-start | bytes 3145736 | tf_op jit(solution)/shard_map/ppermute | solution.py:359
  283.0 21.6 %collective-permute-start.38 = (f32[128,8,256]{2,1,0:T(8,128)S(1)}, f32[128,8,256]{2,1,0:T(8,128)}, u32[]{:S(2)}, u32[]{:S(2)}) collective-permute-start(f32[128,8,256]{2,1,0:T(8,128)S(1)} %pad_maximum_fusion.6.refs_1_), channel_id=1, source_target_pairs={{0,16},{8,24},{16,0},{24,8},{1,17},{9,25},{17,1},{25,9},{2,18},{10... | collective-permute-start | bytes 3145736 | tf_op jit(solution)/shard_map/ppermute | solution.py:347
  284.2 23.5 %collective-permute-start.43 = (f32[128,8,256]{2,1,0:T(8,128)S(1)}, f32[128,8,256]{2,1,0:T(8,128)}, u32[]{:S(2)}, u32[]{:S(2)}) collective-permute-start(f32[128,8,256]{2,1,0:T(8,128)S(1)} %pad_maximum_fusion.6.refs_1_), channel_id=1, source_target_pairs={{2,0},{3,1},{4,2},{5,3},{6,4},{7,5},{10,8},{11,9},{12,10},{13,11},... | collective-permute-start | bytes 3145736 | tf_op jit(solution)/shard_map/ppermute | solution.py:353
  294.0 21.6 %collective-permute-start.44 = (f32[128,8,256]{2,1,0:T(8,128)}, f32[128,8,256]{2,1,0:T(8,128)}, u32[]{:S(2)}, u32[]{:S(2)}) collective-permute-start(f32[128,8,256]{2,1,0:T(8,128)} %get-tuple-element.362), channel_id=1, source_target_pairs={{1,3},{3,5},{5,7},{9,11},{11,13},{13,15},{17,19},{19,21},{21,23},{... | collective-permute-start | bytes 3145736 | tf_op jit(solution)/shard_map/ppermute | solution.py:356
  300.4 21.8 %collective-permute-start.45 = (f32[128,8,256]{2,1,0:T(8,128)}, f32[128,8,256]{2,1,0:T(8,128)S(1)}, u32[]{:S(2)}, u32[]{:S(2)}) collective-permute-start(f32[128,8,256]{2,1,0:T(8,128)} %turn.24), channel_id=1, source_target_pairs={{0,1},{1,0},{2,3},{3,2},{4,5},{5,4},{6,7},{7,6},{8,9},{9,8},{10,11... | collective-permute-start | bytes 3145736 | tf_op jit(solution)/shard_map/ppermute | solution.py:359
  304.6 21.7 %collective-permute-start.42 = (f32[128,8,256]{2,1,0:T(8,128)S(1)}, f32[128,8,256]{2,1,0:T(8,128)}, u32[]{:S(2)}, u32[]{:S(2)}) collective-permute-start(f32[128,8,256]{2,1,0:T(8,128)S(1)} %pad_maximum_fusion.5.refs_1_), channel_id=1, source_target_pairs={{0,16},{8,24},{16,0},{24,8},{1,17},{9,25},{17,1},{25,9},{2,18},{10... | collective-permute-start | bytes 3145736 | tf_op jit(solution)/shard_map/ppermute | solution.py:347
  305.8 23.7 %collective-permute-start.47 = (f32[128,8,256]{2,1,0:T(8,128)S(1)}, f32[128,8,256]{2,1,0:T(8,128)}, u32[]{:S(2)}, u32[]{:S(2)}) collective-permute-start(f32[128,8,256]{2,1,0:T(8,128)S(1)} %pad_maximum_fusion.5.refs_1_), channel_id=1, source_target_pairs={{2,0},{3,1},{4,2},{5,3},{6,4},{7,5},{10,8},{11,9},{12,10},{13,11},... | collective-permute-start | bytes 3145736 | tf_op jit(solution)/shard_map/ppermute | solution.py:353
  315.6 21.6 %collective-permute-start.48 = (f32[128,8,256]{2,1,0:T(8,128)}, f32[128,8,256]{2,1,0:T(8,128)S(1)}, u32[]{:S(2)}, u32[]{:S(2)}) collective-permute-start(f32[128,8,256]{2,1,0:T(8,128)} %get-tuple-element.376), channel_id=1, source_target_pairs={{1,3},{3,5},{5,7},{9,11},{11,13},{13,15},{17,19},{19,21},{21,23},{... | collective-permute-start | bytes 3145736 | tf_op jit(solution)/shard_map/ppermute | solution.py:356
  326.3 21.9 %collective-permute-start.46 = (f32[128,8,256]{2,1,0:T(8,128)S(1)}, f32[128,8,256]{2,1,0:T(8,128)S(1)}, u32[]{:S(2)}, u32[]{:S(2)}) collective-permute-start(f32[128,8,256]{2,1,0:T(8,128)S(1)} %pad_maximum_fusion.4.refs_1_), channel_id=1, source_target_pairs={{0,16},{8,24},{16,0},{24,8},{1,17},{9,25},{17,1},{25,9},{2,18},{10... | collective-permute-start | bytes 3145736 | tf_op jit(solution)/shard_map/ppermute | solution.py:347
  327.6 23.8 %collective-permute-start.51 = (f32[128,8,256]{2,1,0:T(8,128)S(1)}, f32[128,8,256]{2,1,0:T(8,128)}, u32[]{:S(2)}, u32[]{:S(2)}) collective-permute-start(f32[128,8,256]{2,1,0:T(8,128)S(1)} %pad_maximum_fusion.4.refs_1_), channel_id=1, source_target_pairs={{2,0},{3,1},{4,2},{5,3},{6,4},{7,5},{10,8},{11,9},{12,10},{13,11},... | collective-permute-start | bytes 3145736 | tf_op jit(solution)/shard_map/ppermute | solution.py:353
  337.2 21.6 %collective-permute-start.52 = (f32[128,8,256]{2,1,0:T(8,128)}, f32[128,8,256]{2,1,0:T(8,128)S(1)}, u32[]{:S(2)}, u32[]{:S(2)}) collective-permute-start(f32[128,8,256]{2,1,0:T(8,128)} %get-tuple-element.390), channel_id=1, source_target_pairs={{1,3},{3,5},{5,7},{9,11},{11,13},{13,15},{17,19},{19,21},{21,23},{... | collective-permute-start | bytes 3145736 | tf_op jit(solution)/shard_map/ppermute | solution.py:356
  343.5 21.6 %collective-permute-start.53 = (f32[128,8,256]{2,1,0:T(8,128)}, f32[128,8,256]{2,1,0:T(8,128)S(1)}, u32[]{:S(2)}, u32[]{:S(2)}) collective-permute-start(f32[128,8,256]{2,1,0:T(8,128)} %turn.26), channel_id=1, source_target_pairs={{0,1},{1,0},{2,3},{3,2},{4,5},{5,4},{6,7},{7,6},{8,9},{9,8},{10,11... | collective-permute-start | bytes 3145736 | tf_op jit(solution)/shard_map/ppermute | solution.py:359
  349.5 23.3 %collective-permute-start.55 = (f32[128,8,256]{2,1,0:T(8,128)S(1)}, f32[128,8,256]{2,1,0:T(8,128)}, u32[]{:S(2)}, u32[]{:S(2)}) collective-permute-start(f32[128,8,256]{2,1,0:T(8,128)S(1)} %pad_maximum_fusion.3.refs_1_), channel_id=1, source_target_pairs={{2,0},{3,1},{4,2},{5,3},{6,4},{7,5},{10,8},{11,9},{12,10},{13,11},... | collective-permute-start | bytes 3145736 | tf_op jit(solution)/shard_map/ppermute | solution.py:353
  358.8 21.7 %collective-permute-start.56 = (f32[128,8,256]{2,1,0:T(8,128)}, f32[128,8,256]{2,1,0:T(8,128)S(1)}, u32[]{:S(2)}, u32[]{:S(2)}) collective-permute-start(f32[128,8,256]{2,1,0:T(8,128)} %get-tuple-element.404), channel_id=1, source_target_pairs={{1,3},{3,5},{5,7},{9,11},{11,13},{13,15},{17,19},{19,21},{21,23},{... | collective-permute-start | bytes 3145736 | tf_op jit(solution)/shard_map/ppermute | solution.py:356
  365.1 21.8 %collective-permute-start.57 = (f32[128,8,256]{2,1,0:T(8,128)}, f32[128,8,256]{2,1,0:T(8,128)S(1)}, u32[]{:S(2)}, u32[]{:S(2)}) collective-permute-start(f32[128,8,256]{2,1,0:T(8,128)} %turn.27), channel_id=1, source_target_pairs={{0,1},{1,0},{2,3},{3,2},{4,5},{5,4},{6,7},{7,6},{8,9},{9,8},{10,11... | collective-permute-start | bytes 3145736 | tf_op jit(solution)/shard_map/ppermute | solution.py:359
  370.8 23.4 %collective-permute-start.59 = (f32[128,8,256]{2,1,0:T(8,128)S(1)}, f32[128,8,256]{2,1,0:T(8,128)}, u32[]{:S(2)}, u32[]{:S(2)}) collective-permute-start(f32[128,8,256]{2,1,0:T(8,128)S(1)} %pad_maximum_fusion.2.refs_1_), channel_id=1, source_target_pairs={{2,0},{3,1},{4,2},{5,3},{6,4},{7,5},{10,8},{11,9},{12,10},{13,11},... | collective-permute-start | bytes 3145736 | tf_op jit(solution)/shard_map/ppermute | solution.py:353
  380.5 22.5 %collective-permute-start.60 = (f32[128,8,256]{2,1,0:T(8,128)}, f32[128,8,256]{2,1,0:T(8,128)S(1)}, u32[]{:S(2)}, u32[]{:S(2)}) collective-permute-start(f32[128,8,256]{2,1,0:T(8,128)} %get-tuple-element.418), channel_id=1, source_target_pairs={{1,3},{3,5},{5,7},{9,11},{11,13},{13,15},{17,19},{19,21},{21,23},{... | collective-permute-start | bytes 3145736 | tf_op jit(solution)/shard_map/ppermute | solution.py:356
  386.9 22.4 %collective-permute-start.61 = (f32[128,8,256]{2,1,0:T(8,128)}, f32[128,8,256]{2,1,0:T(8,128)S(1)}, u32[]{:S(2)}, u32[]{:S(2)}) collective-permute-start(f32[128,8,256]{2,1,0:T(8,128)} %turn.28), channel_id=1, source_target_pairs={{0,1},{1,0},{2,3},{3,2},{4,5},{5,4},{6,7},{7,6},{8,9},{9,8},{10,11... | collective-permute-start | bytes 3145736 | tf_op jit(solution)/shard_map/ppermute | solution.py:359
  391.1 22.3 %collective-permute-start.58 = (f32[128,8,256]{2,1,0:T(8,128)S(1)}, f32[128,8,256]{2,1,0:T(8,128)S(1)}, u32[]{:S(2)}, u32[]{:S(2)}) collective-permute-start(f32[128,8,256]{2,1,0:T(8,128)S(1)} %pad_maximum_fusion.1.refs_1_), channel_id=1, source_target_pairs={{0,16},{8,24},{16,0},{24,8},{1,17},{9,25},{17,1},{25,9},{2,18},{10... | collective-permute-start | bytes 3145736 | tf_op jit(solution)/shard_map/ppermute | solution.py:347
  392.3 23.7 %collective-permute-start.62 = (f32[128,8,256]{2,1,0:T(8,128)S(1)}, f32[128,8,256]{2,1,0:T(8,128)}, u32[]{:S(2)}, u32[]{:S(2)}) collective-permute-start(f32[128,8,256]{2,1,0:T(8,128)S(1)} %pad_maximum_fusion.1.refs_1_), channel_id=1, source_target_pairs={{2,0},{3,1},{4,2},{5,3},{6,4},{7,5},{10,8},{11,9},{12,10},{13,11},... | collective-permute-start | bytes 3145736 | tf_op jit(solution)/shard_map/ppermute | solution.py:353
  403.0 23.2 %collective-permute-start.63 = (f32[128,8,256]{2,1,0:T(8,128)}, f32[128,8,256]{2,1,0:T(8,128)S(1)}, u32[]{:S(2)}, u32[]{:S(2)}) collective-permute-start(f32[128,8,256]{2,1,0:T(8,128)} %get-tuple-element.432), channel_id=1, source_target_pairs={{1,3},{3,5},{5,7},{9,11},{11,13},{13,15},{17,19},{19,21},{21,23},{... | collective-permute-start | bytes 3145736 | tf_op jit(solution)/shard_map/ppermute | solution.py:356
  409.3 21.6 %collective-permute-start.65 = (f32[128,8,256]{2,1,0:T(8,128)}, f32[128,8,256]{2,1,0:T(8,128)S(1)}, u32[]{:S(2)}, u32[]{:S(2)}) collective-permute-start(f32[128,8,256]{2,1,0:T(8,128)} %turn.29), channel_id=1, source_target_pairs={{0,1},{1,0},{2,3},{3,2},{4,5},{5,4},{6,7},{7,6},{8,9},{9,8},{10,11... | collective-permute-start | bytes 3145736 | tf_op jit(solution)/shard_map/ppermute | solution.py:359
  435.0 46.3 %collective-permute-start.68 = (f32[64,112,256]{2,1,0:T(8,128)}, f32[64,112,256]{2,1,0:T(8,128)S(1)}, u32[]{:S(2)}, u32[]{:S(2)}) collective-permute-start(f32[64,112,256]{2,1,0:T(8,128)} %get-tuple-element.443), channel_id=1, source_target_pairs={{0,8},{8,0},{16,24},{24,16},{1,9},{9,1},{17,25},{25,17},{2,10},{10... | collective-permute-start | bytes 22020104 | tf_op jit(solution)/shard_map/ppermute | solution.py:350
  448.1 27.0 %collective-permute-start.64 = (f32[128,8,256]{2,1,0:T(8,128)}, f32[128,8,256]{2,1,0:T(8,128)}, u32[]{:S(2)}, u32[]{:S(2)}) collective-permute-start(f32[128,8,256]{2,1,0:T(8,128)} %get-tuple-element.433), channel_id=1, source_target_pairs={{1,3},{3,5},{5,7},{9,11},{11,13},{13,15},{17,19},{19,21},{21,23},{... | collective-permute-start | bytes 3145736 | tf_op jit(solution)/shard_map/ppermute | solution.py:356
  450.6 26.9 %collective-permute-start.66 = (f32[128,8,256]{2,1,0:T(8,128)}, f32[128,8,256]{2,1,0:T(8,128)}, u32[]{:S(2)}, u32[]{:S(2)}) collective-permute-start(f32[128,8,256]{2,1,0:T(8,128)} %turn.31), channel_id=1, source_target_pairs={{0,1},{1,0},{2,3},{3,2},{4,5},{5,4},{6,7},{7,6},{8,9},{9,8},{10,11... | collective-permute-start | bytes 3145736 | tf_op jit(solution)/shard_map/ppermute | solution.py:359
  477.4 24.2 %collective-permute-start.67 = (f32[128,8,256]{2,1,0:T(8,128)}, f32[128,8,256]{2,1,0:T(8,128)}, u32[]{:S(2)}, u32[]{:S(2)}) collective-permute-start(f32[128,8,256]{2,1,0:T(8,128)} %turn.30), channel_id=1, source_target_pairs={{0,1},{1,0},{2,3},{3,2},{4,5},{5,4},{6,7},{7,6},{8,9},{9,8},{10,11... | collective-permute-start | bytes 3145736 | tf_op jit(solution)/shard_map/ppermute | solution.py:359
  480.5 25.9 %collective-permute-start.70 = (f32[64,8,256]{2,1,0:T(8,128)}, f32[64,8,256]{2,1,0:T(8,128)S(1)}, u32[]{:S(2)}, u32[]{:S(2)}) collective-permute-start(f32[64,8,256]{2,1,0:T(8,128)} %get-tuple-element.449), channel_id=1, source_target_pairs={{0,8},{8,0},{16,24},{24,16},{1,9},{9,1},{17,25},{25,17},{2,10},{10... | collective-permute-start | bytes 1572872 | tf_op jit(solution)/shard_map/ppermute | solution.py:350
  (69 other events, 678.2 us)
